TPU v7x, 32 devices: a whole 2x2x4 slice. The times are simulated.
32 devices in a mesh: gx: 4 (over y, x), gy: 2 (over core), gz: 4 (over z).
Axes of the slice: x: 2, y: 2, z: 4, core: 2. Of those that a mesh axis runs over, the one named last changes fastest.
Arguments:
- load_vector: float32 [32, 32, 2048], P(('gx', 'gy', 'gz')), may hold values from -24 to 24
- matrix_tiles: float32 [512, 7, 128, 128], P(('gx', 'gy', 'gz')), may hold values from -1 to 6, as said below
- tile_cols: int32 [512, 7], P(('gx', 'gy', 'gz')), may hold values from 0 to 15, as said below
- interior_inv: float32 [384, 128, 128], P(('gx', 'gy', 'gz')), may hold values from -0.1 to 0.3, as said below
- schur_inv: float32 [32, 512, 512], P(('gx', 'gy', 'gz')), may hold values from -0.1 to 0.3, as said below
- coarse_basis: float32 [32, 128, 2048], P(('gx', 'gy', 'gz')), may hold values from -0.125 to 0.125
- coarse_inv: float32 [32, 256, 256], P(('gx', 'gy', 'gz')), may hold values from -0.2 to 0.8, as said below
- row_map: int32 [32, 4, 128], P(('gx', 'gy', 'gz')), may hold values from 0 to 127, each once within a row
- face_link: int32 [32, 4], P(('gx', 'gy', 'gz')), may hold values from 0 to 1, as said below
- coarse_id: int32 [32, 4], P(('gx', 'gy', 'gz')), may hold values from 0 to 31, as said below
Outputs:
- solution: float32 [32, 32, 2048], P(('gx', 'gy', 'gz'))
- residual: float32 [32, 32, 2048], P(('gx', 'gy', 'gz'))
Inputs may be any that keep to these rules, and one draw needn't show every extreme that they name: `matrix_tiles`: tile 0 of each block row is its diagonal tile; each subdomain's matrix is symmetric positive definite: the tile of block row i in column block j is the transpose of the tile of block row j in column block i. `tile_cols`: tile 0 of block row i sits in column block i; tiles 1 to 6 sit in column blocks i + a, i - a, i + b, i - b, i + c, i - c modulo 16, for three distinct offsets a, b, c of that subdomain between 1 and (15) // 2; every column block holds exactly 7 tiles. `interior_inv`: each block is symmetric positive definite. `schur_inv`: symmetric positive definite. `coarse_inv`: symmetric positive definite. For partners d and e of round r, entry k of row_map[d, r] and of row_map[e, r] name the same shared unknown. `face_link`: equal for the two partners of a round. coarse_id = owner * 8 + slot, owner being a gz index within the subdomain's line of 4 devices; blocks with the same target are summed. Each subdomain sends at most 2 blocks to one owner and exactly 2 to some owner.
All inputs are finite; a program needn't handle non-finite values.
Results may differ from a plain program's by a relative error of at most 0.00018.
Values sent between devices are 32-bit elements; how exact they have to be, the bound alone decides.
No kernel may reach another device: no remote copies, remote signals or barrier semaphores. Data moves between devices by JAX's collectives and lax.ppermute only.
A program may use at most 64 MiB of HBM per device.

v0:
```python
import jax
import jax.numpy as jnp
from jax import lax
from jax.sharding import PartitionSpec as P

BS = 128
NIN = 12
NRHS = 32
CW = 32
CB = 4
OCAP = 8
ITERS = 2
NB = 16
NL = 2048


HIGH = lax.Precision.HIGHEST


def partner(value, axis, distance):
    return lax.ppermute(value, axis, [(i, i ^ 1 << distance) for i in range(lax.axis_size(axis))])


def on_device(
    load_vector,
    matrix_tiles,
    tile_cols,
    interior_inv,
    schur_inv,
    coarse_basis,
    coarse_inv,
    row_map,
    face_link,
    coarse_id,
):
    load_rows = load_vector[0]
    link_vals = face_link[0]
    face_maps = row_map[0]
    basis_rows = coarse_basis[0]
    schur_mat = schur_inv[0]
    coarse_mat = coarse_inv[0]
    block_ids = coarse_id[0]
    offset = NIN * BS
    line_size = lax.axis_size("gz")
    depth_z = line_size.bit_length() - 1
    depth_y = lax.axis_size("gy").bit_length() - 1
    swap_bits = [0, 1, depth_z, depth_z + depth_y]
    link_float = link_vals.astype(jnp.float32)
    weight = jnp.concatenate(
        [jnp.ones((offset,), jnp.float32)]
        + [jnp.broadcast_to(1.0 - 0.5 * link_float[round_no], (BS,)) for round_no in range(4)]
    )
    lane_ids = jnp.arange(BS, dtype=jnp.int32)
    onehots = [
        (face_maps[round_no][:, None] == lane_ids[None, :]).astype(jnp.float32)
        for round_no in range(4)
    ]

    def assemble(vector):
        outgoing = []
        for round_no in range(4):
            face_rows = vector[:, offset + round_no * BS : offset + (round_no + 1) * BS]
            outgoing.append(jnp.einsum("nj,kj->nk", face_rows, onehots[round_no], precision=HIGH))
        pieces = [vector[:, :offset]]
        for round_no in range(4):
            incoming = partner(outgoing[round_no], ("gx", "gy", "gz"), swap_bits[round_no])
            returned = jnp.dot(incoming, onehots[round_no], precision=HIGH)
            face_rows = vector[:, offset + round_no * BS : offset + (round_no + 1) * BS]
            pieces.append(face_rows + link_float[round_no] * returned)
        return jnp.concatenate(pieces, axis=1)

    group_rows = jnp.arange(line_size * OCAP, dtype=jnp.int32)
    dense_map = (group_rows[:, None] == block_ids[None, :]).astype(jnp.float32)

    def coarse_solve(summed):
        flat_rows = summed.reshape(OCAP * CW, NRHS)
        return jnp.dot(coarse_mat, flat_rows, precision=HIGH).reshape(OCAP, CW * NRHS)

    def coarse_part(contrib):
        summed = lax.psum_scatter(
            jnp.dot(dense_map, contrib, precision=HIGH), "gz", scatter_dimension=0, tiled=True
        )
        solved = coarse_solve(summed)
        all_solved = lax.all_gather(solved, "gz", axis=0, tiled=True)
        return jnp.einsum("ab,ac->bc", dense_map, all_solved, precision=HIGH)

    def precondition(resid):
        scaled = weight * resid
        inner_part = jnp.einsum(
            "bij,nbj->nbi", interior_inv, scaled[:, :offset].reshape(NRHS, NIN, BS), precision=HIGH
        ).reshape(NRHS, offset)
        outer_part = jnp.einsum("ij,nj->ni", schur_mat, scaled[:, offset:], precision=HIGH)
        contrib = jnp.einsum("cl,nl->cn", basis_rows, scaled, precision=HIGH).reshape(CB, CW * NRHS)
        coarse_back = coarse_part(contrib).reshape(CB * CW, NRHS)
        correction = jnp.einsum("cn,cl->nl", coarse_back, basis_rows, precision=HIGH)
        return assemble(weight * (jnp.concatenate([inner_part, outer_part], axis=1) + correction))

    def local_dot(left, right):
        return jnp.sum(weight * left * right, axis=1)

    resid = assemble(load_rows)
    solution = jnp.zeros_like(resid)
    precond_res = precondition(resid)

    def global_rz(left, right):
        return lax.psum(local_dot(left, right), ("gx", "gy", "gz"))

    direction = precond_res
    rho_now = global_rz(resid, precond_res)
    for turn_no in range(ITERS):
        picked = direction.reshape(NRHS, NB, BS)[:, tile_cols]
        product = jnp.einsum("rtij,nrtj->nri", matrix_tiles, picked, precision=HIGH).reshape(
            NRHS, NL
        )
        product_dir = assemble(product)
        curve_sum = lax.psum(local_dot(direction, product_dir), ("gx", "gy", "gz"))
        step_len = (rho_now / curve_sum)[:, None]
        solution = solution + step_len * direction
        resid = resid - step_len * product_dir
        if turn_no + 1 < ITERS:
            precond_res = precondition(resid)
            rho_next = global_rz(resid, precond_res)
            direction = precond_res + (rho_next / rho_now)[:, None] * direction
            rho_now = rho_next
    return (solution[None], resid[None])


def solution(mesh):
    in_specs = (
        P(("gx", "gy", "gz"), None, None),
        P(("gx", "gy", "gz"), None, None, None),
        P(("gx", "gy", "gz"), None),
        P(("gx", "gy", "gz"), None, None),
        P(("gx", "gy", "gz"), None, None),
        P(("gx", "gy", "gz"), None, None),
        P(("gx", "gy", "gz"), None, None),
        P(("gx", "gy", "gz"), None, None),
        P(("gx", "gy", "gz"), None),
        P(("gx", "gy", "gz"), None),
    )
    out_specs = (P(("gx", "gy", "gz"), None, None), P(("gx", "gy", "gz"), None, None))
    return jax.shard_map(
        on_device, mesh=mesh, in_specs=in_specs, out_specs=out_specs, check_vma=False
    )
```

profile of v0, /device:TPU:0, one launch (start us, length us, event | category | flops | bytes accessed | tf_op | source)
XLA Modules:
  0.0 299.2 jit_solution(18162430448153305590)
XLA Ops:
  8.1 0.9 convolution_bitcast_fusion.7
  9.0 3.1 %collective-permute-start = (f32[32,128]{0,1:T(8,128)S(1)}, f32[32,128]{0,1:T(8,128)S(1)}, u32[]{:S(2)}, u32[]{:S(2)}) collective-permute-start(f32[32,128]{0,1:T(8,128)S(1)} %convolution_bitcast_fusion.7), channel_id=1, source_target_pairs={{0,1},{1,0},{2,3},{3,2},{4,5},{5,4},{6,7},{7,6},{8,9},{9,8},{10,11... | collective-permute-start | bytes 49160 | tf_op jit(solution)/shard_map/ppermute | solution.py:21
  12.1 0.9 convolution_bitcast_fusion.6
  13.1 2.7 collective-permute-start.1
  15.7 0.9 convolution_bitcast_fusion.5
  16.8 0.9 convolution_bitcast_fusion.4
  17.7 1.6 collective-permute-start.3
  19.3 0.9 slice_dynamic-update-slice_fusion.4
  20.2 1.6 bitcast_dynamic-update-slice_fusion.2
  26.6 1.5 constant_dynamic-update-slice_fusion.4
  28.2 1.7 constant_dynamic-update-slice_fusion.3
  29.9 1.6 constant_dynamic-update-slice_fusion.2
  31.5 2.2 constant_dynamic-update-slice_fusion.1
  34.4 1.1 convolution_bitcast_fusion.11
  35.8 1.5 fusion.97
  39.1 1.3 convolution_bitcast_fusion.3
  40.5 1.0 fusion.28
  41.6 12.3 %reduce-scatter.3.cloned.1.call-done = f32[8,1024]{1,0:T(8,128)} async-done(((f32[32,1024]{1,0:T(8,128)}), f32[8,1024]{1,0:T(8,128)}) %reduce-scatter.3.cloned.1.call-update) | async-done | bytes 32784 | tf_op jit(solution)/shard_map/reduce_scatter | solution.py:80
  53.9 0.8 reshape.578
  55.3 13.4 %all_gather.6 = f32[32,1024]{1,0:T(8,128)S(1)} all-gather(f32[8,1024]{1,0:T(8,128)S(1)} %reshape.579), channel_id=1, replica_groups=mesh['gx'=4,'gy'=2,'gz'=4] {'gz'}, dimensions={0}, use_global_device_ids=true | all-gather | bytes 163840 | tf_op jit(solution)/shard_map/all_gather | solution.py:84
  71.4 1.3 collective-permute-start.5
  72.7 1.5 collective-permute-start.7
  76.1 0.9 constant_dynamic-update-slice_fusion.7
  79.5 9.9 %convolution_bitcast_fusion.1 = f32[16,4,8,128]{3,2,1,0:T(8,128)S(1)} fusion(f32[32,16,7,128]{3,0,2,1:T(8,128)S(1)} %bitcast.200, f32[16,7,128,128]{3,2,1,0:T(8,128)} %param.11), kind=kOutput, calls=%fused_computation.7 | convolution fusion | flops 704643072 | bytes 9437184 | tf_op jit(solution)/shard_map/rtij,nrtj->nri/dot_general | solution.py:112
  91.2 2.0 collective-permute-start.8
  94.0 1.6 collective-permute-start.11
  98.8 0.9 constant_dynamic-update-slice_fusion.11
  99.8 0.9 constant_dynamic-update-slice_fusion.10
  100.7 1.5 constant_dynamic-update-slice_fusion.9
  102.3 39.3 %all-reduce = (f32[32]{0:T(128)S(1)}, f32[32]{0:T(128)S(1)}) all-reduce(f32[32]{0:T(128)S(1)} %get-tuple-element.3, f32[32]{0:T(128)S(1)} %get-tuple-element.2), channel_id=1, replica_groups=mesh['gx'=4,'gy'=2,'gz'=4] {'gx','gy','gz'}, use_global_device_ids=true, to_apply=%region_2.0 | all-reduce | flops 64 | bytes 512 | tf_op jit(solution)/shard_map/psum | solution.py:106
  142.9 1.1 convolution_bitcast_fusion.10
  144.2 1.5 fusion.95
  147.6 1.3 constant_dynamic-update-slice_fusion.33
  148.9 1.3 convolution_bitcast_fusion.2
  150.3 1.0 fusion.26
  151.3 14.2 %reduce-scatter.5.cloned.1.call-done = f32[8,1024]{1,0:T(8,128)} async-done(((f32[32,1024]{1,0:T(8,128)}), f32[8,1024]{1,0:T(8,128)}) %reduce-scatter.5.cloned.1.call-update) | async-done | bytes 32784 | tf_op jit(solution)/shard_map/reduce_scatter | solution.py:80
  165.5 0.8 reshape.586
  167.0 13.3 %all_gather.7 = f32[32,1024]{1,0:T(8,128)S(1)} all-gather(f32[8,1024]{1,0:T(8,128)S(1)} %reshape.587), channel_id=1, replica_groups=mesh['gx'=4,'gy'=2,'gz'=4] {'gz'}, dimensions={0}, use_global_device_ids=true | all-gather | bytes 163840 | tf_op jit(solution)/shard_map/all_gather | solution.py:84
  182.3 1.3 collective-permute-start.13
  183.6 1.5 collective-permute-start.15
  187.0 0.9 constant_dynamic-update-slice_fusion.19
  190.5 40.7 %psum.30 = f32[32]{0:T(128)S(1)} all-reduce(f32[32]{0:T(128)S(1)} %multiply_reduce_fusion.1), channel_id=1, replica_groups=mesh['gx'=4,'gy'=2,'gz'=4] {'gx','gy','gz'}, use_global_device_ids=true, to_apply=%region_7.0 | all-reduce | flops 32 | bytes 256 | tf_op jit(solution)/shard_map/psum | solution.py:106
  232.0 9.9 %convolution_bitcast_fusion = f32[16,4,8,128]{3,2,1,0:T(8,128)S(1)} fusion(f32[32,16,7,128]{3,0,2,1:T(8,128)S(1)} %bitcast.199, f32[16,7,128,128]{3,2,1,0:T(8,128)} %param.11), kind=kOutput, calls=%fused_computation.6 | convolution fusion | flops 704643072 | bytes 9437184 | tf_op jit(solution)/shard_map/rtij,nrtj->nri/dot_general | solution.py:112
  243.2 2.1 collective-permute-start.17
  245.3 2.3 collective-permute-start.19
  248.4 0.9 constant_dynamic-update-slice_fusion.39
  251.3 40.0 %psum.31 = f32[32]{0:T(128)S(1)} all-reduce(f32[32]{0:T(128)S(1)} %multiply_reduce_fusion), channel_id=1, replica_groups=mesh['gx'=4,'gy'=2,'gz'=4] {'gx','gy','gz'}, use_global_device_ids=true, to_apply=%region_9.0 | all-reduce | flops 32 | bytes 256 | tf_op jit(solution)/shard_map/psum | solution.py:116
  291.3 1.0 multiply_subtract_fusion
  (198 shorter events, 34.4 us)
Async XLA Ops:
  7.2 27.2 %copy-start = (f32[1,128,2048]{2,1,0:T(8,128)S(1)}, f32[1,128,2048]{2,1,0:T(8,128)}, u32[]{:S(2)}) copy-start(f32[1,128,2048]{2,1,0:T(8,128)} %param.15) | copy-start | bytes 3145732
  7.2 46.7 %reduce-scatter.3.cloned.1.call-start = ((), (), s32[]{:S(2)}) async-start(), calls=%async_computation.2 | async-start | bytes 163840 | tf_op jit(solution)/shard_map/reduce_scatter | solution.py:80
  8.1 25.6 %copy-start.16 = (s32[128]{0:T(128)}, s32[128]{0:T(128)S(1)}, u32[]{:S(2)}) copy-start(s32[128]{0:T(128)S(1)} %get-tuple-element.9) | copy-start | bytes 1540
  8.1 25.6 %copy-start.20 = (s32[128]{0:T(128)}, s32[128]{0:T(128)S(1)}, u32[]{:S(2)}) copy-start(s32[128]{0:T(128)S(1)} %get-tuple-element.7) | copy-start | bytes 1540
  8.1 25.6 %copy-start.23 = (s32[128]{0:T(128)}, s32[128]{0:T(128)S(1)}, u32[]{:S(2)}) copy-start(s32[128]{0:T(128)S(1)} %get-tuple-element.8) | copy-start | bytes 1540
  9.0 17.6 %collective-permute-start = (f32[32,128]{0,1:T(8,128)S(1)}, f32[32,128]{0,1:T(8,128)S(1)}, u32[]{:S(2)}, u32[]{:S(2)}) collective-permute-start(f32[32,128]{0,1:T(8,128)S(1)} %convolution_bitcast_fusion.7), channel_id=1, source_target_pairs={{0,1},{1,0},{2,3},{3,2},{4,5},{5,4},{6,7},{7,6},{8,9},{9,8},{10,11... | collective-permute-start | bytes 49160 | tf_op jit(solution)/shard_map/ppermute | solution.py:21
  13.1 15.1 %collective-permute-start.1 = (f32[32,128]{0,1:T(8,128)S(1)}, f32[32,128]{0,1:T(8,128)S(1)}, u32[]{:S(2)}, u32[]{:S(2)}) collective-permute-start(f32[32,128]{0,1:T(8,128)S(1)} %convolution_bitcast_fusion.6), channel_id=1, source_target_pairs={{0,2},{1,3},{2,0},{3,1},{4,6},{5,7},{6,4},{7,5},{8,10},{9,11},{10,... | collective-permute-start | bytes 49160 | tf_op jit(solution)/shard_map/ppermute | solution.py:21
  16.7 13.2 %collective-permute-start.2 = (f32[32,128]{0,1:T(8,128)S(1)}, f32[32,128]{0,1:T(8,128)S(1)}, u32[]{:S(2)}, u32[]{:S(2)}) collective-permute-start(f32[32,128]{0,1:T(8,128)S(1)} %convolution_bitcast_fusion.5), channel_id=1, source_target_pairs={{0,4},{1,5},{2,6},{3,7},{4,0},{5,1},{6,2},{7,3},{8,12},{9,13},{10,... | collective-permute-start | bytes 49160 | tf_op jit(solution)/shard_map/ppermute | solution.py:21
  17.7 21.4 %copy-start.7 = (f32[12,128,128]{2,1,0:T(8,128)S(1)}, f32[12,128,128]{2,1,0:T(8,128)}, u32[]{:S(2)}) copy-start(f32[12,128,128]{2,1,0:T(8,128)} %param.13) | copy-start | bytes 2359300
  17.7 13.7 %collective-permute-start.3 = (f32[32,128]{0,1:T(8,128)S(1)}, f32[32,128]{0,1:T(8,128)S(1)}, u32[]{:S(2)}, u32[]{:S(2)}) collective-permute-start(f32[32,128]{0,1:T(8,128)S(1)} %convolution_bitcast_fusion.4), channel_id=1, source_target_pairs={{0,8},{1,9},{2,10},{3,11},{4,12},{5,13},{6,14},{7,15},{8,0},{9,1},... | collective-permute-start | bytes 49160 | tf_op jit(solution)/shard_map/ppermute | solution.py:21
  35.6 19.2 %copy-start.9 = (f32[1,256,256]{2,1,0:T(8,128)S(1)}, f32[1,256,256]{2,1,0:T(8,128)}, u32[]{:S(2)}) copy-start(f32[1,256,256]{2,1,0:T(8,128)} %param.16) | copy-start | bytes 786436
  37.3 128.2 %reduce-scatter.5.cloned.1.call-start = ((), (), s32[]{:S(2)}) async-start(), calls=%async_computation.3 | async-start | bytes 163840 | tf_op jit(solution)/shard_map/reduce_scatter | solution.py:80
  39.1 29.5 %copy-start.26 = (s32[1,4]{1,0:T(1,128)S(1)}, s32[1,4]{1,0:T(1,128)}, u32[]{:S(2)}) copy-start(s32[1,4]{1,0:T(1,128)} %param.19) | copy-start | bytes 52
  41.6 28.1 %copy-start.24 = (s32[128]{0:T(128)S(1)}, s32[128]{0:T(128)}, u32[]{:S(2)}) copy-start(s32[128]{0:T(128)} %copy-done.23) | copy-start | bytes 1540
  41.6 28.3 %copy-start.21 = (s32[128]{0:T(128)S(1)}, s32[128]{0:T(128)}, u32[]{:S(2)}) copy-start(s32[128]{0:T(128)} %copy-done.20) | copy-start | bytes 1540
  41.6 28.6 %copy-start.17 = (s32[128]{0:T(128)S(1)}, s32[128]{0:T(128)}, u32[]{:S(2)}) copy-start(s32[128]{0:T(128)} %copy-done.16) | copy-start | bytes 1540
  71.2 3.7 %collective-permute-start.4 = (f32[32,128]{1,0:T(8,128)S(1)}, f32[32,128]{1,0:T(8,128)S(1)}, u32[]{:S(2)}, u32[]{:S(2)}) collective-permute-start(f32[32,128]{1,0:T(8,128)S(1)} %fusion.53), channel_id=1, source_target_pairs={{0,1},{1,0},{2,3},{3,2},{4,5},{5,4},{6,7},{7,6},{8,9},{9,8},{10,11... | collective-permute-start | bytes 49160 | tf_op jit(solution)/shard_map/ppermute | solution.py:21
  71.4 4.7 %collective-permute-start.5 = (f32[32,128]{1,0:T(8,128)S(1)}, f32[32,128]{1,0:T(8,128)S(1)}, u32[]{:S(2)}, u32[]{:S(2)}) collective-permute-start(f32[32,128]{1,0:T(8,128)S(1)} %fusion.49), channel_id=1, source_target_pairs={{0,2},{1,3},{2,0},{3,1},{4,6},{5,7},{6,4},{7,5},{8,10},{9,11},{10,... | collective-permute-start | bytes 49160 | tf_op jit(solution)/shard_map/ppermute | solution.py:21
  72.7 4.3 %collective-permute-start.6 = (f32[32,128]{1,0:T(8,128)S(1)}, f32[32,128]{1,0:T(8,128)S(1)}, u32[]{:S(2)}, u32[]{:S(2)}) collective-permute-start(f32[32,128]{1,0:T(8,128)S(1)} %fusion.45), channel_id=1, source_target_pairs={{0,4},{1,5},{2,6},{3,7},{4,0},{5,1},{6,2},{7,3},{8,12},{9,13},{10,... | collective-permute-start | bytes 49160 | tf_op jit(solution)/shard_map/ppermute | solution.py:21
  72.7 5.2 %collective-permute-start.7 = (f32[32,128]{1,0:T(8,128)S(1)}, f32[32,128]{1,0:T(8,128)S(1)}, u32[]{:S(2)}, u32[]{:S(2)}) collective-permute-start(f32[32,128]{1,0:T(8,128)S(1)} %fusion.41), channel_id=1, source_target_pairs={{0,8},{1,9},{2,10},{3,11},{4,12},{5,13},{6,14},{7,15},{8,0},{9,1},... | collective-permute-start | bytes 49160 | tf_op jit(solution)/shard_map/ppermute | solution.py:21
  79.5 17.9 %copy-start.15 = (f32[32,128]{1,0:T(8,128)S(1)}, f32[32,128]{1,0:T(8,128)}, u32[]{:S(2)}) copy-start(f32[32,128]{1,0:T(8,128)} %get-tuple-element.23) | copy-start | bytes 49156
  89.4 12.8 %copy-start.6 = (f32[32,2048]{1,0:T(8,128)S(1)}, f32[32,2048]{1,0:T(8,128)}, u32[]{:S(2)}) copy-start(f32[32,2048]{1,0:T(8,128)} %copy-done.5) | copy-start | bytes 786436
  91.2 6.8 %collective-permute-start.8 = (f32[32,128]{1,0:T(8,128)S(1)}, f32[32,128]{1,0:T(8,128)S(1)}, u32[]{:S(2)}, u32[]{:S(2)}) collective-permute-start(f32[32,128]{1,0:T(8,128)S(1)} %fusion.52), channel_id=1, source_target_pairs={{0,1},{1,0},{2,3},{3,2},{4,5},{5,4},{6,7},{7,6},{8,9},{9,8},{10,11... | collective-permute-start | bytes 49160 | tf_op jit(solution)/shard_map/ppermute | solution.py:21
  93.2 5.6 %collective-permute-start.9 = (f32[32,128]{1,0:T(8,128)S(1)}, f32[32,128]{1,0:T(8,128)S(1)}, u32[]{:S(2)}, u32[]{:S(2)}) collective-permute-start(f32[32,128]{1,0:T(8,128)S(1)} %fusion.48), channel_id=1, source_target_pairs={{0,2},{1,3},{2,0},{3,1},{4,6},{5,7},{6,4},{7,5},{8,10},{9,11},{10,... | collective-permute-start | bytes 49160 | tf_op jit(solution)/shard_map/ppermute | solution.py:21
  94.0 5.7 %collective-permute-start.10 = (f32[32,128]{1,0:T(8,128)S(1)}, f32[32,128]{1,0:T(8,128)S(1)}, u32[]{:S(2)}, u32[]{:S(2)}) collective-permute-start(f32[32,128]{1,0:T(8,128)S(1)} %fusion.44), channel_id=1, source_target_pairs={{0,4},{1,5},{2,6},{3,7},{4,0},{5,1},{6,2},{7,3},{8,12},{9,13},{10,... | collective-permute-start | bytes 49160 | tf_op jit(solution)/shard_map/ppermute | solution.py:21
  94.0 6.7 %collective-permute-start.11 = (f32[32,128]{1,0:T(8,128)S(1)}, f32[32,128]{1,0:T(8,128)S(1)}, u32[]{:S(2)}, u32[]{:S(2)}) collective-permute-start(f32[32,128]{1,0:T(8,128)S(1)} %fusion.40), channel_id=1, source_target_pairs={{0,8},{1,9},{2,10},{3,11},{4,12},{5,13},{6,14},{7,15},{8,0},{9,1},... | collective-permute-start | bytes 49160 | tf_op jit(solution)/shard_map/ppermute | solution.py:21
  99.8 49.1 %copy-start.8 = (f32[12,128,128]{2,1,0:T(8,128)S(1)}, f32[12,128,128]{2,1,0:T(8,128)}, u32[]{:S(2)}) copy-start(f32[12,128,128]{2,1,0:T(8,128)} %param.13) | copy-start | bytes 2359300
  148.9 31.4 %copy-start.27 = (s32[1,4]{1,0:T(1,128)S(1)}, s32[1,4]{1,0:T(1,128)}, u32[]{:S(2)}) copy-start(s32[1,4]{1,0:T(1,128)} %param.19) | copy-start | bytes 52
  150.2 16.2 %copy-start.10 = (f32[1,256,256]{2,1,0:T(8,128)S(1)}, f32[1,256,256]{2,1,0:T(8,128)}, u32[]{:S(2)}) copy-start(f32[1,256,256]{2,1,0:T(8,128)} %param.16) | copy-start | bytes 786436
  151.3 30.0 %copy-start.25 = (s32[128]{0:T(128)S(1)}, s32[128]{0:T(128)}, u32[]{:S(2)}) copy-start(s32[128]{0:T(128)} %copy-done.23) | copy-start | bytes 1540
  151.3 30.2 %copy-start.22 = (s32[128]{0:T(128)S(1)}, s32[128]{0:T(128)}, u32[]{:S(2)}) copy-start(s32[128]{0:T(128)} %copy-done.20) | copy-start | bytes 1540
  151.3 30.5 %copy-start.19 = (s32[128]{0:T(128)S(1)}, s32[128]{0:T(128)}, u32[]{:S(2)}) copy-start(s32[128]{0:T(128)} %copy-done.16) | copy-start | bytes 1540
  180.3 50.8 %copy-start.31 = (f32[32]{0:T(128)S(1)}, f32[32]{0:T(128)}, u32[]{:S(2)}) copy-start(f32[32]{0:T(128)} %copy-done.30) | copy-start | bytes 388
  182.0 3.8 %collective-permute-start.12 = (f32[32,128]{1,0:T(8,128)S(1)}, f32[32,128]{1,0:T(8,128)S(1)}, u32[]{:S(2)}, u32[]{:S(2)}) collective-permute-start(f32[32,128]{1,0:T(8,128)S(1)} %fusion.51), channel_id=1, source_target_pairs={{0,1},{1,0},{2,3},{3,2},{4,5},{5,4},{6,7},{7,6},{8,9},{9,8},{10,11... | collective-permute-start | bytes 49160 | tf_op jit(solution)/shard_map/ppermute | solution.py:21
  182.3 4.7 %collective-permute-start.13 = (f32[32,128]{1,0:T(8,128)S(1)}, f32[32,128]{1,0:T(8,128)S(1)}, u32[]{:S(2)}, u32[]{:S(2)}) collective-permute-start(f32[32,128]{1,0:T(8,128)S(1)} %fusion.47), channel_id=1, source_target_pairs={{0,2},{1,3},{2,0},{3,1},{4,6},{5,7},{6,4},{7,5},{8,10},{9,11},{10,... | collective-permute-start | bytes 49160 | tf_op jit(solution)/shard_map/ppermute | solution.py:21
  183.6 4.3 %collective-permute-start.14 = (f32[32,128]{1,0:T(8,128)S(1)}, f32[32,128]{1,0:T(8,128)S(1)}, u32[]{:S(2)}, u32[]{:S(2)}) collective-permute-start(f32[32,128]{1,0:T(8,128)S(1)} %fusion.43), channel_id=1, source_target_pairs={{0,4},{1,5},{2,6},{3,7},{4,0},{5,1},{6,2},{7,3},{8,12},{9,13},{10,... | collective-permute-start | bytes 49160 | tf_op jit(solution)/shard_map/ppermute | solution.py:21
  183.6 5.2 %collective-permute-start.15 = (f32[32,128]{1,0:T(8,128)S(1)}, f32[32,128]{1,0:T(8,128)S(1)}, u32[]{:S(2)}, u32[]{:S(2)}) collective-permute-start(f32[32,128]{1,0:T(8,128)S(1)} %fusion.39), channel_id=1, source_target_pairs={{0,8},{1,9},{2,10},{3,11},{4,12},{5,13},{6,14},{7,15},{8,0},{9,1},... | collective-permute-start | bytes 49160 | tf_op jit(solution)/shard_map/ppermute | solution.py:21
  189.6 41.5 %copy-start.3 = (f32[32,2048]{1,0:T(8,128)}, f32[32,2048]{1,0:T(8,128)S(1)}, u32[]{:S(2)}) copy-start(f32[32,2048]{1,0:T(8,128)S(1)} %get-tuple-element.46) | copy-start | bytes 786436
  232.0 15.5 %copy-start.14 = (f32[1,32,2048]{2,1,0:T(8,128)S(1)}, f32[1,32,2048]{2,1,0:T(8,128)}, u32[]{:S(2)}) copy-start(f32[1,32,2048]{2,1,0:T(8,128)} %bitcast_dynamic-update-slice_fusion.3) | copy-start | bytes 786436
  242.0 49.3 %copy-start.33 = (f32[32]{0:T(128)S(1)}, f32[32]{0:T(128)}, u32[]{:S(2)}) copy-start(f32[32]{0:T(128)} %copy-done.32) | copy-start | bytes 388
  242.0 49.3 %copy-start.11 = (f32[1,32,2048]{2,1,0:T(8,128)S(1)}, f32[1,32,2048]{2,1,0:T(8,128)}, u32[]{:S(2)}) copy-start(f32[1,32,2048]{2,1,0:T(8,128)} %constant_dynamic-update-slice_fusion.33) | copy-start | bytes 786436
  242.0 49.3 %copy-start.12 = (f32[1,32,2048]{2,1,0:T(8,128)S(1)}, f32[1,32,2048]{2,1,0:T(8,128)}, u32[]{:S(2)}) copy-start(f32[1,32,2048]{2,1,0:T(8,128)} %get-tuple-element.57) | copy-start | bytes 786436
  242.0 49.3 %copy-start.13 = (f32[1,32,2048]{2,1,0:T(8,128)S(1)}, f32[1,32,2048]{2,1,0:T(8,128)}, u32[]{:S(2)}) copy-start(f32[1,32,2048]{2,1,0:T(8,128)} %get-tuple-element.56) | copy-start | bytes 786436
  242.0 49.3 %copy-start.29 = (f32[32]{0:T(128)S(1)}, f32[32]{0:T(128)}, u32[]{:S(2)}) copy-start(f32[32]{0:T(128)} %copy-done.28) | copy-start | bytes 388
  243.1 4.5 %collective-permute-start.16 = (f32[32,128]{1,0:T(8,128)S(1)}, f32[32,128]{1,0:T(8,128)S(1)}, u32[]{:S(2)}, u32[]{:S(2)}) collective-permute-start(f32[32,128]{1,0:T(8,128)S(1)} %fusion.50), channel_id=1, source_target_pairs={{0,1},{1,0},{2,3},{3,2},{4,5},{5,4},{6,7},{7,6},{8,9},{9,8},{10,11... | collective-permute-start | bytes 49160 | tf_op jit(solution)/shard_map/ppermute | solution.py:21
  243.2 5.2 %collective-permute-start.17 = (f32[32,128]{1,0:T(8,128)S(1)}, f32[32,128]{1,0:T(8,128)S(1)}, u32[]{:S(2)}, u32[]{:S(2)}) collective-permute-start(f32[32,128]{1,0:T(8,128)S(1)} %fusion.46), channel_id=1, source_target_pairs={{0,2},{1,3},{2,0},{3,1},{4,6},{5,7},{6,4},{7,5},{8,10},{9,11},{10,... | collective-permute-start | bytes 49160 | tf_op jit(solution)/shard_map/ppermute | solution.py:21
  245.3 4.0 %collective-permute-start.18 = (f32[32,128]{1,0:T(8,128)S(1)}, f32[32,128]{1,0:T(8,128)S(1)}, u32[]{:S(2)}, u32[]{:S(2)}) collective-permute-start(f32[32,128]{1,0:T(8,128)S(1)} %fusion.42), channel_id=1, source_target_pairs={{0,4},{1,5},{2,6},{3,7},{4,0},{5,1},{6,2},{7,3},{8,12},{9,13},{10,... | collective-permute-start | bytes 49160 | tf_op jit(solution)/shard_map/ppermute | solution.py:21
  245.3 4.9 %collective-permute-start.19 = (f32[32,128]{1,0:T(8,128)S(1)}, f32[32,128]{1,0:T(8,128)S(1)}, u32[]{:S(2)}, u32[]{:S(2)}) collective-permute-start(f32[32,128]{1,0:T(8,128)S(1)} %fusion.38), channel_id=1, source_target_pairs={{0,8},{1,9},{2,10},{3,11},{4,12},{5,13},{6,14},{7,15},{8,0},{9,1},... | collective-permute-start | bytes 49160 | tf_op jit(solution)/shard_map/ppermute | solution.py:21
  (8 other events, 35.6 us)
Sparse Core Ops, SparseCore 0:
  37.4 16.4 reduce-scatter.2
  145.9 19.6 reduce-scatter.4
where the time goes:
time: 300 us; the launch traced here: 299 us
  blocking collectives  147 us (49%)
  matrix products  60.6 us (20%)
  waiting for transfers between devices  28.8 us (10%)
  starting transfers between devices  22 us (7%)
  local copies, waits for them, and re-layouts  20.4 us (7%)
  between operations  17.6 us (6%)
  other arithmetic  3.1 us (1%)
    psum x2, blocking collectives, global_rz(): return lax.psum(local_dot(left, right), ('gx', 'gy', 'gz'))  80 us
    psum x1, blocking collectives, on_device(): curve_sum = lax.psum(local_dot(direction, product_dir), ('gx', 'gy', 'gz'))  40 us
    all_gather x2, blocking collectives, coarse_part(): all_solved = lax.all_gather(solved, 'gz', axis=0, tiled=True)  26.7 us
    reduce_scatter x2, waiting for transfers between devices, coarse_part(): lax.psum_scatter(jnp.dot(dense_map, contrib, precision=HIGH), 'gz', scatt...  26.5 us
    ppermute x20, starting transfers between devices, partner(): lax.ppermute(value, axis, [(i, i ^ 1 << distance) for i in range(lax.axis...  21.9 us
    dot_general x20, matrix products, assemble(): returned = jnp.dot(incoming, onehots[round_no], precision=HIGH)  21 us
    dot_general x2, matrix products, on_device(): jnp.einsum('rtij,nrtj->nri', matrix_tiles, picked, precision=HIGH)  19.8 us
    unnamed x97, local copies, waits for them, and re-layouts  12.5 us
  transfers between devices with their start and end apart: 22, of which 6 were waited for; matrix products, arithmetic and copies ran while one was open for 12% of the time, Pallas kernels for 0%

commit v1 on v0

v1 whole, which is shorter than its diff:
```python
import jax
import jax.numpy as jnp
from jax import lax
from jax.experimental import pallas as pl
from jax.experimental.pallas import tpu as pltpu
from jax.sharding import PartitionSpec as P

BS = 128
NIN = 12
NF = 4
NRHS = 32
CW = 32
CB = 4
OCAP = 8
NB = 16
TPR = 7
NL = 2048
AXES = ("gx", "gy", "gz")
F32 = jnp.float32
BF16 = jnp.bfloat16
NN = (((1,), (0,)), ((), ()))
NT = (((1,), (1,)), ((), ()))


def mm(left, right, dims=NN):
    return lax.dot_general(left, right, dims, preferred_element_type=F32)


def halves(value):
    high = value.astype(BF16)
    return high, (value - high.astype(F32)).astype(BF16)


def dot_halves(left, right, dims=NN):
    (lh, ll), (rh, rl) = left, right
    rows = lh.shape[0]
    both = mm(jnp.concatenate([lh, ll], axis=0), rh, dims)
    return both[:rows] + both[rows:] + mm(lh, rl, dims)


def select_lanes(value, onehot):
    rows = value.shape[0]
    high, rest = halves(value)
    low = (value - high.astype(F32) - rest.astype(F32)).astype(BF16)
    out = mm(jnp.concatenate([high, rest, low], axis=0), onehot)
    return out[:rows] + out[rows : 2 * rows] + out[2 * rows :]


def lanes(block):
    return slice(block * BS, (block + 1) * BS)


def weight_of(link_ref, face):
    return 1.0 - 0.5 * link_ref[0, face].astype(F32)


def interior_body(x_ref, inv_ref, basis_ref, inner_ref, part_ref, *, flat):
    pieces = []
    for b in range(NIN):
        xb = halves(x_ref[:, lanes(b)] if flat else x_ref[b])
        pieces.append(xb)
        inner_ref[b] = dot_halves(xb, halves(inv_ref[b]))
    cat = tuple(jnp.concatenate([p[h] for p in pieces], axis=1) for h in range(2))
    part_ref[...] = dot_halves(cat, halves(basis_ref[:, : NIN * BS]), NT)


def face_solve(faces, link_ref, schur_ref, basis_ref, part_ref, outer_ref, contrib_ref):
    scaled = halves(
        jnp.concatenate([faces[r] * weight_of(link_ref, r) for r in range(NF)], axis=1)
    )
    outer = dot_halves(scaled, halves(schur_ref[...]))
    for r in range(NF):
        outer_ref[r] = outer[:, lanes(r)]
    contrib_ref[...] = part_ref[...] + dot_halves(
        scaled, halves(basis_ref[:, NIN * BS :]), NT
    )


def first_faces_body(
    x_ref, in0, in1, in2, in3, map_ref, link_ref, schur_ref, basis_ref, part_ref,
    face_ref, outer_ref, contrib_ref, swap_ref,
):
    faces = []
    rows = lax.broadcasted_iota(jnp.int32, (BS, BS), 0).astype(F32)
    for r, inc in enumerate((in0, in1, in2, in3)):
        mine = (rows == map_ref[r : r + 1, :].astype(F32)).astype(F32).astype(BF16)
        theirs = (rows == inc[NRHS : NRHS + 1, :]).astype(F32).astype(BF16)
        link = link_ref[0, r].astype(F32)
        swap_ref[r] = mm(mine, theirs, NT).astype(BF16)
        came = select_lanes(inc[:NRHS, :], mm(theirs, mine, NT).astype(BF16))
        faces.append(x_ref[:, lanes(NIN + r)] + link * came)
        face_ref[r] = faces[-1]
    face_solve(faces, link_ref, schur_ref, basis_ref, part_ref, outer_ref, contrib_ref)


def next_faces_body(
    y_ref, in0, in1, in2, in3, link_ref, schur_ref, basis_ref, part_ref,
    face_ref, outer_ref, contrib_ref,
):
    faces = []
    for r, inc in enumerate((in0, in1, in2, in3)):
        faces.append(y_ref[NIN + r] + inc[...])
        face_ref[r] = faces[-1]
    face_solve(faces, link_ref, schur_ref, basis_ref, part_ref, outer_ref, contrib_ref)


def send_face(value, face, link_ref, swap_ref, out_ref):
    out_ref[...] = select_lanes(value, swap_ref[face]) * link_ref[0, face].astype(F32)


def correct(contribs, table, outer_ref, basis_ref, link_ref, swap_ref, back_ref, face_ref, outs):
    back = dot_halves(halves(jnp.concatenate(contribs, axis=1)), table, NT)
    back_ref[...] = back
    corr = dot_halves(halves(back), halves(basis_ref[:, NIN * BS :]))
    for r in range(NF):
        value = weight_of(link_ref, r) * (outer_ref[r] + corr[:, lanes(r)])
        face_ref[r] = value
        send_face(value, r, link_ref, swap_ref, outs[r])


def first_coarse_body(*refs, line):
    target_ref, coarse_ref, id_ref, own_ref = refs[:4]
    others = refs[4 : 3 + line]
    outer_ref, basis_ref, link_ref, swap_ref = refs[3 + line : 7 + line]
    high_ref, low_ref, back_ref, face_ref = refs[7 + line : 11 + line]
    outs = refs[11 + line :]
    targets = jnp.concatenate([target_ref[0:1, :]] + [o[NRHS : NRHS + 1, :] for o in others], axis=1)
    width = line * CB * CW
    rows = lax.broadcasted_iota(jnp.int32, (OCAP * CW, width), 0)
    for b in range(CB):
        block = id_ref[0, b]
        owner = block // OCAP
        start = pl.multiple_of((block % OCAP) * CW, CW)
        picked = (
            (rows + owner * (OCAP * CW)).astype(F32) == targets
        ).astype(F32).astype(BF16)
        high, low = halves(coarse_ref[owner, pl.ds(start, CW), :])
        both = mm(jnp.concatenate([high, low], axis=0), picked)
        high_ref[b * CW : (b + 1) * CW, :] = both[:CW].astype(BF16)
        low_ref[b * CW : (b + 1) * CW, :] = both[CW:].astype(BF16)
    contribs = [own_ref[...]] + [o[:NRHS, :] for o in others]
    correct(contribs, (high_ref[...], low_ref[...]), outer_ref, basis_ref, link_ref, swap_ref,
            back_ref, face_ref, outs)


def next_coarse_body(*refs, line):
    contribs = [ref[...] for ref in refs[:line]]
    high_ref, low_ref, outer_ref, basis_ref, link_ref, swap_ref = refs[line : 6 + line]
    back_ref, face_ref = refs[6 + line : 8 + line]
    correct(contribs, (high_ref[...], low_ref[...]), outer_ref, basis_ref, link_ref, swap_ref,
            back_ref, face_ref, refs[8 + line :])


def add_row(x, i, tiles_ref, cols_ref, acc_ref, base):
    wide = jnp.concatenate([tiles_ref[(i - base) * TPR + t] for t in range(TPR)], axis=1)
    out = dot_halves(halves(x), halves(wide))
    places = [cols_ref[i, t] for t in range(TPR)]
    before = [acc_ref[place] for place in places]
    for t in range(TPR):
        acc_ref[places[t]] = before[t] + out[:, lanes(t)]


def own_apply_body(inner_ref, back_ref, basis_ref, face_ref, tiles_ref, cols_ref, z_ref, acc_ref):
    acc_ref[...] = jnp.zeros_like(acc_ref)
    back = halves(back_ref[...])
    for b in range(NIN):
        z_ref[b] = inner_ref[b] + dot_halves(back, halves(basis_ref[:, lanes(b)]))
    for i in range(NB):
        x = z_ref[i] if i < NIN else face_ref[i - NIN]
        add_row(x, i, tiles_ref, cols_ref, acc_ref, 0)


def face_apply_body(
    acc_ref, in0, in1, in2, in3, face_ref, tiles_ref, cols_ref, link_ref, swap_ref,
    y_ref, z_ref, out0, out1, out2, out3,
):
    y_ref[...] = acc_ref[...]
    for r, inc in enumerate((in0, in1, in2, in3)):
        came = inc[...]
        z_ref[r] = face_ref[r] + came
        add_row(came, NIN + r, tiles_ref, cols_ref, y_ref, 0)
    for r, out in enumerate((out0, out1, out2, out3)):
        send_face(y_ref[NIN + r], r, link_ref, swap_ref, out)


def dots_body(load_ref, zi_ref, zf_ref, y_ref, wi_ref, wf_ref, v_ref, out_ref):
    sums = [jnp.zeros((NRHS, BS), F32) for _ in range(6)]
    for b in range(NB):
        load = load_ref[:, lanes(b)]
        z = zi_ref[b] if b < NIN else zf_ref[b - NIN]
        w = wi_ref[b] if b < NIN else wf_ref[b - NIN]
        y, v = y_ref[b], v_ref[b]
        for k, (left, right) in enumerate(((load, z), (z, y), (load, w), (y, w), (z, v), (w, v))):
            sums[k] = sums[k] + left * right
    place = lax.broadcasted_iota(jnp.int32, (NRHS, BS), 1)
    case = lax.broadcasted_iota(jnp.int32, (NRHS, BS), 0)
    for row in range(2):
        total = jnp.zeros((NRHS, BS), F32)
        for k in range(4 * row, min(4 * row + 4, 6)):
            column = jnp.sum(sums[k], axis=1, keepdims=True)
            total = total + jnp.where(place == case + NRHS * (k % 4), column, 0.0)
        out_ref[row : row + 1, :] = jnp.sum(total, axis=0, keepdims=True)


def final_body(
    coef_ref, load_ref, rf_ref, zi_ref, zf_ref, y_ref, qf_ref, wi_ref, wf_ref, v_ref,
    in0, in1, in2, in3, sol_ref, res_ref,
):
    first = coef_ref[:, 0:1]
    second = coef_ref[:, 1:2]
    for b in range(NB):
        if b < NIN:
            r, z, q, w, v = load_ref[:, lanes(b)], zi_ref[b], y_ref[b], wi_ref[b], v_ref[b]
        else:
            f = b - NIN
            v = v_ref[b] + (in0, in1, in2, in3)[f][...]
            r, z, q, w = rf_ref[f], zf_ref[f], qf_ref[f], wf_ref[f]
        sol_ref[0, :, lanes(b)] = first * z - second * w
        res_ref[0, :, lanes(b)] = r - first * q + second * v


def f32(*shape):
    return jax.ShapeDtypeStruct(shape, F32)


def bf16(*shape):
    return jax.ShapeDtypeStruct(shape, BF16)


SMEM = pl.BlockSpec(memory_space=pltpu.SMEM)
VMEM = pl.BlockSpec(memory_space=pltpu.VMEM)


def call(body, name, outs, specs, *args):
    return pl.pallas_call(
        body,
        name=name,
        out_shape=outs,
        in_specs=specs,
        out_specs=[VMEM] * len(outs),
        compiler_params=pltpu.CompilerParams(vmem_limit_bytes=40 << 20),
    )(*args)


def on_device(
    load_vector, matrix_tiles, tile_cols, interior_inv, schur_inv, coarse_basis, coarse_inv,
    row_map, face_link, coarse_id,
):
    load = load_vector[0]
    basis = coarse_basis[0]
    schur = schur_inv[0]
    maps = row_map[0]
    tiles = matrix_tiles.reshape(NB * TPR, BS, BS)
    line = lax.axis_size("gz")
    devices = line * lax.axis_size("gy") * lax.axis_size("gx")
    depth_z = line.bit_length() - 1
    depth_y = lax.axis_size("gy").bit_length() - 1
    masks = [1, 2, 1 << depth_z, 1 << (depth_z + depth_y)]

    def trade(value, mask):
        return lax.ppermute(value, AXES, [(i, i ^ mask) for i in range(devices)])

    def trade_faces(faces):
        return [trade(face, mask) for face, mask in zip(faces, masks)]

    def trade_line(value):
        return [trade(value, mask) for mask in range(1, line)]

    coarse_all = lax.all_gather(coarse_inv[0], "gz", axis=0)
    pad = jnp.zeros((7, BS), F32)
    came = trade_faces(
        [
            jnp.concatenate([load[:, lanes(NIN + r)], maps[r : r + 1].astype(F32), pad], axis=0)
            for r in range(NF)
        ]
    )
    block = f32(NIN, NRHS, BS)
    face = f32(NF, NRHS, BS)
    small = f32(NRHS, BS)
    inner, part = call(
        lambda *refs: interior_body(*refs, flat=True), "interior_load", [block, small], [VMEM] * 3,
        load, interior_inv, basis,
    )
    r_face, outer, contrib, swap = call(
        first_faces_body, "faces_load", [face, face, small, bf16(NF, BS, BS)],
        [VMEM] * 6 + [SMEM] + [VMEM] * 3,
        load, *came, maps, face_link, schur, basis, part,
    )
    target = (coarse_id[0].astype(F32)[:, None] * CW + jnp.arange(CW, dtype=F32)[None, :]).reshape(1, CB * CW)
    target = jnp.concatenate([target, pad], axis=0)
    others = trade_line(jnp.concatenate([contrib, target], axis=0))
    width = line * CB * CW
    high, low, back, u_face, *sends = call(
        lambda *refs: first_coarse_body(*refs, line=line), "coarse_load",
        [bf16(BS, width), bf16(BS, width), small, face] + [small] * NF,
        [VMEM, VMEM, SMEM] + [VMEM] * line + [VMEM, VMEM, SMEM, VMEM],
        target, coarse_all, coarse_id, contrib, *others, outer, basis, face_link, swap,
    )

    def apply(inner, back, u_face, sends, stage):
        came = trade_faces(sends)
        z, acc = call(
            own_apply_body, "own_" + stage, [block, f32(NB, NRHS, BS)], [VMEM] * 5 + [SMEM],
            inner, back, basis, u_face, tiles, tile_cols,
        )
        y, z_face, *sends = call(
            face_apply_body, "face_" + stage, [f32(NB, NRHS, BS), face] + [small] * NF,
            [VMEM] * 7 + [SMEM, SMEM, VMEM],
            acc, *came, u_face, tiles, tile_cols, face_link, swap,
        )
        return z, z_face, y, sends

    z, z_face, y, sends = apply(inner, back, u_face, sends, "first")
    came = trade_faces(sends)
    inner, part = call(
        lambda *refs: interior_body(*refs, flat=False), "interior_image", [block, small], [VMEM] * 3,
        y, interior_inv, basis,
    )
    q_face, outer, contrib = call(
        next_faces_body, "faces_image", [face, face, small],
        [VMEM] * 5 + [SMEM] + [VMEM] * 3,
        y, *came, face_link, schur, basis, part,
    )
    others = trade_line(contrib)
    back, u_face, *sends = call(
        lambda *refs: next_coarse_body(*refs, line=line), "coarse_image",
        [small, face] + [small] * NF,
        [VMEM] * (line + 4) + [SMEM, VMEM],
        contrib, *others, high, low, outer, basis, face_link, swap,
    )
    w, w_face, v, sends = apply(inner, back, u_face, sends, "second")
    came = trade_faces(sends)
    (dots,) = call(dots_body, "dots", [f32(2, BS)], [VMEM] * 7, load, z, z_face, y, w, w_face, v)
    spread = lax.all_to_all(jnp.broadcast_to(dots[None], (devices, 2, BS)), AXES, 0, 0)
    total = jnp.sum(spread, axis=0).reshape(8, NRHS)
    rz, zq, rw, qw, zv, wv = [total[k] for k in range(6)]
    alpha = rz / zq
    rho = rz - alpha * (rw + zq) + alpha * alpha * qw
    grow = 1.0 + rho / rz
    curve = grow * grow * zq - grow * alpha * (zv + qw) + alpha * alpha * wv
    step = rho / curve
    coef = jnp.stack([alpha + step * grow, step * alpha], axis=1)
    out = f32(1, NRHS, NL)
    return tuple(
        call(
            final_body, "combine", [out, out], [VMEM] * 14,
            coef, load, r_face, z, z_face, y, q_face, w, w_face, v, *came,
        )
    )


def solution(mesh):
    lead = P(AXES, None, None)
    flat = P(AXES, None)
    in_specs = (lead, P(AXES, None, None, None), flat, lead, lead, lead, lead, lead, flat, flat)
    return jax.shard_map(
        on_device, mesh=mesh, in_specs=in_specs, out_specs=(lead, lead), check_vma=False
    )
```

time: 300 us -> 123 us (0.41)
  blocking collectives: 147 us -> 0 us
  matrix products: 60.6 us -> 0 us
  local copies, waits for them, and re-layouts: 20.4 us -> 42.4 us
  waiting for transfers between devices: 28.8 us -> 9.95 us
  Pallas kernels: 0 us -> 15.4 us
  starting transfers between devices: 22 us -> 36.3 us
  between operations: 17.6 us -> 14.4 us
    psum x3 -> x0, blocking collectives: 120 us -> none  [the longest x2 80 us: global_rz(): return lax.psum(local_dot(left, right), ('gx', 'gy', 'gz'))]
    dot_general x56 -> x0, matrix products: 60.6 us -> none  [the longest x20 21 us: assemble(): returned = jnp.dot(incoming, onehots[round_no], precision=HIGH)]
    all_gather x2 -> x0, blocking collectives: 26.7 us -> none  [coarse_part(): all_solved = lax.all_gather(solved, 'gz', axis=0, tiled=True)]
    reduce_scatter x2 -> x0, waiting for transfers between devices: 26.5 us -> none  [coarse_part(): lax.psum_scatter(jnp.dot(dense_map, contrib, precision=HIGH), 'gz', scatt...]
    unnamed x97 -> x131, local copies, waits for them, and re-layouts: 12.5 us -> 38.9 us
    pallas_call x0 -> x12, Pallas kernels: none -> 15.4 us  [call(): pl.pallas_call(body, name=name, out_shape=outs, in_specs=specs, out_specs...]
    ppermute x20 -> x26, starting transfers between devices: 21.9 us -> 32 us  [trade(): return lax.ppermute(value, AXES, [(i, i ^ mask) for i in range(devices)])]
    ppermute x20 -> x26, waiting for transfers between devices: 2.29 us -> 7.55 us  [trade(): return lax.ppermute(value, AXES, [(i, i ^ mask) for i in range(devices)])]
  transfers between devices with their start and end apart: 22 -> 28, of which waited for: 6 -> 8; matrix products, arithmetic and copies ran while one was open for 12% -> 5% of each run, Pallas kernels for 0% -> 6%
where the time goes in v1:
time: 123 us; the launch traced here: 121 us
  local copies, waits for them, and re-layouts  42.4 us (34%)
  starting transfers between devices  36.3 us (30%)
  Pallas kernels  15.4 us (13%)
  between operations  14.4 us (12%)
  waiting for transfers between devices  9.95 us (8%)
  other arithmetic  2.42 us (2%)
    unnamed x131, local copies, waits for them, and re-layouts  38.9 us
    ppermute x26, starting transfers between devices, trade(): return lax.ppermute(value, AXES, [(i, i ^ mask) for i in range(devices)])  32 us
    pallas_call x12, Pallas kernels, call(): pl.pallas_call(body, name=name, out_shape=outs, in_specs=specs, out_specs...  15.4 us
    ppermute x26, waiting for transfers between devices, trade(): return lax.ppermute(value, AXES, [(i, i ^ mask) for i in range(devices)])  7.55 us
    all_to_all x1, starting transfers between devices, on_device(): lax.all_to_all(jnp.broadcast_to(dots[None], (devices, 2, BS)), AXES, 0, 0)  4.3 us
  transfers between devices with their start and end apart: 28, of which 8 were waited for; matrix products, arithmetic and copies ran while one was open for 5% of the time, Pallas kernels for 6%

profile of v1, /device:TPU:0, one launch (start us, length us, event | category | flops | bytes accessed | tf_op | source)
XLA Modules:
  0.0 121.0 jit_solution(18286616860774067261)
XLA Ops:
  9.7 3.0 %collective-permute-start = (f32[40,128]{1,0:T(8,128)S(1)}, f32[40,128]{1,0:T(8,128)S(1)}, u32[]{:S(2)}, u32[]{:S(2)}) collective-permute-start(f32[40,128]{1,0:T(8,128)S(1)} %get-tuple-element.99), channel_id=1, source_target_pairs={{0,1},{1,0},{2,3},{3,2},{4,5},{5,4},{6,7},{7,6},{8,9},{9,8},{10,11... | collective-permute-start | bytes 61448 | tf_op jit(solution)/shard_map/ppermute | solution.py:261
  12.7 2.6 %collective-permute-start.1 = (f32[40,128]{1,0:T(8,128)S(1)}, f32[40,128]{1,0:T(8,128)S(1)}, u32[]{:S(2)}, u32[]{:S(2)}) collective-permute-start(f32[40,128]{1,0:T(8,128)S(1)} %get-tuple-element.97), channel_id=1, source_target_pairs={{0,2},{1,3},{2,0},{3,1},{4,6},{5,7},{6,4},{7,5},{8,10},{9,11},{10,... | collective-permute-start | bytes 61448 | tf_op jit(solution)/shard_map/ppermute | solution.py:261
  15.3 1.5 %collective-permute-start.3 = (f32[40,128]{1,0:T(8,128)S(1)}, f32[40,128]{1,0:T(8,128)S(1)}, u32[]{:S(2)}, u32[]{:S(2)}) collective-permute-start(f32[40,128]{1,0:T(8,128)S(1)} %get-tuple-element.96), channel_id=1, source_target_pairs={{0,8},{1,9},{2,10},{3,11},{4,12},{5,13},{6,14},{7,15},{8,0},{9,1},... | collective-permute-start | bytes 61448 | tf_op jit(solution)/shard_map/ppermute | solution.py:261
  18.1 1.3 %copy-done.1 = f32[1,128,2048]{2,1,0:T(8,128)S(1)} copy-done((f32[1,128,2048]{2,1,0:T(8,128)S(1)}, f32[1,128,2048]{2,1,0:T(8,128)}, u32[]{:S(2)}) %copy-start.1) | copy-done | bytes 1048600
  19.4 1.0 copy-done.6
  20.4 1.1 copy-done.12
  24.5 1.2 %copy-done.2 = f32[1,128,2048]{2,1,0:T(8,128)S(1)} copy-done((f32[1,128,2048]{2,1,0:T(8,128)S(1)}, f32[1,128,2048]{2,1,0:T(8,128)}, u32[]{:S(2)}) %copy-start.2) | copy-done | bytes 1048600
  25.7 1.2 %copy-done.8 = f32[1,512,512]{2,1,0:T(8,128)S(1)} copy-done((f32[1,512,512]{2,1,0:T(8,128)S(1)}, f32[1,512,512]{2,1,0:T(8,128)}, u32[]{:S(2)}) %copy-start.8) | copy-done | bytes 1048600
  31.2 1.7 %faces_load.1 = (f32[4,32,128]{2,1,0:T(8,128)S(1)}, f32[4,32,128]{2,1,0:T(8,128)S(1)}, f32[32,128]{1,0:T(8,128)S(1)}, bf16[4,128,128]{2,1,0:T(8,128)(2,1)S(1)}) custom-call(f32[32,2048]{1,0:T(8,128)S(1)} %bitcast.81, f32[40,128]{1,0:T(8,128)S(1)} %copy-done.36, f32[40,128]{1,0:T(8,128)S(1)} %copy-done.38, f32[40,128]{1,0:T(8,128)S(1)} %copy-done.40, ...), custom_call_target="tpu_custom_call" | custom-call | tf_op jit(solution)/shard_map/faces_load/pallas_call | solution.py:235
  35.6 3.6 %collective-permute-start.6 = (f32[40,128]{1,0:T(8,128)S(1)}, f32[40,128]{1,0:T(8,128)S(1)}, u32[]{:S(2)}, u32[]{:S(2)}) collective-permute-start(f32[40,128]{1,0:T(8,128)S(1)} %maximum_maximum_fusion.4), channel_id=1, source_target_pairs={{0,3},{1,2},{2,1},{3,0},{4,7},{5,6},{6,5},{7,4},{8,11},{9,10},{10,... | collective-permute-start | bytes 61448 | tf_op jit(solution)/shard_map/ppermute | solution.py:261
  39.3 1.2 concatenate.19.refs_0_
  42.8 1.2 %copy-done.3 = f32[1,128,2048]{2,1,0:T(8,128)S(1)} copy-done((f32[1,128,2048]{2,1,0:T(8,128)S(1)}, f32[1,128,2048]{2,1,0:T(8,128)}, u32[]{:S(2)}) %copy-start.3) | copy-done | bytes 1048600
  44.0 1.2 %copy-done.14 = f32[4,256,256]{2,1,0:T(8,128)S(1)} copy-done((f32[4,256,256]{2,1,0:T(8,128)S(1)}, f32[4,256,256]{2,1,0:T(8,128)}, u32[]{:S(2)}) %copy-start.14) | copy-done | bytes 1048600
  45.2 0.8 copy-done.34
  50.2 2.0 %coarse_load.1 = (bf16[128,512]{1,0:T(8,128)(2,1)S(1)}, bf16[128,512]{1,0:T(8,128)(2,1)S(1)}, f32[32,128]{1,0:T(8,128)S(1)}, f32[4,32,128]{2,1,0:T(8,128)S(1)}, ...) custom-call(f32[8,128]{1,0:T(8,128)S(1)} %copy-done.55, ...), custom_call_target="tpu_custom_call" | custom-call | tf_op jit(solution)/shard_map/coarse_load/pallas_call | solution.py:235
  54.7 2.7 %collective-permute-start.8 = (f32[32,128]{1,0:T(8,128)}, f32[32,128]{1,0:T(8,128)}, u32[]{:S(2)}, u32[]{:S(2)}) collective-permute-start(f32[32,128]{1,0:T(8,128)} %get-tuple-element.53), channel_id=1, source_target_pairs={{0,2},{1,3},{2,0},{3,1},{4,6},{5,7},{6,4},{7,5},{8,10},{9,11},{10,... | collective-permute-start | bytes 49160 | tf_op jit(solution)/shard_map/ppermute | solution.py:261
  58.7 3.1 %copy-done = f32[16,7,128,128]{3,2,1,0:T(8,128)S(1)} copy-done((f32[16,7,128,128]{3,2,1,0:T(8,128)S(1)}, f32[16,7,128,128]{3,2,1,0:T(8,128)}, u32[]{:S(2)}) %copy-start) | copy-done | bytes 7340056
  61.7 1.2 %copy-done.4 = f32[1,128,2048]{2,1,0:T(8,128)S(1)} copy-done((f32[1,128,2048]{2,1,0:T(8,128)S(1)}, f32[1,128,2048]{2,1,0:T(8,128)}, u32[]{:S(2)}) %copy-start.4) | copy-done | bytes 1048600
  63.7 2.3 %own_first.1 = (f32[12,32,128]{2,1,0:T(8,128)S(1)}, f32[16,32,128]{2,1,0:T(8,128)S(1)}) custom-call(f32[12,32,128]{2,1,0:T(8,128)S(1)} %get-tuple-element.43.inner_ref, f32[32,128]{1,0:T(8,128)S(1)} %copy-done.54, f32[128,2048]{1,0:T(8,128)S(1)} %bitcast.74, f32[4,32,128]{2,1,0:T(8,128)S(1)} %get-tuple-element.49.face_ref, f32[112,128,128]{2,1,0:T(8,128)S(1)} %bitcast.65, ...), custom_call_target="tpu_custom_call" | custom-call | tf_op jit(solution)/shard_map/own_first/pallas_call | solution.py:235
  66.8 1.4 %face_first.1 = (f32[16,32,128]{2,1,0:T(8,128)S(1)}, f32[4,32,128]{2,1,0:T(8,128)S(1)}, f32[32,128]{1,0:T(8,128)S(1)}, f32[32,128]{1,0:T(8,128)S(1)}, f32[32,128]{1,0:T(8,128)S(1)}, /*index=5*/f32[32,128]{1,0:T(8,128)S(1)}) custom-call(f32[16,32,128]{2,1,0:T(8,128)S(1)} %get-tuple-element.51.acc_ref, f32[32,128]{1,0:T(8,128)} %collective-permute-done.7.in0, ...), custom_call_target="tpu_custom_call" | custom-call | tf_op jit(solution)/shard_map/face_first/pallas_call | solution.py:235
  68.7 2.0 %collective-permute-start.12 = (f32[32,128]{1,0:T(8,128)S(1)}, f32[32,128]{1,0:T(8,128)S(1)}, u32[]{:S(2)}, u32[]{:S(2)}) collective-permute-start(f32[32,128]{1,0:T(8,128)S(1)} %get-tuple-element.60), channel_id=1, source_target_pairs={{0,2},{1,3},{2,0},{3,1},{4,6},{5,7},{6,4},{7,5},{8,10},{9,11},{10,... | collective-permute-start | bytes 49160 | tf_op jit(solution)/shard_map/ppermute | solution.py:261
  70.7 0.9 collective-permute-start.14
  72.2 1.4 %collective-permute-done.12.in1 = f32[32,128]{1,0:T(8,128)S(1)} collective-permute-done((f32[32,128]{1,0:T(8,128)S(1)}, f32[32,128]{1,0:T(8,128)S(1)}, u32[]{:S(2)}, u32[]{:S(2)}) %collective-permute-start.12) | collective-permute-done | bytes 16416 | tf_op jit(solution)/shard_map/ppermute | solution.py:261
  73.5 0.9 collective-permute-done.14.in3
  74.4 0.9 faces_image.1
  75.4 0.9 collective-permute-start.15
  76.3 1.7 %collective-permute-start.16 = (f32[32,128]{1,0:T(8,128)S(1)}, f32[32,128]{1,0:T(8,128)S(1)}, u32[]{:S(2)}, u32[]{:S(2)}) collective-permute-start(f32[32,128]{1,0:T(8,128)S(1)} %get-tuple-element.64.refs_0_), channel_id=1, source_target_pairs={{0,2},{1,3},{2,0},{3,1},{4,6},{5,7},{6,4},{7,5},{8,10},{9,11},{10,... | collective-permute-start | bytes 49160 | tf_op jit(solution)/shard_map/ppermute | solution.py:261
  78.0 1.8 %collective-permute-start.17 = (f32[32,128]{1,0:T(8,128)S(1)}, f32[32,128]{1,0:T(8,128)S(1)}, u32[]{:S(2)}, u32[]{:S(2)}) collective-permute-start(f32[32,128]{1,0:T(8,128)S(1)} %get-tuple-element.64.refs_0_), channel_id=1, source_target_pairs={{0,3},{1,2},{2,1},{3,0},{4,7},{5,6},{6,5},{7,4},{8,11},{9,10},{10,... | collective-permute-start | bytes 49160 | tf_op jit(solution)/shard_map/ppermute | solution.py:261
  79.8 1.1 collective-permute-done.16.refs_2_
  80.9 2.6 %collective-permute-done.17.refs_3_ = f32[32,128]{1,0:T(8,128)S(1)} collective-permute-done((f32[32,128]{1,0:T(8,128)S(1)}, f32[32,128]{1,0:T(8,128)S(1)}, u32[]{:S(2)}, u32[]{:S(2)}) %collective-permute-start.17) | collective-permute-done | bytes 16416 | tf_op jit(solution)/shard_map/ppermute | solution.py:261
  83.6 1.1 coarse_image.1
  84.8 2.3 %collective-permute-start.19 = (f32[32,128]{1,0:T(8,128)S(1)}, f32[32,128]{1,0:T(8,128)S(1)}, u32[]{:S(2)}, u32[]{:S(2)}) collective-permute-start(f32[32,128]{1,0:T(8,128)S(1)} %get-tuple-element.73), channel_id=1, source_target_pairs={{0,2},{1,3},{2,0},{3,1},{4,6},{5,7},{6,4},{7,5},{8,10},{9,11},{10,... | collective-permute-start | bytes 49160 | tf_op jit(solution)/shard_map/ppermute | solution.py:261
  87.1 0.9 collective-permute-start.21
  88.0 2.3 %own_second.1 = (f32[12,32,128]{2,1,0:T(8,128)S(1)}, f32[16,32,128]{2,1,0:T(8,128)S(1)}) custom-call(f32[12,32,128]{2,1,0:T(8,128)S(1)} %get-tuple-element.58.inner_ref, f32[32,128]{1,0:T(8,128)S(1)} %get-tuple-element.68.back_ref, f32[128,2048]{1,0:T(8,128)S(1)} %bitcast.78, f32[4,32,128]{2,1,0:T(8,128)S(1)} %get-tuple-element.69.face_ref, ...), custom_call_target="tpu_custom_call" | custom-call | tf_op jit(solution)/shard_map/own_second/pallas_call | solution.py:235
  90.9 1.3 %face_second.1 = (f32[16,32,128]{2,1,0:T(8,128)S(1)}, f32[4,32,128]{2,1,0:T(8,128)S(1)}, f32[32,128]{1,0:T(8,128)S(1)}, f32[32,128]{1,0:T(8,128)S(1)}, f32[32,128]{1,0:T(8,128)S(1)}, /*index=5*/f32[32,128]{1,0:T(8,128)S(1)}) custom-call(f32[16,32,128]{2,1,0:T(8,128)S(1)} %get-tuple-element.71.acc_ref, f32[32,128]{1,0:T(8,128)S(1)} %collective-permute-done.18.in0, ...), custom_call_target="tpu_custom_call" | custom-call | tf_op jit(solution)/shard_map/face_second/pallas_call | solution.py:235
  93.5 4.3 %all-to-all-start = ((f32[32,2,128]{2,1,0:T(2,128)}), f32[32,2,128]{2,1,0:T(2,128)S(1)}, u32[]{:S(2)}, u32[]{:S(2)}) async-start(f32[32,2,128]{2,1,0:T(2,128)} %broadcast_in_dim.5), calls=%async_computation | async-start | bytes 65536 | tf_op jit(solution)/shard_map/all_to_all | solution.py:334
  97.8 1.8 %collective-permute-start.22 = (f32[32,128]{1,0:T(8,128)}, f32[32,128]{1,0:T(8,128)S(1)}, u32[]{:S(2)}, u32[]{:S(2)}) collective-permute-start(f32[32,128]{1,0:T(8,128)} %copy-done.61), channel_id=1, source_target_pairs={{0,1},{1,0},{2,3},{3,2},{4,5},{5,4},{6,7},{7,6},{8,9},{9,8},{10,11... | collective-permute-start | bytes 49160 | tf_op jit(solution)/shard_map/ppermute | solution.py:261
  99.7 2.4 %collective-permute-start.23 = (f32[32,128]{1,0:T(8,128)}, f32[32,128]{1,0:T(8,128)S(1)}, u32[]{:S(2)}, u32[]{:S(2)}) collective-permute-start(f32[32,128]{1,0:T(8,128)} %copy-done.60), channel_id=1, source_target_pairs={{0,2},{1,3},{2,0},{3,1},{4,6},{5,7},{6,4},{7,5},{8,10},{9,11},{10,... | collective-permute-start | bytes 49160 | tf_op jit(solution)/shard_map/ppermute | solution.py:261
  102.1 1.5 %collective-permute-start.25 = (f32[32,128]{1,0:T(8,128)}, f32[32,128]{1,0:T(8,128)S(1)}, u32[]{:S(2)}, u32[]{:S(2)}) collective-permute-start(f32[32,128]{1,0:T(8,128)} %copy-done.58), channel_id=1, source_target_pairs={{0,8},{1,9},{2,10},{3,11},{4,12},{5,13},{6,14},{7,15},{8,0},{9,1},... | collective-permute-start | bytes 49160 | tf_op jit(solution)/shard_map/ppermute | solution.py:261
  103.6 1.7 %all-to-all-done = f32[32,2,128]{2,1,0:T(2,128)S(1)} async-done(((f32[32,2,128]{2,1,0:T(2,128)}), f32[32,2,128]{2,1,0:T(2,128)S(1)}, u32[]{:S(2)}, u32[]{:S(2)}) %all-to-all-start) | async-done | bytes 32800 | tf_op jit(solution)/shard_map/all_to_all | solution.py:334
  106.0 0.9 copy-done.11
  107.0 0.9 copy-done.16
  107.9 0.9 copy-done.18
  108.9 0.9 copy-done.20
  109.8 0.8 copy-done.22
  110.6 0.8 copy-done.24
  111.5 0.8 copy-done.30
  113.1 1.0 combine.1
  (171 shorter events, 30.0 us)
Async XLA Ops:
  7.2 35.6 %all-gather.2.cloned.1.call-start = ((), (), s32[]{:S(2)}) async-start(), calls=%async_computation.1 | async-start | bytes 1310720 | tf_op jit(solution)/shard_map/all_gather | solution.py:269
  8.0 8.8 %copy-start.62 = (f32[40]{0:T(128)}, f32[40]{0:T(128)S(1)}, u32[]{:S(2)}) copy-start(f32[40]{0:T(128)S(1)} %pad.17.clone) | copy-start | bytes 484
  9.7 12.4 %collective-permute-start = (f32[40,128]{1,0:T(8,128)S(1)}, f32[40,128]{1,0:T(8,128)S(1)}, u32[]{:S(2)}, u32[]{:S(2)}) collective-permute-start(f32[40,128]{1,0:T(8,128)S(1)} %get-tuple-element.99), channel_id=1, source_target_pairs={{0,1},{1,0},{2,3},{3,2},{4,5},{5,4},{6,7},{7,6},{8,9},{9,8},{10,11... | collective-permute-start | bytes 61448 | tf_op jit(solution)/shard_map/ppermute | solution.py:261
  12.7 10.0 %collective-permute-start.1 = (f32[40,128]{1,0:T(8,128)S(1)}, f32[40,128]{1,0:T(8,128)S(1)}, u32[]{:S(2)}, u32[]{:S(2)}) collective-permute-start(f32[40,128]{1,0:T(8,128)S(1)} %get-tuple-element.97), channel_id=1, source_target_pairs={{0,2},{1,3},{2,0},{3,1},{4,6},{5,7},{6,4},{7,5},{8,10},{9,11},{10,... | collective-permute-start | bytes 61448 | tf_op jit(solution)/shard_map/ppermute | solution.py:261
  15.3 8.0 %collective-permute-start.2 = (f32[40,128]{1,0:T(8,128)S(1)}, f32[40,128]{1,0:T(8,128)S(1)}, u32[]{:S(2)}, u32[]{:S(2)}) collective-permute-start(f32[40,128]{1,0:T(8,128)S(1)} %get-tuple-element.98), channel_id=1, source_target_pairs={{0,4},{1,5},{2,6},{3,7},{4,0},{5,1},{6,2},{7,3},{8,12},{9,13},{10,... | collective-permute-start | bytes 61448 | tf_op jit(solution)/shard_map/ppermute | solution.py:261
  15.3 8.6 %collective-permute-start.3 = (f32[40,128]{1,0:T(8,128)S(1)}, f32[40,128]{1,0:T(8,128)S(1)}, u32[]{:S(2)}, u32[]{:S(2)}) collective-permute-start(f32[40,128]{1,0:T(8,128)S(1)} %get-tuple-element.96), channel_id=1, source_target_pairs={{0,8},{1,9},{2,10},{3,11},{4,12},{5,13},{6,14},{7,15},{8,0},{9,1},... | collective-permute-start | bytes 61448 | tf_op jit(solution)/shard_map/ppermute | solution.py:261
  18.1 1.3 %copy-start.1 = (f32[1,128,2048]{2,1,0:T(8,128)S(1)}, f32[1,128,2048]{2,1,0:T(8,128)}, u32[]{:S(2)}) copy-start(f32[1,128,2048]{2,1,0:T(8,128)} %param.15) | copy-start | bytes 3145732
  21.5 44.6 %slice-start = ((s8[7340032]{0:T(1024)(128)(4,1)}), s8[3145728]{0:T(1024)(128)(4,1)S(1)}, s32[]{:S(2)}) async-start(s8[7340032]{0:T(1024)(128)(4,1)} %bitcast.66), calls=%async_computation.2 | async-start | bytes 6291456
  24.5 1.2 %copy-start.2 = (f32[1,128,2048]{2,1,0:T(8,128)S(1)}, f32[1,128,2048]{2,1,0:T(8,128)}, u32[]{:S(2)}) copy-start(f32[1,128,2048]{2,1,0:T(8,128)} %param.15) | copy-start | bytes 3145732
  25.7 1.2 %copy-start.8 = (f32[1,512,512]{2,1,0:T(8,128)S(1)}, f32[1,512,512]{2,1,0:T(8,128)}, u32[]{:S(2)}) copy-start(f32[1,512,512]{2,1,0:T(8,128)} %param.14) | copy-start | bytes 3145732
  34.9 5.6 %collective-permute-start.4 = (f32[40,128]{1,0:T(8,128)S(1)}, f32[40,128]{1,0:T(8,128)S(1)}, u32[]{:S(2)}, u32[]{:S(2)}) collective-permute-start(f32[40,128]{1,0:T(8,128)S(1)} %maximum_maximum_fusion.4), channel_id=1, source_target_pairs={{0,1},{1,0},{2,3},{3,2},{4,5},{5,4},{6,7},{7,6},{8,9},{9,8},{10,11... | collective-permute-start | bytes 61448 | tf_op jit(solution)/shard_map/ppermute | solution.py:261
  35.3 6.2 %collective-permute-start.5 = (f32[40,128]{1,0:T(8,128)S(1)}, f32[40,128]{1,0:T(8,128)S(1)}, u32[]{:S(2)}, u32[]{:S(2)}) collective-permute-start(f32[40,128]{1,0:T(8,128)S(1)} %maximum_maximum_fusion.4), channel_id=1, source_target_pairs={{0,2},{1,3},{2,0},{3,1},{4,6},{5,7},{6,4},{7,5},{8,10},{9,11},{10,... | collective-permute-start | bytes 61448 | tf_op jit(solution)/shard_map/ppermute | solution.py:261
  35.6 6.6 %collective-permute-start.6 = (f32[40,128]{1,0:T(8,128)S(1)}, f32[40,128]{1,0:T(8,128)S(1)}, u32[]{:S(2)}, u32[]{:S(2)}) collective-permute-start(f32[40,128]{1,0:T(8,128)S(1)} %maximum_maximum_fusion.4), channel_id=1, source_target_pairs={{0,3},{1,2},{2,1},{3,0},{4,7},{5,6},{6,5},{7,4},{8,11},{9,10},{10,... | collective-permute-start | bytes 61448 | tf_op jit(solution)/shard_map/ppermute | solution.py:261
  42.8 1.2 %copy-start.3 = (f32[1,128,2048]{2,1,0:T(8,128)S(1)}, f32[1,128,2048]{2,1,0:T(8,128)}, u32[]{:S(2)}) copy-start(f32[1,128,2048]{2,1,0:T(8,128)} %param.15) | copy-start | bytes 3145732
  54.1 11.9 %collective-permute-start.7 = (f32[32,128]{1,0:T(8,128)}, f32[32,128]{1,0:T(8,128)}, u32[]{:S(2)}, u32[]{:S(2)}) collective-permute-start(f32[32,128]{1,0:T(8,128)} %get-tuple-element.52), channel_id=1, source_target_pairs={{0,1},{1,0},{2,3},{3,2},{4,5},{5,4},{6,7},{7,6},{8,9},{9,8},{10,11... | collective-permute-start | bytes 49160 | tf_op jit(solution)/shard_map/ppermute | solution.py:261
  54.7 11.4 %collective-permute-start.8 = (f32[32,128]{1,0:T(8,128)}, f32[32,128]{1,0:T(8,128)}, u32[]{:S(2)}, u32[]{:S(2)}) collective-permute-start(f32[32,128]{1,0:T(8,128)} %get-tuple-element.53), channel_id=1, source_target_pairs={{0,2},{1,3},{2,0},{3,1},{4,6},{5,7},{6,4},{7,5},{8,10},{9,11},{10,... | collective-permute-start | bytes 49160 | tf_op jit(solution)/shard_map/ppermute | solution.py:261
  57.4 8.7 %collective-permute-start.9 = (f32[32,128]{1,0:T(8,128)}, f32[32,128]{1,0:T(8,128)}, u32[]{:S(2)}, u32[]{:S(2)}) collective-permute-start(f32[32,128]{1,0:T(8,128)} %get-tuple-element.54), channel_id=1, source_target_pairs={{0,4},{1,5},{2,6},{3,7},{4,0},{5,1},{6,2},{7,3},{8,12},{9,13},{10,... | collective-permute-start | bytes 49160 | tf_op jit(solution)/shard_map/ppermute | solution.py:261
  57.4 8.7 %collective-permute-start.10 = (f32[32,128]{1,0:T(8,128)}, f32[32,128]{1,0:T(8,128)}, u32[]{:S(2)}, u32[]{:S(2)}) collective-permute-start(f32[32,128]{1,0:T(8,128)} %get-tuple-element.55), channel_id=1, source_target_pairs={{0,8},{1,9},{2,10},{3,11},{4,12},{5,13},{6,14},{7,15},{8,0},{9,1},... | collective-permute-start | bytes 49160 | tf_op jit(solution)/shard_map/ppermute | solution.py:261
  58.7 3.1 %copy-start = (f32[16,7,128,128]{3,2,1,0:T(8,128)S(1)}, f32[16,7,128,128]{3,2,1,0:T(8,128)}, u32[]{:S(2)}) copy-start(f32[16,7,128,128]{3,2,1,0:T(8,128)} %param.11) | copy-start | bytes 22020100
  63.7 2.4 %slice-start.1 = ((s8[7340032]{0:T(1024)(128)(4,1)}), s8[4194304]{0:T(1024)(128)(4,1)S(1)}, s32[]{:S(2)}) async-start(s8[7340032]{0:T(1024)(128)(4,1)} %bitcast.66), calls=%async_computation.3 | async-start | bytes 8388608
  63.7 7.9 %copy-start.5 = (f32[1,128,2048]{2,1,0:T(8,128)S(1)}, f32[1,128,2048]{2,1,0:T(8,128)}, u32[]{:S(2)}) copy-start(f32[1,128,2048]{2,1,0:T(8,128)} %param.15) | copy-start | bytes 3145732
  63.7 7.9 %copy-start.13 = (f32[12,128,128]{2,1,0:T(8,128)S(1)}, f32[12,128,128]{2,1,0:T(8,128)}, u32[]{:S(2)}) copy-start(f32[12,128,128]{2,1,0:T(8,128)} %refs_1_.3) | copy-start | bytes 2359300
  63.7 10.7 %copy-start.9 = (f32[1,512,512]{2,1,0:T(8,128)S(1)}, f32[1,512,512]{2,1,0:T(8,128)}, u32[]{:S(2)}) copy-start(f32[1,512,512]{2,1,0:T(8,128)} %param.14) | copy-start | bytes 3145732
  66.0 26.2 %copy-start.17 = (f32[12,32,128]{2,1,0:T(8,128)}, f32[12,32,128]{2,1,0:T(8,128)S(1)}, u32[]{:S(2)}) copy-start(f32[12,32,128]{2,1,0:T(8,128)S(1)} %get-tuple-element.50.zi_ref) | copy-start | bytes 589828
  66.0 17.5 %copy-start.26 = (bf16[128,512]{1,0:T(8,128)(2,1)S(1)}, bf16[128,512]{1,0:T(8,128)(2,1)}, u32[]{:S(2)}) copy-start(bf16[128,512]{1,0:T(8,128)(2,1)} %copy-done.25) | copy-start | bytes 393220
  66.1 17.5 %copy-start.28 = (bf16[128,512]{1,0:T(8,128)(2,1)S(1)}, bf16[128,512]{1,0:T(8,128)(2,1)}, u32[]{:S(2)}) copy-start(bf16[128,512]{1,0:T(8,128)(2,1)} %copy-done.27) | copy-start | bytes 393220
  68.2 24.0 %copy-start.10 = (f32[16,32,128]{2,1,0:T(8,128)}, f32[16,32,128]{2,1,0:T(8,128)S(1)}, u32[]{:S(2)}) copy-start(f32[16,32,128]{2,1,0:T(8,128)S(1)} %get-tuple-element.57.refs_0_.y_ref) | copy-start | bytes 786436
  68.3 24.0 %copy-start.21 = (f32[4,32,128]{2,1,0:T(8,128)}, f32[4,32,128]{2,1,0:T(8,128)S(1)}, u32[]{:S(2)}) copy-start(f32[4,32,128]{2,1,0:T(8,128)S(1)} %get-tuple-element.56.zf_ref) | copy-start | bytes 196612
  68.3 3.9 %collective-permute-start.11 = (f32[32,128]{1,0:T(8,128)S(1)}, f32[32,128]{1,0:T(8,128)S(1)}, u32[]{:S(2)}, u32[]{:S(2)}) collective-permute-start(f32[32,128]{1,0:T(8,128)S(1)} %get-tuple-element.59), channel_id=1, source_target_pairs={{0,1},{1,0},{2,3},{3,2},{4,5},{5,4},{6,7},{7,6},{8,9},{9,8},{10,11... | collective-permute-start | bytes 49160 | tf_op jit(solution)/shard_map/ppermute | solution.py:261
  68.7 4.8 %collective-permute-start.12 = (f32[32,128]{1,0:T(8,128)S(1)}, f32[32,128]{1,0:T(8,128)S(1)}, u32[]{:S(2)}, u32[]{:S(2)}) collective-permute-start(f32[32,128]{1,0:T(8,128)S(1)} %get-tuple-element.60), channel_id=1, source_target_pairs={{0,2},{1,3},{2,0},{3,1},{4,6},{5,7},{6,4},{7,5},{8,10},{9,11},{10,... | collective-permute-start | bytes 49160 | tf_op jit(solution)/shard_map/ppermute | solution.py:261
  70.7 2.9 %collective-permute-start.13 = (f32[32,128]{1,0:T(8,128)S(1)}, f32[32,128]{1,0:T(8,128)S(1)}, u32[]{:S(2)}, u32[]{:S(2)}) collective-permute-start(f32[32,128]{1,0:T(8,128)S(1)} %get-tuple-element.61), channel_id=1, source_target_pairs={{0,4},{1,5},{2,6},{3,7},{4,0},{5,1},{6,2},{7,3},{8,12},{9,13},{10,... | collective-permute-start | bytes 49160 | tf_op jit(solution)/shard_map/ppermute | solution.py:261
  70.7 3.7 %collective-permute-start.14 = (f32[32,128]{1,0:T(8,128)S(1)}, f32[32,128]{1,0:T(8,128)S(1)}, u32[]{:S(2)}, u32[]{:S(2)}) collective-permute-start(f32[32,128]{1,0:T(8,128)S(1)} %get-tuple-element.62), channel_id=1, source_target_pairs={{0,8},{1,9},{2,10},{3,11},{4,12},{5,13},{6,14},{7,15},{8,0},{9,1},... | collective-permute-start | bytes 49160 | tf_op jit(solution)/shard_map/ppermute | solution.py:261
  71.6 19.3 %copy-start.52 = (s32[1,4]{1,0:T(1,128)S(1)}, s32[1,4]{1,0:T(1,128)}, u32[]{:S(2)}) copy-start(s32[1,4]{1,0:T(1,128)} %link_ref.7) | copy-start | bytes 52
  75.4 16.8 %copy-start.31 = (f32[4,32,128]{2,1,0:T(8,128)}, f32[4,32,128]{2,1,0:T(8,128)S(1)}, u32[]{:S(2)}) copy-start(f32[4,32,128]{2,1,0:T(8,128)S(1)} %get-tuple-element.79.qf_ref) | copy-start | bytes 196612
  75.4 4.5 %collective-permute-start.15 = (f32[32,128]{1,0:T(8,128)S(1)}, f32[32,128]{1,0:T(8,128)S(1)}, u32[]{:S(2)}, u32[]{:S(2)}) collective-permute-start(f32[32,128]{1,0:T(8,128)S(1)} %get-tuple-element.64.refs_0_), channel_id=1, source_target_pairs={{0,1},{1,0},{2,3},{3,2},{4,5},{5,4},{6,7},{7,6},{8,9},{9,8},{10,11... | collective-permute-start | bytes 49160 | tf_op jit(solution)/shard_map/ppermute | solution.py:261
  76.3 4.6 %collective-permute-start.16 = (f32[32,128]{1,0:T(8,128)S(1)}, f32[32,128]{1,0:T(8,128)S(1)}, u32[]{:S(2)}, u32[]{:S(2)}) collective-permute-start(f32[32,128]{1,0:T(8,128)S(1)} %get-tuple-element.64.refs_0_), channel_id=1, source_target_pairs={{0,2},{1,3},{2,0},{3,1},{4,6},{5,7},{6,4},{7,5},{8,10},{9,11},{10,... | collective-permute-start | bytes 49160 | tf_op jit(solution)/shard_map/ppermute | solution.py:261
  78.0 5.5 %collective-permute-start.17 = (f32[32,128]{1,0:T(8,128)S(1)}, f32[32,128]{1,0:T(8,128)S(1)}, u32[]{:S(2)}, u32[]{:S(2)}) collective-permute-start(f32[32,128]{1,0:T(8,128)S(1)} %get-tuple-element.64.refs_0_), channel_id=1, source_target_pairs={{0,3},{1,2},{2,1},{3,0},{4,7},{5,6},{6,5},{7,4},{8,11},{9,10},{10,... | collective-permute-start | bytes 49160 | tf_op jit(solution)/shard_map/ppermute | solution.py:261
  84.7 5.6 %collective-permute-start.18 = (f32[32,128]{1,0:T(8,128)S(1)}, f32[32,128]{1,0:T(8,128)S(1)}, u32[]{:S(2)}, u32[]{:S(2)}) collective-permute-start(f32[32,128]{1,0:T(8,128)S(1)} %get-tuple-element.72), channel_id=1, source_target_pairs={{0,1},{1,0},{2,3},{3,2},{4,5},{5,4},{6,7},{7,6},{8,9},{9,8},{10,11... | collective-permute-start | bytes 49160 | tf_op jit(solution)/shard_map/ppermute | solution.py:261
  84.8 5.6 %collective-permute-start.19 = (f32[32,128]{1,0:T(8,128)S(1)}, f32[32,128]{1,0:T(8,128)S(1)}, u32[]{:S(2)}, u32[]{:S(2)}) collective-permute-start(f32[32,128]{1,0:T(8,128)S(1)} %get-tuple-element.73), channel_id=1, source_target_pairs={{0,2},{1,3},{2,0},{3,1},{4,6},{5,7},{6,4},{7,5},{8,10},{9,11},{10,... | collective-permute-start | bytes 49160 | tf_op jit(solution)/shard_map/ppermute | solution.py:261
  87.1 3.2 %collective-permute-start.20 = (f32[32,128]{1,0:T(8,128)S(1)}, f32[32,128]{1,0:T(8,128)S(1)}, u32[]{:S(2)}, u32[]{:S(2)}) collective-permute-start(f32[32,128]{1,0:T(8,128)S(1)} %get-tuple-element.74), channel_id=1, source_target_pairs={{0,4},{1,5},{2,6},{3,7},{4,0},{5,1},{6,2},{7,3},{8,12},{9,13},{10,... | collective-permute-start | bytes 49160 | tf_op jit(solution)/shard_map/ppermute | solution.py:261
  87.1 3.7 %collective-permute-start.21 = (f32[32,128]{1,0:T(8,128)S(1)}, f32[32,128]{1,0:T(8,128)S(1)}, u32[]{:S(2)}, u32[]{:S(2)}) collective-permute-start(f32[32,128]{1,0:T(8,128)S(1)} %get-tuple-element.75), channel_id=1, source_target_pairs={{0,8},{1,9},{2,10},{3,11},{4,12},{5,13},{6,14},{7,15},{8,0},{9,1},... | collective-permute-start | bytes 49160 | tf_op jit(solution)/shard_map/ppermute | solution.py:261
  88.0 4.3 %copy-start.7 = (f32[1,32,2048]{2,1,0:T(8,128)S(1)}, f32[1,32,2048]{2,1,0:T(8,128)}, u32[]{:S(2)}) copy-start(f32[1,32,2048]{2,1,0:T(8,128)} %param.10) | copy-start | bytes 786436
  90.3 2.2 %copy-start.19 = (f32[12,32,128]{2,1,0:T(8,128)}, f32[12,32,128]{2,1,0:T(8,128)S(1)}, u32[]{:S(2)}) copy-start(f32[12,32,128]{2,1,0:T(8,128)S(1)} %get-tuple-element.70.wi_ref) | copy-start | bytes 589828
  93.5 11.8 %all-to-all-start = ((f32[32,2,128]{2,1,0:T(2,128)}), f32[32,2,128]{2,1,0:T(2,128)S(1)}, u32[]{:S(2)}, u32[]{:S(2)}) async-start(f32[32,2,128]{2,1,0:T(2,128)} %broadcast_in_dim.5), calls=%async_computation | async-start | bytes 65536 | tf_op jit(solution)/shard_map/all_to_all | solution.py:334
  97.8 7.7 %collective-permute-start.22 = (f32[32,128]{1,0:T(8,128)}, f32[32,128]{1,0:T(8,128)S(1)}, u32[]{:S(2)}, u32[]{:S(2)}) collective-permute-start(f32[32,128]{1,0:T(8,128)} %copy-done.61), channel_id=1, source_target_pairs={{0,1},{1,0},{2,3},{3,2},{4,5},{5,4},{6,7},{7,6},{8,9},{9,8},{10,11... | collective-permute-start | bytes 49160 | tf_op jit(solution)/shard_map/ppermute | solution.py:261
  99.7 5.9 %collective-permute-start.23 = (f32[32,128]{1,0:T(8,128)}, f32[32,128]{1,0:T(8,128)S(1)}, u32[]{:S(2)}, u32[]{:S(2)}) collective-permute-start(f32[32,128]{1,0:T(8,128)} %copy-done.60), channel_id=1, source_target_pairs={{0,2},{1,3},{2,0},{3,1},{4,6},{5,7},{6,4},{7,5},{8,10},{9,11},{10,... | collective-permute-start | bytes 49160 | tf_op jit(solution)/shard_map/ppermute | solution.py:261
  102.1 3.5 %collective-permute-start.24 = (f32[32,128]{1,0:T(8,128)}, f32[32,128]{1,0:T(8,128)S(1)}, u32[]{:S(2)}, u32[]{:S(2)}) collective-permute-start(f32[32,128]{1,0:T(8,128)} %copy-done.59), channel_id=1, source_target_pairs={{0,4},{1,5},{2,6},{3,7},{4,0},{5,1},{6,2},{7,3},{8,12},{9,13},{10,... | collective-permute-start | bytes 49160 | tf_op jit(solution)/shard_map/ppermute | solution.py:261
  102.1 3.9 %collective-permute-start.25 = (f32[32,128]{1,0:T(8,128)}, f32[32,128]{1,0:T(8,128)S(1)}, u32[]{:S(2)}, u32[]{:S(2)}) collective-permute-start(f32[32,128]{1,0:T(8,128)} %copy-done.58), channel_id=1, source_target_pairs={{0,8},{1,9},{2,10},{3,11},{4,12},{5,13},{6,14},{7,15},{8,0},{9,1},... | collective-permute-start | bytes 49160 | tf_op jit(solution)/shard_map/ppermute | solution.py:261
  (45 other events, 33.9 us)
Sparse Core Ops, SparseCore 0:
  9.6 31.2 all-gather.1

commit v2 on v1

v2 whole, which is shorter than its diff:
```python
import jax
import jax.numpy as jnp
from jax import lax
from jax.experimental import pallas as pl
from jax.experimental.pallas import tpu as pltpu
from jax.sharding import PartitionSpec as P

BS = 128
NIN = 12
NF = 4
NRHS = 32
CW = 32
CB = 4
OCAP = 8
NB = 16
TPR = 7
NL = 2048
AXES = ("gx", "gy", "gz")
F32 = jnp.float32
BF16 = jnp.bfloat16
NN = (((1,), (0,)), ((), ()))
NT = (((1,), (1,)), ((), ()))


def mm(left, right, dims=NN):
    return lax.dot_general(left, right, dims, preferred_element_type=F32)


def halves(value):
    high = value.astype(BF16)
    return high, (value - high.astype(F32)).astype(BF16)


def dot_halves(left, right, dims=NN):
    (lh, ll), (rh, rl) = left, right
    rows = lh.shape[0]
    both = mm(jnp.concatenate([lh, ll], axis=0), rh, dims)
    return both[:rows] + both[rows:] + mm(lh, rl, dims)


def select_lanes(value, onehot):
    rows = value.shape[0]
    high, rest = halves(value)
    low = (value - high.astype(F32) - rest.astype(F32)).astype(BF16)
    out = mm(jnp.concatenate([high, rest, low], axis=0), onehot)
    return out[:rows] + out[rows : 2 * rows] + out[2 * rows :]


def lanes(block):
    return slice(block * BS, (block + 1) * BS)


def start_all(sems, *pairs):
    copies = [pltpu.make_async_copy(src, dst, sems.at[k]) for k, (src, dst) in enumerate(pairs)]
    for copy in copies:
        copy.start()
    return copies


def prepare_body(
    load_ref, map_ref, id_ref, link_ref, target_ref, column_ref, weight_ref, side0, side1, side2, side3,
    ids, links, maps, faces, sems,
):
    copies = start_all(
        sems,
        (id_ref, ids),
        (link_ref, links),
        (map_ref, maps),
        (load_ref.at[0, :, NIN * BS :], faces),
    )
    copies[0].wait()
    lane = lax.broadcasted_iota(jnp.int32, (8, BS), 1)
    row = lax.broadcasted_iota(jnp.int32, (BS, BS), 0)
    target = lane % CW
    column = row % CW
    for b in range(CB):
        target = jnp.where(lane // CW == b, target + ids[0, b] * CW, target)
        column = jnp.where(row // CW == b, column + ids[0, b] * CW, column)
    target_ref[...] = target.astype(F32)
    column_ref[...] = column.astype(F32)
    copies[1].wait()
    for r in range(NF):
        link = jnp.full((1, BS), links[0, r], jnp.int32).astype(F32)
        weight_ref[r : r + 1, :] = 1.0 - 0.5 * link
        weight_ref[NF + r : NF + r + 1, :] = link
    copies[2].wait()
    copies[3].wait()
    for r, out in enumerate((side0, side1, side2, side3)):
        out[:NRHS, :] = faces[:, lanes(r)]
        out[NRHS:, :] = jnp.broadcast_to(maps[0, r : r + 1, :], (8, BS)).astype(F32)


def interior_body(
    x_ref, inv_ref, basis_ref, schur_ref,
    inner_ref, part_ref, schur_high, schur_low, basis_high, basis_low, *scratch, flat,
):
    inv, basis, schur = scratch[:3]
    sems = scratch[-1]
    pairs = [(inv_ref, inv), (basis_ref.at[0], basis), (schur_ref.at[0], schur)]
    if flat:
        pairs.append((x_ref.at[0, :, : NIN * BS], scratch[3]))
    copies = start_all(sems, *pairs)
    if flat:
        copies[3].wait()
    copies[0].wait()
    pieces = []
    for b in range(NIN):
        xb = halves(scratch[3][:, lanes(b)] if flat else x_ref[b])
        pieces.append(xb)
        inner_ref[b] = dot_halves(xb, halves(inv[b]))
    cat = tuple(jnp.concatenate([p[h] for p in pieces], axis=1) for h in range(2))
    copies[1].wait()
    part_ref[...] = dot_halves(cat, halves(basis[:, : NIN * BS]), NT)
    basis_high[...], basis_low[...] = halves(basis[:, NIN * BS :])
    copies[2].wait()
    schur_high[...], schur_low[...] = halves(schur[...])


def face_solve(faces, mats, weight_ref, part_ref, outer_ref, contrib_ref):
    schur_high, schur_low, basis_high, basis_low = mats
    scaled = halves(
        jnp.concatenate([faces[r] * weight_ref[r : r + 1, :] for r in range(NF)], axis=1)
    )
    contrib_ref[:NRHS, :] = part_ref[...] + dot_halves(
        scaled, (basis_high[...], basis_low[...]), NT
    )
    outer = dot_halves(scaled, (schur_high[...], schur_low[...]))
    for r in range(NF):
        outer_ref[r] = outer[:, lanes(r)]


def first_faces_body(
    own0, own1, own2, own3, in0, in1, in2, in3, target_ref, weight_ref,
    schur_high, schur_low, basis_high, basis_low, part_ref,
    face_ref, outer_ref, contrib_ref, swap_ref,
):
    faces = []
    rows = lax.broadcasted_iota(jnp.int32, (BS, BS), 0).astype(F32)
    for r, (own, inc) in enumerate(zip((own0, own1, own2, own3), (in0, in1, in2, in3))):
        mine = (rows == own[NRHS : NRHS + 1, :]).astype(F32).astype(BF16)
        theirs = (rows == inc[NRHS : NRHS + 1, :]).astype(F32).astype(BF16)
        link = weight_ref[NF + r : NF + r + 1, :]
        swap_ref[r] = (mm(mine, theirs, NT) * link).astype(BF16)
        came = select_lanes(inc[:NRHS, :], (mm(theirs, mine, NT) * link).astype(BF16))
        faces.append(own[:NRHS, :] + came)
        face_ref[r] = faces[-1]
    contrib_ref[NRHS:, :] = target_ref[...]
    mats = (schur_high, schur_low, basis_high, basis_low)
    face_solve(faces, mats, weight_ref, part_ref, outer_ref, contrib_ref)


def next_faces_body(
    y_ref, in0, in1, in2, in3, weight_ref, schur_high, schur_low, basis_high, basis_low, part_ref,
    face_ref, outer_ref, contrib_ref,
):
    faces = []
    for r, inc in enumerate((in0, in1, in2, in3)):
        faces.append(y_ref[NIN + r] + inc[...])
        face_ref[r] = faces[-1]
    mats = (schur_high, schur_low, basis_high, basis_low)
    face_solve(faces, mats, weight_ref, part_ref, outer_ref, contrib_ref)


def correct(contribs, table, outer_ref, basis, weight_ref, swap_ref, back_ref, face_ref, outs):
    back = dot_halves(halves(jnp.concatenate(contribs, axis=1)), table, NT)
    back_ref[...] = back
    corr = dot_halves(halves(back), basis)
    for r in range(NF):
        value = weight_ref[r : r + 1, :] * (outer_ref[r] + corr[:, lanes(r)])
        face_ref[r] = value
        outs[r][...] = select_lanes(value, swap_ref[r])


def first_coarse_body(*refs, line):
    coarse_hbm, column_ref = refs[:2]
    sides = refs[2 : 2 + line]
    outer_ref, basis_high, basis_low, weight_ref, swap_ref = refs[2 + line : 7 + line]
    high_ref, low_ref, back_ref, face_ref = refs[7 + line : 11 + line]
    outs = refs[11 + line : 11 + line + NF]
    coarse, sems = refs[11 + line + NF :]
    copies = start_all(sems, *[(coarse_hbm.at[o], coarse.at[o]) for o in range(line)])
    targets = jnp.concatenate([side[NRHS : NRHS + 1, :] for side in sides], axis=1)
    own = OCAP * CW
    rows = lax.broadcasted_iota(jnp.int32, (own, line * CB * CW), 0).astype(F32)
    places = lax.broadcasted_iota(jnp.int32, (BS, own), 1).astype(F32)
    column = jnp.concatenate([column_ref[...]] * (own // BS), axis=1)
    table = jnp.zeros((2 * BS, line * CB * CW), F32)
    for o in range(line):
        pick = (rows + float(o * own) == targets).astype(F32).astype(BF16)
        take = (places + float(o * own) == column).astype(F32).astype(BF16)
        copies[o].wait()
        high, low = halves(coarse[o])
        both = jnp.concatenate([mm(take, high).astype(BF16), mm(take, low).astype(BF16)], axis=0)
        table = table + mm(both, pick)
    high_ref[...] = table[:BS].astype(BF16)
    low_ref[...] = table[BS:].astype(BF16)
    contribs = [side[:NRHS, :] for side in sides]
    correct(contribs, (high_ref[...], low_ref[...]), outer_ref, (basis_high[...], basis_low[...]),
            weight_ref, swap_ref, back_ref, face_ref, outs)


def next_coarse_body(*refs, line):
    contribs = [ref[...] for ref in refs[:line]]
    high_ref, low_ref, outer_ref, basis_high, basis_low, weight_ref, swap_ref = refs[line : 7 + line]
    back_ref, face_ref = refs[7 + line : 9 + line]
    correct(contribs, (high_ref[...], low_ref[...]), outer_ref, (basis_high[...], basis_low[...]),
            weight_ref, swap_ref, back_ref, face_ref, refs[9 + line :])


def add_row(x, i, wide, cols_ref, acc_ref):
    out = dot_halves(halves(x), wide)
    places = [cols_ref[t, i] for t in range(TPR)]
    before = [acc_ref[place] for place in places]
    for t in range(TPR):
        acc_ref[places[t]] = before[t] + out[:, lanes(t)]


def own_apply_body(
    inner_ref, back_ref, basis_ref, face_ref, tiles_ref, cols_ref, z_ref, acc_ref, wide_high, wide_low,
    basis, tiles, sems,
):
    pairs = [(basis_ref.at[0, :, : NIN * BS], basis)]
    pairs += [(tiles_ref.at[i], tiles.at[i]) for i in range(NB)]
    copies = start_all(sems, *pairs)
    acc_ref[...] = jnp.zeros_like(acc_ref)
    back = halves(back_ref[...])
    copies[0].wait()
    for b in range(NIN):
        z_ref[b] = inner_ref[b] + dot_halves(back, halves(basis[:, lanes(b)]))
    for i in range(NB):
        copies[1 + i].wait()
        wide = halves(jnp.concatenate([tiles[i, t] for t in range(TPR)], axis=1))
        if i >= NIN:
            wide_high[i - NIN], wide_low[i - NIN] = wide
        add_row(z_ref[i] if i < NIN else face_ref[i - NIN], i, wide, cols_ref, acc_ref)


def face_apply_body(
    acc_ref, in0, in1, in2, in3, face_ref, wide_high, wide_low, cols_ref, swap_ref,
    y_ref, z_ref, out0, out1, out2, out3,
):
    y_ref[...] = acc_ref[...]
    for r, inc in enumerate((in0, in1, in2, in3)):
        came = inc[...]
        z_ref[r] = face_ref[r] + came
        add_row(came, NIN + r, (wide_high[r], wide_low[r]), cols_ref, y_ref)
    for r, out in enumerate((out0, out1, out2, out3)):
        out[...] = select_lanes(y_ref[NIN + r], swap_ref[r])


def dots_body(load_hbm, zi, zf, y, wi, wf_ref, v_ref, out_ref, load_ref, sems):
    (copy,) = start_all(sems, (load_hbm.at[0], load_ref))
    copy.wait()
    sums = [jnp.zeros((NRHS, BS), F32) for _ in range(6)]
    for b in range(NB):
        load = load_ref[:, lanes(b)]
        z = zi[b] if b < NIN else zf[b - NIN]
        w = wi[b] if b < NIN else wf_ref[b - NIN]
        q, v = y[b], v_ref[b]
        for k, (left, right) in enumerate(((load, z), (z, q), (load, w), (q, w), (z, v), (w, v))):
            sums[k] = sums[k] + left * right
    place = lax.broadcasted_iota(jnp.int32, (NRHS, BS), 1)
    case = lax.broadcasted_iota(jnp.int32, (NRHS, BS), 0)
    for row in range(2):
        total = jnp.zeros((NRHS, BS), F32)
        for k in range(4 * row, min(4 * row + 4, 6)):
            column = jnp.sum(sums[k], axis=1, keepdims=True)
            total = total + jnp.where(place == case + NRHS * (k % 4), column, 0.0)
        total = jnp.sum(total, axis=0, keepdims=True)
        out_ref[:, row : row + 1, :] = jnp.broadcast_to(total[None], (out_ref.shape[0], 1, BS))


def final_body(
    dots_ref, in0, in1, in2, in3, load_h, rf, zi, zf, y, qf, wi, wf, v, sol_ref, res_ref, load, sems,
):
    copies = start_all(sems, (load_h.at[0, :, : NIN * BS], load))
    place = lax.broadcasted_iota(jnp.int32, (NRHS, BS), 1)
    case = lax.broadcasted_iota(jnp.int32, (NRHS, BS), 0)
    total = jnp.sum(dots_ref[...], axis=0)
    rz, zq, rw, qw, zv, wv = [
        jnp.sum(
            jnp.where(place == case + NRHS * (k % 4), total[k // 4 : k // 4 + 1, :], 0.0),
            axis=1,
            keepdims=True,
        )
        for k in range(6)
    ]
    alpha = rz / zq
    rho = rz - alpha * (rw + zq) + alpha * alpha * qw
    grow = 1.0 + rho / rz
    curve = grow * grow * zq - grow * alpha * (zv + qw) + alpha * alpha * wv
    step = rho / curve
    first = alpha + step * grow
    second = step * alpha
    for copy in copies:
        copy.wait()
    for b in range(NB):
        if b < NIN:
            r_b, z_b, q_b, w_b, v_b = load[:, lanes(b)], zi[b], y[b], wi[b], v[b]
        else:
            f = b - NIN
            r_b, z_b, q_b, w_b = rf[f], zf[f], qf[f], wf[f]
            v_b = v[b] + (in0, in1, in2, in3)[f][...]
        sol_ref[0, :, lanes(b)] = first * z_b - second * w_b
        res_ref[0, :, lanes(b)] = r_b - first * q_b + second * v_b


def f32(*shape):
    return jax.ShapeDtypeStruct(shape, F32)


def bf16(*shape):
    return jax.ShapeDtypeStruct(shape, BF16)


SMEM = pl.BlockSpec(memory_space=pltpu.SMEM)
VMEM = pl.BlockSpec(memory_space=pltpu.VMEM)
HBM = pl.BlockSpec(memory_space=pltpu.HBM)


def call(body, name, outs, specs, *args, scratch=(), copies=0):
    scratch = [pltpu.VMEM(shape, F32) if isinstance(shape, tuple) else shape for shape in scratch]
    if copies:
        scratch.append(pltpu.SemaphoreType.DMA((copies,)))
    args = [
        pltpu.with_memory_space_constraint(arg, pltpu.HBM) if spec is HBM else arg
        for arg, spec in zip(args, specs, strict=True)
    ]
    return pl.pallas_call(
        body,
        name=name,
        out_shape=outs,
        in_specs=specs,
        out_specs=[VMEM] * len(outs),
        scratch_shapes=scratch,
        compiler_params=pltpu.CompilerParams(vmem_limit_bytes=16 << 20),
    )(*args)


def on_device(
    load_vector, matrix_tiles, tile_cols, interior_inv, schur_inv, coarse_basis, coarse_inv,
    row_map, face_link, coarse_id,
):
    cols = tile_cols.T
    line = lax.axis_size("gz")
    devices = line * lax.axis_size("gy") * lax.axis_size("gx")
    depth_z = line.bit_length() - 1
    depth_y = lax.axis_size("gy").bit_length() - 1
    masks = [1, 2, 1 << depth_z, 1 << (depth_z + depth_y)]

    def trade(value, mask):
        return lax.ppermute(value, AXES, [(i, i ^ mask) for i in range(devices)])

    def trade_faces(faces):
        return [trade(face, mask) for face, mask in zip(faces, masks)]

    def trade_line(value):
        return [trade(value, mask) for mask in range(1, line)]

    coarse_all = lax.all_gather(coarse_inv[0], "gz", axis=0)
    inside = (NIN, NRHS, BS)
    around = (NF, NRHS, BS)
    every = (NB, NRHS, BS)
    block, face, small, side = f32(*inside), f32(*around), f32(NRHS, BS), f32(NRHS + 8, BS)
    nf = NF * BS
    width = line * CB * CW
    target, column, weight, *sides = call(
        prepare_body, "prepare", [f32(8, BS), f32(BS, BS), f32(2 * NF, BS)] + [side] * NF, [HBM] * 4,
        load_vector, row_map, coarse_id, face_link,
        scratch=[pltpu.SMEM((1, CB), jnp.int32), pltpu.SMEM((1, NF), jnp.int32),
                 pltpu.VMEM((1, NF, BS), jnp.int32), (NRHS, nf)],
        copies=4,
    )
    came = trade_faces(sides)

    def inside_solve(x, stage):
        flat = stage == "load"
        outs = [block, small, bf16(nf, nf), bf16(nf, nf), bf16(BS, nf), bf16(BS, nf)]
        scratch = [(NIN, BS, BS), (BS, NL), (nf, nf)] + [(NRHS, NIN * BS)] * flat
        return call(
            lambda *refs: interior_body(*refs, flat=flat), "interior_" + stage, outs,
            [HBM if flat else VMEM] + [HBM] * 3, x, interior_inv, coarse_basis, schur_inv,
            scratch=scratch, copies=4,
        )

    inner, part, *mats = inside_solve(load_vector, "load")
    r_face, outer, contrib, swap = call(
        first_faces_body, "faces_load", [face, face, side, bf16(NF, BS, BS)], [VMEM] * 15,
        *sides, *came, target, weight, *mats, part,
    )
    others = trade_line(contrib)
    high, low, back, u_face, *sends = call(
        lambda *refs: first_coarse_body(*refs, line=line), "coarse_load",
        [bf16(BS, width), bf16(BS, width), small, face] + [small] * NF, [HBM] + [VMEM] * (line + 6),
        coarse_all, column, contrib, *others, outer, *mats[2:], weight, swap,
        scratch=[(line, OCAP * CW, OCAP * CW)], copies=line,
    )

    def apply(inner, back, u_face, sends, stage):
        came = trade_faces(sends)
        wide = bf16(NF, BS, TPR * BS)
        z, acc, *wides = call(
            own_apply_body, "own_" + stage, [block, f32(*every), wide, wide],
            [VMEM, VMEM, HBM, VMEM, HBM, SMEM],
            inner, back, coarse_basis, u_face, matrix_tiles, cols,
            scratch=[(BS, NIN * BS), (NB, TPR, BS, BS)], copies=1 + NB,
        )
        y, z_face, *sends = call(
            face_apply_body, "face_" + stage, [f32(*every), face] + [small] * NF,
            [VMEM] * 8 + [SMEM, VMEM],
            acc, *came, u_face, *wides, cols, swap,
        )
        return z, z_face, y, sends

    z, z_face, y, sends = apply(inner, back, u_face, sends, "first")
    came = trade_faces(sends)
    inner, part, *mats = inside_solve(y, "image")
    q_face, outer, contrib = call(
        next_faces_body, "faces_image", [face, face, small], [VMEM] * 11,
        y, *came, weight, *mats, part,
    )
    others = trade_line(contrib)
    back, u_face, *sends = call(
        lambda *refs: next_coarse_body(*refs, line=line), "coarse_image",
        [small, face] + [small] * NF, [VMEM] * (line + 7),
        contrib, *others, high, low, outer, *mats[2:], weight, swap,
    )
    w, w_face, v, sends = apply(inner, back, u_face, sends, "second")
    came = trade_faces(sends)
    (dots,) = call(
        dots_body, "dots", [f32(devices, 2, BS)], [HBM] + [VMEM] * 6,
        load_vector, z, z_face, y, w, w_face, v, scratch=[(NRHS, NL)], copies=1,
    )
    spread = lax.all_to_all(dots, AXES, 0, 0)
    out = f32(1, NRHS, NL)
    return tuple(
        call(
            final_body, "combine", [out, out], [VMEM] * 5 + [HBM] + [VMEM] * 8,
            spread, *came, load_vector, r_face, z, z_face, y, q_face, w, w_face, v,
            scratch=[(NRHS, NIN * BS)], copies=1,
        )
    )


def solution(mesh):
    lead = P(AXES, None, None)
    flat = P(AXES, None)
    in_specs = (lead, P(AXES, None, None, None), flat, lead, lead, lead, lead, lead, flat, flat)
    return jax.shard_map(
        on_device, mesh=mesh, in_specs=in_specs, out_specs=(lead, lead), check_vma=False
    )
```

time: 123 us -> 103 us (0.84); the launches traced: 121 us -> 103 us
  local copies, waits for them, and re-layouts: 42.4 us -> 0.69 us
  waiting for transfers between devices: 9.95 us -> 23.5 us
  Pallas kernels: 15.4 us -> 27.9 us
  other arithmetic: 2.42 us -> 0 us
    unnamed x131 -> x4, local copies, waits for them, and re-layouts: 38.9 us -> 0.69 us
    all_gather x1, waiting for transfers between devices: 0.01 us -> 13.9 us  [on_device(): coarse_all = lax.all_gather(coarse_inv[0], 'gz', axis=0)]
    pallas_call x12 -> x13, Pallas kernels: 15.4 us -> 27.9 us  [call(): pl.pallas_call(body, name=name, out_shape=outs, in_specs=specs, out_specs...]
    all_to_all x1, waiting for transfers between devices: 1.71 us -> 0.01 us  [on_device(): spread = lax.all_to_all(dots, AXES, 0, 0)]
    ppermute x26, waiting for transfers between devices: 7.55 us -> 8.95 us  [trade(): return lax.ppermute(value, AXES, [(i, i ^ mask) for i in range(devices)])]
    concatenate x2 -> x0, local copies, waits for them, and re-layouts: 1.28 us -> none  [the longest x1 1.2 us: on_device(): target = jnp.concatenate([target, pad], axis=0)]
  transfers between devices with their start and end apart: 28 -> 28, of which waited for: 8 -> 10; matrix products, arithmetic and copies ran while one was open for 5% -> 0% of each run, Pallas kernels for 6% -> 18%
where the time goes in v2:
time: 103 us
  starting transfers between devices  36.4 us (35%)
  Pallas kernels  27.9 us (27%)
  waiting for transfers between devices  23.5 us (23%)
  between operations  14.2 us (14%)
    ppermute x26, starting transfers between devices, trade(): return lax.ppermute(value, AXES, [(i, i ^ mask) for i in range(devices)])  32.1 us
    pallas_call x13, Pallas kernels, call(): pl.pallas_call(body, name=name, out_shape=outs, in_specs=specs, out_specs...  27.9 us
    all_gather x1, waiting for transfers between devices, on_device(): coarse_all = lax.all_gather(coarse_inv[0], 'gz', axis=0)  13.9 us
    ppermute x26, waiting for transfers between devices, trade(): return lax.ppermute(value, AXES, [(i, i ^ mask) for i in range(devices)])  8.95 us
    all_to_all x1, starting transfers between devices, on_device(): spread = lax.all_to_all(dots, AXES, 0, 0)  4.22 us
  transfers between devices with their start and end apart: 28, of which 10 were waited for; matrix products, arithmetic and copies ran while one was open for 0% of the time, Pallas kernels for 18%

profile of v2, /device:TPU:0, one launch (start us, length us, event | category | flops | bytes accessed | tf_op | source)
XLA Modules:
  0.0 102.7 jit_solution(2133885920401908897)
XLA Ops:
  7.2 0.0 all-gather.2.cloned.1.call-start
  7.2 0.7 all-gather.2.cloned.1.call-update
  7.9 0.9 prepare.1
  8.8 3.1 %collective-permute-start = (f32[40,128]{1,0:T(8,128)S(1)}, f32[40,128]{1,0:T(8,128)S(1)}, u32[]{:S(2)}, u32[]{:S(2)}) collective-permute-start(f32[40,128]{1,0:T(8,128)S(1)} %get-tuple-element.64.own0), channel_id=1, source_target_pairs={{0,1},{1,0},{2,3},{3,2},{4,5},{5,4},{6,7},{7,6},{8,9},{9,8},{10,11... | collective-permute-start | bytes 61448 | tf_op jit(solution)/shard_map/ppermute | solution.py:352
  11.9 2.6 %collective-permute-start.1 = (f32[40,128]{1,0:T(8,128)S(1)}, f32[40,128]{1,0:T(8,128)S(1)}, u32[]{:S(2)}, u32[]{:S(2)}) collective-permute-start(f32[40,128]{1,0:T(8,128)S(1)} %get-tuple-element.65.own1), channel_id=1, source_target_pairs={{0,2},{1,3},{2,0},{3,1},{4,6},{5,7},{6,4},{7,5},{8,10},{9,11},{10,... | collective-permute-start | bytes 61448 | tf_op jit(solution)/shard_map/ppermute | solution.py:352
  14.5 1.5 %collective-permute-start.3 = (f32[40,128]{1,0:T(8,128)S(1)}, f32[40,128]{1,0:T(8,128)S(1)}, u32[]{:S(2)}, u32[]{:S(2)}) collective-permute-start(f32[40,128]{1,0:T(8,128)S(1)} %get-tuple-element.67.own3), channel_id=1, source_target_pairs={{0,8},{1,9},{2,10},{3,11},{4,12},{5,13},{6,14},{7,15},{8,0},{9,1},... | collective-permute-start | bytes 61448 | tf_op jit(solution)/shard_map/ppermute | solution.py:352
  16.0 2.7 %interior_load.1 = (f32[12,32,128]{2,1,0:T(8,128)S(1)}, f32[32,128]{1,0:T(8,128)S(1)}, bf16[512,512]{1,0:T(8,128)(2,1)S(1)}, bf16[512,512]{1,0:T(8,128)(2,1)S(1)...) custom-call(f32[1,32,2048]{2,1,0:T(8,128)} %load_h.1, f32[12,128,128]{2,1,0:T(8,128)} %refs_1_.3, ...), custom_call_target="tpu_custom_call" | custom-call | tf_op jit(solution)/shard_map/interior_load/pallas_call | solution.py:329
  18.8 1.2 %faces_load.1 = (f32[4,32,128]{2,1,0:T(8,128)S(1)}, f32[4,32,128]{2,1,0:T(8,128)S(1)}, f32[40,128]{1,0:T(8,128)S(1)}, bf16[4,128,128]{2,1,0:T(8,128)(2,1)S(1)}) custom-call(f32[40,128]{1,0:T(8,128)S(1)} %get-tuple-element.64.own0, f32[40,128]{1,0:T(8,128)S(1)} %get-tuple-element.65.own1, f32[40,128]{1,0:T(8,128)S(1)} %get-tuple-element.66.own2, ...), custom_call_target="tpu_custom_call" | custom-call | tf_op jit(solution)/shard_map/faces_load/pallas_call | solution.py:329
  19.9 0.3 collective-permute-start.6
  20.2 1.6 %collective-permute-start.5 = (f32[40,128]{1,0:T(8,128)S(1)}, f32[40,128]{1,0:T(8,128)S(1)}, u32[]{:S(2)}, u32[]{:S(2)}) collective-permute-start(f32[40,128]{1,0:T(8,128)S(1)} %get-tuple-element.75.refs_2_), channel_id=1, source_target_pairs={{0,2},{1,3},{2,0},{3,1},{4,6},{5,7},{6,4},{7,5},{8,10},{9,11},{10,... | collective-permute-start | bytes 61448 | tf_op jit(solution)/shard_map/ppermute | solution.py:352
  21.8 2.5 %collective-permute-start.4 = (f32[40,128]{1,0:T(8,128)S(1)}, f32[40,128]{1,0:T(8,128)S(1)}, u32[]{:S(2)}, u32[]{:S(2)}) collective-permute-start(f32[40,128]{1,0:T(8,128)S(1)} %get-tuple-element.75.refs_2_), channel_id=1, source_target_pairs={{0,1},{1,0},{2,3},{3,2},{4,5},{5,4},{6,7},{7,6},{8,9},{9,8},{10,11... | collective-permute-start | bytes 61448 | tf_op jit(solution)/shard_map/ppermute | solution.py:352
  24.3 1.4 %collective-permute-done.6.refs_5_ = f32[40,128]{1,0:T(8,128)S(1)} collective-permute-done((f32[40,128]{1,0:T(8,128)S(1)}, f32[40,128]{1,0:T(8,128)S(1)}, u32[]{:S(2)}, u32[]{:S(2)}) %collective-permute-start.6) | collective-permute-done | bytes 20512 | tf_op jit(solution)/shard_map/ppermute | solution.py:352
  25.7 0.6 collective-permute-done.5.refs_4_
  26.3 1.2 %collective-permute-done.4.refs_3_ = f32[40,128]{1,0:T(8,128)S(1)} collective-permute-done((f32[40,128]{1,0:T(8,128)S(1)}, f32[40,128]{1,0:T(8,128)S(1)}, u32[]{:S(2)}, u32[]{:S(2)}) %collective-permute-start.4) | collective-permute-done | bytes 20512 | tf_op jit(solution)/shard_map/ppermute | solution.py:352
  27.5 13.9 %all-gather.2.cloned.1.call-done.refs_0_ = f32[4,256,256]{2,1,0:T(8,128)} async-done(((f32[1,256,256]{2,1,0:T(8,128)}), f32[4,256,256]{2,1,0:T(8,128)}) %all-gather.2.cloned.1.call-update) | async-done | bytes 1048592 | tf_op jit(solution)/shard_map/all_gather | solution.py:360
  41.4 2.7 %coarse_load.1 = (bf16[128,512]{1,0:T(8,128)(2,1)S(1)}, bf16[128,512]{1,0:T(8,128)(2,1)S(1)}, f32[32,128]{1,0:T(8,128)S(1)}, f32[4,32,128]{2,1,0:T(8,128)S(1)}, ...) custom-call(f32[4,256,256]{2,1,0:T(8,128)} %all-gather.2.cloned.1.call-done.refs_0, ...), custom_call_target="tpu_custom_call" | custom-call | tf_op jit(solution)/shard_map/coarse_load/pallas_call | solution.py:329
  44.2 1.5 %collective-permute-start.7 = (f32[32,128]{1,0:T(8,128)S(1)}, f32[32,128]{1,0:T(8,128)S(1)}, u32[]{:S(2)}, u32[]{:S(2)}) collective-permute-start(f32[32,128]{1,0:T(8,128)S(1)} %get-tuple-element.82), channel_id=1, source_target_pairs={{0,1},{1,0},{2,3},{3,2},{4,5},{5,4},{6,7},{7,6},{8,9},{9,8},{10,11... | collective-permute-start | bytes 49160 | tf_op jit(solution)/shard_map/ppermute | solution.py:352
  45.7 1.1 %collective-permute-start.8 = (f32[32,128]{1,0:T(8,128)S(1)}, f32[32,128]{1,0:T(8,128)S(1)}, u32[]{:S(2)}, u32[]{:S(2)}) collective-permute-start(f32[32,128]{1,0:T(8,128)S(1)} %get-tuple-element.83), channel_id=1, source_target_pairs={{0,2},{1,3},{2,0},{3,1},{4,6},{5,7},{6,4},{7,5},{8,10},{9,11},{10,... | collective-permute-start | bytes 49160 | tf_op jit(solution)/shard_map/ppermute | solution.py:352
  46.8 1.5 %collective-permute-start.10 = (f32[32,128]{1,0:T(8,128)S(1)}, f32[32,128]{1,0:T(8,128)S(1)}, u32[]{:S(2)}, u32[]{:S(2)}) collective-permute-start(f32[32,128]{1,0:T(8,128)S(1)} %get-tuple-element.85), channel_id=1, source_target_pairs={{0,8},{1,9},{2,10},{3,11},{4,12},{5,13},{6,14},{7,15},{8,0},{9,1},... | collective-permute-start | bytes 49160 | tf_op jit(solution)/shard_map/ppermute | solution.py:352
  48.2 0.7 copy-done
  48.9 5.7 %own_first.1 = (f32[12,32,128]{2,1,0:T(8,128)S(1)}, f32[16,32,128]{2,1,0:T(8,128)S(1)}, bf16[4,128,896]{2,1,0:T(8,128)(2,1)S(1)}, bf16[4,128,896]{2,1,0:T(8,128)(2,1)S(1)}) custom-call(f32[12,32,128]{2,1,0:T(8,128)S(1)} %get-tuple-element.62.inner_ref, f32[32,128]{1,0:T(8,128)S(1)} %get-tuple-element.78.back_ref, f32[1,128,2048]{2,1,0:T(8,128)} %basis_ref.3, ...), custom_call_target="tpu_custom_call" | custom-call | tf_op jit(solution)/shard_map/own_first/pallas_call | solution.py:329
  54.6 1.2 %face_first.1 = (f32[16,32,128]{2,1,0:T(8,128)S(1)}, f32[4,32,128]{2,1,0:T(8,128)S(1)}, f32[32,128]{1,0:T(8,128)S(1)}, f32[32,128]{1,0:T(8,128)S(1)}, f32[32,128]{1,0:T(8,128)S(1)}, /*index=5*/f32[32,128]{1,0:T(8,128)S(1)}) custom-call(f32[16,32,128]{2,1,0:T(8,128)S(1)} %get-tuple-element.81.acc_ref, f32[32,128]{1,0:T(8,128)S(1)} %collective-permute-done.7.in0, ...), custom_call_target="tpu_custom_call" | custom-call | tf_op jit(solution)/shard_map/face_first/pallas_call | solution.py:329
  55.8 0.9 collective-permute-start.11
  56.7 2.0 %collective-permute-start.12 = (f32[32,128]{1,0:T(8,128)S(1)}, f32[32,128]{1,0:T(8,128)S(1)}, u32[]{:S(2)}, u32[]{:S(2)}) collective-permute-start(f32[32,128]{1,0:T(8,128)S(1)} %get-tuple-element.92), channel_id=1, source_target_pairs={{0,2},{1,3},{2,0},{3,1},{4,6},{5,7},{6,4},{7,5},{8,10},{9,11},{10,... | collective-permute-start | bytes 49160 | tf_op jit(solution)/shard_map/ppermute | solution.py:352
  58.7 0.1 collective-permute-start.14
  58.9 2.1 %interior_image.1 = (f32[12,32,128]{2,1,0:T(8,128)S(1)}, f32[32,128]{1,0:T(8,128)S(1)}, bf16[512,512]{1,0:T(8,128)(2,1)S(1)}, bf16[512,512]{1,0:T(8,128)(2,1)S(1...) custom-call(f32[16,32,128]{2,1,0:T(8,128)S(1)} %get-tuple-element.89.refs_0_.y_ref.y, ...), custom_call_target="tpu_custom_call" | custom-call | tf_op jit(solution)/shard_map/interior_image/pallas_call | solution.py:329
  60.9 0.4 collective-permute-done.12.in1
  61.4 1.1 %collective-permute-done.14.in3 = f32[32,128]{1,0:T(8,128)S(1)} collective-permute-done((f32[32,128]{1,0:T(8,128)S(1)}, f32[32,128]{1,0:T(8,128)S(1)}, u32[]{:S(2)}, u32[]{:S(2)}) %collective-permute-start.14) | collective-permute-done | bytes 16416 | tf_op jit(solution)/shard_map/ppermute | solution.py:352
  62.5 0.4 faces_image.1
  62.9 1.5 %collective-permute-start.17 = (f32[32,128]{1,0:T(8,128)S(1)}, f32[32,128]{1,0:T(8,128)S(1)}, u32[]{:S(2)}, u32[]{:S(2)}) collective-permute-start(f32[32,128]{1,0:T(8,128)S(1)} %get-tuple-element.100.refs_0_), channel_id=1, source_target_pairs={{0,3},{1,2},{2,1},{3,0},{4,7},{5,6},{6,5},{7,4},{8,11},{9,10},{10,... | collective-permute-start | bytes 49160 | tf_op jit(solution)/shard_map/ppermute | solution.py:352
  64.4 0.4 collective-permute-start.16
  64.8 2.5 %collective-permute-start.15 = (f32[32,128]{1,0:T(8,128)S(1)}, f32[32,128]{1,0:T(8,128)S(1)}, u32[]{:S(2)}, u32[]{:S(2)}) collective-permute-start(f32[32,128]{1,0:T(8,128)S(1)} %get-tuple-element.100.refs_0_), channel_id=1, source_target_pairs={{0,1},{1,0},{2,3},{3,2},{4,5},{5,4},{6,7},{7,6},{8,9},{9,8},{10,11... | collective-permute-start | bytes 49160 | tf_op jit(solution)/shard_map/ppermute | solution.py:352
  67.3 1.2 %collective-permute-done.17.refs_3_ = f32[32,128]{1,0:T(8,128)S(1)} collective-permute-done((f32[32,128]{1,0:T(8,128)S(1)}, f32[32,128]{1,0:T(8,128)S(1)}, u32[]{:S(2)}, u32[]{:S(2)}) %collective-permute-start.17) | collective-permute-done | bytes 16416 | tf_op jit(solution)/shard_map/ppermute | solution.py:352
  68.5 0.6 collective-permute-done.16.refs_2_
  69.1 0.6 coarse_image.1
  69.7 1.9 %collective-permute-start.18 = (f32[32,128]{1,0:T(8,128)S(1)}, f32[32,128]{1,0:T(8,128)S(1)}, u32[]{:S(2)}, u32[]{:S(2)}) collective-permute-start(f32[32,128]{1,0:T(8,128)S(1)} %get-tuple-element.108), channel_id=1, source_target_pairs={{0,1},{1,0},{2,3},{3,2},{4,5},{5,4},{6,7},{7,6},{8,9},{9,8},{10,11... | collective-permute-start | bytes 49160 | tf_op jit(solution)/shard_map/ppermute | solution.py:352
  71.6 0.9 collective-permute-start.19
  72.5 0.6 collective-permute-start.21
  73.1 5.7 %own_second.1 = (f32[12,32,128]{2,1,0:T(8,128)S(1)}, f32[16,32,128]{2,1,0:T(8,128)S(1)}, bf16[4,128,896]{2,1,0:T(8,128)(2,1)S(1)}, bf16[4,128,896]{2,1,0:T(8,128)(2,1)S(1)}) custom-call(f32[12,32,128]{2,1,0:T(8,128)S(1)} %get-tuple-element.90.inner_ref, f32[32,128]{1,0:T(8,128)S(1)} %get-tuple-element.104.back_ref, f32[1,128,2048]{2,1,0:T(8,128)} %basis_ref.3, ...), custom_call_target="tpu_custom_call" | custom-call | tf_op jit(solution)/shard_map/own_second/pallas_call | solution.py:329
  78.8 1.2 %face_second.1 = (f32[16,32,128]{2,1,0:T(8,128)S(1)}, f32[4,32,128]{2,1,0:T(8,128)S(1)}, f32[32,128]{1,0:T(8,128)S(1)}, f32[32,128]{1,0:T(8,128)S(1)}, f32[32,128]{1,0:T(8,128)S(1)}, /*index=5*/f32[32,128]{1,0:T(8,128)S(1)}) custom-call(f32[16,32,128]{2,1,0:T(8,128)S(1)} %get-tuple-element.107.acc_ref, f32[32,128]{1,0:T(8,128)S(1)} %collective-permute-done.18.in0, ...), custom_call_target="tpu_custom_call" | custom-call | tf_op jit(solution)/shard_map/face_second/pallas_call | solution.py:329
  80.0 1.8 %dots.1 = f32[32,2,128]{2,1,0:T(2,128)} custom-call(f32[1,32,2048]{2,1,0:T(8,128)} %load_h.1, f32[12,32,128]{2,1,0:T(8,128)S(1)} %get-tuple-element.80.zi, f32[4,32,128]{2,1,0:T(8,128)S(1)} %get-tuple-element.88.zf, f32[16,32,128]{2,1,0:T(8,128)S(1)} %get-tuple-element.89.refs_0_.y_ref.y, f32[12,32,128]{2,1,0:T(8,128)S(1)} %get-tuple-element.106.wi, ...), custom_call_target="tpu_custom_call" | custom-call | tf_op jit(solution)/shard_map/dots/pallas_call | solution.py:329
  81.9 4.2 %all-to-all-start = ((f32[32,2,128]{2,1,0:T(2,128)}), f32[32,2,128]{2,1,0:T(2,128)S(1)}, u32[]{:S(2)}, u32[]{:S(2)}) async-start(f32[32,2,128]{2,1,0:T(2,128)} %dots.1), calls=%async_computation | async-start | bytes 65536 | tf_op jit(solution)/shard_map/all_to_all | solution.py:434
  86.1 1.8 %collective-permute-start.22 = (f32[32,128]{1,0:T(8,128)S(1)}, f32[32,128]{1,0:T(8,128)S(1)}, u32[]{:S(2)}, u32[]{:S(2)}) collective-permute-start(f32[32,128]{1,0:T(8,128)S(1)} %get-tuple-element.116), channel_id=1, source_target_pairs={{0,1},{1,0},{2,3},{3,2},{4,5},{5,4},{6,7},{7,6},{8,9},{9,8},{10,11... | collective-permute-start | bytes 49160 | tf_op jit(solution)/shard_map/ppermute | solution.py:352
  87.9 2.4 %collective-permute-start.23 = (f32[32,128]{1,0:T(8,128)S(1)}, f32[32,128]{1,0:T(8,128)S(1)}, u32[]{:S(2)}, u32[]{:S(2)}) collective-permute-start(f32[32,128]{1,0:T(8,128)S(1)} %get-tuple-element.117), channel_id=1, source_target_pairs={{0,2},{1,3},{2,0},{3,1},{4,6},{5,7},{6,4},{7,5},{8,10},{9,11},{10,... | collective-permute-start | bytes 49160 | tf_op jit(solution)/shard_map/ppermute | solution.py:352
  90.3 1.5 %collective-permute-start.25 = (f32[32,128]{1,0:T(8,128)S(1)}, f32[32,128]{1,0:T(8,128)S(1)}, u32[]{:S(2)}, u32[]{:S(2)}) collective-permute-start(f32[32,128]{1,0:T(8,128)S(1)} %get-tuple-element.119), channel_id=1, source_target_pairs={{0,8},{1,9},{2,10},{3,11},{4,12},{5,13},{6,14},{7,15},{8,0},{9,1},... | collective-permute-start | bytes 49160 | tf_op jit(solution)/shard_map/ppermute | solution.py:352
  91.8 0.7 collective-permute-done.23.in1
  92.6 1.5 %collective-permute-done.25.in3 = f32[32,128]{1,0:T(8,128)S(1)} collective-permute-done((f32[32,128]{1,0:T(8,128)S(1)}, f32[32,128]{1,0:T(8,128)S(1)}, u32[]{:S(2)}, u32[]{:S(2)}) %collective-permute-start.25) | collective-permute-done | bytes 16416 | tf_op jit(solution)/shard_map/ppermute | solution.py:352
  94.1 1.8 %combine.1 = (f32[1,32,2048]{2,1,0:T(8,128)}, f32[1,32,2048]{2,1,0:T(8,128)}) custom-call(f32[32,2,128]{2,1,0:T(2,128)S(1)} %all-to-all-done.dots_ref, f32[32,128]{1,0:T(8,128)S(1)} %collective-permute-done.22.in0, f32[32,128]{1,0:T(8,128)S(1)} %collective-permute-done.23.in1, f32[32,128]{1,0:T(8,128)S(1)} %collective-permute-done.24.in2, ...), custom_call_target="tpu_custom_call" | custom-call | tf_op jit(solution)/shard_map/combine/pallas_call | solution.py:329
  (26 shorter events, 0.1 us)
Async XLA Ops:
  7.2 34.3 %all-gather.2.cloned.1.call-start = ((), (), s32[]{:S(2)}) async-start(), calls=%async_computation.1 | async-start | bytes 1310720 | tf_op jit(solution)/shard_map/all_gather | solution.py:360
  8.8 9.9 %collective-permute-start = (f32[40,128]{1,0:T(8,128)S(1)}, f32[40,128]{1,0:T(8,128)S(1)}, u32[]{:S(2)}, u32[]{:S(2)}) collective-permute-start(f32[40,128]{1,0:T(8,128)S(1)} %get-tuple-element.64.own0), channel_id=1, source_target_pairs={{0,1},{1,0},{2,3},{3,2},{4,5},{5,4},{6,7},{7,6},{8,9},{9,8},{10,11... | collective-permute-start | bytes 61448 | tf_op jit(solution)/shard_map/ppermute | solution.py:352
  11.9 6.8 %collective-permute-start.1 = (f32[40,128]{1,0:T(8,128)S(1)}, f32[40,128]{1,0:T(8,128)S(1)}, u32[]{:S(2)}, u32[]{:S(2)}) collective-permute-start(f32[40,128]{1,0:T(8,128)S(1)} %get-tuple-element.65.own1), channel_id=1, source_target_pairs={{0,2},{1,3},{2,0},{3,1},{4,6},{5,7},{6,4},{7,5},{8,10},{9,11},{10,... | collective-permute-start | bytes 61448 | tf_op jit(solution)/shard_map/ppermute | solution.py:352
  14.5 4.2 %collective-permute-start.2 = (f32[40,128]{1,0:T(8,128)S(1)}, f32[40,128]{1,0:T(8,128)S(1)}, u32[]{:S(2)}, u32[]{:S(2)}) collective-permute-start(f32[40,128]{1,0:T(8,128)S(1)} %get-tuple-element.66.own2), channel_id=1, source_target_pairs={{0,4},{1,5},{2,6},{3,7},{4,0},{5,1},{6,2},{7,3},{8,12},{9,13},{10,... | collective-permute-start | bytes 61448 | tf_op jit(solution)/shard_map/ppermute | solution.py:352
  14.5 4.3 %collective-permute-start.3 = (f32[40,128]{1,0:T(8,128)S(1)}, f32[40,128]{1,0:T(8,128)S(1)}, u32[]{:S(2)}, u32[]{:S(2)}) collective-permute-start(f32[40,128]{1,0:T(8,128)S(1)} %get-tuple-element.67.own3), channel_id=1, source_target_pairs={{0,8},{1,9},{2,10},{3,11},{4,12},{5,13},{6,14},{7,15},{8,0},{9,1},... | collective-permute-start | bytes 61448 | tf_op jit(solution)/shard_map/ppermute | solution.py:352
  19.9 5.8 %collective-permute-start.6 = (f32[40,128]{1,0:T(8,128)S(1)}, f32[40,128]{1,0:T(8,128)S(1)}, u32[]{:S(2)}, u32[]{:S(2)}) collective-permute-start(f32[40,128]{1,0:T(8,128)S(1)} %get-tuple-element.75.refs_2_), channel_id=1, source_target_pairs={{0,3},{1,2},{2,1},{3,0},{4,7},{5,6},{6,5},{7,4},{8,11},{9,10},{10,... | collective-permute-start | bytes 61448 | tf_op jit(solution)/shard_map/ppermute | solution.py:352
  20.2 6.1 %collective-permute-start.5 = (f32[40,128]{1,0:T(8,128)S(1)}, f32[40,128]{1,0:T(8,128)S(1)}, u32[]{:S(2)}, u32[]{:S(2)}) collective-permute-start(f32[40,128]{1,0:T(8,128)S(1)} %get-tuple-element.75.refs_2_), channel_id=1, source_target_pairs={{0,2},{1,3},{2,0},{3,1},{4,6},{5,7},{6,4},{7,5},{8,10},{9,11},{10,... | collective-permute-start | bytes 61448 | tf_op jit(solution)/shard_map/ppermute | solution.py:352
  21.8 5.7 %collective-permute-start.4 = (f32[40,128]{1,0:T(8,128)S(1)}, f32[40,128]{1,0:T(8,128)S(1)}, u32[]{:S(2)}, u32[]{:S(2)}) collective-permute-start(f32[40,128]{1,0:T(8,128)S(1)} %get-tuple-element.75.refs_2_), channel_id=1, source_target_pairs={{0,1},{1,0},{2,3},{3,2},{4,5},{5,4},{6,7},{7,6},{8,9},{9,8},{10,11... | collective-permute-start | bytes 61448 | tf_op jit(solution)/shard_map/ppermute | solution.py:352
  44.2 10.4 %collective-permute-start.7 = (f32[32,128]{1,0:T(8,128)S(1)}, f32[32,128]{1,0:T(8,128)S(1)}, u32[]{:S(2)}, u32[]{:S(2)}) collective-permute-start(f32[32,128]{1,0:T(8,128)S(1)} %get-tuple-element.82), channel_id=1, source_target_pairs={{0,1},{1,0},{2,3},{3,2},{4,5},{5,4},{6,7},{7,6},{8,9},{9,8},{10,11... | collective-permute-start | bytes 49160 | tf_op jit(solution)/shard_map/ppermute | solution.py:352
  45.7 8.9 %collective-permute-start.8 = (f32[32,128]{1,0:T(8,128)S(1)}, f32[32,128]{1,0:T(8,128)S(1)}, u32[]{:S(2)}, u32[]{:S(2)}) collective-permute-start(f32[32,128]{1,0:T(8,128)S(1)} %get-tuple-element.83), channel_id=1, source_target_pairs={{0,2},{1,3},{2,0},{3,1},{4,6},{5,7},{6,4},{7,5},{8,10},{9,11},{10,... | collective-permute-start | bytes 49160 | tf_op jit(solution)/shard_map/ppermute | solution.py:352
  46.8 7.9 %collective-permute-start.9 = (f32[32,128]{1,0:T(8,128)S(1)}, f32[32,128]{1,0:T(8,128)S(1)}, u32[]{:S(2)}, u32[]{:S(2)}) collective-permute-start(f32[32,128]{1,0:T(8,128)S(1)} %get-tuple-element.84), channel_id=1, source_target_pairs={{0,4},{1,5},{2,6},{3,7},{4,0},{5,1},{6,2},{7,3},{8,12},{9,13},{10,... | collective-permute-start | bytes 49160 | tf_op jit(solution)/shard_map/ppermute | solution.py:352
  46.8 7.9 %collective-permute-start.10 = (f32[32,128]{1,0:T(8,128)S(1)}, f32[32,128]{1,0:T(8,128)S(1)}, u32[]{:S(2)}, u32[]{:S(2)}) collective-permute-start(f32[32,128]{1,0:T(8,128)S(1)} %get-tuple-element.85), channel_id=1, source_target_pairs={{0,8},{1,9},{2,10},{3,11},{4,12},{5,13},{6,14},{7,15},{8,0},{9,1},... | collective-permute-start | bytes 49160 | tf_op jit(solution)/shard_map/ppermute | solution.py:352
  48.2 0.7 copy-start
  48.9 24.2 %copy-start.1 = (s32[16,7]{0,1:T(8,128)S(1)}, s32[16,7]{0,1:T(8,128)}, u32[]{:S(2)}) copy-start(s32[16,7]{0,1:T(8,128)} %param.12) | copy-start | bytes 1348
  55.8 5.1 %collective-permute-start.11 = (f32[32,128]{1,0:T(8,128)S(1)}, f32[32,128]{1,0:T(8,128)S(1)}, u32[]{:S(2)}, u32[]{:S(2)}) collective-permute-start(f32[32,128]{1,0:T(8,128)S(1)} %get-tuple-element.91), channel_id=1, source_target_pairs={{0,1},{1,0},{2,3},{3,2},{4,5},{5,4},{6,7},{7,6},{8,9},{9,8},{10,11... | collective-permute-start | bytes 49160 | tf_op jit(solution)/shard_map/ppermute | solution.py:352
  56.7 4.6 %collective-permute-start.12 = (f32[32,128]{1,0:T(8,128)S(1)}, f32[32,128]{1,0:T(8,128)S(1)}, u32[]{:S(2)}, u32[]{:S(2)}) collective-permute-start(f32[32,128]{1,0:T(8,128)S(1)} %get-tuple-element.92), channel_id=1, source_target_pairs={{0,2},{1,3},{2,0},{3,1},{4,6},{5,7},{6,4},{7,5},{8,10},{9,11},{10,... | collective-permute-start | bytes 49160 | tf_op jit(solution)/shard_map/ppermute | solution.py:352
  58.7 2.6 %collective-permute-start.13 = (f32[32,128]{1,0:T(8,128)S(1)}, f32[32,128]{1,0:T(8,128)S(1)}, u32[]{:S(2)}, u32[]{:S(2)}) collective-permute-start(f32[32,128]{1,0:T(8,128)S(1)} %get-tuple-element.93), channel_id=1, source_target_pairs={{0,4},{1,5},{2,6},{3,7},{4,0},{5,1},{6,2},{7,3},{8,12},{9,13},{10,... | collective-permute-start | bytes 49160 | tf_op jit(solution)/shard_map/ppermute | solution.py:352
  58.7 3.7 %collective-permute-start.14 = (f32[32,128]{1,0:T(8,128)S(1)}, f32[32,128]{1,0:T(8,128)S(1)}, u32[]{:S(2)}, u32[]{:S(2)}) collective-permute-start(f32[32,128]{1,0:T(8,128)S(1)} %get-tuple-element.94), channel_id=1, source_target_pairs={{0,8},{1,9},{2,10},{3,11},{4,12},{5,13},{6,14},{7,15},{8,0},{9,1},... | collective-permute-start | bytes 49160 | tf_op jit(solution)/shard_map/ppermute | solution.py:352
  62.9 5.6 %collective-permute-start.17 = (f32[32,128]{1,0:T(8,128)S(1)}, f32[32,128]{1,0:T(8,128)S(1)}, u32[]{:S(2)}, u32[]{:S(2)}) collective-permute-start(f32[32,128]{1,0:T(8,128)S(1)} %get-tuple-element.100.refs_0_), channel_id=1, source_target_pairs={{0,3},{1,2},{2,1},{3,0},{4,7},{5,6},{6,5},{7,4},{8,11},{9,10},{10,... | collective-permute-start | bytes 49160 | tf_op jit(solution)/shard_map/ppermute | solution.py:352
  64.4 4.7 %collective-permute-start.16 = (f32[32,128]{1,0:T(8,128)S(1)}, f32[32,128]{1,0:T(8,128)S(1)}, u32[]{:S(2)}, u32[]{:S(2)}) collective-permute-start(f32[32,128]{1,0:T(8,128)S(1)} %get-tuple-element.100.refs_0_), channel_id=1, source_target_pairs={{0,2},{1,3},{2,0},{3,1},{4,6},{5,7},{6,4},{7,5},{8,10},{9,11},{10,... | collective-permute-start | bytes 49160 | tf_op jit(solution)/shard_map/ppermute | solution.py:352
  64.8 4.4 %collective-permute-start.15 = (f32[32,128]{1,0:T(8,128)S(1)}, f32[32,128]{1,0:T(8,128)S(1)}, u32[]{:S(2)}, u32[]{:S(2)}) collective-permute-start(f32[32,128]{1,0:T(8,128)S(1)} %get-tuple-element.100.refs_0_), channel_id=1, source_target_pairs={{0,1},{1,0},{2,3},{3,2},{4,5},{5,4},{6,7},{7,6},{8,9},{9,8},{10,11... | collective-permute-start | bytes 49160 | tf_op jit(solution)/shard_map/ppermute | solution.py:352
  69.7 9.1 %collective-permute-start.18 = (f32[32,128]{1,0:T(8,128)S(1)}, f32[32,128]{1,0:T(8,128)S(1)}, u32[]{:S(2)}, u32[]{:S(2)}) collective-permute-start(f32[32,128]{1,0:T(8,128)S(1)} %get-tuple-element.108), channel_id=1, source_target_pairs={{0,1},{1,0},{2,3},{3,2},{4,5},{5,4},{6,7},{7,6},{8,9},{9,8},{10,11... | collective-permute-start | bytes 49160 | tf_op jit(solution)/shard_map/ppermute | solution.py:352
  71.6 7.2 %collective-permute-start.19 = (f32[32,128]{1,0:T(8,128)S(1)}, f32[32,128]{1,0:T(8,128)S(1)}, u32[]{:S(2)}, u32[]{:S(2)}) collective-permute-start(f32[32,128]{1,0:T(8,128)S(1)} %get-tuple-element.109), channel_id=1, source_target_pairs={{0,2},{1,3},{2,0},{3,1},{4,6},{5,7},{6,4},{7,5},{8,10},{9,11},{10,... | collective-permute-start | bytes 49160 | tf_op jit(solution)/shard_map/ppermute | solution.py:352
  72.5 6.3 %collective-permute-start.20 = (f32[32,128]{1,0:T(8,128)S(1)}, f32[32,128]{1,0:T(8,128)S(1)}, u32[]{:S(2)}, u32[]{:S(2)}) collective-permute-start(f32[32,128]{1,0:T(8,128)S(1)} %get-tuple-element.110), channel_id=1, source_target_pairs={{0,4},{1,5},{2,6},{3,7},{4,0},{5,1},{6,2},{7,3},{8,12},{9,13},{10,... | collective-permute-start | bytes 49160 | tf_op jit(solution)/shard_map/ppermute | solution.py:352
  72.5 6.3 %collective-permute-start.21 = (f32[32,128]{1,0:T(8,128)S(1)}, f32[32,128]{1,0:T(8,128)S(1)}, u32[]{:S(2)}, u32[]{:S(2)}) collective-permute-start(f32[32,128]{1,0:T(8,128)S(1)} %get-tuple-element.111), channel_id=1, source_target_pairs={{0,8},{1,9},{2,10},{3,11},{4,12},{5,13},{6,14},{7,15},{8,0},{9,1},... | collective-permute-start | bytes 49160 | tf_op jit(solution)/shard_map/ppermute | solution.py:352
  81.9 12.2 %all-to-all-start = ((f32[32,2,128]{2,1,0:T(2,128)}), f32[32,2,128]{2,1,0:T(2,128)S(1)}, u32[]{:S(2)}, u32[]{:S(2)}) async-start(f32[32,2,128]{2,1,0:T(2,128)} %dots.1), calls=%async_computation | async-start | bytes 65536 | tf_op jit(solution)/shard_map/all_to_all | solution.py:434
  86.1 5.7 %collective-permute-start.22 = (f32[32,128]{1,0:T(8,128)S(1)}, f32[32,128]{1,0:T(8,128)S(1)}, u32[]{:S(2)}, u32[]{:S(2)}) collective-permute-start(f32[32,128]{1,0:T(8,128)S(1)} %get-tuple-element.116), channel_id=1, source_target_pairs={{0,1},{1,0},{2,3},{3,2},{4,5},{5,4},{6,7},{7,6},{8,9},{9,8},{10,11... | collective-permute-start | bytes 49160 | tf_op jit(solution)/shard_map/ppermute | solution.py:352
  87.9 4.6 %collective-permute-start.23 = (f32[32,128]{1,0:T(8,128)S(1)}, f32[32,128]{1,0:T(8,128)S(1)}, u32[]{:S(2)}, u32[]{:S(2)}) collective-permute-start(f32[32,128]{1,0:T(8,128)S(1)} %get-tuple-element.117), channel_id=1, source_target_pairs={{0,2},{1,3},{2,0},{3,1},{4,6},{5,7},{6,4},{7,5},{8,10},{9,11},{10,... | collective-permute-start | bytes 49160 | tf_op jit(solution)/shard_map/ppermute | solution.py:352
  90.3 2.2 %collective-permute-start.24 = (f32[32,128]{1,0:T(8,128)S(1)}, f32[32,128]{1,0:T(8,128)S(1)}, u32[]{:S(2)}, u32[]{:S(2)}) collective-permute-start(f32[32,128]{1,0:T(8,128)S(1)} %get-tuple-element.118), channel_id=1, source_target_pairs={{0,4},{1,5},{2,6},{3,7},{4,0},{5,1},{6,2},{7,3},{8,12},{9,13},{10,... | collective-permute-start | bytes 49160 | tf_op jit(solution)/shard_map/ppermute | solution.py:352
  90.3 3.7 %collective-permute-start.25 = (f32[32,128]{1,0:T(8,128)S(1)}, f32[32,128]{1,0:T(8,128)S(1)}, u32[]{:S(2)}, u32[]{:S(2)}) collective-permute-start(f32[32,128]{1,0:T(8,128)S(1)} %get-tuple-element.119), channel_id=1, source_target_pairs={{0,8},{1,9},{2,10},{3,11},{4,12},{5,13},{6,14},{7,15},{8,0},{9,1},... | collective-permute-start | bytes 49160 | tf_op jit(solution)/shard_map/ppermute | solution.py:352
Sparse Core Ops, SparseCore 0:
  9.6 31.8 all-gather.1

commit v3 on v2

--- a/solution.py
+++ b/solution.py
@@ -12,6 +12,8 @@
 CW = 32
 CB = 4
 OCAP = 8
+SCAP = 2
+AHEAD = 4
 NB = 16
 TPR = 7
 NL = 2048
@@ -69,15 +71,24 @@
         (load_ref.at[0, :, NIN * BS :], faces),
     )
     copies[0].wait()
-    lane = lax.broadcasted_iota(jnp.int32, (8, BS), 1)
-    row = lax.broadcasted_iota(jnp.int32, (BS, BS), 0)
-    target = lane % CW
-    column = row % CW
+    along = lax.broadcasted_iota(jnp.int32, (8, BS), 1)
+    down = lax.broadcasted_iota(jnp.int32, (BS, BS), 0)
+    target, place = along % CW, along % CW
+    column, spot = down % CW, down % CW
     for b in range(CB):
-        target = jnp.where(lane // CW == b, target + ids[0, b] * CW, target)
-        column = jnp.where(row // CW == b, column + ids[0, b] * CW, column)
-    target_ref[...] = target.astype(F32)
-    column_ref[...] = column.astype(F32)
+        start = ids[0, b] * CW
+        before = jnp.int32(0)
+        for other in range(b):
+            before = before + jnp.where(ids[0, other] // OCAP == ids[0, b] // OCAP, CW, 0)
+        target = jnp.where(along // CW == b, target + start, target)
+        place = jnp.where(along // CW == b, place + before, place)
+        column = jnp.where(down // CW == b, column + start, column)
+        spot = jnp.where(down // CW == b, spot + before, spot)
+    line = lax.broadcasted_iota(jnp.int32, (8, BS), 0)
+    target = jnp.where(line == 1, place, target).astype(F32)
+    target_ref[...] = target
+    column_ref[0] = column
+    column_ref[1] = spot
     copies[1].wait()
     for r in range(NF):
         link = jnp.full((1, BS), links[0, r], jnp.int32).astype(F32)
@@ -87,18 +98,25 @@
     copies[3].wait()
     for r, out in enumerate((side0, side1, side2, side3)):
         out[:NRHS, :] = faces[:, lanes(r)]
-        out[NRHS:, :] = jnp.broadcast_to(maps[0, r : r + 1, :], (8, BS)).astype(F32)
+        out[NRHS : NRHS + 8, :] = jnp.broadcast_to(maps[0, r : r + 1, :], (8, BS)).astype(F32)
+        out[NRHS + 8 :, :] = target
 
 
 def interior_body(
     x_ref, inv_ref, basis_ref, schur_ref,
-    inner_ref, part_ref, schur_high, schur_low, basis_high, basis_low, *scratch, flat,
-):
+    *rest, flat,
+):
+    if flat:
+        coarse_ref, *rest = rest
+    inner_ref, part_ref, schur_high, schur_low, basis_high, basis_low, *scratch = rest
+    if flat:
+        coarse_parts, *scratch = scratch
     inv, basis, schur = scratch[:3]
     sems = scratch[-1]
     pairs = [(inv_ref, inv), (basis_ref.at[0], basis), (schur_ref.at[0], schur)]
     if flat:
         pairs.append((x_ref.at[0, :, : NIN * BS], scratch[3]))
+        pairs.append((coarse_ref.at[0], scratch[4]))
     copies = start_all(sems, *pairs)
     if flat:
         copies[3].wait()
@@ -114,6 +132,12 @@
     basis_high[...], basis_low[...] = halves(basis[:, NIN * BS :])
     copies[2].wait()
     schur_high[...], schur_low[...] = halves(schur[...])
+    if flat:
+        copies[4].wait()
+        value = scratch[4][...]
+        for k in range(3):
+            coarse_parts[k] = value.astype(BF16)
+            value = value - coarse_parts[k].astype(F32)
 
 
 def face_solve(faces, mats, weight_ref, part_ref, outer_ref, contrib_ref):
@@ -131,9 +155,12 @@
 
 def first_faces_body(
     own0, own1, own2, own3, in0, in1, in2, in3, target_ref, weight_ref,
-    schur_high, schur_low, basis_high, basis_low, part_ref,
-    face_ref, outer_ref, contrib_ref, swap_ref,
-):
+    schur_high, schur_low, basis_high, basis_low, part_ref, coarse_ref, *rest, line,
+):
+    targets = [target_ref[...], in0[NRHS + 8 :, :], in1[NRHS + 8 :, :]] + [
+        ref[...] for ref in rest[: line - 3]
+    ]
+    face_ref, outer_ref, contrib_ref, swap_ref, all_ref, rows_ref, *sides = rest[line - 3 :]
     faces = []
     rows = lax.broadcasted_iota(jnp.int32, (BS, BS), 0).astype(F32)
     for r, (own, inc) in enumerate(zip((own0, own1, own2, own3), (in0, in1, in2, in3))):
@@ -144,9 +171,26 @@
         came = select_lanes(inc[:NRHS, :], (mm(theirs, mine, NT) * link).astype(BF16))
         faces.append(own[:NRHS, :] + came)
         face_ref[r] = faces[-1]
-    contrib_ref[NRHS:, :] = target_ref[...]
     mats = (schur_high, schur_low, basis_high, basis_low)
     face_solve(faces, mats, weight_ref, part_ref, outer_ref, contrib_ref)
+    here = lax.axis_index("gz")
+    own = OCAP * CW
+    slots = lax.broadcasted_iota(jnp.int32, (SCAP * CW, BS), 0)
+    places = lax.broadcasted_iota(jnp.int32, (own, BS), 0)
+    all_ref[...] = jnp.concatenate([t[0:1, :] for t in targets], axis=1)
+    for m, target in enumerate(targets):
+        goal = target.astype(jnp.int32)
+        into = (slots == goal[1:2, :]).astype(F32).astype(BF16)
+        out_of = (places == goal[0:1, :] - here * own).astype(F32).astype(BF16)
+        take = mm(into, out_of, NT).astype(BF16)
+        rows = mm(take, coarse_ref[0]) + mm(take, coarse_ref[1]) + mm(take, coarse_ref[2])
+        if m == 0:
+            rows_ref[: SCAP * CW, :] = rows[:, :BS]
+            rows_ref[SCAP * CW :, :] = rows[:, BS:]
+        else:
+            sides[m - 1][:NRHS, :] = contrib_ref[...]
+            sides[m - 1][NRHS : NRHS + SCAP * CW, :] = rows[:, :BS]
+            sides[m - 1][NRHS + SCAP * CW :, :] = rows[:, BS:]
 
 
 def next_faces_body(
@@ -161,8 +205,7 @@
     face_solve(faces, mats, weight_ref, part_ref, outer_ref, contrib_ref)
 
 
-def correct(contribs, table, outer_ref, basis, weight_ref, swap_ref, back_ref, face_ref, outs):
-    back = dot_halves(halves(jnp.concatenate(contribs, axis=1)), table, NT)
+def finish(back, outer_ref, basis, weight_ref, swap_ref, back_ref, face_ref, outs):
     back_ref[...] = back
     corr = dot_halves(halves(back), basis)
     for r in range(NF):
@@ -171,40 +214,61 @@
         outs[r][...] = select_lanes(value, swap_ref[r])
 
 
-def first_coarse_body(*refs, line):
-    coarse_hbm, column_ref = refs[:2]
-    sides = refs[2 : 2 + line]
-    outer_ref, basis_high, basis_low, weight_ref, swap_ref = refs[2 + line : 7 + line]
-    high_ref, low_ref, back_ref, face_ref = refs[7 + line : 11 + line]
-    outs = refs[11 + line : 11 + line + NF]
-    coarse, sems = refs[11 + line + NF :]
-    copies = start_all(sems, *[(coarse_hbm.at[o], coarse.at[o]) for o in range(line)])
-    targets = jnp.concatenate([side[NRHS : NRHS + 1, :] for side in sides], axis=1)
-    own = OCAP * CW
-    rows = lax.broadcasted_iota(jnp.int32, (own, line * CB * CW), 0).astype(F32)
-    places = lax.broadcasted_iota(jnp.int32, (BS, own), 1).astype(F32)
-    column = jnp.concatenate([column_ref[...]] * (own // BS), axis=1)
-    table = jnp.zeros((2 * BS, line * CB * CW), F32)
-    for o in range(line):
-        pick = (rows + float(o * own) == targets).astype(F32).astype(BF16)
-        take = (places + float(o * own) == column).astype(F32).astype(BF16)
-        copies[o].wait()
-        high, low = halves(coarse[o])
+def owner_rows(side, m):
+    first = NRHS if m else 0
+    return jnp.concatenate(
+        [side[first : first + SCAP * CW, :], side[first + SCAP * CW :, :]], axis=1
+    )
+
+
+def pick_of(all_ref, owner):
+    rows = lax.broadcasted_iota(jnp.int32, (OCAP * CW, all_ref.shape[1]), 0)
+    return (rows + owner * (OCAP * CW) == all_ref[...].astype(jnp.int32)).astype(F32).astype(BF16)
+
+
+def first_coarse_body(own_ref, rows_ref, all_ref, target_ref, *refs, line):
+    sides = (rows_ref,) + refs[: line - 1]
+    outer_ref, basis_high, basis_low, weight_ref, swap_ref, back_ref, face_ref, *outs = refs[line - 1 :]
+    here = lax.axis_index("gz")
+    contribs = halves(jnp.concatenate([own_ref[...]] + [s[:NRHS, :] for s in sides[1:]], axis=1))
+    stack = jnp.concatenate(contribs, axis=0)
+    slots = lax.broadcasted_iota(jnp.int32, (SCAP * CW, BS), 0)
+    goal = target_ref[...].astype(jnp.int32)
+    back = jnp.zeros((NRHS, BS), F32)
+    for m in range(line):
+        owner = jnp.bitwise_xor(here, m)
+        both = mm(stack, pick_of(all_ref, owner), NT)
+        solved = dot_halves(halves(both[:NRHS] + both[NRHS:]), halves(owner_rows(sides[m], m)), NT)
+        mine = (slots == goal[1:2, :]) & (goal[0:1, :] // (OCAP * CW) == owner)
+        back = back + select_lanes(solved, mine.astype(F32).astype(BF16))
+    finish(back, outer_ref, (basis_high[...], basis_low[...]), weight_ref, swap_ref, back_ref, face_ref, outs)
+
+
+def table_body(rows_ref, all_ref, column_ref, *refs, line):
+    sides = (rows_ref,) + refs[: line - 1]
+    high_ref, low_ref = refs[line - 1 :]
+    here = lax.axis_index("gz")
+    slots = lax.broadcasted_iota(jnp.int32, (BS, BS), 1)
+    table = jnp.zeros((2 * BS, all_ref.shape[1]), F32)
+    for m in range(line):
+        owner = jnp.bitwise_xor(here, m)
+        mine = (slots == column_ref[1]) & (column_ref[0] // (OCAP * CW) == owner)
+        take = mine.astype(F32).astype(BF16)[:, : SCAP * CW]
+        high, low = halves(owner_rows(sides[m], m))
         both = jnp.concatenate([mm(take, high).astype(BF16), mm(take, low).astype(BF16)], axis=0)
-        table = table + mm(both, pick)
+        table = table + mm(both, pick_of(all_ref, owner))
     high_ref[...] = table[:BS].astype(BF16)
     low_ref[...] = table[BS:].astype(BF16)
-    contribs = [side[:NRHS, :] for side in sides]
-    correct(contribs, (high_ref[...], low_ref[...]), outer_ref, (basis_high[...], basis_low[...]),
-            weight_ref, swap_ref, back_ref, face_ref, outs)
 
 
 def next_coarse_body(*refs, line):
     contribs = [ref[...] for ref in refs[:line]]
     high_ref, low_ref, outer_ref, basis_high, basis_low, weight_ref, swap_ref = refs[line : 7 + line]
     back_ref, face_ref = refs[7 + line : 9 + line]
-    correct(contribs, (high_ref[...], low_ref[...]), outer_ref, (basis_high[...], basis_low[...]),
-            weight_ref, swap_ref, back_ref, face_ref, refs[9 + line :])
+    table = (high_ref[...], low_ref[...])
+    back = dot_halves(halves(jnp.concatenate(contribs, axis=1)), table, NT)
+    finish(back, outer_ref, (basis_high[...], basis_low[...]), weight_ref, swap_ref, back_ref, face_ref,
+           refs[9 + line :])
 
 
 def add_row(x, i, wide, cols_ref, acc_ref):
@@ -221,7 +285,9 @@
 ):
     pairs = [(basis_ref.at[0, :, : NIN * BS], basis)]
     pairs += [(tiles_ref.at[i], tiles.at[i]) for i in range(NB)]
-    copies = start_all(sems, *pairs)
+    copies = [pltpu.make_async_copy(src, dst, sems.at[k]) for k, (src, dst) in enumerate(pairs)]
+    for copy in copies[: 1 + AHEAD]:
+        copy.start()
     acc_ref[...] = jnp.zeros_like(acc_ref)
     back = halves(back_ref[...])
     copies[0].wait()
@@ -229,6 +295,8 @@
         z_ref[b] = inner_ref[b] + dot_halves(back, halves(basis[:, lanes(b)]))
     for i in range(NB):
         copies[1 + i].wait()
+        if i + AHEAD < NB:
+            copies[1 + i + AHEAD].start()
         wide = halves(jnp.concatenate([tiles[i, t] for t in range(TPR)], axis=1))
         if i >= NIN:
             wide_high[i - NIN], wide_low[i - NIN] = wide
@@ -357,43 +425,52 @@
     def trade_line(value):
         return [trade(value, mask) for mask in range(1, line)]
 
-    coarse_all = lax.all_gather(coarse_inv[0], "gz", axis=0)
     inside = (NIN, NRHS, BS)
     around = (NF, NRHS, BS)
     every = (NB, NRHS, BS)
-    block, face, small, side = f32(*inside), f32(*around), f32(NRHS, BS), f32(NRHS + 8, BS)
+    block, face, small, side = f32(*inside), f32(*around), f32(NRHS, BS), f32(NRHS + 16, BS)
     nf = NF * BS
     width = line * CB * CW
     target, column, weight, *sides = call(
-        prepare_body, "prepare", [f32(8, BS), f32(BS, BS), f32(2 * NF, BS)] + [side] * NF, [HBM] * 4,
+        prepare_body, "prepare", [f32(8, BS), jax.ShapeDtypeStruct((2, BS, BS), jnp.int32), f32(2 * NF, BS)] + [side] * NF, [HBM] * 4,
         load_vector, row_map, coarse_id, face_link,
         scratch=[pltpu.SMEM((1, CB), jnp.int32), pltpu.SMEM((1, NF), jnp.int32),
                  pltpu.VMEM((1, NF, BS), jnp.int32), (NRHS, nf)],
         copies=4,
     )
     came = trade_faces(sides)
+    far = [trade(target, mask) for mask in range(3, line)]
 
     def inside_solve(x, stage):
         flat = stage == "load"
         outs = [block, small, bf16(nf, nf), bf16(nf, nf), bf16(BS, nf), bf16(BS, nf)]
-        scratch = [(NIN, BS, BS), (BS, NL), (nf, nf)] + [(NRHS, NIN * BS)] * flat
+        scratch = [(NIN, BS, BS), (BS, NL), (nf, nf)]
+        args = [x, interior_inv, coarse_basis, schur_inv]
+        if flat:
+            own = OCAP * CW
+            outs.append(bf16(3, own, own))
+            scratch += [(NRHS, NIN * BS), (own, own)]
+            args.append(coarse_inv)
         return call(
             lambda *refs: interior_body(*refs, flat=flat), "interior_" + stage, outs,
-            [HBM if flat else VMEM] + [HBM] * 3, x, interior_inv, coarse_basis, schur_inv,
-            scratch=scratch, copies=4,
+            [HBM if flat else VMEM] + [HBM] * (len(args) - 1), *args, scratch=scratch, copies=5,
         )
 
-    inner, part, *mats = inside_solve(load_vector, "load")
-    r_face, outer, contrib, swap = call(
-        first_faces_body, "faces_load", [face, face, side, bf16(NF, BS, BS)], [VMEM] * 15,
-        *sides, *came, target, weight, *mats, part,
-    )
-    others = trade_line(contrib)
-    high, low, back, u_face, *sends = call(
+    inner, part, *mats, coarse_parts = inside_solve(load_vector, "load")
+    width = line * CB * CW
+    half = 2 * SCAP * CW
+    r_face, outer, contrib, swap, targets, rows, *sides = call(
+        lambda *refs: first_faces_body(*refs, line=line), "faces_load",
+        [face, face, small, bf16(NF, BS, BS), f32(1, width), f32(half, BS)]
+        + [f32(NRHS + half, BS)] * (line - 1),
+        [VMEM] * (13 + line),
+        *sides, *came, target, weight, *mats, part, coarse_parts, *far,
+    )
+    others = [trade(value, mask) for value, mask in zip(sides, range(1, line))]
+    back, u_face, *sends = call(
         lambda *refs: first_coarse_body(*refs, line=line), "coarse_load",
-        [bf16(BS, width), bf16(BS, width), small, face] + [small] * NF, [HBM] + [VMEM] * (line + 6),
-        coarse_all, column, contrib, *others, outer, *mats[2:], weight, swap,
-        scratch=[(line, OCAP * CW, OCAP * CW)], copies=line,
+        [small, face] + [small] * NF, [VMEM] * (line + 8),
+        contrib, rows, targets, target, *others, outer, *mats[2:], weight, swap,
     )
 
     def apply(inner, back, u_face, sends, stage):
@@ -415,6 +492,10 @@
     z, z_face, y, sends = apply(inner, back, u_face, sends, "first")
     came = trade_faces(sends)
     inner, part, *mats = inside_solve(y, "image")
+    high, low = call(
+        lambda *refs: table_body(*refs, line=line), "table", [bf16(BS, width), bf16(BS, width)],
+        [VMEM] * (line + 2), rows, targets, column, *others,
+    )
     q_face, outer, contrib = call(
         next_faces_body, "faces_image", [face, face, small], [VMEM] * 11,
         y, *came, weight, *mats, part,

time: 103 us -> 79.2 us (0.77)
  between operations: 14.2 us -> 0.82 us
  waiting for transfers between devices: 23.5 us -> 10.9 us
  Pallas kernels: 27.9 us -> 30.1 us
    all_gather x1 -> x0, waiting for transfers between devices: 13.9 us -> none  [on_device(): coarse_all = lax.all_gather(coarse_inv[0], 'gz', axis=0)]
    pallas_call x13 -> x14, Pallas kernels: 27.9 us -> 30.1 us  [call(): pl.pallas_call(body, name=name, out_shape=outs, in_specs=specs, out_specs...]
    ppermute x26 -> x27, waiting for transfers between devices: 8.95 us -> 10.9 us  [trade(): return lax.ppermute(value, AXES, [(i, i ^ mask) for i in range(devices)])]
    all_to_all x1, starting transfers between devices: 4.22 us -> 3.17 us  [on_device(): spread = lax.all_to_all(dots, AXES, 0, 0)]
    ppermute x26 -> x27, starting transfers between devices: 32.1 us -> 33.1 us  [trade(): return lax.ppermute(value, AXES, [(i, i ^ mask) for i in range(devices)])]
  transfers between devices with their start and end apart: 28 -> 28, of which waited for: 10 -> 8; matrix products, arithmetic and copies ran while one was open for 0% -> 0% of each run, Pallas kernels for 18% -> 24%
where the time goes in v3:
time: 79.2 us; the launch traced here: 78.7 us
  starting transfers between devices  36.2 us (46%)
  Pallas kernels  30.1 us (38%)
  waiting for transfers between devices  10.9 us (14%)
  between operations  0.82 us (1%)
    ppermute x27, starting transfers between devices, trade(): return lax.ppermute(value, AXES, [(i, i ^ mask) for i in range(devices)])  33.1 us
    pallas_call x14, Pallas kernels, call(): pl.pallas_call(body, name=name, out_shape=outs, in_specs=specs, out_specs...  30.1 us
    ppermute x27, waiting for transfers between devices, trade(): return lax.ppermute(value, AXES, [(i, i ^ mask) for i in range(devices)])  10.9 us
    all_to_all x1, starting transfers between devices, on_device(): spread = lax.all_to_all(dots, AXES, 0, 0)  3.17 us
  transfers between devices with their start and end apart: 28, of which 8 were waited for; matrix products, arithmetic and copies ran while one was open for 0% of the time, Pallas kernels for 24%

profile of v3, /device:TPU:0, one launch (start us, length us, event | category | flops | bytes accessed | tf_op | source)
XLA Modules:
  0.0 78.7 jit_solution(8831341642596182116)
XLA Ops:
  0.6 0.9 %prepare.1 = (f32[8,128]{1,0:T(8,128)S(1)}, s32[2,128,128]{2,1,0:T(8,128)S(1)}, f32[8,128]{1,0:T(8,128)S(1)}, f32[48,128]{1,0:T(8,128)S(1)}, f32[48,128]{1,0:T(8...) custom-call(f32[1,32,2048]{2,1,0:T(8,128)} %load_h.1, s32[1,4,128]{2,1,0:T(4,128)} %map_ref.1, s32[1,4]{1,0:T(1,128)} %id_ref.1, ...), custom_call_target="tpu_custom_call" | custom-call | tf_op jit(solution)/shard_map/prepare/pallas_call | solution.py:397
  1.5 3.1 %collective-permute-start = (f32[48,128]{1,0:T(8,128)S(1)}, f32[48,128]{1,0:T(8,128)S(1)}, u32[]{:S(2)}, u32[]{:S(2)}) collective-permute-start(f32[48,128]{1,0:T(8,128)S(1)} %get-tuple-element.69.refs_0_), channel_id=1, source_target_pairs={{0,1},{1,0},{2,3},{3,2},{4,5},{5,4},{6,7},{7,6},{8,9},{9,8},{10,11... | collective-permute-start | bytes 73736 | tf_op jit(solution)/shard_map/ppermute | solution.py:420
  4.6 2.6 %collective-permute-start.1 = (f32[48,128]{1,0:T(8,128)S(1)}, f32[48,128]{1,0:T(8,128)S(1)}, u32[]{:S(2)}, u32[]{:S(2)}) collective-permute-start(f32[48,128]{1,0:T(8,128)S(1)} %get-tuple-element.70.refs_1_), channel_id=1, source_target_pairs={{0,2},{1,3},{2,0},{3,1},{4,6},{5,7},{6,4},{7,5},{8,10},{9,11},{10,... | collective-permute-start | bytes 73736 | tf_op jit(solution)/shard_map/ppermute | solution.py:420
  7.2 1.5 %collective-permute-start.3 = (f32[48,128]{1,0:T(8,128)S(1)}, f32[48,128]{1,0:T(8,128)S(1)}, u32[]{:S(2)}, u32[]{:S(2)}) collective-permute-start(f32[48,128]{1,0:T(8,128)S(1)} %get-tuple-element.72.refs_3_), channel_id=1, source_target_pairs={{0,8},{1,9},{2,10},{3,11},{4,12},{5,13},{6,14},{7,15},{8,0},{9,1},... | collective-permute-start | bytes 73736 | tf_op jit(solution)/shard_map/ppermute | solution.py:420
  8.7 0.2 collective-permute-start.4
  8.9 2.8 %interior_load.1 = (f32[12,32,128]{2,1,0:T(8,128)S(1)}, f32[32,128]{1,0:T(8,128)S(1)}, bf16[512,512]{1,0:T(8,128)(2,1)S(1)}, bf16[512,512]{1,0:T(8,128)(2,1)S(1)...) custom-call(f32[1,32,2048]{2,1,0:T(8,128)} %load_h.1, ...), custom_call_target="tpu_custom_call" | custom-call | tf_op jit(solution)/shard_map/interior_load/pallas_call | solution.py:397
  11.7 2.4 %collective-permute-done.4.refs_16_ = f32[8,128]{1,0:T(8,128)S(1)} collective-permute-done((f32[8,128]{1,0:T(8,128)S(1)}, f32[8,128]{1,0:T(8,128)S(1)}, u32[]{:S(2)}, u32[]{:S(2)}) %collective-permute-start.4) | collective-permute-done | bytes 4128 | tf_op jit(solution)/shard_map/ppermute | solution.py:420
  14.1 0.0 collective-permute-done.3.refs_7_
  14.1 1.7 %faces_load.1 = (f32[4,32,128]{2,1,0:T(8,128)S(1)}, f32[4,32,128]{2,1,0:T(8,128)S(1)}, f32[32,128]{1,0:T(8,128)S(1)}, bf16[4,128,128]{2,1,0:T(8,128)(2,1)S(1)}, ...) custom-call(f32[48,128]{1,0:T(8,128)S(1)} %get-tuple-element.69.refs, ...), custom_call_target="tpu_custom_call" | custom-call | tf_op jit(solution)/shard_map/faces_load/pallas_call | solution.py:397
  15.8 0.1 collective-permute-start.5
  15.9 1.8 %collective-permute-start.6 = (f32[160,128]{1,0:T(8,128)S(1)}, f32[160,128]{1,0:T(8,128)S(1)}, u32[]{:S(2)}, u32[]{:S(2)}) collective-permute-start(f32[160,128]{1,0:T(8,128)S(1)} %get-tuple-element.85), channel_id=1, source_target_pairs={{0,2},{1,3},{2,0},{3,1},{4,6},{5,7},{6,4},{7,5},{8,10},{9,11},{10,... | collective-permute-start | bytes 245768 | tf_op jit(solution)/shard_map/ppermute | solution.py:420
  17.7 2.6 %collective-permute-start.7 = (f32[160,128]{1,0:T(8,128)S(1)}, f32[160,128]{1,0:T(8,128)S(1)}, u32[]{:S(2)}, u32[]{:S(2)}) collective-permute-start(f32[160,128]{1,0:T(8,128)S(1)} %get-tuple-element.86), channel_id=1, source_target_pairs={{0,3},{1,2},{2,1},{3,0},{4,7},{5,6},{6,5},{7,4},{8,11},{9,10},{10,... | collective-permute-start | bytes 245768 | tf_op jit(solution)/shard_map/ppermute | solution.py:420
  20.3 0.1 collective-permute-done.5.refs_4_.refs_3_
  20.3 4.4 %collective-permute-done.6.refs_5_.refs_4_ = f32[160,128]{1,0:T(8,128)S(1)} collective-permute-done((f32[160,128]{1,0:T(8,128)S(1)}, f32[160,128]{1,0:T(8,128)S(1)}, u32[]{:S(2)}, u32[]{:S(2)}) %collective-permute-start.6) | collective-permute-done | bytes 81952 | tf_op jit(solution)/shard_map/ppermute | solution.py:420
  24.7 0.0 collective-permute-done.7.refs_6_.refs_5_
  24.7 1.9 %coarse_load.1 = (f32[32,128]{1,0:T(8,128)S(1)}, f32[4,32,128]{2,1,0:T(8,128)S(1)}, f32[32,128]{1,0:T(8,128)S(1)}, f32[32,128]{1,0:T(8,128)S(1)}, f32[32,128]{1,0:T(8,128)S(1)}, /*index=5*/f32[32,128]{1,0:T(8,128)S(1)}) custom-call(f32[32,128]{1,0:T(8,128)S(1)} %get-tuple-element.81.refs_0_, f32[128,128]{1,0:T(8,128)S(1)} %get-tuple-element.82.refs_1_.refs_0_, ...), custom_call_target="tpu_custom_call" | custom-call | tf_op jit(solution)/shard_map/coarse_load/pallas_call | solution.py:397
  26.7 1.5 %collective-permute-start.8 = (f32[32,128]{1,0:T(8,128)S(1)}, f32[32,128]{1,0:T(8,128)S(1)}, u32[]{:S(2)}, u32[]{:S(2)}) collective-permute-start(f32[32,128]{1,0:T(8,128)S(1)} %get-tuple-element.93), channel_id=1, source_target_pairs={{0,1},{1,0},{2,3},{3,2},{4,5},{5,4},{6,7},{7,6},{8,9},{9,8},{10,11... | collective-permute-start | bytes 49160 | tf_op jit(solution)/shard_map/ppermute | solution.py:420
  28.1 1.2 %collective-permute-start.9 = (f32[32,128]{1,0:T(8,128)S(1)}, f32[32,128]{1,0:T(8,128)S(1)}, u32[]{:S(2)}, u32[]{:S(2)}) collective-permute-start(f32[32,128]{1,0:T(8,128)S(1)} %get-tuple-element.94), channel_id=1, source_target_pairs={{0,2},{1,3},{2,0},{3,1},{4,6},{5,7},{6,4},{7,5},{8,10},{9,11},{10,... | collective-permute-start | bytes 49160 | tf_op jit(solution)/shard_map/ppermute | solution.py:420
  29.3 0.5 collective-permute-start.11
  29.8 0.7 copy-done
  30.5 6.5 %own_first.1 = (f32[12,32,128]{2,1,0:T(8,128)S(1)}, f32[16,32,128]{2,1,0:T(8,128)S(1)}, bf16[4,128,896]{2,1,0:T(8,128)(2,1)S(1)}, bf16[4,128,896]{2,1,0:T(8,128)(2,1)S(1)}) custom-call(f32[12,32,128]{2,1,0:T(8,128)S(1)} %get-tuple-element.68.inner_ref, f32[32,128]{1,0:T(8,128)S(1)} %get-tuple-element.89.back_ref, f32[1,128,2048]{2,1,0:T(8,128)} %basis_ref.3, ...), custom_call_target="tpu_custom_call" | custom-call | tf_op jit(solution)/shard_map/own_first/pallas_call | solution.py:397
  37.0 1.2 %face_first.1 = (f32[16,32,128]{2,1,0:T(8,128)S(1)}, f32[4,32,128]{2,1,0:T(8,128)S(1)}, f32[32,128]{1,0:T(8,128)S(1)}, f32[32,128]{1,0:T(8,128)S(1)}, f32[32,128]{1,0:T(8,128)S(1)}, /*index=5*/f32[32,128]{1,0:T(8,128)S(1)}) custom-call(f32[16,32,128]{2,1,0:T(8,128)S(1)} %get-tuple-element.92.acc_ref, f32[32,128]{1,0:T(8,128)S(1)} %collective-permute-done.8.in0, ...), custom_call_target="tpu_custom_call" | custom-call | tf_op jit(solution)/shard_map/face_first/pallas_call | solution.py:397
  38.2 1.5 %collective-permute-start.12 = (f32[32,128]{1,0:T(8,128)S(1)}, f32[32,128]{1,0:T(8,128)S(1)}, u32[]{:S(2)}, u32[]{:S(2)}) collective-permute-start(f32[32,128]{1,0:T(8,128)S(1)} %get-tuple-element.102), channel_id=1, source_target_pairs={{0,1},{1,0},{2,3},{3,2},{4,5},{5,4},{6,7},{7,6},{8,9},{9,8},{10,11... | collective-permute-start | bytes 49160 | tf_op jit(solution)/shard_map/ppermute | solution.py:420
  39.7 0.9 %collective-permute-start.13 = (f32[32,128]{1,0:T(8,128)S(1)}, f32[32,128]{1,0:T(8,128)S(1)}, u32[]{:S(2)}, u32[]{:S(2)}) collective-permute-start(f32[32,128]{1,0:T(8,128)S(1)} %get-tuple-element.103), channel_id=1, source_target_pairs={{0,2},{1,3},{2,0},{3,1},{4,6},{5,7},{6,4},{7,5},{8,10},{9,11},{10,... | collective-permute-start | bytes 49160 | tf_op jit(solution)/shard_map/ppermute | solution.py:420
  40.6 1.5 %collective-permute-start.15 = (f32[32,128]{1,0:T(8,128)S(1)}, f32[32,128]{1,0:T(8,128)S(1)}, u32[]{:S(2)}, u32[]{:S(2)}) collective-permute-start(f32[32,128]{1,0:T(8,128)S(1)} %get-tuple-element.105), channel_id=1, source_target_pairs={{0,8},{1,9},{2,10},{3,11},{4,12},{5,13},{6,14},{7,15},{8,0},{9,1},... | collective-permute-start | bytes 49160 | tf_op jit(solution)/shard_map/ppermute | solution.py:420
  42.1 2.1 %interior_image.1 = (f32[12,32,128]{2,1,0:T(8,128)S(1)}, f32[32,128]{1,0:T(8,128)S(1)}, bf16[512,512]{1,0:T(8,128)(2,1)S(1)}, bf16[512,512]{1,0:T(8,128)(2,1)S(1...) custom-call(f32[16,32,128]{2,1,0:T(8,128)S(1)} %get-tuple-element.100.refs_0_.y_ref.y, ...), custom_call_target="tpu_custom_call" | custom-call | tf_op jit(solution)/shard_map/interior_image/pallas_call | solution.py:397
  44.1 0.4 collective-permute-done.13.in1
  44.5 0.4 faces_image.1
  44.9 1.9 %collective-permute-start.18 = (f32[32,128]{1,0:T(8,128)S(1)}, f32[32,128]{1,0:T(8,128)S(1)}, u32[]{:S(2)}, u32[]{:S(2)}) collective-permute-start(f32[32,128]{1,0:T(8,128)S(1)} %get-tuple-element.111.refs_0_), channel_id=1, source_target_pairs={{0,3},{1,2},{2,1},{3,0},{4,7},{5,6},{6,5},{7,4},{8,11},{9,10},{10,... | collective-permute-start | bytes 49160 | tf_op jit(solution)/shard_map/ppermute | solution.py:420
  46.7 0.8 %collective-permute-start.17 = (f32[32,128]{1,0:T(8,128)S(1)}, f32[32,128]{1,0:T(8,128)S(1)}, u32[]{:S(2)}, u32[]{:S(2)}) collective-permute-start(f32[32,128]{1,0:T(8,128)S(1)} %get-tuple-element.111.refs_0_), channel_id=1, source_target_pairs={{0,2},{1,3},{2,0},{3,1},{4,6},{5,7},{6,4},{7,5},{8,10},{9,11},{10,... | collective-permute-start | bytes 49160 | tf_op jit(solution)/shard_map/ppermute | solution.py:420
  47.6 1.7 %collective-permute-start.16 = (f32[32,128]{1,0:T(8,128)S(1)}, f32[32,128]{1,0:T(8,128)S(1)}, u32[]{:S(2)}, u32[]{:S(2)}) collective-permute-start(f32[32,128]{1,0:T(8,128)S(1)} %get-tuple-element.111.refs_0_), channel_id=1, source_target_pairs={{0,1},{1,0},{2,3},{3,2},{4,5},{5,4},{6,7},{7,6},{8,9},{9,8},{10,11... | collective-permute-start | bytes 49160 | tf_op jit(solution)/shard_map/ppermute | solution.py:420
  49.3 0.9 %table.1 = (bf16[128,512]{1,0:T(8,128)(2,1)S(1)}, bf16[128,512]{1,0:T(8,128)(2,1)S(1)}) custom-call(f32[128,128]{1,0:T(8,128)S(1)} %get-tuple-element.82.refs_1_.refs_0_, f32[1,512]{1,0:T(1,128)S(1)} %get-tuple-element.83.refs_2_.refs_1_, s32[2,128,128]{2,1,0:T(8,128)S(1)} %get-tuple-element.112.refs_2_, ...), custom_call_target="tpu_custom_call" | custom-call | tf_op jit(solution)/shard_map/table/pallas_call | solution.py:397
  50.1 0.3 collective-permute-done.18.refs_3_
  50.4 1.1 %collective-permute-done.17.refs_2_ = f32[32,128]{1,0:T(8,128)S(1)} collective-permute-done((f32[32,128]{1,0:T(8,128)S(1)}, f32[32,128]{1,0:T(8,128)S(1)}, u32[]{:S(2)}, u32[]{:S(2)}) %collective-permute-start.17) | collective-permute-done | bytes 16416 | tf_op jit(solution)/shard_map/ppermute | solution.py:420
  51.5 0.6 coarse_image.1
  52.1 1.5 %collective-permute-start.19 = (f32[32,128]{1,0:T(8,128)S(1)}, f32[32,128]{1,0:T(8,128)S(1)}, u32[]{:S(2)}, u32[]{:S(2)}) collective-permute-start(f32[32,128]{1,0:T(8,128)S(1)} %get-tuple-element.120), channel_id=1, source_target_pairs={{0,1},{1,0},{2,3},{3,2},{4,5},{5,4},{6,7},{7,6},{8,9},{9,8},{10,11... | collective-permute-start | bytes 49160 | tf_op jit(solution)/shard_map/ppermute | solution.py:420
  53.6 1.1 %collective-permute-start.20 = (f32[32,128]{1,0:T(8,128)S(1)}, f32[32,128]{1,0:T(8,128)S(1)}, u32[]{:S(2)}, u32[]{:S(2)}) collective-permute-start(f32[32,128]{1,0:T(8,128)S(1)} %get-tuple-element.121), channel_id=1, source_target_pairs={{0,2},{1,3},{2,0},{3,1},{4,6},{5,7},{6,4},{7,5},{8,10},{9,11},{10,... | collective-permute-start | bytes 49160 | tf_op jit(solution)/shard_map/ppermute | solution.py:420
  54.7 1.5 %collective-permute-start.22 = (f32[32,128]{1,0:T(8,128)S(1)}, f32[32,128]{1,0:T(8,128)S(1)}, u32[]{:S(2)}, u32[]{:S(2)}) collective-permute-start(f32[32,128]{1,0:T(8,128)S(1)} %get-tuple-element.123), channel_id=1, source_target_pairs={{0,8},{1,9},{2,10},{3,11},{4,12},{5,13},{6,14},{7,15},{8,0},{9,1},... | collective-permute-start | bytes 49160 | tf_op jit(solution)/shard_map/ppermute | solution.py:420
  56.2 6.5 %own_second.1 = (f32[12,32,128]{2,1,0:T(8,128)S(1)}, f32[16,32,128]{2,1,0:T(8,128)S(1)}, bf16[4,128,896]{2,1,0:T(8,128)(2,1)S(1)}, bf16[4,128,896]{2,1,0:T(8,128)(2,1)S(1)}) custom-call(f32[12,32,128]{2,1,0:T(8,128)S(1)} %get-tuple-element.101.inner_ref, f32[32,128]{1,0:T(8,128)S(1)} %get-tuple-element.116.back_ref, f32[1,128,2048]{2,1,0:T(8,128)} %basis_ref.3, ...), custom_call_target="tpu_custom_call" | custom-call | tf_op jit(solution)/shard_map/own_second/pallas_call | solution.py:397
  62.7 1.2 %face_second.1 = (f32[16,32,128]{2,1,0:T(8,128)S(1)}, f32[4,32,128]{2,1,0:T(8,128)S(1)}, f32[32,128]{1,0:T(8,128)S(1)}, f32[32,128]{1,0:T(8,128)S(1)}, f32[32,128]{1,0:T(8,128)S(1)}, /*index=5*/f32[32,128]{1,0:T(8,128)S(1)}) custom-call(f32[16,32,128]{2,1,0:T(8,128)S(1)} %get-tuple-element.119.acc_ref, f32[32,128]{1,0:T(8,128)S(1)} %collective-permute-done.19.in0, ...), custom_call_target="tpu_custom_call" | custom-call | tf_op jit(solution)/shard_map/face_second/pallas_call | solution.py:397
  63.9 1.8 %dots.1 = f32[32,2,128]{2,1,0:T(2,128)} custom-call(f32[1,32,2048]{2,1,0:T(8,128)} %load_h.1, f32[12,32,128]{2,1,0:T(8,128)S(1)} %get-tuple-element.91.zi, f32[4,32,128]{2,1,0:T(8,128)S(1)} %get-tuple-element.99.zf, f32[16,32,128]{2,1,0:T(8,128)S(1)} %get-tuple-element.100.refs_0_.y_ref.y, f32[12,32,128]{2,1,0:T(8,128)S(1)} %get-tuple-element.118.wi, ...), custom_call_target="tpu_custom_call" | custom-call | tf_op jit(solution)/shard_map/dots/pallas_call | solution.py:397
  65.7 3.2 %all-to-all-start = ((f32[32,2,128]{2,1,0:T(2,128)}), f32[32,2,128]{2,1,0:T(2,128)S(1)}, u32[]{:S(2)}, u32[]{:S(2)}) async-start(f32[32,2,128]{2,1,0:T(2,128)} %dots.1), calls=%async_computation | async-start | bytes 65536 | tf_op jit(solution)/shard_map/all_to_all | solution.py:515
  68.9 1.8 %collective-permute-start.23 = (f32[32,128]{1,0:T(8,128)S(1)}, f32[32,128]{1,0:T(8,128)S(1)}, u32[]{:S(2)}, u32[]{:S(2)}) collective-permute-start(f32[32,128]{1,0:T(8,128)S(1)} %get-tuple-element.128), channel_id=1, source_target_pairs={{0,1},{1,0},{2,3},{3,2},{4,5},{5,4},{6,7},{7,6},{8,9},{9,8},{10,11... | collective-permute-start | bytes 49160 | tf_op jit(solution)/shard_map/ppermute | solution.py:420
  70.8 2.4 %collective-permute-start.24 = (f32[32,128]{1,0:T(8,128)S(1)}, f32[32,128]{1,0:T(8,128)S(1)}, u32[]{:S(2)}, u32[]{:S(2)}) collective-permute-start(f32[32,128]{1,0:T(8,128)S(1)} %get-tuple-element.129), channel_id=1, source_target_pairs={{0,2},{1,3},{2,0},{3,1},{4,6},{5,7},{6,4},{7,5},{8,10},{9,11},{10,... | collective-permute-start | bytes 49160 | tf_op jit(solution)/shard_map/ppermute | solution.py:420
  73.2 1.5 %collective-permute-start.26 = (f32[32,128]{1,0:T(8,128)S(1)}, f32[32,128]{1,0:T(8,128)S(1)}, u32[]{:S(2)}, u32[]{:S(2)}) collective-permute-start(f32[32,128]{1,0:T(8,128)S(1)} %get-tuple-element.131), channel_id=1, source_target_pairs={{0,8},{1,9},{2,10},{3,11},{4,12},{5,13},{6,14},{7,15},{8,0},{9,1},... | collective-permute-start | bytes 49160 | tf_op jit(solution)/shard_map/ppermute | solution.py:420
  74.7 0.7 collective-permute-done.24.in1
  75.4 1.5 %collective-permute-done.26.in3 = f32[32,128]{1,0:T(8,128)S(1)} collective-permute-done((f32[32,128]{1,0:T(8,128)S(1)}, f32[32,128]{1,0:T(8,128)S(1)}, u32[]{:S(2)}, u32[]{:S(2)}) %collective-permute-start.26) | collective-permute-done | bytes 16416 | tf_op jit(solution)/shard_map/ppermute | solution.py:420
  76.9 1.8 %combine.1 = (f32[1,32,2048]{2,1,0:T(8,128)}, f32[1,32,2048]{2,1,0:T(8,128)}) custom-call(f32[32,2,128]{2,1,0:T(2,128)S(1)} %all-to-all-done.dots_ref, f32[32,128]{1,0:T(8,128)S(1)} %collective-permute-done.23.in0, f32[32,128]{1,0:T(8,128)S(1)} %collective-permute-done.24.in1, f32[32,128]{1,0:T(8,128)S(1)} %collective-permute-done.25.in2, ...), custom_call_target="tpu_custom_call" | custom-call | tf_op jit(solution)/shard_map/combine/pallas_call | solution.py:397
  (26 shorter events, 0.1 us)
Async XLA Ops:
  1.5 12.6 %collective-permute-start = (f32[48,128]{1,0:T(8,128)S(1)}, f32[48,128]{1,0:T(8,128)S(1)}, u32[]{:S(2)}, u32[]{:S(2)}) collective-permute-start(f32[48,128]{1,0:T(8,128)S(1)} %get-tuple-element.69.refs_0_), channel_id=1, source_target_pairs={{0,1},{1,0},{2,3},{3,2},{4,5},{5,4},{6,7},{7,6},{8,9},{9,8},{10,11... | collective-permute-start | bytes 73736 | tf_op jit(solution)/shard_map/ppermute | solution.py:420
  4.6 9.5 %collective-permute-start.1 = (f32[48,128]{1,0:T(8,128)S(1)}, f32[48,128]{1,0:T(8,128)S(1)}, u32[]{:S(2)}, u32[]{:S(2)}) collective-permute-start(f32[48,128]{1,0:T(8,128)S(1)} %get-tuple-element.70.refs_1_), channel_id=1, source_target_pairs={{0,2},{1,3},{2,0},{3,1},{4,6},{5,7},{6,4},{7,5},{8,10},{9,11},{10,... | collective-permute-start | bytes 73736 | tf_op jit(solution)/shard_map/ppermute | solution.py:420
  7.2 6.9 %collective-permute-start.2 = (f32[48,128]{1,0:T(8,128)S(1)}, f32[48,128]{1,0:T(8,128)S(1)}, u32[]{:S(2)}, u32[]{:S(2)}) collective-permute-start(f32[48,128]{1,0:T(8,128)S(1)} %get-tuple-element.71.refs_2_), channel_id=1, source_target_pairs={{0,4},{1,5},{2,6},{3,7},{4,0},{5,1},{6,2},{7,3},{8,12},{9,13},{10,... | collective-permute-start | bytes 73736 | tf_op jit(solution)/shard_map/ppermute | solution.py:420
  7.2 6.9 %collective-permute-start.3 = (f32[48,128]{1,0:T(8,128)S(1)}, f32[48,128]{1,0:T(8,128)S(1)}, u32[]{:S(2)}, u32[]{:S(2)}) collective-permute-start(f32[48,128]{1,0:T(8,128)S(1)} %get-tuple-element.72.refs_3_), channel_id=1, source_target_pairs={{0,8},{1,9},{2,10},{3,11},{4,12},{5,13},{6,14},{7,15},{8,0},{9,1},... | collective-permute-start | bytes 73736 | tf_op jit(solution)/shard_map/ppermute | solution.py:420
  8.7 5.4 %collective-permute-start.4 = (f32[8,128]{1,0:T(8,128)S(1)}, f32[8,128]{1,0:T(8,128)S(1)}, u32[]{:S(2)}, u32[]{:S(2)}) collective-permute-start(f32[8,128]{1,0:T(8,128)S(1)} %get-tuple-element.73.refs_8_.refs_3_), channel_id=1, source_target_pairs={{0,3},{1,2},{2,1},{3,0},{4,7},{5,6},{6,5},{7,4},{8,11},{9,10},{10,... | collective-permute-start | bytes 12296 | tf_op jit(solution)/shard_map/ppermute | solution.py:420
  15.8 4.5 %collective-permute-start.5 = (f32[160,128]{1,0:T(8,128)S(1)}, f32[160,128]{1,0:T(8,128)S(1)}, u32[]{:S(2)}, u32[]{:S(2)}) collective-permute-start(f32[160,128]{1,0:T(8,128)S(1)} %get-tuple-element.84), channel_id=1, source_target_pairs={{0,1},{1,0},{2,3},{3,2},{4,5},{5,4},{6,7},{7,6},{8,9},{9,8},{10,11... | collective-permute-start | bytes 245768 | tf_op jit(solution)/shard_map/ppermute | solution.py:420
  15.9 8.8 %collective-permute-start.6 = (f32[160,128]{1,0:T(8,128)S(1)}, f32[160,128]{1,0:T(8,128)S(1)}, u32[]{:S(2)}, u32[]{:S(2)}) collective-permute-start(f32[160,128]{1,0:T(8,128)S(1)} %get-tuple-element.85), channel_id=1, source_target_pairs={{0,2},{1,3},{2,0},{3,1},{4,6},{5,7},{6,4},{7,5},{8,10},{9,11},{10,... | collective-permute-start | bytes 245768 | tf_op jit(solution)/shard_map/ppermute | solution.py:420
  17.7 7.0 %collective-permute-start.7 = (f32[160,128]{1,0:T(8,128)S(1)}, f32[160,128]{1,0:T(8,128)S(1)}, u32[]{:S(2)}, u32[]{:S(2)}) collective-permute-start(f32[160,128]{1,0:T(8,128)S(1)} %get-tuple-element.86), channel_id=1, source_target_pairs={{0,3},{1,2},{2,1},{3,0},{4,7},{5,6},{6,5},{7,4},{8,11},{9,10},{10,... | collective-permute-start | bytes 245768 | tf_op jit(solution)/shard_map/ppermute | solution.py:420
  26.7 10.3 %collective-permute-start.8 = (f32[32,128]{1,0:T(8,128)S(1)}, f32[32,128]{1,0:T(8,128)S(1)}, u32[]{:S(2)}, u32[]{:S(2)}) collective-permute-start(f32[32,128]{1,0:T(8,128)S(1)} %get-tuple-element.93), channel_id=1, source_target_pairs={{0,1},{1,0},{2,3},{3,2},{4,5},{5,4},{6,7},{7,6},{8,9},{9,8},{10,11... | collective-permute-start | bytes 49160 | tf_op jit(solution)/shard_map/ppermute | solution.py:420
  28.1 8.9 %collective-permute-start.9 = (f32[32,128]{1,0:T(8,128)S(1)}, f32[32,128]{1,0:T(8,128)S(1)}, u32[]{:S(2)}, u32[]{:S(2)}) collective-permute-start(f32[32,128]{1,0:T(8,128)S(1)} %get-tuple-element.94), channel_id=1, source_target_pairs={{0,2},{1,3},{2,0},{3,1},{4,6},{5,7},{6,4},{7,5},{8,10},{9,11},{10,... | collective-permute-start | bytes 49160 | tf_op jit(solution)/shard_map/ppermute | solution.py:420
  29.3 7.7 %collective-permute-start.10 = (f32[32,128]{1,0:T(8,128)S(1)}, f32[32,128]{1,0:T(8,128)S(1)}, u32[]{:S(2)}, u32[]{:S(2)}) collective-permute-start(f32[32,128]{1,0:T(8,128)S(1)} %get-tuple-element.95), channel_id=1, source_target_pairs={{0,4},{1,5},{2,6},{3,7},{4,0},{5,1},{6,2},{7,3},{8,12},{9,13},{10,... | collective-permute-start | bytes 49160 | tf_op jit(solution)/shard_map/ppermute | solution.py:420
  29.3 7.7 %collective-permute-start.11 = (f32[32,128]{1,0:T(8,128)S(1)}, f32[32,128]{1,0:T(8,128)S(1)}, u32[]{:S(2)}, u32[]{:S(2)}) collective-permute-start(f32[32,128]{1,0:T(8,128)S(1)} %get-tuple-element.96), channel_id=1, source_target_pairs={{0,8},{1,9},{2,10},{3,11},{4,12},{5,13},{6,14},{7,15},{8,0},{9,1},... | collective-permute-start | bytes 49160 | tf_op jit(solution)/shard_map/ppermute | solution.py:420
  29.8 0.7 copy-start
  30.5 25.7 %copy-start.1 = (s32[16,7]{0,1:T(8,128)S(1)}, s32[16,7]{0,1:T(8,128)}, u32[]{:S(2)}) copy-start(s32[16,7]{0,1:T(8,128)} %param.12) | copy-start | bytes 1348
  38.2 5.9 %collective-permute-start.12 = (f32[32,128]{1,0:T(8,128)S(1)}, f32[32,128]{1,0:T(8,128)S(1)}, u32[]{:S(2)}, u32[]{:S(2)}) collective-permute-start(f32[32,128]{1,0:T(8,128)S(1)} %get-tuple-element.102), channel_id=1, source_target_pairs={{0,1},{1,0},{2,3},{3,2},{4,5},{5,4},{6,7},{7,6},{8,9},{9,8},{10,11... | collective-permute-start | bytes 49160 | tf_op jit(solution)/shard_map/ppermute | solution.py:420
  39.7 4.8 %collective-permute-start.13 = (f32[32,128]{1,0:T(8,128)S(1)}, f32[32,128]{1,0:T(8,128)S(1)}, u32[]{:S(2)}, u32[]{:S(2)}) collective-permute-start(f32[32,128]{1,0:T(8,128)S(1)} %get-tuple-element.103), channel_id=1, source_target_pairs={{0,2},{1,3},{2,0},{3,1},{4,6},{5,7},{6,4},{7,5},{8,10},{9,11},{10,... | collective-permute-start | bytes 49160 | tf_op jit(solution)/shard_map/ppermute | solution.py:420
  40.6 3.9 %collective-permute-start.14 = (f32[32,128]{1,0:T(8,128)S(1)}, f32[32,128]{1,0:T(8,128)S(1)}, u32[]{:S(2)}, u32[]{:S(2)}) collective-permute-start(f32[32,128]{1,0:T(8,128)S(1)} %get-tuple-element.104), channel_id=1, source_target_pairs={{0,4},{1,5},{2,6},{3,7},{4,0},{5,1},{6,2},{7,3},{8,12},{9,13},{10,... | collective-permute-start | bytes 49160 | tf_op jit(solution)/shard_map/ppermute | solution.py:420
  40.6 3.9 %collective-permute-start.15 = (f32[32,128]{1,0:T(8,128)S(1)}, f32[32,128]{1,0:T(8,128)S(1)}, u32[]{:S(2)}, u32[]{:S(2)}) collective-permute-start(f32[32,128]{1,0:T(8,128)S(1)} %get-tuple-element.105), channel_id=1, source_target_pairs={{0,8},{1,9},{2,10},{3,11},{4,12},{5,13},{6,14},{7,15},{8,0},{9,1},... | collective-permute-start | bytes 49160 | tf_op jit(solution)/shard_map/ppermute | solution.py:420
  44.9 5.6 %collective-permute-start.18 = (f32[32,128]{1,0:T(8,128)S(1)}, f32[32,128]{1,0:T(8,128)S(1)}, u32[]{:S(2)}, u32[]{:S(2)}) collective-permute-start(f32[32,128]{1,0:T(8,128)S(1)} %get-tuple-element.111.refs_0_), channel_id=1, source_target_pairs={{0,3},{1,2},{2,1},{3,0},{4,7},{5,6},{6,5},{7,4},{8,11},{9,10},{10,... | collective-permute-start | bytes 49160 | tf_op jit(solution)/shard_map/ppermute | solution.py:420
  46.7 4.8 %collective-permute-start.17 = (f32[32,128]{1,0:T(8,128)S(1)}, f32[32,128]{1,0:T(8,128)S(1)}, u32[]{:S(2)}, u32[]{:S(2)}) collective-permute-start(f32[32,128]{1,0:T(8,128)S(1)} %get-tuple-element.111.refs_0_), channel_id=1, source_target_pairs={{0,2},{1,3},{2,0},{3,1},{4,6},{5,7},{6,4},{7,5},{8,10},{9,11},{10,... | collective-permute-start | bytes 49160 | tf_op jit(solution)/shard_map/ppermute | solution.py:420
  47.6 4.0 %collective-permute-start.16 = (f32[32,128]{1,0:T(8,128)S(1)}, f32[32,128]{1,0:T(8,128)S(1)}, u32[]{:S(2)}, u32[]{:S(2)}) collective-permute-start(f32[32,128]{1,0:T(8,128)S(1)} %get-tuple-element.111.refs_0_), channel_id=1, source_target_pairs={{0,1},{1,0},{2,3},{3,2},{4,5},{5,4},{6,7},{7,6},{8,9},{9,8},{10,11... | collective-permute-start | bytes 49160 | tf_op jit(solution)/shard_map/ppermute | solution.py:420
  52.1 10.6 %collective-permute-start.19 = (f32[32,128]{1,0:T(8,128)S(1)}, f32[32,128]{1,0:T(8,128)S(1)}, u32[]{:S(2)}, u32[]{:S(2)}) collective-permute-start(f32[32,128]{1,0:T(8,128)S(1)} %get-tuple-element.120), channel_id=1, source_target_pairs={{0,1},{1,0},{2,3},{3,2},{4,5},{5,4},{6,7},{7,6},{8,9},{9,8},{10,11... | collective-permute-start | bytes 49160 | tf_op jit(solution)/shard_map/ppermute | solution.py:420
  53.6 9.1 %collective-permute-start.20 = (f32[32,128]{1,0:T(8,128)S(1)}, f32[32,128]{1,0:T(8,128)S(1)}, u32[]{:S(2)}, u32[]{:S(2)}) collective-permute-start(f32[32,128]{1,0:T(8,128)S(1)} %get-tuple-element.121), channel_id=1, source_target_pairs={{0,2},{1,3},{2,0},{3,1},{4,6},{5,7},{6,4},{7,5},{8,10},{9,11},{10,... | collective-permute-start | bytes 49160 | tf_op jit(solution)/shard_map/ppermute | solution.py:420
  54.7 8.0 %collective-permute-start.21 = (f32[32,128]{1,0:T(8,128)S(1)}, f32[32,128]{1,0:T(8,128)S(1)}, u32[]{:S(2)}, u32[]{:S(2)}) collective-permute-start(f32[32,128]{1,0:T(8,128)S(1)} %get-tuple-element.122), channel_id=1, source_target_pairs={{0,4},{1,5},{2,6},{3,7},{4,0},{5,1},{6,2},{7,3},{8,12},{9,13},{10,... | collective-permute-start | bytes 49160 | tf_op jit(solution)/shard_map/ppermute | solution.py:420
  54.7 8.0 %collective-permute-start.22 = (f32[32,128]{1,0:T(8,128)S(1)}, f32[32,128]{1,0:T(8,128)S(1)}, u32[]{:S(2)}, u32[]{:S(2)}) collective-permute-start(f32[32,128]{1,0:T(8,128)S(1)} %get-tuple-element.123), channel_id=1, source_target_pairs={{0,8},{1,9},{2,10},{3,11},{4,12},{5,13},{6,14},{7,15},{8,0},{9,1},... | collective-permute-start | bytes 49160 | tf_op jit(solution)/shard_map/ppermute | solution.py:420
  65.7 11.2 %all-to-all-start = ((f32[32,2,128]{2,1,0:T(2,128)}), f32[32,2,128]{2,1,0:T(2,128)S(1)}, u32[]{:S(2)}, u32[]{:S(2)}) async-start(f32[32,2,128]{2,1,0:T(2,128)} %dots.1), calls=%async_computation | async-start | bytes 65536 | tf_op jit(solution)/shard_map/all_to_all | solution.py:515
  68.9 5.7 %collective-permute-start.23 = (f32[32,128]{1,0:T(8,128)S(1)}, f32[32,128]{1,0:T(8,128)S(1)}, u32[]{:S(2)}, u32[]{:S(2)}) collective-permute-start(f32[32,128]{1,0:T(8,128)S(1)} %get-tuple-element.128), channel_id=1, source_target_pairs={{0,1},{1,0},{2,3},{3,2},{4,5},{5,4},{6,7},{7,6},{8,9},{9,8},{10,11... | collective-permute-start | bytes 49160 | tf_op jit(solution)/shard_map/ppermute | solution.py:420
  70.8 4.6 %collective-permute-start.24 = (f32[32,128]{1,0:T(8,128)S(1)}, f32[32,128]{1,0:T(8,128)S(1)}, u32[]{:S(2)}, u32[]{:S(2)}) collective-permute-start(f32[32,128]{1,0:T(8,128)S(1)} %get-tuple-element.129), channel_id=1, source_target_pairs={{0,2},{1,3},{2,0},{3,1},{4,6},{5,7},{6,4},{7,5},{8,10},{9,11},{10,... | collective-permute-start | bytes 49160 | tf_op jit(solution)/shard_map/ppermute | solution.py:420
  73.2 2.2 %collective-permute-start.25 = (f32[32,128]{1,0:T(8,128)S(1)}, f32[32,128]{1,0:T(8,128)S(1)}, u32[]{:S(2)}, u32[]{:S(2)}) collective-permute-start(f32[32,128]{1,0:T(8,128)S(1)} %get-tuple-element.130), channel_id=1, source_target_pairs={{0,4},{1,5},{2,6},{3,7},{4,0},{5,1},{6,2},{7,3},{8,12},{9,13},{10,... | collective-permute-start | bytes 49160 | tf_op jit(solution)/shard_map/ppermute | solution.py:420
  73.2 3.7 %collective-permute-start.26 = (f32[32,128]{1,0:T(8,128)S(1)}, f32[32,128]{1,0:T(8,128)S(1)}, u32[]{:S(2)}, u32[]{:S(2)}) collective-permute-start(f32[32,128]{1,0:T(8,128)S(1)} %get-tuple-element.131), channel_id=1, source_target_pairs={{0,8},{1,9},{2,10},{3,11},{4,12},{5,13},{6,14},{7,15},{8,0},{9,1},... | collective-permute-start | bytes 49160 | tf_op jit(solution)/shard_map/ppermute | solution.py:420

commit v4 on v3

--- a/solution.py
+++ b/solution.py
@@ -13,7 +13,7 @@
 CB = 4
 OCAP = 8
 SCAP = 2
-AHEAD = 4
+CHUNKS = (4, 4, 3, 1)
 NB = 16
 TPR = 7
 NL = 2048
@@ -102,28 +102,19 @@
         out[NRHS + 8 :, :] = target
 
 
-def interior_body(
-    x_ref, inv_ref, basis_ref, schur_ref,
-    *rest, flat,
-):
-    if flat:
-        coarse_ref, *rest = rest
-    inner_ref, part_ref, schur_high, schur_low, basis_high, basis_low, *scratch = rest
-    if flat:
-        coarse_parts, *scratch = scratch
-    inv, basis, schur = scratch[:3]
-    sems = scratch[-1]
-    pairs = [(inv_ref, inv), (basis_ref.at[0], basis), (schur_ref.at[0], schur)]
-    if flat:
-        pairs.append((x_ref.at[0, :, : NIN * BS], scratch[3]))
-        pairs.append((coarse_ref.at[0], scratch[4]))
-    copies = start_all(sems, *pairs)
-    if flat:
-        copies[3].wait()
+def face_rows(acc_ref, face_ref, tiles, cols, out_ref, spare_ref):
+    spare_ref[...] = acc_ref[...]
+    for r in range(NF):
+        add_row(face_ref[r], NIN + r, tiles[r], cols, spare_ref)
+    out_ref[...] = spare_ref[:NIN]
+
+
+def solve_inside(x_of, inv, basis, schur, copies, inner_ref, part_ref, mats):
+    schur_high, schur_low, basis_high, basis_low = mats
     copies[0].wait()
     pieces = []
     for b in range(NIN):
-        xb = halves(scratch[3][:, lanes(b)] if flat else x_ref[b])
+        xb = halves(x_of(b))
         pieces.append(xb)
         inner_ref[b] = dot_halves(xb, halves(inv[b]))
     cat = tuple(jnp.concatenate([p[h] for p in pieces], axis=1) for h in range(2))
@@ -132,12 +123,63 @@
     basis_high[...], basis_low[...] = halves(basis[:, NIN * BS :])
     copies[2].wait()
     schur_high[...], schur_low[...] = halves(schur[...])
-    if flat:
-        copies[4].wait()
-        value = scratch[4][...]
-        for k in range(3):
-            coarse_parts[k] = value.astype(BF16)
-            value = value - coarse_parts[k].astype(F32)
+
+
+def load_inside_body(
+    x_ref, inv_ref, basis_ref, schur_ref, coarse_ref,
+    inner_ref, part_ref, schur_high, schur_low, basis_high, basis_low, coarse_parts,
+    inv, basis, schur, x, coarse, sems,
+):
+    copies = start_all(
+        sems, (inv_ref, inv), (basis_ref.at[0], basis), (schur_ref.at[0], schur),
+        (x_ref.at[0, :, : NIN * BS], x), (coarse_ref.at[0], coarse),
+    )
+    copies[3].wait()
+    mats = (schur_high, schur_low, basis_high, basis_low)
+    solve_inside(lambda b: x[:, lanes(b)], inv, basis, schur, copies, inner_ref, part_ref, mats)
+    copies[4].wait()
+    value = coarse[...]
+    for k in range(3):
+        coarse_parts[k] = value.astype(BF16)
+        value = value - coarse_parts[k].astype(F32)
+
+
+def image_inside_body(
+    acc_ref, face_ref, cols_ref, tiles_ref, inv_ref, basis_ref, schur_ref,
+    y_ref, inner_ref, part_ref, schur_high, schur_low, basis_high, basis_low,
+    inv, basis, schur, tiles, spare, cols, sems,
+):
+    copies = start_all(
+        sems, (inv_ref, inv), (basis_ref.at[0], basis), (schur_ref.at[0], schur),
+        (cols_ref, cols), (tiles_ref.at[NIN:], tiles),
+    )
+    copies[3].wait()
+    copies[4].wait()
+    face_rows(acc_ref, face_ref, [wide_of(tiles, r) for r in range(NF)], cols, y_ref, spare)
+    mats = (schur_high, schur_low, basis_high, basis_low)
+    solve_inside(lambda b: y_ref[b], inv, basis, schur, copies, inner_ref, part_ref, mats)
+
+
+def last_image_body(acc_ref, face_ref, cols_ref, tiles_ref, y_ref, tiles, spare, cols, sems):
+    copies = start_all(sems, (cols_ref, cols), (tiles_ref.at[NIN:], tiles))
+    for copy in copies:
+        copy.wait()
+    face_rows(acc_ref, face_ref, [wide_of(tiles, r) for r in range(NF)], cols, y_ref, spare)
+
+
+def face_block_body(tiles_ref, cols_ref, high_ref, low_ref, tiles, cols, sems):
+    copies = start_all(sems, (cols_ref, cols), (tiles_ref.at[NIN:], tiles))
+    high_ref[...] = jnp.zeros_like(high_ref)
+    low_ref[...] = jnp.zeros_like(low_ref)
+    for copy in copies:
+        copy.wait()
+    for r in range(NF):
+        for t in range(TPR):
+            place = cols[t, NIN + r] - NIN
+
+            @pl.when(place >= 0)
+            def _(r=r, t=t, place=place):
+                high_ref[r, place], low_ref[r, place] = halves(tiles[r, t])
 
 
 def face_solve(faces, mats, weight_ref, part_ref, outer_ref, contrib_ref):
@@ -199,7 +241,7 @@
 ):
     faces = []
     for r, inc in enumerate((in0, in1, in2, in3)):
-        faces.append(y_ref[NIN + r] + inc[...])
+        faces.append(y_ref[r] + inc[...])
         face_ref[r] = faces[-1]
     mats = (schur_high, schur_low, basis_high, basis_low)
     face_solve(faces, mats, weight_ref, part_ref, outer_ref, contrib_ref)
@@ -228,7 +270,7 @@
 
 def first_coarse_body(own_ref, rows_ref, all_ref, target_ref, *refs, line):
     sides = (rows_ref,) + refs[: line - 1]
-    outer_ref, basis_high, basis_low, weight_ref, swap_ref, back_ref, face_ref, *outs = refs[line - 1 :]
+    outer_ref, basis_high, basis_low, weight_ref, swap_ref, _, back_ref, face_ref, *outs = refs[line - 1 :]
     here = lax.axis_index("gz")
     contribs = halves(jnp.concatenate([own_ref[...]] + [s[:NRHS, :] for s in sides[1:]], axis=1))
     stack = jnp.concatenate(contribs, axis=0)
@@ -279,96 +321,144 @@
         acc_ref[places[t]] = before[t] + out[:, lanes(t)]
 
 
-def own_apply_body(
-    inner_ref, back_ref, basis_ref, face_ref, tiles_ref, cols_ref, z_ref, acc_ref, wide_high, wide_low,
-    basis, tiles, sems,
-):
-    pairs = [(basis_ref.at[0, :, : NIN * BS], basis)]
-    pairs += [(tiles_ref.at[i], tiles.at[i]) for i in range(NB)]
-    copies = [pltpu.make_async_copy(src, dst, sems.at[k]) for k, (src, dst) in enumerate(pairs)]
-    for copy in copies[: 1 + AHEAD]:
-        copy.start()
+def wide_of(tiles, i):
+    return halves(jnp.concatenate([tiles[i, t] for t in range(TPR)], axis=1))
+
+
+def own_apply(inner_ref, back_ref, basis_ref, tiles_ref, cols_ref, z_ref, acc_ref, basis, tiles, cols, sems):
+    pairs = [(cols_ref, cols), (basis_ref.at[0, :, : NIN * BS], basis)]
+    first = 0
+    for count in CHUNKS:
+        pairs.append((tiles_ref.at[first : first + count], tiles.at[first : first + count]))
+        first += count
+    copies = start_all(sems, *pairs)
     acc_ref[...] = jnp.zeros_like(acc_ref)
     back = halves(back_ref[...])
     copies[0].wait()
+    copies[1].wait()
+    corr = dot_halves(back, halves(basis[...]))
     for b in range(NIN):
-        z_ref[b] = inner_ref[b] + dot_halves(back, halves(basis[:, lanes(b)]))
-    for i in range(NB):
-        copies[1 + i].wait()
-        if i + AHEAD < NB:
-            copies[1 + i + AHEAD].start()
-        wide = halves(jnp.concatenate([tiles[i, t] for t in range(TPR)], axis=1))
-        if i >= NIN:
-            wide_high[i - NIN], wide_low[i - NIN] = wide
-        add_row(z_ref[i] if i < NIN else face_ref[i - NIN], i, wide, cols_ref, acc_ref)
-
-
-def face_apply_body(
-    acc_ref, in0, in1, in2, in3, face_ref, wide_high, wide_low, cols_ref, swap_ref,
+        z_ref[b] = inner_ref[b] + corr[:, lanes(b)]
+    first = 0
+    for k, count in enumerate(CHUNKS):
+        copies[2 + k].wait()
+        for i in range(first, first + count):
+            add_row(z_ref[i], i, wide_of(tiles, i), cols, acc_ref)
+        first += count
+
+
+def first_apply_body(*refs):
+    own_apply(*refs)
+
+
+def pair_sums(pairs):
+    return [sum(left * right for left, right in blocks) for blocks in pairs]
+
+
+def second_apply_body(
+    inner_ref, back_ref, basis_ref, tiles_ref, cols_ref, load_hbm, zi, zf, yi, yf,
+    z_ref, acc_ref, sums_ref, load_ref, basis, tiles, load, cols, sems, more,
+):
+    (copy,) = start_all(more, (load_hbm.at[0], load))
+    own_apply(inner_ref, back_ref, basis_ref, tiles_ref, cols_ref, z_ref, acc_ref, basis, tiles, cols, sems)
+    copy.wait()
+    sums = pair_sums(
+        (
+            [(load[:, lanes(b)], zi[b]) for b in range(NIN)]
+            + [(load[:, lanes(NIN + r)], zf[r]) for r in range(NF)],
+            [(zi[b], yi[b]) for b in range(NIN)] + [(zf[r], yf[r]) for r in range(NF)],
+            [(load[:, lanes(b)], z_ref[b]) for b in range(NIN)],
+            [(yi[b], z_ref[b]) for b in range(NIN)],
+            [(z_ref[b], acc_ref[b]) for b in range(NIN)],
+        )
+    )
+    for k, value in enumerate(sums):
+        sums_ref[k] = value
+    for b in range(NB):
+        load_ref[b] = load[:, lanes(b)]
+
+
+def face_apply(acc_ref, incs, face_ref, block_high, block_low, swap_ref, y_ref, z_ref, outs):
+    faces = [face_ref[r] + inc[...] for r, inc in enumerate(incs)]
+    wide = [
+        jnp.concatenate(
+            [jnp.concatenate([ref[r, c] for c in range(NF)], axis=1) for r in range(NF)], axis=0
+        )
+        for ref in (block_high, block_low)
+    ]
+    more = dot_halves(halves(jnp.concatenate(faces, axis=1)), wide)
+    for r, out in enumerate(outs):
+        z_ref[r] = faces[r]
+        y_ref[r] = acc_ref[NIN + r] + more[:, lanes(r)]
+        out[...] = select_lanes(y_ref[r], swap_ref[r])
+    return faces, more
+
+
+def first_face_body(
+    acc_ref, in0, in1, in2, in3, face_ref, block_high, block_low, swap_ref,
     y_ref, z_ref, out0, out1, out2, out3,
 ):
-    y_ref[...] = acc_ref[...]
-    for r, inc in enumerate((in0, in1, in2, in3)):
-        came = inc[...]
-        z_ref[r] = face_ref[r] + came
-        add_row(came, NIN + r, (wide_high[r], wide_low[r]), cols_ref, y_ref)
-    for r, out in enumerate((out0, out1, out2, out3)):
-        out[...] = select_lanes(y_ref[NIN + r], swap_ref[r])
-
-
-def dots_body(load_hbm, zi, zf, y, wi, wf_ref, v_ref, out_ref, load_ref, sems):
-    (copy,) = start_all(sems, (load_hbm.at[0], load_ref))
-    copy.wait()
-    sums = [jnp.zeros((NRHS, BS), F32) for _ in range(6)]
-    for b in range(NB):
-        load = load_ref[:, lanes(b)]
-        z = zi[b] if b < NIN else zf[b - NIN]
-        w = wi[b] if b < NIN else wf_ref[b - NIN]
-        q, v = y[b], v_ref[b]
-        for k, (left, right) in enumerate(((load, z), (z, q), (load, w), (q, w), (z, v), (w, v))):
-            sums[k] = sums[k] + left * right
+    face_apply(
+        acc_ref, (in0, in1, in2, in3), face_ref, block_high, block_low, swap_ref, y_ref, z_ref,
+        (out0, out1, out2, out3),
+    )
+
+
+def second_face_body(
+    acc_ref, in0, in1, in2, in3, face_ref, block_high, block_low, swap_ref, sums_ref, load_ref, yf,
+    y_ref, z_ref, dots_ref, out0, out1, out2, out3,
+):
+    faces, more = face_apply(
+        acc_ref, (in0, in1, in2, in3), face_ref, block_high, block_low, swap_ref, y_ref, z_ref,
+        (out0, out1, out2, out3),
+    )
+    late = pair_sums(
+        (
+            [(load_ref[NIN + r], faces[r]) for r in range(NF)],
+            [(yf[r], faces[r]) for r in range(NF)],
+            [(faces[r], 2.0 * acc_ref[NIN + r] + more[:, lanes(r)]) for r in range(NF)],
+        )
+    )
+    sums = [sums_ref[0], sums_ref[1]] + [sums_ref[2 + k] + late[k] for k in range(3)]
     place = lax.broadcasted_iota(jnp.int32, (NRHS, BS), 1)
     case = lax.broadcasted_iota(jnp.int32, (NRHS, BS), 0)
     for row in range(2):
         total = jnp.zeros((NRHS, BS), F32)
-        for k in range(4 * row, min(4 * row + 4, 6)):
+        for k in range(4 * row, min(4 * row + 4, len(sums))):
             column = jnp.sum(sums[k], axis=1, keepdims=True)
             total = total + jnp.where(place == case + NRHS * (k % 4), column, 0.0)
         total = jnp.sum(total, axis=0, keepdims=True)
-        out_ref[:, row : row + 1, :] = jnp.broadcast_to(total[None], (out_ref.shape[0], 1, BS))
+        dots_ref[:, row : row + 1, :] = jnp.broadcast_to(total[None], (dots_ref.shape[0], 1, BS))
 
 
 def final_body(
-    dots_ref, in0, in1, in2, in3, load_h, rf, zi, zf, y, qf, wi, wf, v, sol_ref, res_ref, load, sems,
-):
-    copies = start_all(sems, (load_h.at[0, :, : NIN * BS], load))
+    dots_ref, in0, in1, in2, in3, load, rf, zi, zf, yi, qf, wi, wf, vi, vf, sol_ref, res_ref,
+):
     place = lax.broadcasted_iota(jnp.int32, (NRHS, BS), 1)
     case = lax.broadcasted_iota(jnp.int32, (NRHS, BS), 0)
     total = jnp.sum(dots_ref[...], axis=0)
-    rz, zq, rw, qw, zv, wv = [
+    rz, zq, rw, qw, wv = [
         jnp.sum(
             jnp.where(place == case + NRHS * (k % 4), total[k // 4 : k // 4 + 1, :], 0.0),
             axis=1,
             keepdims=True,
         )
-        for k in range(6)
+        for k in range(5)
     ]
     alpha = rz / zq
     rho = rz - alpha * (rw + zq) + alpha * alpha * qw
     grow = 1.0 + rho / rz
-    curve = grow * grow * zq - grow * alpha * (zv + qw) + alpha * alpha * wv
+    curve = grow * grow * zq - 2.0 * grow * alpha * qw + alpha * alpha * wv
     step = rho / curve
     first = alpha + step * grow
     second = step * alpha
-    for copy in copies:
-        copy.wait()
     for b in range(NB):
         if b < NIN:
-            r_b, z_b, q_b, w_b, v_b = load[:, lanes(b)], zi[b], y[b], wi[b], v[b]
+            r_b, z_b, q_b, w_b, v_b = load[b], zi[b], yi[b], wi[b], vi[b]
         else:
             f = b - NIN
             r_b, z_b, q_b, w_b = rf[f], zf[f], qf[f], wf[f]
-            v_b = v[b] + (in0, in1, in2, in3)[f][...]
+            v_b = vf[f] + (in0, in1, in2, in3)[f][...]
         sol_ref[0, :, lanes(b)] = first * z_b - second * w_b
         res_ref[0, :, lanes(b)] = r_b - first * q_b + second * v_b
 
@@ -441,22 +531,17 @@
     came = trade_faces(sides)
     far = [trade(target, mask) for mask in range(3, line)]
 
-    def inside_solve(x, stage):
-        flat = stage == "load"
-        outs = [block, small, bf16(nf, nf), bf16(nf, nf), bf16(BS, nf), bf16(BS, nf)]
-        scratch = [(NIN, BS, BS), (BS, NL), (nf, nf)]
-        args = [x, interior_inv, coarse_basis, schur_inv]
-        if flat:
-            own = OCAP * CW
-            outs.append(bf16(3, own, own))
-            scratch += [(NRHS, NIN * BS), (own, own)]
-            args.append(coarse_inv)
-        return call(
-            lambda *refs: interior_body(*refs, flat=flat), "interior_" + stage, outs,
-            [HBM if flat else VMEM] + [HBM] * (len(args) - 1), *args, scratch=scratch, copies=5,
-        )
-
-    inner, part, *mats, coarse_parts = inside_solve(load_vector, "load")
+    own = OCAP * CW
+    mat_outs = [block, small, bf16(nf, nf), bf16(nf, nf), bf16(BS, nf), bf16(BS, nf)]
+    mat_scratch = [(NIN, BS, BS), (BS, NL), (nf, nf)]
+    cols_scratch = pltpu.SMEM((TPR, NB), jnp.int32)
+    face_tiles = (NF, TPR, BS, BS)
+
+    inner, part, *mats, coarse_parts = call(
+        load_inside_body, "inside_load", mat_outs + [bf16(3, own, own)], [HBM] * 5,
+        load_vector, interior_inv, coarse_basis, schur_inv, coarse_inv,
+        scratch=mat_scratch + [(NRHS, NIN * BS), (own, own)], copies=5,
+    )
     width = line * CB * CW
     half = 2 * SCAP * CW
     r_face, outer, contrib, swap, targets, rows, *sides = call(
@@ -467,38 +552,40 @@
         *sides, *came, target, weight, *mats, part, coarse_parts, *far,
     )
     others = [trade(value, mask) for value, mask in zip(sides, range(1, line))]
+    blocks = call(
+        face_block_body, "face_block", [bf16(NF, NF, BS, BS)] * 2, [HBM] * 2, matrix_tiles, cols,
+        scratch=[face_tiles, cols_scratch], copies=2,
+    )
     back, u_face, *sends = call(
         lambda *refs: first_coarse_body(*refs, line=line), "coarse_load",
-        [small, face] + [small] * NF, [VMEM] * (line + 8),
-        contrib, rows, targets, target, *others, outer, *mats[2:], weight, swap,
-    )
-
-    def apply(inner, back, u_face, sends, stage):
-        came = trade_faces(sends)
-        wide = bf16(NF, BS, TPR * BS)
-        z, acc, *wides = call(
-            own_apply_body, "own_" + stage, [block, f32(*every), wide, wide],
-            [VMEM, VMEM, HBM, VMEM, HBM, SMEM],
-            inner, back, coarse_basis, u_face, matrix_tiles, cols,
-            scratch=[(BS, NIN * BS), (NB, TPR, BS, BS)], copies=1 + NB,
-        )
-        y, z_face, *sends = call(
-            face_apply_body, "face_" + stage, [f32(*every), face] + [small] * NF,
-            [VMEM] * 8 + [SMEM, VMEM],
-            acc, *came, u_face, *wides, cols, swap,
-        )
-        return z, z_face, y, sends
-
-    z, z_face, y, sends = apply(inner, back, u_face, sends, "first")
+        [small, face] + [small] * NF, [VMEM] * (line + 9),
+        contrib, rows, targets, target, *others, outer, *mats[2:], weight, swap, blocks[0],
+    )
+
     came = trade_faces(sends)
-    inner, part, *mats = inside_solve(y, "image")
+    own_scratch = [(BS, NIN * BS), (NIN, TPR, BS, BS)]
+    z, acc = call(
+        first_apply_body, "own_first", [block, f32(*every)], [VMEM, VMEM] + [HBM] * 3,
+        inner, back, coarse_basis, matrix_tiles, cols,
+        scratch=own_scratch + [cols_scratch], copies=2 + len(CHUNKS),
+    )
+    y_face, z_face, *sends = call(
+        first_face_body, "face_first", [face, face] + [small] * NF, [VMEM] * 9,
+        acc, *came, u_face, *blocks, swap,
+    )
+    came = trade_faces(sends)
+    y, inner, part, *mats = call(
+        image_inside_body, "inside_image", [block] + mat_outs, [VMEM] * 2 + [HBM] * 5,
+        acc, z_face, cols, matrix_tiles, interior_inv, coarse_basis, schur_inv,
+        scratch=mat_scratch + [face_tiles, every, cols_scratch], copies=5,
+    )
     high, low = call(
         lambda *refs: table_body(*refs, line=line), "table", [bf16(BS, width), bf16(BS, width)],
         [VMEM] * (line + 2), rows, targets, column, *others,
     )
     q_face, outer, contrib = call(
         next_faces_body, "faces_image", [face, face, small], [VMEM] * 11,
-        y, *came, weight, *mats, part,
+        y_face, *came, weight, *mats, part,
     )
     others = trade_line(contrib)
     back, u_face, *sends = call(
@@ -506,19 +593,29 @@
         [small, face] + [small] * NF, [VMEM] * (line + 7),
         contrib, *others, high, low, outer, *mats[2:], weight, swap,
     )
-    w, w_face, v, sends = apply(inner, back, u_face, sends, "second")
     came = trade_faces(sends)
-    (dots,) = call(
-        dots_body, "dots", [f32(devices, 2, BS)], [HBM] + [VMEM] * 6,
-        load_vector, z, z_face, y, w, w_face, v, scratch=[(NRHS, NL)], copies=1,
+    w, acc, sums, load = call(
+        second_apply_body, "own_second", [block, f32(*every), f32(5, NRHS, BS), f32(*every)],
+        [VMEM, VMEM] + [HBM] * 4 + [VMEM] * 4,
+        inner, back, coarse_basis, matrix_tiles, cols, load_vector, z, z_face, y, y_face,
+        scratch=own_scratch + [(NRHS, NL), cols_scratch, pltpu.SemaphoreType.DMA((2 + len(CHUNKS),))],
+        copies=1,
+    )
+    v_face, w_face, dots, *sends = call(
+        second_face_body, "face_second", [face, face, f32(devices, 2, BS)] + [small] * NF, [VMEM] * 12,
+        acc, *came, u_face, *blocks, swap, sums, load, y_face,
     )
     spread = lax.all_to_all(dots, AXES, 0, 0)
+    came = trade_faces(sends)
+    (v,) = call(
+        last_image_body, "inside_last", [block], [VMEM] * 2 + [HBM] * 2, acc, w_face, cols, matrix_tiles,
+        scratch=[face_tiles, every, cols_scratch], copies=2,
+    )
     out = f32(1, NRHS, NL)
     return tuple(
         call(
-            final_body, "combine", [out, out], [VMEM] * 5 + [HBM] + [VMEM] * 8,
-            spread, *came, load_vector, r_face, z, z_face, y, q_face, w, w_face, v,
-            scratch=[(NRHS, NIN * BS)], copies=1,
+            final_body, "combine", [out, out], [VMEM] * 15,
+            spread, *came, load, r_face, z, z_face, y, q_face, w, w_face, v, v_face,
         )
     )
 

time: 79.2 us -> 71.8 us (0.907)
  Pallas kernels: 30.1 us -> 26 us
  waiting for transfers between devices: 10.9 us -> 8.1 us
    pallas_call x14 -> x15, Pallas kernels: 30.1 us -> 26 us  [call(): pl.pallas_call(body, name=name, out_shape=outs, in_specs=specs, out_specs...]
    ppermute x27, waiting for transfers between devices: 10.9 us -> 8.1 us  [trade(): return lax.ppermute(value, AXES, [(i, i ^ mask) for i in range(devices)])]
    all_to_all x1, starting transfers between devices: 3.17 us -> 4.01 us  [on_device(): spread = lax.all_to_all(dots, AXES, 0, 0)]
  transfers between devices with their start and end apart: 28 -> 28, of which waited for: 8 -> 6; matrix products, arithmetic and copies ran while one was open for 0% -> 0% of each run, Pallas kernels for 24% -> 25%
where the time goes in v4:
time: 71.8 us; the launch traced here: 71.5 us
  starting transfers between devices  36.5 us (51%)
  Pallas kernels  26 us (36%)
  waiting for transfers between devices  8.1 us (11%)
  between operations  0.88 us (1%)
    ppermute x27, starting transfers between devices, trade(): return lax.ppermute(value, AXES, [(i, i ^ mask) for i in range(devices)])  32.5 us
    pallas_call x15, Pallas kernels, call(): pl.pallas_call(body, name=name, out_shape=outs, in_specs=specs, out_specs...  26 us
    ppermute x27, waiting for transfers between devices, trade(): return lax.ppermute(value, AXES, [(i, i ^ mask) for i in range(devices)])  8.1 us
    all_to_all x1, starting transfers between devices, on_device(): spread = lax.all_to_all(dots, AXES, 0, 0)  4.01 us
  transfers between devices with their start and end apart: 28, of which 6 were waited for; matrix products, arithmetic and copies ran while one was open for 0% of the time, Pallas kernels for 25%

profile of v4, /device:TPU:0, one launch (start us, length us, event | category | flops | bytes accessed | tf_op | source)
XLA Modules:
  0.0 71.5 jit_solution(11417361009381306484)
XLA Ops:
  0.6 0.9 %prepare.1 = (f32[8,128]{1,0:T(8,128)S(1)}, s32[2,128,128]{2,1,0:T(8,128)S(1)}, f32[8,128]{1,0:T(8,128)S(1)}, f32[48,128]{1,0:T(8,128)S(1)}, f32[48,128]{1,0:T(8...) custom-call(f32[1,32,2048]{2,1,0:T(8,128)} %load_hbm.1, s32[1,4,128]{2,1,0:T(4,128)} %map_ref.1, s32[1,4]{1,0:T(1,128)} %id_ref.1, ...), custom_call_target="tpu_custom_call" | custom-call | tf_op jit(solution)/shard_map/prepare/pallas_call | solution.py:487
  1.5 3.1 %collective-permute-start = (f32[48,128]{1,0:T(8,128)S(1)}, f32[48,128]{1,0:T(8,128)S(1)}, u32[]{:S(2)}, u32[]{:S(2)}) collective-permute-start(f32[48,128]{1,0:T(8,128)S(1)} %get-tuple-element.71.refs_0_), channel_id=1, source_target_pairs={{0,1},{1,0},{2,3},{3,2},{4,5},{5,4},{6,7},{7,6},{8,9},{9,8},{10,11... | collective-permute-start | bytes 73736 | tf_op jit(solution)/shard_map/ppermute | solution.py:510
  4.6 2.6 %collective-permute-start.1 = (f32[48,128]{1,0:T(8,128)S(1)}, f32[48,128]{1,0:T(8,128)S(1)}, u32[]{:S(2)}, u32[]{:S(2)}) collective-permute-start(f32[48,128]{1,0:T(8,128)S(1)} %get-tuple-element.72.refs_1_), channel_id=1, source_target_pairs={{0,2},{1,3},{2,0},{3,1},{4,6},{5,7},{6,4},{7,5},{8,10},{9,11},{10,... | collective-permute-start | bytes 73736 | tf_op jit(solution)/shard_map/ppermute | solution.py:510
  7.2 1.5 %collective-permute-start.3 = (f32[48,128]{1,0:T(8,128)S(1)}, f32[48,128]{1,0:T(8,128)S(1)}, u32[]{:S(2)}, u32[]{:S(2)}) collective-permute-start(f32[48,128]{1,0:T(8,128)S(1)} %get-tuple-element.74.refs_3_), channel_id=1, source_target_pairs={{0,8},{1,9},{2,10},{3,11},{4,12},{5,13},{6,14},{7,15},{8,0},{9,1},... | collective-permute-start | bytes 73736 | tf_op jit(solution)/shard_map/ppermute | solution.py:510
  8.7 0.2 collective-permute-start.4
  8.9 2.8 %inside_load.1 = (f32[12,32,128]{2,1,0:T(8,128)S(1)}, f32[32,128]{1,0:T(8,128)S(1)}, bf16[512,512]{1,0:T(8,128)(2,1)S(1)}, bf16[512,512]{1,0:T(8,128)(2,1)S(1)},...) custom-call(f32[1,32,2048]{2,1,0:T(8,128)} %load_hbm.1, ...), custom_call_target="tpu_custom_call" | custom-call | tf_op jit(solution)/shard_map/inside_load/pallas_call | solution.py:487
  11.7 2.4 %collective-permute-done.4.refs_16_ = f32[8,128]{1,0:T(8,128)S(1)} collective-permute-done((f32[8,128]{1,0:T(8,128)S(1)}, f32[8,128]{1,0:T(8,128)S(1)}, u32[]{:S(2)}, u32[]{:S(2)}) %collective-permute-start.4) | collective-permute-done | bytes 4128 | tf_op jit(solution)/shard_map/ppermute | solution.py:510
  14.1 0.0 collective-permute-done.refs_4_
  14.1 0.0 collective-permute-done.1.refs_5_
  14.1 0.0 collective-permute-done.2.refs_6_
  14.1 1.7 %faces_load.1 = (f32[4,32,128]{2,1,0:T(8,128)S(1)}, f32[4,32,128]{2,1,0:T(8,128)S(1)}, f32[32,128]{1,0:T(8,128)S(1)}, bf16[4,128,128]{2,1,0:T(8,128)(2,1)S(1)}, ...) custom-call(f32[48,128]{1,0:T(8,128)S(1)} %get-tuple-element.71.refs, ...), custom_call_target="tpu_custom_call" | custom-call | tf_op jit(solution)/shard_map/faces_load/pallas_call | solution.py:487
  15.8 0.1 collective-permute-start.5
  15.9 1.8 %collective-permute-start.6 = (f32[160,128]{1,0:T(8,128)S(1)}, f32[160,128]{1,0:T(8,128)S(1)}, u32[]{:S(2)}, u32[]{:S(2)}) collective-permute-start(f32[160,128]{1,0:T(8,128)S(1)} %get-tuple-element.87), channel_id=1, source_target_pairs={{0,2},{1,3},{2,0},{3,1},{4,6},{5,7},{6,4},{7,5},{8,10},{9,11},{10,... | collective-permute-start | bytes 245768 | tf_op jit(solution)/shard_map/ppermute | solution.py:510
  17.7 2.6 %collective-permute-start.7 = (f32[160,128]{1,0:T(8,128)S(1)}, f32[160,128]{1,0:T(8,128)S(1)}, u32[]{:S(2)}, u32[]{:S(2)}) collective-permute-start(f32[160,128]{1,0:T(8,128)S(1)} %get-tuple-element.88), channel_id=1, source_target_pairs={{0,3},{1,2},{2,1},{3,0},{4,7},{5,6},{6,5},{7,4},{8,11},{9,10},{10,... | collective-permute-start | bytes 245768 | tf_op jit(solution)/shard_map/ppermute | solution.py:510
  20.3 1.8 %face_block.1 = (bf16[4,4,128,128]{3,2,1,0:T(8,128)(2,1)S(1)}, bf16[4,4,128,128]{3,2,1,0:T(8,128)(2,1)S(1)}) custom-call(f32[16,7,128,128]{3,2,1,0:T(8,128)} %tiles_ref.7, s32[7,16]{1,0:T(8,128)} %bitcast.1), custom_call_target="tpu_custom_call" | custom-call | tf_op jit(solution)/shard_map/face_block/pallas_call | solution.py:487
  22.1 2.7 %collective-permute-done.6.refs_5_.refs_4_ = f32[160,128]{1,0:T(8,128)S(1)} collective-permute-done((f32[160,128]{1,0:T(8,128)S(1)}, f32[160,128]{1,0:T(8,128)S(1)}, u32[]{:S(2)}, u32[]{:S(2)}) %collective-permute-start.6) | collective-permute-done | bytes 81952 | tf_op jit(solution)/shard_map/ppermute | solution.py:510
  24.7 1.9 %coarse_load.1 = (f32[32,128]{1,0:T(8,128)S(1)}, f32[4,32,128]{2,1,0:T(8,128)S(1)}, f32[32,128]{1,0:T(8,128)S(1)}, f32[32,128]{1,0:T(8,128)S(1)}, f32[32,128]{1,0:T(8,128)S(1)}, /*index=5*/f32[32,128]{1,0:T(8,128)S(1)}) custom-call(f32[32,128]{1,0:T(8,128)S(1)} %get-tuple-element.83.refs_0_, f32[128,128]{1,0:T(8,128)S(1)} %get-tuple-element.84.refs_1_.refs_0_, ...), custom_call_target="tpu_custom_call" | custom-call | tf_op jit(solution)/shard_map/coarse_load/pallas_call | solution.py:487
  26.7 0.0 collective-permute-start.10
  26.7 0.6 collective-permute-start.11
  27.3 1.4 %collective-permute-start.8 = (f32[32,128]{1,0:T(8,128)S(1)}, f32[32,128]{1,0:T(8,128)S(1)}, u32[]{:S(2)}, u32[]{:S(2)}) collective-permute-start(f32[32,128]{1,0:T(8,128)S(1)} %get-tuple-element.94), channel_id=1, source_target_pairs={{0,1},{1,0},{2,3},{3,2},{4,5},{5,4},{6,7},{7,6},{8,9},{9,8},{10,11... | collective-permute-start | bytes 49160 | tf_op jit(solution)/shard_map/ppermute | solution.py:510
  28.7 1.2 %collective-permute-start.9 = (f32[32,128]{1,0:T(8,128)S(1)}, f32[32,128]{1,0:T(8,128)S(1)}, u32[]{:S(2)}, u32[]{:S(2)}) collective-permute-start(f32[32,128]{1,0:T(8,128)S(1)} %get-tuple-element.95), channel_id=1, source_target_pairs={{0,2},{1,3},{2,0},{3,1},{4,6},{5,7},{6,4},{7,5},{8,10},{9,11},{10,... | collective-permute-start | bytes 49160 | tf_op jit(solution)/shard_map/ppermute | solution.py:510
  29.9 3.4 %own_first.1 = (f32[12,32,128]{2,1,0:T(8,128)S(1)}, f32[16,32,128]{2,1,0:T(8,128)S(1)}) custom-call(f32[12,32,128]{2,1,0:T(8,128)S(1)} %get-tuple-element.70.refs_0_, f32[32,128]{1,0:T(8,128)S(1)} %get-tuple-element.92.refs_1_, f32[1,128,2048]{2,1,0:T(8,128)} %basis_ref.5, f32[16,7,128,128]{3,2,1,0:T(8,128)} %tiles_ref.7, s32[7,16]{1,0:T(8,128)} %bitcast.2), custom_call_target="tpu_custom_call" | custom-call | tf_op jit(solution)/shard_map/own_first/pallas_call | solution.py:487
  33.3 0.2 collective-permute-done.9.in1
  33.5 0.4 face_first.1
  33.9 1.3 %collective-permute-start.12 = (f32[32,128]{1,0:T(8,128)S(1)}, f32[32,128]{1,0:T(8,128)S(1)}, u32[]{:S(2)}, u32[]{:S(2)}) collective-permute-start(f32[32,128]{1,0:T(8,128)S(1)} %get-tuple-element.103), channel_id=1, source_target_pairs={{0,1},{1,0},{2,3},{3,2},{4,5},{5,4},{6,7},{7,6},{8,9},{9,8},{10,11... | collective-permute-start | bytes 49160 | tf_op jit(solution)/shard_map/ppermute | solution.py:510
  35.2 1.3 %collective-permute-start.13 = (f32[32,128]{1,0:T(8,128)S(1)}, f32[32,128]{1,0:T(8,128)S(1)}, u32[]{:S(2)}, u32[]{:S(2)}) collective-permute-start(f32[32,128]{1,0:T(8,128)S(1)} %get-tuple-element.104), channel_id=1, source_target_pairs={{0,2},{1,3},{2,0},{3,1},{4,6},{5,7},{6,4},{7,5},{8,10},{9,11},{10,... | collective-permute-start | bytes 49160 | tf_op jit(solution)/shard_map/ppermute | solution.py:510
  36.6 1.5 %collective-permute-start.15 = (f32[32,128]{1,0:T(8,128)S(1)}, f32[32,128]{1,0:T(8,128)S(1)}, u32[]{:S(2)}, u32[]{:S(2)}) collective-permute-start(f32[32,128]{1,0:T(8,128)S(1)} %get-tuple-element.106), channel_id=1, source_target_pairs={{0,8},{1,9},{2,10},{3,11},{4,12},{5,13},{6,14},{7,15},{8,0},{9,1},... | collective-permute-start | bytes 49160 | tf_op jit(solution)/shard_map/ppermute | solution.py:510
  38.1 3.8 %inside_image.1 = (f32[12,32,128]{2,1,0:T(8,128)S(1)}, f32[12,32,128]{2,1,0:T(8,128)S(1)}, f32[32,128]{1,0:T(8,128)S(1)}, bf16[512,512]{1,0:T(8,128)(2,1)S(1)}, ...) custom-call(f32[16,32,128]{2,1,0:T(8,128)S(1)} %get-tuple-element.93.acc_ref, ...), custom_call_target="tpu_custom_call" | custom-call | tf_op jit(solution)/shard_map/inside_image/pallas_call | solution.py:487
  41.9 0.4 faces_image.1
  42.3 1.0 %collective-permute-start.16 = (f32[32,128]{1,0:T(8,128)S(1)}, f32[32,128]{1,0:T(8,128)S(1)}, u32[]{:S(2)}, u32[]{:S(2)}) collective-permute-start(f32[32,128]{1,0:T(8,128)S(1)} %get-tuple-element.112.refs_0_), channel_id=1, source_target_pairs={{0,1},{1,0},{2,3},{3,2},{4,5},{5,4},{6,7},{7,6},{8,9},{9,8},{10,11... | collective-permute-start | bytes 49160 | tf_op jit(solution)/shard_map/ppermute | solution.py:510
  43.3 1.4 %collective-permute-start.17 = (f32[32,128]{1,0:T(8,128)S(1)}, f32[32,128]{1,0:T(8,128)S(1)}, u32[]{:S(2)}, u32[]{:S(2)}) collective-permute-start(f32[32,128]{1,0:T(8,128)S(1)} %get-tuple-element.112.refs_0_), channel_id=1, source_target_pairs={{0,2},{1,3},{2,0},{3,1},{4,6},{5,7},{6,4},{7,5},{8,10},{9,11},{10,... | collective-permute-start | bytes 49160 | tf_op jit(solution)/shard_map/ppermute | solution.py:510
  44.6 2.1 %collective-permute-start.18 = (f32[32,128]{1,0:T(8,128)S(1)}, f32[32,128]{1,0:T(8,128)S(1)}, u32[]{:S(2)}, u32[]{:S(2)}) collective-permute-start(f32[32,128]{1,0:T(8,128)S(1)} %get-tuple-element.112.refs_0_), channel_id=1, source_target_pairs={{0,3},{1,2},{2,1},{3,0},{4,7},{5,6},{6,5},{7,4},{8,11},{9,10},{10,... | collective-permute-start | bytes 49160 | tf_op jit(solution)/shard_map/ppermute | solution.py:510
  46.7 0.9 %table.1 = (bf16[128,512]{1,0:T(8,128)(2,1)S(1)}, bf16[128,512]{1,0:T(8,128)(2,1)S(1)}) custom-call(f32[128,128]{1,0:T(8,128)S(1)} %get-tuple-element.84.refs_1_.refs_0_, f32[1,512]{1,0:T(1,128)S(1)} %get-tuple-element.85.refs_2_.refs_1_, s32[2,128,128]{2,1,0:T(8,128)S(1)} %get-tuple-element.113.refs_2_, ...), custom_call_target="tpu_custom_call" | custom-call | tf_op jit(solution)/shard_map/table/pallas_call | solution.py:487
  47.6 0.4 collective-permute-done.17.refs_2_
  47.9 2.2 %collective-permute-done.18.refs_3_ = f32[32,128]{1,0:T(8,128)S(1)} collective-permute-done((f32[32,128]{1,0:T(8,128)S(1)}, f32[32,128]{1,0:T(8,128)S(1)}, u32[]{:S(2)}, u32[]{:S(2)}) %collective-permute-start.18) | collective-permute-done | bytes 16416 | tf_op jit(solution)/shard_map/ppermute | solution.py:510
  50.2 0.6 coarse_image.1
  50.7 0.1 collective-permute-start.19
  50.8 2.6 %collective-permute-start.20 = (f32[32,128]{1,0:T(8,128)S(1)}, f32[32,128]{1,0:T(8,128)S(1)}, u32[]{:S(2)}, u32[]{:S(2)}) collective-permute-start(f32[32,128]{1,0:T(8,128)S(1)} %get-tuple-element.122), channel_id=1, source_target_pairs={{0,2},{1,3},{2,0},{3,1},{4,6},{5,7},{6,4},{7,5},{8,10},{9,11},{10,... | collective-permute-start | bytes 49160 | tf_op jit(solution)/shard_map/ppermute | solution.py:510
  53.4 0.5 collective-permute-start.22
  53.9 3.5 %own_second.1 = (f32[12,32,128]{2,1,0:T(8,128)S(1)}, f32[16,32,128]{2,1,0:T(8,128)S(1)}, f32[5,32,128]{2,1,0:T(8,128)S(1)}, f32[16,32,128]{2,1,0:T(8,128)S(1)}) custom-call(f32[12,32,128]{2,1,0:T(8,128)S(1)} %get-tuple-element.101.inner_ref, f32[32,128]{1,0:T(8,128)S(1)} %get-tuple-element.117.back_ref, f32[1,128,2048]{2,1,0:T(8,128)} %basis_ref.5, ...), custom_call_target="tpu_custom_call" | custom-call | tf_op jit(solution)/shard_map/own_second/pallas_call | solution.py:487
  57.5 1.0 %face_second.1 = (f32[4,32,128]{2,1,0:T(8,128)S(1)}, f32[4,32,128]{2,1,0:T(8,128)S(1)}, f32[32,2,128]{2,1,0:T(2,128)}, f32[32,128]{1,0:T(8,128)S(1)}, f32[32,128...) custom-call(f32[16,32,128]{2,1,0:T(8,128)S(1)} %get-tuple-element.120.acc_ref, ...), custom_call_target="tpu_custom_call" | custom-call | tf_op jit(solution)/shard_map/face_second/pallas_call | solution.py:487
  58.5 4.0 %all-to-all-start = ((f32[32,2,128]{2,1,0:T(2,128)}), f32[32,2,128]{2,1,0:T(2,128)S(1)}, u32[]{:S(2)}, u32[]{:S(2)}) async-start(f32[32,2,128]{2,1,0:T(2,128)} %get-tuple-element.128), calls=%async_computation | async-start | bytes 65536 | tf_op jit(solution)/shard_map/all_to_all | solution.py:608
  62.5 1.8 %collective-permute-start.23 = (f32[32,128]{1,0:T(8,128)S(1)}, f32[32,128]{1,0:T(8,128)S(1)}, u32[]{:S(2)}, u32[]{:S(2)}) collective-permute-start(f32[32,128]{1,0:T(8,128)S(1)} %get-tuple-element.129), channel_id=1, source_target_pairs={{0,1},{1,0},{2,3},{3,2},{4,5},{5,4},{6,7},{7,6},{8,9},{9,8},{10,11... | collective-permute-start | bytes 49160 | tf_op jit(solution)/shard_map/ppermute | solution.py:510
  64.4 2.4 %collective-permute-start.24 = (f32[32,128]{1,0:T(8,128)S(1)}, f32[32,128]{1,0:T(8,128)S(1)}, u32[]{:S(2)}, u32[]{:S(2)}) collective-permute-start(f32[32,128]{1,0:T(8,128)S(1)} %get-tuple-element.130), channel_id=1, source_target_pairs={{0,2},{1,3},{2,0},{3,1},{4,6},{5,7},{6,4},{7,5},{8,10},{9,11},{10,... | collective-permute-start | bytes 49160 | tf_op jit(solution)/shard_map/ppermute | solution.py:510
  66.8 1.5 %collective-permute-start.26 = (f32[32,128]{1,0:T(8,128)S(1)}, f32[32,128]{1,0:T(8,128)S(1)}, u32[]{:S(2)}, u32[]{:S(2)}) collective-permute-start(f32[32,128]{1,0:T(8,128)S(1)} %get-tuple-element.132), channel_id=1, source_target_pairs={{0,8},{1,9},{2,10},{3,11},{4,12},{5,13},{6,14},{7,15},{8,0},{9,1},... | collective-permute-start | bytes 49160 | tf_op jit(solution)/shard_map/ppermute | solution.py:510
  68.3 2.0 %inside_last.1.vi = f32[12,32,128]{2,1,0:T(8,128)S(1)} custom-call(f32[16,32,128]{2,1,0:T(8,128)S(1)} %get-tuple-element.120.acc_ref, f32[4,32,128]{2,1,0:T(8,128)S(1)} %get-tuple-element.136.face_ref.wf, s32[7,16]{1,0:T(8,128)} %bitcast.5, f32[16,7,128,128]{3,2,1,0:T(8,128)} %tiles_ref.7), custom_call_target="tpu_custom_call" | custom-call | tf_op jit(solution)/shard_map/inside_last/pallas_call | solution.py:487
  70.3 0.2 collective-permute-done.26.in3
  70.5 1.0 %combine.1 = (f32[1,32,2048]{2,1,0:T(8,128)}, f32[1,32,2048]{2,1,0:T(8,128)}) custom-call(f32[32,2,128]{2,1,0:T(2,128)S(1)} %all-to-all-done.dots_ref, f32[32,128]{1,0:T(8,128)S(1)} %collective-permute-done.23.in0, f32[32,128]{1,0:T(8,128)S(1)} %collective-permute-done.24.in1, f32[32,128]{1,0:T(8,128)S(1)} %collective-permute-done.25.in2, ...), custom_call_target="tpu_custom_call" | custom-call | tf_op jit(solution)/shard_map/combine/pallas_call | solution.py:487
  (23 shorter events, 0.1 us)
Async XLA Ops:
  1.5 12.6 %collective-permute-start = (f32[48,128]{1,0:T(8,128)S(1)}, f32[48,128]{1,0:T(8,128)S(1)}, u32[]{:S(2)}, u32[]{:S(2)}) collective-permute-start(f32[48,128]{1,0:T(8,128)S(1)} %get-tuple-element.71.refs_0_), channel_id=1, source_target_pairs={{0,1},{1,0},{2,3},{3,2},{4,5},{5,4},{6,7},{7,6},{8,9},{9,8},{10,11... | collective-permute-start | bytes 73736 | tf_op jit(solution)/shard_map/ppermute | solution.py:510
  4.6 9.5 %collective-permute-start.1 = (f32[48,128]{1,0:T(8,128)S(1)}, f32[48,128]{1,0:T(8,128)S(1)}, u32[]{:S(2)}, u32[]{:S(2)}) collective-permute-start(f32[48,128]{1,0:T(8,128)S(1)} %get-tuple-element.72.refs_1_), channel_id=1, source_target_pairs={{0,2},{1,3},{2,0},{3,1},{4,6},{5,7},{6,4},{7,5},{8,10},{9,11},{10,... | collective-permute-start | bytes 73736 | tf_op jit(solution)/shard_map/ppermute | solution.py:510
  7.2 6.9 %collective-permute-start.2 = (f32[48,128]{1,0:T(8,128)S(1)}, f32[48,128]{1,0:T(8,128)S(1)}, u32[]{:S(2)}, u32[]{:S(2)}) collective-permute-start(f32[48,128]{1,0:T(8,128)S(1)} %get-tuple-element.73.refs_2_), channel_id=1, source_target_pairs={{0,4},{1,5},{2,6},{3,7},{4,0},{5,1},{6,2},{7,3},{8,12},{9,13},{10,... | collective-permute-start | bytes 73736 | tf_op jit(solution)/shard_map/ppermute | solution.py:510
  7.2 6.9 %collective-permute-start.3 = (f32[48,128]{1,0:T(8,128)S(1)}, f32[48,128]{1,0:T(8,128)S(1)}, u32[]{:S(2)}, u32[]{:S(2)}) collective-permute-start(f32[48,128]{1,0:T(8,128)S(1)} %get-tuple-element.74.refs_3_), channel_id=1, source_target_pairs={{0,8},{1,9},{2,10},{3,11},{4,12},{5,13},{6,14},{7,15},{8,0},{9,1},... | collective-permute-start | bytes 73736 | tf_op jit(solution)/shard_map/ppermute | solution.py:510
  8.7 5.4 %collective-permute-start.4 = (f32[8,128]{1,0:T(8,128)S(1)}, f32[8,128]{1,0:T(8,128)S(1)}, u32[]{:S(2)}, u32[]{:S(2)}) collective-permute-start(f32[8,128]{1,0:T(8,128)S(1)} %get-tuple-element.75.refs_8_.refs_3_), channel_id=1, source_target_pairs={{0,3},{1,2},{2,1},{3,0},{4,7},{5,6},{6,5},{7,4},{8,11},{9,10},{10,... | collective-permute-start | bytes 12296 | tf_op jit(solution)/shard_map/ppermute | solution.py:510
  15.8 6.3 %collective-permute-start.5 = (f32[160,128]{1,0:T(8,128)S(1)}, f32[160,128]{1,0:T(8,128)S(1)}, u32[]{:S(2)}, u32[]{:S(2)}) collective-permute-start(f32[160,128]{1,0:T(8,128)S(1)} %get-tuple-element.86), channel_id=1, source_target_pairs={{0,1},{1,0},{2,3},{3,2},{4,5},{5,4},{6,7},{7,6},{8,9},{9,8},{10,11... | collective-permute-start | bytes 245768 | tf_op jit(solution)/shard_map/ppermute | solution.py:510
  15.9 8.8 %collective-permute-start.6 = (f32[160,128]{1,0:T(8,128)S(1)}, f32[160,128]{1,0:T(8,128)S(1)}, u32[]{:S(2)}, u32[]{:S(2)}) collective-permute-start(f32[160,128]{1,0:T(8,128)S(1)} %get-tuple-element.87), channel_id=1, source_target_pairs={{0,2},{1,3},{2,0},{3,1},{4,6},{5,7},{6,4},{7,5},{8,10},{9,11},{10,... | collective-permute-start | bytes 245768 | tf_op jit(solution)/shard_map/ppermute | solution.py:510
  17.7 7.0 %collective-permute-start.7 = (f32[160,128]{1,0:T(8,128)S(1)}, f32[160,128]{1,0:T(8,128)S(1)}, u32[]{:S(2)}, u32[]{:S(2)}) collective-permute-start(f32[160,128]{1,0:T(8,128)S(1)} %get-tuple-element.88), channel_id=1, source_target_pairs={{0,3},{1,2},{2,1},{3,0},{4,7},{5,6},{6,5},{7,4},{8,11},{9,10},{10,... | collective-permute-start | bytes 245768 | tf_op jit(solution)/shard_map/ppermute | solution.py:510
  26.7 6.6 %collective-permute-start.10 = (f32[32,128]{1,0:T(8,128)S(1)}, f32[32,128]{1,0:T(8,128)S(1)}, u32[]{:S(2)}, u32[]{:S(2)}) collective-permute-start(f32[32,128]{1,0:T(8,128)S(1)} %get-tuple-element.96), channel_id=1, source_target_pairs={{0,4},{1,5},{2,6},{3,7},{4,0},{5,1},{6,2},{7,3},{8,12},{9,13},{10,... | collective-permute-start | bytes 49160 | tf_op jit(solution)/shard_map/ppermute | solution.py:510
  26.7 6.6 %collective-permute-start.11 = (f32[32,128]{1,0:T(8,128)S(1)}, f32[32,128]{1,0:T(8,128)S(1)}, u32[]{:S(2)}, u32[]{:S(2)}) collective-permute-start(f32[32,128]{1,0:T(8,128)S(1)} %get-tuple-element.97), channel_id=1, source_target_pairs={{0,8},{1,9},{2,10},{3,11},{4,12},{5,13},{6,14},{7,15},{8,0},{9,1},... | collective-permute-start | bytes 49160 | tf_op jit(solution)/shard_map/ppermute | solution.py:510
  27.3 6.1 %collective-permute-start.8 = (f32[32,128]{1,0:T(8,128)S(1)}, f32[32,128]{1,0:T(8,128)S(1)}, u32[]{:S(2)}, u32[]{:S(2)}) collective-permute-start(f32[32,128]{1,0:T(8,128)S(1)} %get-tuple-element.94), channel_id=1, source_target_pairs={{0,1},{1,0},{2,3},{3,2},{4,5},{5,4},{6,7},{7,6},{8,9},{9,8},{10,11... | collective-permute-start | bytes 49160 | tf_op jit(solution)/shard_map/ppermute | solution.py:510
  28.7 4.8 %collective-permute-start.9 = (f32[32,128]{1,0:T(8,128)S(1)}, f32[32,128]{1,0:T(8,128)S(1)}, u32[]{:S(2)}, u32[]{:S(2)}) collective-permute-start(f32[32,128]{1,0:T(8,128)S(1)} %get-tuple-element.95), channel_id=1, source_target_pairs={{0,2},{1,3},{2,0},{3,1},{4,6},{5,7},{6,4},{7,5},{8,10},{9,11},{10,... | collective-permute-start | bytes 49160 | tf_op jit(solution)/shard_map/ppermute | solution.py:510
  33.9 8.0 %collective-permute-start.12 = (f32[32,128]{1,0:T(8,128)S(1)}, f32[32,128]{1,0:T(8,128)S(1)}, u32[]{:S(2)}, u32[]{:S(2)}) collective-permute-start(f32[32,128]{1,0:T(8,128)S(1)} %get-tuple-element.103), channel_id=1, source_target_pairs={{0,1},{1,0},{2,3},{3,2},{4,5},{5,4},{6,7},{7,6},{8,9},{9,8},{10,11... | collective-permute-start | bytes 49160 | tf_op jit(solution)/shard_map/ppermute | solution.py:510
  35.2 6.7 %collective-permute-start.13 = (f32[32,128]{1,0:T(8,128)S(1)}, f32[32,128]{1,0:T(8,128)S(1)}, u32[]{:S(2)}, u32[]{:S(2)}) collective-permute-start(f32[32,128]{1,0:T(8,128)S(1)} %get-tuple-element.104), channel_id=1, source_target_pairs={{0,2},{1,3},{2,0},{3,1},{4,6},{5,7},{6,4},{7,5},{8,10},{9,11},{10,... | collective-permute-start | bytes 49160 | tf_op jit(solution)/shard_map/ppermute | solution.py:510
  36.6 5.3 %collective-permute-start.14 = (f32[32,128]{1,0:T(8,128)S(1)}, f32[32,128]{1,0:T(8,128)S(1)}, u32[]{:S(2)}, u32[]{:S(2)}) collective-permute-start(f32[32,128]{1,0:T(8,128)S(1)} %get-tuple-element.105), channel_id=1, source_target_pairs={{0,4},{1,5},{2,6},{3,7},{4,0},{5,1},{6,2},{7,3},{8,12},{9,13},{10,... | collective-permute-start | bytes 49160 | tf_op jit(solution)/shard_map/ppermute | solution.py:510
  36.6 5.3 %collective-permute-start.15 = (f32[32,128]{1,0:T(8,128)S(1)}, f32[32,128]{1,0:T(8,128)S(1)}, u32[]{:S(2)}, u32[]{:S(2)}) collective-permute-start(f32[32,128]{1,0:T(8,128)S(1)} %get-tuple-element.106), channel_id=1, source_target_pairs={{0,8},{1,9},{2,10},{3,11},{4,12},{5,13},{6,14},{7,15},{8,0},{9,1},... | collective-permute-start | bytes 49160 | tf_op jit(solution)/shard_map/ppermute | solution.py:510
  42.3 5.3 %collective-permute-start.16 = (f32[32,128]{1,0:T(8,128)S(1)}, f32[32,128]{1,0:T(8,128)S(1)}, u32[]{:S(2)}, u32[]{:S(2)}) collective-permute-start(f32[32,128]{1,0:T(8,128)S(1)} %get-tuple-element.112.refs_0_), channel_id=1, source_target_pairs={{0,1},{1,0},{2,3},{3,2},{4,5},{5,4},{6,7},{7,6},{8,9},{9,8},{10,11... | collective-permute-start | bytes 49160 | tf_op jit(solution)/shard_map/ppermute | solution.py:510
  43.3 4.7 %collective-permute-start.17 = (f32[32,128]{1,0:T(8,128)S(1)}, f32[32,128]{1,0:T(8,128)S(1)}, u32[]{:S(2)}, u32[]{:S(2)}) collective-permute-start(f32[32,128]{1,0:T(8,128)S(1)} %get-tuple-element.112.refs_0_), channel_id=1, source_target_pairs={{0,2},{1,3},{2,0},{3,1},{4,6},{5,7},{6,4},{7,5},{8,10},{9,11},{10,... | collective-permute-start | bytes 49160 | tf_op jit(solution)/shard_map/ppermute | solution.py:510
  44.6 5.5 %collective-permute-start.18 = (f32[32,128]{1,0:T(8,128)S(1)}, f32[32,128]{1,0:T(8,128)S(1)}, u32[]{:S(2)}, u32[]{:S(2)}) collective-permute-start(f32[32,128]{1,0:T(8,128)S(1)} %get-tuple-element.112.refs_0_), channel_id=1, source_target_pairs={{0,3},{1,2},{2,1},{3,0},{4,7},{5,6},{6,5},{7,4},{8,11},{9,10},{10,... | collective-permute-start | bytes 49160 | tf_op jit(solution)/shard_map/ppermute | solution.py:510
  50.7 6.7 %collective-permute-start.19 = (f32[32,128]{1,0:T(8,128)S(1)}, f32[32,128]{1,0:T(8,128)S(1)}, u32[]{:S(2)}, u32[]{:S(2)}) collective-permute-start(f32[32,128]{1,0:T(8,128)S(1)} %get-tuple-element.121), channel_id=1, source_target_pairs={{0,1},{1,0},{2,3},{3,2},{4,5},{5,4},{6,7},{7,6},{8,9},{9,8},{10,11... | collective-permute-start | bytes 49160 | tf_op jit(solution)/shard_map/ppermute | solution.py:510
  50.8 6.7 %collective-permute-start.20 = (f32[32,128]{1,0:T(8,128)S(1)}, f32[32,128]{1,0:T(8,128)S(1)}, u32[]{:S(2)}, u32[]{:S(2)}) collective-permute-start(f32[32,128]{1,0:T(8,128)S(1)} %get-tuple-element.122), channel_id=1, source_target_pairs={{0,2},{1,3},{2,0},{3,1},{4,6},{5,7},{6,4},{7,5},{8,10},{9,11},{10,... | collective-permute-start | bytes 49160 | tf_op jit(solution)/shard_map/ppermute | solution.py:510
  53.4 4.1 %collective-permute-start.21 = (f32[32,128]{1,0:T(8,128)S(1)}, f32[32,128]{1,0:T(8,128)S(1)}, u32[]{:S(2)}, u32[]{:S(2)}) collective-permute-start(f32[32,128]{1,0:T(8,128)S(1)} %get-tuple-element.123), channel_id=1, source_target_pairs={{0,4},{1,5},{2,6},{3,7},{4,0},{5,1},{6,2},{7,3},{8,12},{9,13},{10,... | collective-permute-start | bytes 49160 | tf_op jit(solution)/shard_map/ppermute | solution.py:510
  53.4 4.1 %collective-permute-start.22 = (f32[32,128]{1,0:T(8,128)S(1)}, f32[32,128]{1,0:T(8,128)S(1)}, u32[]{:S(2)}, u32[]{:S(2)}) collective-permute-start(f32[32,128]{1,0:T(8,128)S(1)} %get-tuple-element.124), channel_id=1, source_target_pairs={{0,8},{1,9},{2,10},{3,11},{4,12},{5,13},{6,14},{7,15},{8,0},{9,1},... | collective-permute-start | bytes 49160 | tf_op jit(solution)/shard_map/ppermute | solution.py:510
  58.5 12.0 %all-to-all-start = ((f32[32,2,128]{2,1,0:T(2,128)}), f32[32,2,128]{2,1,0:T(2,128)S(1)}, u32[]{:S(2)}, u32[]{:S(2)}) async-start(f32[32,2,128]{2,1,0:T(2,128)} %get-tuple-element.128), calls=%async_computation | async-start | bytes 65536 | tf_op jit(solution)/shard_map/all_to_all | solution.py:608
  62.5 7.7 %collective-permute-start.23 = (f32[32,128]{1,0:T(8,128)S(1)}, f32[32,128]{1,0:T(8,128)S(1)}, u32[]{:S(2)}, u32[]{:S(2)}) collective-permute-start(f32[32,128]{1,0:T(8,128)S(1)} %get-tuple-element.129), channel_id=1, source_target_pairs={{0,1},{1,0},{2,3},{3,2},{4,5},{5,4},{6,7},{7,6},{8,9},{9,8},{10,11... | collective-permute-start | bytes 49160 | tf_op jit(solution)/shard_map/ppermute | solution.py:510
  64.4 5.9 %collective-permute-start.24 = (f32[32,128]{1,0:T(8,128)S(1)}, f32[32,128]{1,0:T(8,128)S(1)}, u32[]{:S(2)}, u32[]{:S(2)}) collective-permute-start(f32[32,128]{1,0:T(8,128)S(1)} %get-tuple-element.130), channel_id=1, source_target_pairs={{0,2},{1,3},{2,0},{3,1},{4,6},{5,7},{6,4},{7,5},{8,10},{9,11},{10,... | collective-permute-start | bytes 49160 | tf_op jit(solution)/shard_map/ppermute | solution.py:510
  66.8 3.5 %collective-permute-start.25 = (f32[32,128]{1,0:T(8,128)S(1)}, f32[32,128]{1,0:T(8,128)S(1)}, u32[]{:S(2)}, u32[]{:S(2)}) collective-permute-start(f32[32,128]{1,0:T(8,128)S(1)} %get-tuple-element.131), channel_id=1, source_target_pairs={{0,4},{1,5},{2,6},{3,7},{4,0},{5,1},{6,2},{7,3},{8,12},{9,13},{10,... | collective-permute-start | bytes 49160 | tf_op jit(solution)/shard_map/ppermute | solution.py:510
  66.8 3.7 %collective-permute-start.26 = (f32[32,128]{1,0:T(8,128)S(1)}, f32[32,128]{1,0:T(8,128)S(1)}, u32[]{:S(2)}, u32[]{:S(2)}) collective-permute-start(f32[32,128]{1,0:T(8,128)S(1)} %get-tuple-element.132), channel_id=1, source_target_pairs={{0,8},{1,9},{2,10},{3,11},{4,12},{5,13},{6,14},{7,15},{8,0},{9,1},... | collective-permute-start | bytes 49160 | tf_op jit(solution)/shard_map/ppermute | solution.py:510

commit v5 on v4

--- a/solution.py
+++ b/solution.py
@@ -13,7 +13,8 @@
 CB = 4
 OCAP = 8
 SCAP = 2
-CHUNKS = (4, 4, 3, 1)
+EARLY = 4
+CHUNKS = (4, 3, 1)
 NB = 16
 TPR = 7
 NL = 2048
@@ -109,8 +110,7 @@
     out_ref[...] = spare_ref[:NIN]
 
 
-def solve_inside(x_of, inv, basis, schur, copies, inner_ref, part_ref, mats):
-    schur_high, schur_low, basis_high, basis_low = mats
+def solve_inside(x_of, inv, basis, copies, inner_ref, part_ref):
     copies[0].wait()
     pieces = []
     for b in range(NIN):
@@ -120,9 +120,6 @@
     cat = tuple(jnp.concatenate([p[h] for p in pieces], axis=1) for h in range(2))
     copies[1].wait()
     part_ref[...] = dot_halves(cat, halves(basis[:, : NIN * BS]), NT)
-    basis_high[...], basis_low[...] = halves(basis[:, NIN * BS :])
-    copies[2].wait()
-    schur_high[...], schur_low[...] = halves(schur[...])
 
 
 def load_inside_body(
@@ -130,14 +127,16 @@
     inner_ref, part_ref, schur_high, schur_low, basis_high, basis_low, coarse_parts,
     inv, basis, schur, x, coarse, sems,
 ):
-    copies = start_all(
-        sems, (inv_ref, inv), (basis_ref.at[0], basis), (schur_ref.at[0], schur),
-        (x_ref.at[0, :, : NIN * BS], x), (coarse_ref.at[0], coarse),
-    )
+    first, *copies = start_all(
+        sems, (x_ref.at[0, :, : NIN * BS], x), (inv_ref, inv), (basis_ref.at[0], basis),
+        (schur_ref.at[0], schur), (coarse_ref.at[0], coarse),
+    )
+    first.wait()
+    solve_inside(lambda b: x[:, lanes(b)], inv, basis, copies, inner_ref, part_ref)
+    basis_high[...], basis_low[...] = halves(basis[:, NIN * BS :])
+    copies[2].wait()
+    schur_high[...], schur_low[...] = halves(schur[...])
     copies[3].wait()
-    mats = (schur_high, schur_low, basis_high, basis_low)
-    solve_inside(lambda b: x[:, lanes(b)], inv, basis, schur, copies, inner_ref, part_ref, mats)
-    copies[4].wait()
     value = coarse[...]
     for k in range(3):
         coarse_parts[k] = value.astype(BF16)
@@ -145,19 +144,17 @@
 
 
 def image_inside_body(
-    acc_ref, face_ref, cols_ref, tiles_ref, inv_ref, basis_ref, schur_ref,
-    y_ref, inner_ref, part_ref, schur_high, schur_low, basis_high, basis_low,
-    inv, basis, schur, tiles, spare, cols, sems,
-):
-    copies = start_all(
-        sems, (inv_ref, inv), (basis_ref.at[0], basis), (schur_ref.at[0], schur),
-        (cols_ref, cols), (tiles_ref.at[NIN:], tiles),
-    )
-    copies[3].wait()
-    copies[4].wait()
+    acc_ref, face_ref, cols_ref, tiles_ref, inv_ref, basis_ref, y_ref, inner_ref, part_ref,
+    inv, basis, tiles, spare, cols, sems,
+):
+    first, second, *copies = start_all(
+        sems, (cols_ref, cols), (tiles_ref.at[NIN:], tiles), (inv_ref, inv),
+        (basis_ref.at[0, :, : NIN * BS], basis),
+    )
+    first.wait()
+    second.wait()
     face_rows(acc_ref, face_ref, [wide_of(tiles, r) for r in range(NF)], cols, y_ref, spare)
-    mats = (schur_high, schur_low, basis_high, basis_low)
-    solve_inside(lambda b: y_ref[b], inv, basis, schur, copies, inner_ref, part_ref, mats)
+    solve_inside(lambda b: y_ref[b], inv, basis, copies, inner_ref, part_ref)
 
 
 def last_image_body(acc_ref, face_ref, cols_ref, tiles_ref, y_ref, tiles, spare, cols, sems):
@@ -167,8 +164,100 @@
     face_rows(acc_ref, face_ref, [wide_of(tiles, r) for r in range(NF)], cols, y_ref, spare)
 
 
-def face_block_body(tiles_ref, cols_ref, high_ref, low_ref, tiles, cols, sems):
-    copies = start_all(sems, (cols_ref, cols), (tiles_ref.at[NIN:], tiles))
+def scaled_faces(faces, weight_ref):
+    return halves(
+        jnp.concatenate([faces[r] * weight_ref[r : r + 1, :] for r in range(NF)], axis=1)
+    )
+
+
+def add_faces(faces, weight_ref, basis_high, basis_low, part_ref, contrib_ref):
+    scaled = scaled_faces(faces, weight_ref)
+    contrib_ref[...] = part_ref[...] + dot_halves(scaled, (basis_high[...], basis_low[...]), NT)
+
+
+def solve_faces(face_ref, weight_ref, schur_high, schur_low, outer_ref):
+    outer = dot_halves(scaled_faces(face_ref, weight_ref), (schur_high[...], schur_low[...]))
+    for r in range(NF):
+        outer_ref[r] = outer[:, lanes(r)]
+
+
+def onehot(equal):
+    return equal.astype(F32).astype(BF16)
+
+
+def maps_of(own, inc):
+    rows = lax.broadcasted_iota(jnp.int32, (BS, BS), 0).astype(F32)
+    return onehot(rows == own[NRHS : NRHS + 1, :]), onehot(rows == inc[NRHS : NRHS + 1, :])
+
+
+def rows_for(target, coarse_ref):
+    here = lax.axis_index("gz")
+    slots = lax.broadcasted_iota(jnp.int32, (SCAP * CW, BS), 0)
+    places = lax.broadcasted_iota(jnp.int32, (OCAP * CW, BS), 0)
+    goal = target.astype(jnp.int32)
+    into = onehot(slots == goal[1:2, :])
+    out_of = onehot(places == goal[0:1, :] - here * (OCAP * CW))
+    take = mm(into, out_of, NT).astype(BF16)
+    return mm(take, coarse_ref[0]) + mm(take, coarse_ref[1]) + mm(take, coarse_ref[2])
+
+
+def put_rows(ref, first, rows):
+    ref[first : first + SCAP * CW, :] = rows[:, :BS]
+    ref[first + SCAP * CW : first + 2 * SCAP * CW, :] = rows[:, BS:]
+
+
+def first_faces_body(
+    own0, own1, own2, own3, in0, in1, in2, in3, target_ref, weight_ref,
+    basis_high, basis_low, part_ref, coarse_ref, *rest, line,
+):
+    targets = [target_ref[...], in0[NRHS + 8 :, :], in1[NRHS + 8 :, :]] + [
+        ref[...] for ref in rest[: line - 3]
+    ]
+    face_ref, contrib_ref, all_ref, *sides = rest[line - 3 :]
+    faces = []
+    for r, (own, inc) in enumerate(zip((own0, own1, own2, own3), (in0, in1, in2, in3))):
+        mine, theirs = maps_of(own, inc)
+        link = weight_ref[NF + r : NF + r + 1, :]
+        came = select_lanes(inc[:NRHS, :], (mm(theirs, mine, NT) * link).astype(BF16))
+        faces.append(own[:NRHS, :] + came)
+        face_ref[r] = faces[-1]
+    add_faces(faces, weight_ref, basis_high, basis_low, part_ref, contrib_ref)
+    all_ref[...] = jnp.concatenate([t[0:1, :] for t in targets], axis=1)
+    for side, target in zip(sides, targets[1:]):
+        side[:NRHS, :] = contrib_ref[...]
+        put_rows(side, NRHS, rows_for(target, coarse_ref))
+
+
+def under_line_body(
+    own0, own1, own2, own3, in0, in1, in2, in3, target_ref, weight_ref, face_ref, schur_high, schur_low,
+    coarse_ref, all_ref, tiles_ref, cols_ref,
+    basis_ref, high_ref, low_ref, outer_ref, swap_ref, rows_ref, pick_ref, mine_ref, early_ref, inside_ref,
+    tiles, cols, sems, *, line,
+):
+    *copies, third, fourth = start_all(
+        sems, (cols_ref, cols), (tiles_ref.at[NIN:], tiles), (tiles_ref.at[:EARLY], early_ref),
+        (basis_ref.at[0, :, : NIN * BS], inside_ref),
+    )
+    solve_faces(face_ref, weight_ref, schur_high, schur_low, outer_ref)
+    for r, (own, inc) in enumerate(zip((own0, own1, own2, own3), (in0, in1, in2, in3))):
+        mine, theirs = maps_of(own, inc)
+        swap_ref[r] = (mm(mine, theirs, NT) * weight_ref[NF + r : NF + r + 1, :]).astype(BF16)
+    put_rows(rows_ref, 0, rows_for(target_ref[...], coarse_ref))
+    here = lax.axis_index("gz")
+    own = OCAP * CW
+    goal = target_ref[...].astype(jnp.int32)
+    slots = lax.broadcasted_iota(jnp.int32, (SCAP * CW, BS), 0)
+    places = lax.broadcasted_iota(jnp.int32, (BS, own), 1)
+    for e in range(line):
+        down = jnp.broadcast_to(all_ref[:, lanes(e)], (BS, BS)).T.astype(jnp.int32)
+        down = jnp.concatenate([down] * (own // BS), axis=1)
+        for m in range(line):
+            owner = jnp.bitwise_xor(here, m)
+            pick_ref[lanes(e), m * own : (m + 1) * own] = onehot(places + owner * own == down)
+    for m in range(line):
+        owner = jnp.bitwise_xor(here, m)
+        mine = (slots == goal[1:2, :]) & (goal[0:1, :] // own == owner)
+        mine_ref[m * SCAP * CW : (m + 1) * SCAP * CW, :] = onehot(mine)
     high_ref[...] = jnp.zeros_like(high_ref)
     low_ref[...] = jnp.zeros_like(low_ref)
     for copy in copies:
@@ -181,70 +270,18 @@
             def _(r=r, t=t, place=place):
                 high_ref[r, place], low_ref[r, place] = halves(tiles[r, t])
 
-
-def face_solve(faces, mats, weight_ref, part_ref, outer_ref, contrib_ref):
-    schur_high, schur_low, basis_high, basis_low = mats
-    scaled = halves(
-        jnp.concatenate([faces[r] * weight_ref[r : r + 1, :] for r in range(NF)], axis=1)
-    )
-    contrib_ref[:NRHS, :] = part_ref[...] + dot_halves(
-        scaled, (basis_high[...], basis_low[...]), NT
-    )
-    outer = dot_halves(scaled, (schur_high[...], schur_low[...]))
-    for r in range(NF):
-        outer_ref[r] = outer[:, lanes(r)]
-
-
-def first_faces_body(
-    own0, own1, own2, own3, in0, in1, in2, in3, target_ref, weight_ref,
-    schur_high, schur_low, basis_high, basis_low, part_ref, coarse_ref, *rest, line,
-):
-    targets = [target_ref[...], in0[NRHS + 8 :, :], in1[NRHS + 8 :, :]] + [
-        ref[...] for ref in rest[: line - 3]
-    ]
-    face_ref, outer_ref, contrib_ref, swap_ref, all_ref, rows_ref, *sides = rest[line - 3 :]
-    faces = []
-    rows = lax.broadcasted_iota(jnp.int32, (BS, BS), 0).astype(F32)
-    for r, (own, inc) in enumerate(zip((own0, own1, own2, own3), (in0, in1, in2, in3))):
-        mine = (rows == own[NRHS : NRHS + 1, :]).astype(F32).astype(BF16)
-        theirs = (rows == inc[NRHS : NRHS + 1, :]).astype(F32).astype(BF16)
-        link = weight_ref[NF + r : NF + r + 1, :]
-        swap_ref[r] = (mm(mine, theirs, NT) * link).astype(BF16)
-        came = select_lanes(inc[:NRHS, :], (mm(theirs, mine, NT) * link).astype(BF16))
-        faces.append(own[:NRHS, :] + came)
-        face_ref[r] = faces[-1]
-    mats = (schur_high, schur_low, basis_high, basis_low)
-    face_solve(faces, mats, weight_ref, part_ref, outer_ref, contrib_ref)
-    here = lax.axis_index("gz")
-    own = OCAP * CW
-    slots = lax.broadcasted_iota(jnp.int32, (SCAP * CW, BS), 0)
-    places = lax.broadcasted_iota(jnp.int32, (own, BS), 0)
-    all_ref[...] = jnp.concatenate([t[0:1, :] for t in targets], axis=1)
-    for m, target in enumerate(targets):
-        goal = target.astype(jnp.int32)
-        into = (slots == goal[1:2, :]).astype(F32).astype(BF16)
-        out_of = (places == goal[0:1, :] - here * own).astype(F32).astype(BF16)
-        take = mm(into, out_of, NT).astype(BF16)
-        rows = mm(take, coarse_ref[0]) + mm(take, coarse_ref[1]) + mm(take, coarse_ref[2])
-        if m == 0:
-            rows_ref[: SCAP * CW, :] = rows[:, :BS]
-            rows_ref[SCAP * CW :, :] = rows[:, BS:]
-        else:
-            sides[m - 1][:NRHS, :] = contrib_ref[...]
-            sides[m - 1][NRHS : NRHS + SCAP * CW, :] = rows[:, :BS]
-            sides[m - 1][NRHS + SCAP * CW :, :] = rows[:, BS:]
+    third.wait()
+    fourth.wait()
 
 
 def next_faces_body(
-    y_ref, in0, in1, in2, in3, weight_ref, schur_high, schur_low, basis_high, basis_low, part_ref,
-    face_ref, outer_ref, contrib_ref,
+    y_ref, in0, in1, in2, in3, weight_ref, basis_high, basis_low, part_ref, face_ref, contrib_ref,
 ):
     faces = []
     for r, inc in enumerate((in0, in1, in2, in3)):
         faces.append(y_ref[r] + inc[...])
         face_ref[r] = faces[-1]
-    mats = (schur_high, schur_low, basis_high, basis_low)
-    face_solve(faces, mats, weight_ref, part_ref, outer_ref, contrib_ref)
+    add_faces(faces, weight_ref, basis_high, basis_low, part_ref, contrib_ref)
 
 
 def finish(back, outer_ref, basis, weight_ref, swap_ref, back_ref, face_ref, outs):
@@ -268,27 +305,30 @@
     return (rows + owner * (OCAP * CW) == all_ref[...].astype(jnp.int32)).astype(F32).astype(BF16)
 
 
-def first_coarse_body(own_ref, rows_ref, all_ref, target_ref, *refs, line):
+def first_coarse_body(own_ref, rows_ref, pick_ref, mine_ref, *refs, line):
     sides = (rows_ref,) + refs[: line - 1]
-    outer_ref, basis_high, basis_low, weight_ref, swap_ref, _, back_ref, face_ref, *outs = refs[line - 1 :]
-    here = lax.axis_index("gz")
+    outer_ref, basis_high, basis_low, weight_ref, swap_ref, back_ref, face_ref, *outs = refs[line - 1 :]
     contribs = halves(jnp.concatenate([own_ref[...]] + [s[:NRHS, :] for s in sides[1:]], axis=1))
-    stack = jnp.concatenate(contribs, axis=0)
-    slots = lax.broadcasted_iota(jnp.int32, (SCAP * CW, BS), 0)
-    goal = target_ref[...].astype(jnp.int32)
-    back = jnp.zeros((NRHS, BS), F32)
-    for m in range(line):
-        owner = jnp.bitwise_xor(here, m)
-        both = mm(stack, pick_of(all_ref, owner), NT)
-        solved = dot_halves(halves(both[:NRHS] + both[NRHS:]), halves(owner_rows(sides[m], m)), NT)
-        mine = (slots == goal[1:2, :]) & (goal[0:1, :] // (OCAP * CW) == owner)
-        back = back + select_lanes(solved, mine.astype(F32).astype(BF16))
+    both = mm(jnp.concatenate(contribs, axis=0), pick_ref[...])
+    gathered = both[:NRHS] + both[NRHS:]
+    own = OCAP * CW
+    solved = [
+        dot_halves(halves(gathered[:, m * own : (m + 1) * own]), halves(owner_rows(side, m)), NT)
+        for m, side in enumerate(sides)
+    ]
+    back = select_lanes(jnp.concatenate(solved, axis=1), mine_ref[...])
     finish(back, outer_ref, (basis_high[...], basis_low[...]), weight_ref, swap_ref, back_ref, face_ref, outs)
 
 
-def table_body(rows_ref, all_ref, column_ref, *refs, line):
+def table_body(
+    tiles_ref, basis_ref, rows_ref, all_ref, column_ref, face_ref, weight_ref, schur_high, schur_low, *refs, line
+):
     sides = (rows_ref,) + refs[: line - 1]
-    high_ref, low_ref = refs[line - 1 :]
+    high_ref, low_ref, outer_ref, early_ref, inside_ref, sems = refs[line - 1 :]
+    copies = start_all(
+        sems, (tiles_ref.at[:EARLY], early_ref), (basis_ref.at[0, :, : NIN * BS], inside_ref)
+    )
+    solve_faces(face_ref, weight_ref, schur_high, schur_low, outer_ref)
     here = lax.axis_index("gz")
     slots = lax.broadcasted_iota(jnp.int32, (BS, BS), 1)
     table = jnp.zeros((2 * BS, all_ref.shape[1]), F32)
@@ -301,6 +341,8 @@
         table = table + mm(both, pick_of(all_ref, owner))
     high_ref[...] = table[:BS].astype(BF16)
     low_ref[...] = table[BS:].astype(BF16)
+    for copy in copies:
+        copy.wait()
 
 
 def next_coarse_body(*refs, line):
@@ -325,25 +367,30 @@
     return halves(jnp.concatenate([tiles[i, t] for t in range(TPR)], axis=1))
 
 
-def own_apply(inner_ref, back_ref, basis_ref, tiles_ref, cols_ref, z_ref, acc_ref, basis, tiles, cols, sems):
-    pairs = [(cols_ref, cols), (basis_ref.at[0, :, : NIN * BS], basis)]
-    first = 0
+def own_apply(
+    inner_ref, back_ref, early_ref, basis, tiles_ref, cols_ref, z_ref, acc_ref, tiles, cols, sems
+):
+    pairs = [(cols_ref, cols)]
+    first = EARLY
     for count in CHUNKS:
-        pairs.append((tiles_ref.at[first : first + count], tiles.at[first : first + count]))
+        pairs.append(
+            (tiles_ref.at[first : first + count], tiles.at[first - EARLY : first - EARLY + count])
+        )
         first += count
     copies = start_all(sems, *pairs)
     acc_ref[...] = jnp.zeros_like(acc_ref)
     back = halves(back_ref[...])
-    copies[0].wait()
-    copies[1].wait()
     corr = dot_halves(back, halves(basis[...]))
     for b in range(NIN):
         z_ref[b] = inner_ref[b] + corr[:, lanes(b)]
-    first = 0
+    copies[0].wait()
+    for i in range(EARLY):
+        add_row(z_ref[i], i, wide_of(early_ref, i), cols, acc_ref)
+    first = EARLY
     for k, count in enumerate(CHUNKS):
-        copies[2 + k].wait()
+        copies[1 + k].wait()
         for i in range(first, first + count):
-            add_row(z_ref[i], i, wide_of(tiles, i), cols, acc_ref)
+            add_row(z_ref[i], i, wide_of(tiles, i - EARLY), cols, acc_ref)
         first += count
 
 
@@ -356,11 +403,11 @@
 
 
 def second_apply_body(
-    inner_ref, back_ref, basis_ref, tiles_ref, cols_ref, load_hbm, zi, zf, yi, yf,
-    z_ref, acc_ref, sums_ref, load_ref, basis, tiles, load, cols, sems, more,
+    inner_ref, back_ref, early_ref, basis, tiles_ref, cols_ref, load_hbm, zi, zf, yi, yf,
+    z_ref, acc_ref, sums_ref, load_ref, tiles, load, cols, sems, more,
 ):
     (copy,) = start_all(more, (load_hbm.at[0], load))
-    own_apply(inner_ref, back_ref, basis_ref, tiles_ref, cols_ref, z_ref, acc_ref, basis, tiles, cols, sems)
+    own_apply(inner_ref, back_ref, early_ref, basis, tiles_ref, cols_ref, z_ref, acc_ref, tiles, cols, sems)
     copy.wait()
     sums = pair_sums(
         (
@@ -544,66 +591,70 @@
     )
     width = line * CB * CW
     half = 2 * SCAP * CW
-    r_face, outer, contrib, swap, targets, rows, *sides = call(
+    own_sides = sides
+    pre_outs = [f32(EARLY, TPR, BS, BS), f32(BS, NIN * BS)]
+    r_face, contrib, targets, *sides = call(
         lambda *refs: first_faces_body(*refs, line=line), "faces_load",
-        [face, face, small, bf16(NF, BS, BS), f32(1, width), f32(half, BS)]
-        + [f32(NRHS + half, BS)] * (line - 1),
-        [VMEM] * (13 + line),
-        *sides, *came, target, weight, *mats, part, coarse_parts, *far,
+        [face, small, f32(1, width)] + [f32(NRHS + half, BS)] * (line - 1), [VMEM] * (11 + line),
+        *own_sides, *came, target, weight, *mats[2:], part, coarse_parts, *far,
     )
     others = [trade(value, mask) for value, mask in zip(sides, range(1, line))]
-    blocks = call(
-        face_block_body, "face_block", [bf16(NF, NF, BS, BS)] * 2, [HBM] * 2, matrix_tiles, cols,
-        scratch=[face_tiles, cols_scratch], copies=2,
+    block_high, block_low, outer, swap, rows, picks, mine, *early = call(
+        lambda *refs: under_line_body(*refs, line=line), "under_line",
+        [bf16(NF, NF, BS, BS)] * 2 + [face, bf16(NF, BS, BS), f32(half, BS)]
+        + [bf16(width, line * own), bf16(line * SCAP * CW, BS)] + pre_outs,
+        [VMEM] * 15 + [HBM] * 3,
+        *own_sides, *came, target, weight, r_face, *mats[:2], coarse_parts, targets, matrix_tiles, cols, coarse_basis,
+        scratch=[face_tiles, cols_scratch], copies=4,
     )
     back, u_face, *sends = call(
         lambda *refs: first_coarse_body(*refs, line=line), "coarse_load",
-        [small, face] + [small] * NF, [VMEM] * (line + 9),
-        contrib, rows, targets, target, *others, outer, *mats[2:], weight, swap, blocks[0],
+        [small, face] + [small] * NF, [VMEM] * (line + 8),
+        contrib, rows, picks, mine, *others, outer, *mats[2:], weight, swap,
     )
 
     came = trade_faces(sends)
-    own_scratch = [(BS, NIN * BS), (NIN, TPR, BS, BS)]
+    own_scratch = [(NIN - EARLY, TPR, BS, BS)]
     z, acc = call(
-        first_apply_body, "own_first", [block, f32(*every)], [VMEM, VMEM] + [HBM] * 3,
-        inner, back, coarse_basis, matrix_tiles, cols,
-        scratch=own_scratch + [cols_scratch], copies=2 + len(CHUNKS),
+        first_apply_body, "own_first", [block, f32(*every)], [VMEM] * 4 + [HBM] * 2,
+        inner, back, *early, matrix_tiles, cols,
+        scratch=own_scratch + [cols_scratch], copies=1 + len(CHUNKS),
     )
     y_face, z_face, *sends = call(
         first_face_body, "face_first", [face, face] + [small] * NF, [VMEM] * 9,
-        acc, *came, u_face, *blocks, swap,
+        acc, *came, u_face, block_high, block_low, swap,
     )
     came = trade_faces(sends)
-    y, inner, part, *mats = call(
-        image_inside_body, "inside_image", [block] + mat_outs, [VMEM] * 2 + [HBM] * 5,
-        acc, z_face, cols, matrix_tiles, interior_inv, coarse_basis, schur_inv,
-        scratch=mat_scratch + [face_tiles, every, cols_scratch], copies=5,
-    )
-    high, low = call(
-        lambda *refs: table_body(*refs, line=line), "table", [bf16(BS, width), bf16(BS, width)],
-        [VMEM] * (line + 2), rows, targets, column, *others,
-    )
-    q_face, outer, contrib = call(
-        next_faces_body, "faces_image", [face, face, small], [VMEM] * 11,
-        y_face, *came, weight, *mats, part,
-    )
-    others = trade_line(contrib)
+    y, inner, part = call(
+        image_inside_body, "inside_image", [block, block, small], [VMEM] * 2 + [HBM] * 4,
+        acc, z_face, cols, matrix_tiles, interior_inv, coarse_basis,
+        scratch=[(NIN, BS, BS), (BS, NIN * BS), face_tiles, every, cols_scratch], copies=4,
+    )
+    q_face, contrib = call(
+        next_faces_body, "faces_image", [face, small], [VMEM] * 9,
+        y_face, *came, weight, *mats[2:], part,
+    )
+    sides = trade_line(contrib)
+    high, low, outer, *early = call(
+        lambda *refs: table_body(*refs, line=line), "table", [bf16(BS, width)] * 2 + [face] + pre_outs,
+        [HBM] * 2 + [VMEM] * (line + 6), matrix_tiles, coarse_basis, rows, targets, column, q_face, weight, *mats[:2], *others, copies=2,
+    )
     back, u_face, *sends = call(
         lambda *refs: next_coarse_body(*refs, line=line), "coarse_image",
         [small, face] + [small] * NF, [VMEM] * (line + 7),
-        contrib, *others, high, low, outer, *mats[2:], weight, swap,
+        contrib, *sides, high, low, outer, *mats[2:], weight, swap,
     )
     came = trade_faces(sends)
     w, acc, sums, load = call(
         second_apply_body, "own_second", [block, f32(*every), f32(5, NRHS, BS), f32(*every)],
-        [VMEM, VMEM] + [HBM] * 4 + [VMEM] * 4,
-        inner, back, coarse_basis, matrix_tiles, cols, load_vector, z, z_face, y, y_face,
-        scratch=own_scratch + [(NRHS, NL), cols_scratch, pltpu.SemaphoreType.DMA((2 + len(CHUNKS),))],
+        [VMEM] * 4 + [HBM] * 3 + [VMEM] * 4,
+        inner, back, *early, matrix_tiles, cols, load_vector, z, z_face, y, y_face,
+        scratch=own_scratch + [(NRHS, NL), cols_scratch, pltpu.SemaphoreType.DMA((1 + len(CHUNKS),))],
         copies=1,
     )
     v_face, w_face, dots, *sends = call(
         second_face_body, "face_second", [face, face, f32(devices, 2, BS)] + [small] * NF, [VMEM] * 12,
-        acc, *came, u_face, *blocks, swap, sums, load, y_face,
+        acc, *came, u_face, block_high, block_low, swap, sums, load, y_face,
     )
     spread = lax.all_to_all(dots, AXES, 0, 0)
     came = trade_faces(sends)

time: 71.8 us -> 66 us (0.919)
  Pallas kernels: 26 us -> 23.4 us
  waiting for transfers between devices: 8.1 us -> 5.7 us
  starting transfers between devices: 36.5 us -> 35.7 us
    pallas_call x15, Pallas kernels: 26 us -> 23.4 us  [call(): pl.pallas_call(body, name=name, out_shape=outs, in_specs=specs, out_specs...]
    ppermute x27, waiting for transfers between devices: 8.1 us -> 5.7 us  [trade(): return lax.ppermute(value, AXES, [(i, i ^ mask) for i in range(devices)])]
  transfers between devices with their start and end apart: 28 -> 28, of which waited for: 6 -> 6; matrix products, arithmetic and copies ran while one was open for 0% -> 0% of each run, Pallas kernels for 25% -> 26%
where the time goes in v5:
time: 66 us; the launch traced here: 65.7 us
  starting transfers between devices  35.7 us (54%)
  Pallas kernels  23.4 us (35%)
  waiting for transfers between devices  5.7 us (9%)
  between operations  0.86 us (1%)
    ppermute x27, starting transfers between devices, trade(): return lax.ppermute(value, AXES, [(i, i ^ mask) for i in range(devices)])  32 us
    pallas_call x15, Pallas kernels, call(): pl.pallas_call(body, name=name, out_shape=outs, in_specs=specs, out_specs...  23.4 us
    ppermute x27, waiting for transfers between devices, trade(): return lax.ppermute(value, AXES, [(i, i ^ mask) for i in range(devices)])  5.7 us
    all_to_all x1, starting transfers between devices, on_device(): spread = lax.all_to_all(dots, AXES, 0, 0)  3.71 us
  transfers between devices with their start and end apart: 28, of which 6 were waited for; matrix products, arithmetic and copies ran while one was open for 0% of the time, Pallas kernels for 26%

profile of v5, /device:TPU:0, one launch (start us, length us, event | category | flops | bytes accessed | tf_op | source)
XLA Modules:
  0.0 65.7 jit_solution(15424990393270412851)
XLA Ops:
  0.6 0.9 %prepare.1 = (f32[8,128]{1,0:T(8,128)S(1)}, s32[2,128,128]{2,1,0:T(8,128)S(1)}, f32[8,128]{1,0:T(8,128)S(1)}, f32[48,128]{1,0:T(8,128)S(1)}, f32[48,128]{1,0:T(8...) custom-call(f32[1,32,2048]{2,1,0:T(8,128)} %load_hbm.1, s32[1,4,128]{2,1,0:T(4,128)} %map_ref.1, s32[1,4]{1,0:T(1,128)} %id_ref.1, ...), custom_call_target="tpu_custom_call" | custom-call | tf_op jit(solution)/shard_map/prepare/pallas_call | solution.py:534
  1.5 3.1 %collective-permute-start = (f32[48,128]{1,0:T(8,128)S(1)}, f32[48,128]{1,0:T(8,128)S(1)}, u32[]{:S(2)}, u32[]{:S(2)}) collective-permute-start(f32[48,128]{1,0:T(8,128)S(1)} %get-tuple-element.73.refs_0_), channel_id=1, source_target_pairs={{0,1},{1,0},{2,3},{3,2},{4,5},{5,4},{6,7},{7,6},{8,9},{9,8},{10,11... | collective-permute-start | bytes 73736 | tf_op jit(solution)/shard_map/ppermute | solution.py:557
  4.6 2.6 %collective-permute-start.1 = (f32[48,128]{1,0:T(8,128)S(1)}, f32[48,128]{1,0:T(8,128)S(1)}, u32[]{:S(2)}, u32[]{:S(2)}) collective-permute-start(f32[48,128]{1,0:T(8,128)S(1)} %get-tuple-element.74.refs_1_), channel_id=1, source_target_pairs={{0,2},{1,3},{2,0},{3,1},{4,6},{5,7},{6,4},{7,5},{8,10},{9,11},{10,... | collective-permute-start | bytes 73736 | tf_op jit(solution)/shard_map/ppermute | solution.py:557
  7.2 1.5 %collective-permute-start.3 = (f32[48,128]{1,0:T(8,128)S(1)}, f32[48,128]{1,0:T(8,128)S(1)}, u32[]{:S(2)}, u32[]{:S(2)}) collective-permute-start(f32[48,128]{1,0:T(8,128)S(1)} %get-tuple-element.76.refs_3_), channel_id=1, source_target_pairs={{0,8},{1,9},{2,10},{3,11},{4,12},{5,13},{6,14},{7,15},{8,0},{9,1},... | collective-permute-start | bytes 73736 | tf_op jit(solution)/shard_map/ppermute | solution.py:557
  8.7 0.2 collective-permute-start.4
  8.9 2.2 %inside_load.1 = (f32[12,32,128]{2,1,0:T(8,128)S(1)}, f32[32,128]{1,0:T(8,128)S(1)}, bf16[512,512]{1,0:T(8,128)(2,1)S(1)}, bf16[512,512]{1,0:T(8,128)(2,1)S(1)},...) custom-call(f32[1,32,2048]{2,1,0:T(8,128)} %load_hbm.1, ...), custom_call_target="tpu_custom_call" | custom-call | tf_op jit(solution)/shard_map/inside_load/pallas_call | solution.py:534
  11.2 2.9 %collective-permute-done.4.refs_14_ = f32[8,128]{1,0:T(8,128)S(1)} collective-permute-done((f32[8,128]{1,0:T(8,128)S(1)}, f32[8,128]{1,0:T(8,128)S(1)}, u32[]{:S(2)}, u32[]{:S(2)}) %collective-permute-start.4) | collective-permute-done | bytes 4128 | tf_op jit(solution)/shard_map/ppermute | solution.py:557
  14.1 0.0 collective-permute-done.refs_4_
  14.1 0.0 collective-permute-done.1.refs_5_
  14.1 0.0 collective-permute-done.2.refs_6_
  14.1 1.2 %faces_load.1 = (f32[4,32,128]{2,1,0:T(8,128)S(1)}, f32[32,128]{1,0:T(8,128)S(1)}, f32[1,512]{1,0:T(1,128)S(1)}, f32[160,128]{1,0:T(8,128)S(1)}, f32[160,128]{1,0:T(8,128)S(1)}, /*index=5*/f32[160,128]{1,0:T(8,128)S(1)}) custom-call(f32[48,128]{1,0:T(8,128)S(1)} %get-tuple-element.73.refs_0_, f32[48,128]{1,0:T(8,128)S(1)} %get-tuple-element.74.refs_1_, ...), custom_call_target="tpu_custom_call" | custom-call | tf_op jit(solution)/shard_map/faces_load/pallas_call | solution.py:534
  15.4 0.1 collective-permute-start.5
  15.4 1.3 %collective-permute-start.6 = (f32[160,128]{1,0:T(8,128)S(1)}, f32[160,128]{1,0:T(8,128)S(1)}, u32[]{:S(2)}, u32[]{:S(2)}) collective-permute-start(f32[160,128]{1,0:T(8,128)S(1)} %get-tuple-element.92), channel_id=1, source_target_pairs={{0,2},{1,3},{2,0},{3,1},{4,6},{5,7},{6,4},{7,5},{8,10},{9,11},{10,... | collective-permute-start | bytes 245768 | tf_op jit(solution)/shard_map/ppermute | solution.py:557
  16.7 3.1 %collective-permute-start.7 = (f32[160,128]{1,0:T(8,128)S(1)}, f32[160,128]{1,0:T(8,128)S(1)}, u32[]{:S(2)}, u32[]{:S(2)}) collective-permute-start(f32[160,128]{1,0:T(8,128)S(1)} %get-tuple-element.93), channel_id=1, source_target_pairs={{0,3},{1,2},{2,1},{3,0},{4,7},{5,6},{6,5},{7,4},{8,11},{9,10},{10,... | collective-permute-start | bytes 245768 | tf_op jit(solution)/shard_map/ppermute | solution.py:557
  19.8 2.8 %under_line.1 = (bf16[4,4,128,128]{3,2,1,0:T(8,128)(2,1)S(1)}, bf16[4,4,128,128]{3,2,1,0:T(8,128)(2,1)S(1)}, f32[4,32,128]{2,1,0:T(8,128)S(1)}, bf16[4,128,128]{...) custom-call(f32[48,128]{1,0:T(8,128)S(1)} %get-tuple-element.73.refs, ...), custom_call_target="tpu_custom_call" | custom-call | tf_op jit(solution)/shard_map/under_line/pallas_call | solution.py:534
  22.6 0.0 collective-permute-done.5.refs_4_.refs_9_
  22.6 1.6 %collective-permute-done.6.refs_5_.refs_10_ = f32[160,128]{1,0:T(8,128)S(1)} collective-permute-done((f32[160,128]{1,0:T(8,128)S(1)}, f32[160,128]{1,0:T(8,128)S(1)}, u32[]{:S(2)}, u32[]{:S(2)}) %collective-permute-start.6) | collective-permute-done | bytes 81952 | tf_op jit(solution)/shard_map/ppermute | solution.py:557
  24.2 1.0 %coarse_load.1 = (f32[32,128]{1,0:T(8,128)S(1)}, f32[4,32,128]{2,1,0:T(8,128)S(1)}, f32[32,128]{1,0:T(8,128)S(1)}, f32[32,128]{1,0:T(8,128)S(1)}, f32[32,128]{1,0:T(8,128)S(1)}, /*index=5*/f32[32,128]{1,0:T(8,128)S(1)}) custom-call(f32[32,128]{1,0:T(8,128)S(1)} %get-tuple-element.83.refs_0_, f32[128,128]{1,0:T(8,128)S(1)} %get-tuple-element.88.refs_1_.refs_2_, ...), custom_call_target="tpu_custom_call" | custom-call | tf_op jit(solution)/shard_map/coarse_load/pallas_call | solution.py:534
  25.2 1.5 %collective-permute-start.8 = (f32[32,128]{1,0:T(8,128)S(1)}, f32[32,128]{1,0:T(8,128)S(1)}, u32[]{:S(2)}, u32[]{:S(2)}) collective-permute-start(f32[32,128]{1,0:T(8,128)S(1)} %get-tuple-element.100), channel_id=1, source_target_pairs={{0,1},{1,0},{2,3},{3,2},{4,5},{5,4},{6,7},{7,6},{8,9},{9,8},{10,11... | collective-permute-start | bytes 49160 | tf_op jit(solution)/shard_map/ppermute | solution.py:557
  26.6 1.1 %collective-permute-start.9 = (f32[32,128]{1,0:T(8,128)S(1)}, f32[32,128]{1,0:T(8,128)S(1)}, u32[]{:S(2)}, u32[]{:S(2)}) collective-permute-start(f32[32,128]{1,0:T(8,128)S(1)} %get-tuple-element.101), channel_id=1, source_target_pairs={{0,2},{1,3},{2,0},{3,1},{4,6},{5,7},{6,4},{7,5},{8,10},{9,11},{10,... | collective-permute-start | bytes 49160 | tf_op jit(solution)/shard_map/ppermute | solution.py:557
  27.7 0.5 collective-permute-start.11
  28.2 2.7 %own_first.1 = (f32[12,32,128]{2,1,0:T(8,128)S(1)}, f32[16,32,128]{2,1,0:T(8,128)S(1)}) custom-call(f32[12,32,128]{2,1,0:T(8,128)S(1)} %get-tuple-element.72.refs_0_, f32[32,128]{1,0:T(8,128)S(1)} %get-tuple-element.96.refs_1_, f32[4,7,128,128]{3,2,1,0:T(8,128)S(1)} %get-tuple-element.97.refs_2_, f32[128,1536]{1,0:T(8,128)S(1)} %get-tuple-element.98.refs_3_, ...), custom_call_target="tpu_custom_call" | custom-call | tf_op jit(solution)/shard_map/own_first/pallas_call | solution.py:534
  30.9 0.5 collective-permute-done.9.in1
  31.5 0.4 face_first.1
  31.9 1.3 %collective-permute-start.12 = (f32[32,128]{1,0:T(8,128)S(1)}, f32[32,128]{1,0:T(8,128)S(1)}, u32[]{:S(2)}, u32[]{:S(2)}) collective-permute-start(f32[32,128]{1,0:T(8,128)S(1)} %get-tuple-element.110), channel_id=1, source_target_pairs={{0,1},{1,0},{2,3},{3,2},{4,5},{5,4},{6,7},{7,6},{8,9},{9,8},{10,11... | collective-permute-start | bytes 49160 | tf_op jit(solution)/shard_map/ppermute | solution.py:557
  33.1 1.2 %collective-permute-start.13 = (f32[32,128]{1,0:T(8,128)S(1)}, f32[32,128]{1,0:T(8,128)S(1)}, u32[]{:S(2)}, u32[]{:S(2)}) collective-permute-start(f32[32,128]{1,0:T(8,128)S(1)} %get-tuple-element.111), channel_id=1, source_target_pairs={{0,2},{1,3},{2,0},{3,1},{4,6},{5,7},{6,4},{7,5},{8,10},{9,11},{10,... | collective-permute-start | bytes 49160 | tf_op jit(solution)/shard_map/ppermute | solution.py:557
  34.3 1.0 %collective-permute-start.15 = (f32[32,128]{1,0:T(8,128)S(1)}, f32[32,128]{1,0:T(8,128)S(1)}, u32[]{:S(2)}, u32[]{:S(2)}) collective-permute-start(f32[32,128]{1,0:T(8,128)S(1)} %get-tuple-element.113), channel_id=1, source_target_pairs={{0,8},{1,9},{2,10},{3,11},{4,12},{5,13},{6,14},{7,15},{8,0},{9,1},... | collective-permute-start | bytes 49160 | tf_op jit(solution)/shard_map/ppermute | solution.py:557
  35.3 2.7 %inside_image.1 = (f32[12,32,128]{2,1,0:T(8,128)S(1)}, f32[12,32,128]{2,1,0:T(8,128)S(1)}, f32[32,128]{1,0:T(8,128)S(1)}) custom-call(f32[16,32,128]{2,1,0:T(8,128)S(1)} %get-tuple-element.99.acc_ref, f32[4,32,128]{2,1,0:T(8,128)S(1)} %get-tuple-element.107.face_ref.zf, s32[7,16]{1,0:T(8,128)} %bitcast.3, f32[16,7,128,128]{3,2,1,0:T(8,128)} %tiles_ref.5, ...), custom_call_target="tpu_custom_call" | custom-call | tf_op jit(solution)/shard_map/inside_image/pallas_call | solution.py:534
  38.1 0.2 faces_image.1
  38.3 2.0 %collective-permute-start.18 = (f32[32,128]{1,0:T(8,128)S(1)}, f32[32,128]{1,0:T(8,128)S(1)}, u32[]{:S(2)}, u32[]{:S(2)}) collective-permute-start(f32[32,128]{1,0:T(8,128)S(1)} %get-tuple-element.115.refs_0_), channel_id=1, source_target_pairs={{0,3},{1,2},{2,1},{3,0},{4,7},{5,6},{6,5},{7,4},{8,11},{9,10},{10,... | collective-permute-start | bytes 49160 | tf_op jit(solution)/shard_map/ppermute | solution.py:557
  40.3 1.0 %collective-permute-start.17 = (f32[32,128]{1,0:T(8,128)S(1)}, f32[32,128]{1,0:T(8,128)S(1)}, u32[]{:S(2)}, u32[]{:S(2)}) collective-permute-start(f32[32,128]{1,0:T(8,128)S(1)} %get-tuple-element.115.refs_0_), channel_id=1, source_target_pairs={{0,2},{1,3},{2,0},{3,1},{4,6},{5,7},{6,4},{7,5},{8,10},{9,11},{10,... | collective-permute-start | bytes 49160 | tf_op jit(solution)/shard_map/ppermute | solution.py:557
  41.3 1.5 %collective-permute-start.16 = (f32[32,128]{1,0:T(8,128)S(1)}, f32[32,128]{1,0:T(8,128)S(1)}, u32[]{:S(2)}, u32[]{:S(2)}) collective-permute-start(f32[32,128]{1,0:T(8,128)S(1)} %get-tuple-element.115.refs_0_), channel_id=1, source_target_pairs={{0,1},{1,0},{2,3},{3,2},{4,5},{5,4},{6,7},{7,6},{8,9},{9,8},{10,11... | collective-permute-start | bytes 49160 | tf_op jit(solution)/shard_map/ppermute | solution.py:557
  42.7 2.0 %table.1 = (bf16[128,512]{1,0:T(8,128)(2,1)S(1)}, bf16[128,512]{1,0:T(8,128)(2,1)S(1)}, f32[4,32,128]{2,1,0:T(8,128)S(1)}, f32[4,7,128,128]{3,2,1,0:T(8,128)S(1)}, f32[128,1536]{1,0:T(8,128)S(1)}) custom-call(f32[16,7,128,128]{3,2,1,0:T(8,128)} %tiles_ref.5, f32[1,128,2048]{2,1,0:T(8,128)} %refs_1_.1, f32[128,128]{1,0:T(8,128)S(1)} %get-tuple-element.88.refs_1_.refs_2_, ...), custom_call_target="tpu_custom_call" | custom-call | tf_op jit(solution)/shard_map/table/pallas_call | solution.py:534
  44.7 0.2 collective-permute-done.17.refs_2_
  44.9 0.2 collective-permute-done.16.refs_1_
  45.1 0.6 coarse_image.1
  45.7 1.4 %collective-permute-start.19 = (f32[32,128]{1,0:T(8,128)S(1)}, f32[32,128]{1,0:T(8,128)S(1)}, u32[]{:S(2)}, u32[]{:S(2)}) collective-permute-start(f32[32,128]{1,0:T(8,128)S(1)} %get-tuple-element.127), channel_id=1, source_target_pairs={{0,1},{1,0},{2,3},{3,2},{4,5},{5,4},{6,7},{7,6},{8,9},{9,8},{10,11... | collective-permute-start | bytes 49160 | tf_op jit(solution)/shard_map/ppermute | solution.py:557
  47.1 1.1 %collective-permute-start.20 = (f32[32,128]{1,0:T(8,128)S(1)}, f32[32,128]{1,0:T(8,128)S(1)}, u32[]{:S(2)}, u32[]{:S(2)}) collective-permute-start(f32[32,128]{1,0:T(8,128)S(1)} %get-tuple-element.128), channel_id=1, source_target_pairs={{0,2},{1,3},{2,0},{3,1},{4,6},{5,7},{6,4},{7,5},{8,10},{9,11},{10,... | collective-permute-start | bytes 49160 | tf_op jit(solution)/shard_map/ppermute | solution.py:557
  48.2 1.0 %collective-permute-start.22 = (f32[32,128]{1,0:T(8,128)S(1)}, f32[32,128]{1,0:T(8,128)S(1)}, u32[]{:S(2)}, u32[]{:S(2)}) collective-permute-start(f32[32,128]{1,0:T(8,128)S(1)} %get-tuple-element.130), channel_id=1, source_target_pairs={{0,8},{1,9},{2,10},{3,11},{4,12},{5,13},{6,14},{7,15},{8,0},{9,1},... | collective-permute-start | bytes 49160 | tf_op jit(solution)/shard_map/ppermute | solution.py:557
  49.2 2.8 %own_second.1 = (f32[12,32,128]{2,1,0:T(8,128)S(1)}, f32[16,32,128]{2,1,0:T(8,128)S(1)}, f32[5,32,128]{2,1,0:T(8,128)S(1)}, f32[16,32,128]{2,1,0:T(8,128)S(1)}) custom-call(f32[12,32,128]{2,1,0:T(8,128)S(1)} %get-tuple-element.108.inner_ref, f32[32,128]{1,0:T(8,128)S(1)} %get-tuple-element.121.back_ref, f32[4,7,128,128]{3,2,1,0:T(8,128)S(1)} %get-tuple-element.122.early_ref, ...), custom_call_target="tpu_custom_call" | custom-call | tf_op jit(solution)/shard_map/own_second/pallas_call | solution.py:534
  52.0 1.0 %face_second.1 = (f32[4,32,128]{2,1,0:T(8,128)S(1)}, f32[4,32,128]{2,1,0:T(8,128)S(1)}, f32[32,2,128]{2,1,0:T(2,128)}, f32[32,128]{1,0:T(8,128)S(1)}, f32[32,128...) custom-call(f32[16,32,128]{2,1,0:T(8,128)S(1)} %get-tuple-element.126.acc_ref, ...), custom_call_target="tpu_custom_call" | custom-call | tf_op jit(solution)/shard_map/face_second/pallas_call | solution.py:534
  53.0 3.7 %all-to-all-start = ((f32[32,2,128]{2,1,0:T(2,128)}), f32[32,2,128]{2,1,0:T(2,128)S(1)}, u32[]{:S(2)}, u32[]{:S(2)}) async-start(f32[32,2,128]{2,1,0:T(2,128)} %get-tuple-element.134), calls=%async_computation | async-start | bytes 65536 | tf_op jit(solution)/shard_map/all_to_all | solution.py:659
  56.8 1.8 %collective-permute-start.23 = (f32[32,128]{1,0:T(8,128)S(1)}, f32[32,128]{1,0:T(8,128)S(1)}, u32[]{:S(2)}, u32[]{:S(2)}) collective-permute-start(f32[32,128]{1,0:T(8,128)S(1)} %get-tuple-element.135), channel_id=1, source_target_pairs={{0,1},{1,0},{2,3},{3,2},{4,5},{5,4},{6,7},{7,6},{8,9},{9,8},{10,11... | collective-permute-start | bytes 49160 | tf_op jit(solution)/shard_map/ppermute | solution.py:557
  58.6 2.4 %collective-permute-start.24 = (f32[32,128]{1,0:T(8,128)S(1)}, f32[32,128]{1,0:T(8,128)S(1)}, u32[]{:S(2)}, u32[]{:S(2)}) collective-permute-start(f32[32,128]{1,0:T(8,128)S(1)} %get-tuple-element.136), channel_id=1, source_target_pairs={{0,2},{1,3},{2,0},{3,1},{4,6},{5,7},{6,4},{7,5},{8,10},{9,11},{10,... | collective-permute-start | bytes 49160 | tf_op jit(solution)/shard_map/ppermute | solution.py:557
  61.0 1.5 %collective-permute-start.26 = (f32[32,128]{1,0:T(8,128)S(1)}, f32[32,128]{1,0:T(8,128)S(1)}, u32[]{:S(2)}, u32[]{:S(2)}) collective-permute-start(f32[32,128]{1,0:T(8,128)S(1)} %get-tuple-element.138), channel_id=1, source_target_pairs={{0,8},{1,9},{2,10},{3,11},{4,12},{5,13},{6,14},{7,15},{8,0},{9,1},... | collective-permute-start | bytes 49160 | tf_op jit(solution)/shard_map/ppermute | solution.py:557
  62.5 2.0 %inside_last.1.vi = f32[12,32,128]{2,1,0:T(8,128)S(1)} custom-call(f32[16,32,128]{2,1,0:T(8,128)S(1)} %get-tuple-element.126.acc_ref, f32[4,32,128]{2,1,0:T(8,128)S(1)} %get-tuple-element.140.face_ref.wf, s32[7,16]{1,0:T(8,128)} %bitcast.5, f32[16,7,128,128]{3,2,1,0:T(8,128)} %tiles_ref.5), custom_call_target="tpu_custom_call" | custom-call | tf_op jit(solution)/shard_map/inside_last/pallas_call | solution.py:534
  64.5 0.2 collective-permute-done.26.in3
  64.8 1.0 %combine.1 = (f32[1,32,2048]{2,1,0:T(8,128)}, f32[1,32,2048]{2,1,0:T(8,128)}) custom-call(f32[32,2,128]{2,1,0:T(2,128)S(1)} %all-to-all-done.dots_ref, f32[32,128]{1,0:T(8,128)S(1)} %collective-permute-done.23.in0, f32[32,128]{1,0:T(8,128)S(1)} %collective-permute-done.24.in1, f32[32,128]{1,0:T(8,128)S(1)} %collective-permute-done.25.in2, ...), custom_call_target="tpu_custom_call" | custom-call | tf_op jit(solution)/shard_map/combine/pallas_call | solution.py:534
  (23 shorter events, 0.1 us)
Async XLA Ops:
  1.5 12.6 %collective-permute-start = (f32[48,128]{1,0:T(8,128)S(1)}, f32[48,128]{1,0:T(8,128)S(1)}, u32[]{:S(2)}, u32[]{:S(2)}) collective-permute-start(f32[48,128]{1,0:T(8,128)S(1)} %get-tuple-element.73.refs_0_), channel_id=1, source_target_pairs={{0,1},{1,0},{2,3},{3,2},{4,5},{5,4},{6,7},{7,6},{8,9},{9,8},{10,11... | collective-permute-start | bytes 73736 | tf_op jit(solution)/shard_map/ppermute | solution.py:557
  4.6 9.5 %collective-permute-start.1 = (f32[48,128]{1,0:T(8,128)S(1)}, f32[48,128]{1,0:T(8,128)S(1)}, u32[]{:S(2)}, u32[]{:S(2)}) collective-permute-start(f32[48,128]{1,0:T(8,128)S(1)} %get-tuple-element.74.refs_1_), channel_id=1, source_target_pairs={{0,2},{1,3},{2,0},{3,1},{4,6},{5,7},{6,4},{7,5},{8,10},{9,11},{10,... | collective-permute-start | bytes 73736 | tf_op jit(solution)/shard_map/ppermute | solution.py:557
  7.2 6.9 %collective-permute-start.2 = (f32[48,128]{1,0:T(8,128)S(1)}, f32[48,128]{1,0:T(8,128)S(1)}, u32[]{:S(2)}, u32[]{:S(2)}) collective-permute-start(f32[48,128]{1,0:T(8,128)S(1)} %get-tuple-element.75.refs_2_), channel_id=1, source_target_pairs={{0,4},{1,5},{2,6},{3,7},{4,0},{5,1},{6,2},{7,3},{8,12},{9,13},{10,... | collective-permute-start | bytes 73736 | tf_op jit(solution)/shard_map/ppermute | solution.py:557
  7.2 6.9 %collective-permute-start.3 = (f32[48,128]{1,0:T(8,128)S(1)}, f32[48,128]{1,0:T(8,128)S(1)}, u32[]{:S(2)}, u32[]{:S(2)}) collective-permute-start(f32[48,128]{1,0:T(8,128)S(1)} %get-tuple-element.76.refs_3_), channel_id=1, source_target_pairs={{0,8},{1,9},{2,10},{3,11},{4,12},{5,13},{6,14},{7,15},{8,0},{9,1},... | collective-permute-start | bytes 73736 | tf_op jit(solution)/shard_map/ppermute | solution.py:557
  8.7 5.4 %collective-permute-start.4 = (f32[8,128]{1,0:T(8,128)S(1)}, f32[8,128]{1,0:T(8,128)S(1)}, u32[]{:S(2)}, u32[]{:S(2)}) collective-permute-start(f32[8,128]{1,0:T(8,128)S(1)} %get-tuple-element.77.refs_8_), channel_id=1, source_target_pairs={{0,3},{1,2},{2,1},{3,0},{4,7},{5,6},{6,5},{7,4},{8,11},{9,10},{10,... | collective-permute-start | bytes 12296 | tf_op jit(solution)/shard_map/ppermute | solution.py:557
  15.4 7.2 %collective-permute-start.5 = (f32[160,128]{1,0:T(8,128)S(1)}, f32[160,128]{1,0:T(8,128)S(1)}, u32[]{:S(2)}, u32[]{:S(2)}) collective-permute-start(f32[160,128]{1,0:T(8,128)S(1)} %get-tuple-element.91), channel_id=1, source_target_pairs={{0,1},{1,0},{2,3},{3,2},{4,5},{5,4},{6,7},{7,6},{8,9},{9,8},{10,11... | collective-permute-start | bytes 245768 | tf_op jit(solution)/shard_map/ppermute | solution.py:557
  15.4 8.8 %collective-permute-start.6 = (f32[160,128]{1,0:T(8,128)S(1)}, f32[160,128]{1,0:T(8,128)S(1)}, u32[]{:S(2)}, u32[]{:S(2)}) collective-permute-start(f32[160,128]{1,0:T(8,128)S(1)} %get-tuple-element.92), channel_id=1, source_target_pairs={{0,2},{1,3},{2,0},{3,1},{4,6},{5,7},{6,4},{7,5},{8,10},{9,11},{10,... | collective-permute-start | bytes 245768 | tf_op jit(solution)/shard_map/ppermute | solution.py:557
  16.7 7.5 %collective-permute-start.7 = (f32[160,128]{1,0:T(8,128)S(1)}, f32[160,128]{1,0:T(8,128)S(1)}, u32[]{:S(2)}, u32[]{:S(2)}) collective-permute-start(f32[160,128]{1,0:T(8,128)S(1)} %get-tuple-element.93), channel_id=1, source_target_pairs={{0,3},{1,2},{2,1},{3,0},{4,7},{5,6},{6,5},{7,4},{8,11},{9,10},{10,... | collective-permute-start | bytes 245768 | tf_op jit(solution)/shard_map/ppermute | solution.py:557
  25.2 5.7 %collective-permute-start.8 = (f32[32,128]{1,0:T(8,128)S(1)}, f32[32,128]{1,0:T(8,128)S(1)}, u32[]{:S(2)}, u32[]{:S(2)}) collective-permute-start(f32[32,128]{1,0:T(8,128)S(1)} %get-tuple-element.100), channel_id=1, source_target_pairs={{0,1},{1,0},{2,3},{3,2},{4,5},{5,4},{6,7},{7,6},{8,9},{9,8},{10,11... | collective-permute-start | bytes 49160 | tf_op jit(solution)/shard_map/ppermute | solution.py:557
  26.6 4.8 %collective-permute-start.9 = (f32[32,128]{1,0:T(8,128)S(1)}, f32[32,128]{1,0:T(8,128)S(1)}, u32[]{:S(2)}, u32[]{:S(2)}) collective-permute-start(f32[32,128]{1,0:T(8,128)S(1)} %get-tuple-element.101), channel_id=1, source_target_pairs={{0,2},{1,3},{2,0},{3,1},{4,6},{5,7},{6,4},{7,5},{8,10},{9,11},{10,... | collective-permute-start | bytes 49160 | tf_op jit(solution)/shard_map/ppermute | solution.py:557
  27.7 3.8 %collective-permute-start.10 = (f32[32,128]{1,0:T(8,128)S(1)}, f32[32,128]{1,0:T(8,128)S(1)}, u32[]{:S(2)}, u32[]{:S(2)}) collective-permute-start(f32[32,128]{1,0:T(8,128)S(1)} %get-tuple-element.102), channel_id=1, source_target_pairs={{0,4},{1,5},{2,6},{3,7},{4,0},{5,1},{6,2},{7,3},{8,12},{9,13},{10,... | collective-permute-start | bytes 49160 | tf_op jit(solution)/shard_map/ppermute | solution.py:557
  27.7 3.8 %collective-permute-start.11 = (f32[32,128]{1,0:T(8,128)S(1)}, f32[32,128]{1,0:T(8,128)S(1)}, u32[]{:S(2)}, u32[]{:S(2)}) collective-permute-start(f32[32,128]{1,0:T(8,128)S(1)} %get-tuple-element.103), channel_id=1, source_target_pairs={{0,8},{1,9},{2,10},{3,11},{4,12},{5,13},{6,14},{7,15},{8,0},{9,1},... | collective-permute-start | bytes 49160 | tf_op jit(solution)/shard_map/ppermute | solution.py:557
  31.9 6.2 %collective-permute-start.12 = (f32[32,128]{1,0:T(8,128)S(1)}, f32[32,128]{1,0:T(8,128)S(1)}, u32[]{:S(2)}, u32[]{:S(2)}) collective-permute-start(f32[32,128]{1,0:T(8,128)S(1)} %get-tuple-element.110), channel_id=1, source_target_pairs={{0,1},{1,0},{2,3},{3,2},{4,5},{5,4},{6,7},{7,6},{8,9},{9,8},{10,11... | collective-permute-start | bytes 49160 | tf_op jit(solution)/shard_map/ppermute | solution.py:557
  33.1 4.9 %collective-permute-start.13 = (f32[32,128]{1,0:T(8,128)S(1)}, f32[32,128]{1,0:T(8,128)S(1)}, u32[]{:S(2)}, u32[]{:S(2)}) collective-permute-start(f32[32,128]{1,0:T(8,128)S(1)} %get-tuple-element.111), channel_id=1, source_target_pairs={{0,2},{1,3},{2,0},{3,1},{4,6},{5,7},{6,4},{7,5},{8,10},{9,11},{10,... | collective-permute-start | bytes 49160 | tf_op jit(solution)/shard_map/ppermute | solution.py:557
  34.3 3.8 %collective-permute-start.14 = (f32[32,128]{1,0:T(8,128)S(1)}, f32[32,128]{1,0:T(8,128)S(1)}, u32[]{:S(2)}, u32[]{:S(2)}) collective-permute-start(f32[32,128]{1,0:T(8,128)S(1)} %get-tuple-element.112), channel_id=1, source_target_pairs={{0,4},{1,5},{2,6},{3,7},{4,0},{5,1},{6,2},{7,3},{8,12},{9,13},{10,... | collective-permute-start | bytes 49160 | tf_op jit(solution)/shard_map/ppermute | solution.py:557
  34.3 3.8 %collective-permute-start.15 = (f32[32,128]{1,0:T(8,128)S(1)}, f32[32,128]{1,0:T(8,128)S(1)}, u32[]{:S(2)}, u32[]{:S(2)}) collective-permute-start(f32[32,128]{1,0:T(8,128)S(1)} %get-tuple-element.113), channel_id=1, source_target_pairs={{0,8},{1,9},{2,10},{3,11},{4,12},{5,13},{6,14},{7,15},{8,0},{9,1},... | collective-permute-start | bytes 49160 | tf_op jit(solution)/shard_map/ppermute | solution.py:557
  38.3 6.4 %collective-permute-start.18 = (f32[32,128]{1,0:T(8,128)S(1)}, f32[32,128]{1,0:T(8,128)S(1)}, u32[]{:S(2)}, u32[]{:S(2)}) collective-permute-start(f32[32,128]{1,0:T(8,128)S(1)} %get-tuple-element.115.refs_0_), channel_id=1, source_target_pairs={{0,3},{1,2},{2,1},{3,0},{4,7},{5,6},{6,5},{7,4},{8,11},{9,10},{10,... | collective-permute-start | bytes 49160 | tf_op jit(solution)/shard_map/ppermute | solution.py:557
  40.3 4.6 %collective-permute-start.17 = (f32[32,128]{1,0:T(8,128)S(1)}, f32[32,128]{1,0:T(8,128)S(1)}, u32[]{:S(2)}, u32[]{:S(2)}) collective-permute-start(f32[32,128]{1,0:T(8,128)S(1)} %get-tuple-element.115.refs_0_), channel_id=1, source_target_pairs={{0,2},{1,3},{2,0},{3,1},{4,6},{5,7},{6,4},{7,5},{8,10},{9,11},{10,... | collective-permute-start | bytes 49160 | tf_op jit(solution)/shard_map/ppermute | solution.py:557
  41.3 3.8 %collective-permute-start.16 = (f32[32,128]{1,0:T(8,128)S(1)}, f32[32,128]{1,0:T(8,128)S(1)}, u32[]{:S(2)}, u32[]{:S(2)}) collective-permute-start(f32[32,128]{1,0:T(8,128)S(1)} %get-tuple-element.115.refs_0_), channel_id=1, source_target_pairs={{0,1},{1,0},{2,3},{3,2},{4,5},{5,4},{6,7},{7,6},{8,9},{9,8},{10,11... | collective-permute-start | bytes 49160 | tf_op jit(solution)/shard_map/ppermute | solution.py:557
  45.7 6.3 %collective-permute-start.19 = (f32[32,128]{1,0:T(8,128)S(1)}, f32[32,128]{1,0:T(8,128)S(1)}, u32[]{:S(2)}, u32[]{:S(2)}) collective-permute-start(f32[32,128]{1,0:T(8,128)S(1)} %get-tuple-element.127), channel_id=1, source_target_pairs={{0,1},{1,0},{2,3},{3,2},{4,5},{5,4},{6,7},{7,6},{8,9},{9,8},{10,11... | collective-permute-start | bytes 49160 | tf_op jit(solution)/shard_map/ppermute | solution.py:557
  47.1 4.9 %collective-permute-start.20 = (f32[32,128]{1,0:T(8,128)S(1)}, f32[32,128]{1,0:T(8,128)S(1)}, u32[]{:S(2)}, u32[]{:S(2)}) collective-permute-start(f32[32,128]{1,0:T(8,128)S(1)} %get-tuple-element.128), channel_id=1, source_target_pairs={{0,2},{1,3},{2,0},{3,1},{4,6},{5,7},{6,4},{7,5},{8,10},{9,11},{10,... | collective-permute-start | bytes 49160 | tf_op jit(solution)/shard_map/ppermute | solution.py:557
  48.2 3.9 %collective-permute-start.21 = (f32[32,128]{1,0:T(8,128)S(1)}, f32[32,128]{1,0:T(8,128)S(1)}, u32[]{:S(2)}, u32[]{:S(2)}) collective-permute-start(f32[32,128]{1,0:T(8,128)S(1)} %get-tuple-element.129), channel_id=1, source_target_pairs={{0,4},{1,5},{2,6},{3,7},{4,0},{5,1},{6,2},{7,3},{8,12},{9,13},{10,... | collective-permute-start | bytes 49160 | tf_op jit(solution)/shard_map/ppermute | solution.py:557
  48.2 3.9 %collective-permute-start.22 = (f32[32,128]{1,0:T(8,128)S(1)}, f32[32,128]{1,0:T(8,128)S(1)}, u32[]{:S(2)}, u32[]{:S(2)}) collective-permute-start(f32[32,128]{1,0:T(8,128)S(1)} %get-tuple-element.130), channel_id=1, source_target_pairs={{0,8},{1,9},{2,10},{3,11},{4,12},{5,13},{6,14},{7,15},{8,0},{9,1},... | collective-permute-start | bytes 49160 | tf_op jit(solution)/shard_map/ppermute | solution.py:557
  53.0 11.7 %all-to-all-start = ((f32[32,2,128]{2,1,0:T(2,128)}), f32[32,2,128]{2,1,0:T(2,128)S(1)}, u32[]{:S(2)}, u32[]{:S(2)}) async-start(f32[32,2,128]{2,1,0:T(2,128)} %get-tuple-element.134), calls=%async_computation | async-start | bytes 65536 | tf_op jit(solution)/shard_map/all_to_all | solution.py:659
  56.8 7.7 %collective-permute-start.23 = (f32[32,128]{1,0:T(8,128)S(1)}, f32[32,128]{1,0:T(8,128)S(1)}, u32[]{:S(2)}, u32[]{:S(2)}) collective-permute-start(f32[32,128]{1,0:T(8,128)S(1)} %get-tuple-element.135), channel_id=1, source_target_pairs={{0,1},{1,0},{2,3},{3,2},{4,5},{5,4},{6,7},{7,6},{8,9},{9,8},{10,11... | collective-permute-start | bytes 49160 | tf_op jit(solution)/shard_map/ppermute | solution.py:557
  58.6 5.9 %collective-permute-start.24 = (f32[32,128]{1,0:T(8,128)S(1)}, f32[32,128]{1,0:T(8,128)S(1)}, u32[]{:S(2)}, u32[]{:S(2)}) collective-permute-start(f32[32,128]{1,0:T(8,128)S(1)} %get-tuple-element.136), channel_id=1, source_target_pairs={{0,2},{1,3},{2,0},{3,1},{4,6},{5,7},{6,4},{7,5},{8,10},{9,11},{10,... | collective-permute-start | bytes 49160 | tf_op jit(solution)/shard_map/ppermute | solution.py:557
  61.0 3.5 %collective-permute-start.25 = (f32[32,128]{1,0:T(8,128)S(1)}, f32[32,128]{1,0:T(8,128)S(1)}, u32[]{:S(2)}, u32[]{:S(2)}) collective-permute-start(f32[32,128]{1,0:T(8,128)S(1)} %get-tuple-element.137), channel_id=1, source_target_pairs={{0,4},{1,5},{2,6},{3,7},{4,0},{5,1},{6,2},{7,3},{8,12},{9,13},{10,... | collective-permute-start | bytes 49160 | tf_op jit(solution)/shard_map/ppermute | solution.py:557
  61.0 3.7 %collective-permute-start.26 = (f32[32,128]{1,0:T(8,128)S(1)}, f32[32,128]{1,0:T(8,128)S(1)}, u32[]{:S(2)}, u32[]{:S(2)}) collective-permute-start(f32[32,128]{1,0:T(8,128)S(1)} %get-tuple-element.138), channel_id=1, source_target_pairs={{0,8},{1,9},{2,10},{3,11},{4,12},{5,13},{6,14},{7,15},{8,0},{9,1},... | collective-permute-start | bytes 49160 | tf_op jit(solution)/shard_map/ppermute | solution.py:557

commit v6 on v5

--- a/solution.py
+++ b/solution.py
@@ -13,8 +13,9 @@
 CB = 4
 OCAP = 8
 SCAP = 2
-EARLY = 4
-CHUNKS = (4, 3, 1)
+EARLY = 6
+LINE_PADS = (8, 16, 0)
+CHUNKS = (4, 2)
 NB = 16
 TPR = 7
 NL = 2048
@@ -61,7 +62,7 @@
 
 
 def prepare_body(
-    load_ref, map_ref, id_ref, link_ref, target_ref, column_ref, weight_ref, side0, side1, side2, side3,
+    load_ref, map_ref, id_ref, link_ref, target_ref, far_ref, column_ref, weight_ref, side0, side1, side2, side3,
     ids, links, maps, faces, sems,
 ):
     copies = start_all(
@@ -88,6 +89,8 @@
     line = lax.broadcasted_iota(jnp.int32, (8, BS), 0)
     target = jnp.where(line == 1, place, target).astype(F32)
     target_ref[...] = target
+    far_ref[...] = jnp.zeros_like(far_ref)
+    far_ref[:8, :] = target
     column_ref[0] = column
     column_ref[1] = spot
     copies[1].wait()
@@ -124,13 +127,17 @@
 
 def load_inside_body(
     x_ref, inv_ref, basis_ref, schur_ref, coarse_ref,
-    inner_ref, part_ref, schur_high, schur_low, basis_high, basis_low, coarse_parts,
+    own0, own1, own2, own3,
+    inner_ref, part_ref, schur_high, schur_low, basis_high, basis_low, coarse_parts, mine_ref,
     inv, basis, schur, x, coarse, sems,
 ):
     first, *copies = start_all(
         sems, (x_ref.at[0, :, : NIN * BS], x), (inv_ref, inv), (basis_ref.at[0], basis),
         (schur_ref.at[0], schur), (coarse_ref.at[0], coarse),
     )
+    rows = lax.broadcasted_iota(jnp.int32, (BS, BS), 0).astype(F32)
+    for r, side in enumerate((own0, own1, own2, own3)):
+        mine_ref[r] = (rows == side[NRHS : NRHS + 1, :]).astype(F32).T.astype(BF16)
     first.wait()
     solve_inside(lambda b: x[:, lanes(b)], inv, basis, copies, inner_ref, part_ref)
     basis_high[...], basis_low[...] = halves(basis[:, NIN * BS :])
@@ -190,15 +197,19 @@
     return onehot(rows == own[NRHS : NRHS + 1, :]), onehot(rows == inc[NRHS : NRHS + 1, :])
 
 
-def rows_for(target, coarse_ref):
+def rows_for(targets, coarse_ref):
     here = lax.axis_index("gz")
     slots = lax.broadcasted_iota(jnp.int32, (SCAP * CW, BS), 0)
     places = lax.broadcasted_iota(jnp.int32, (OCAP * CW, BS), 0)
-    goal = target.astype(jnp.int32)
-    into = onehot(slots == goal[1:2, :])
-    out_of = onehot(places == goal[0:1, :] - here * (OCAP * CW))
-    take = mm(into, out_of, NT).astype(BF16)
-    return mm(take, coarse_ref[0]) + mm(take, coarse_ref[1]) + mm(take, coarse_ref[2])
+    takes = []
+    for target in targets:
+        goal = target.astype(jnp.int32)
+        into = onehot(slots == goal[1:2, :])
+        out_of = onehot(places == goal[0:1, :] - here * (OCAP * CW))
+        takes.append(mm(into, out_of, NT).astype(BF16))
+    take = jnp.concatenate(takes, axis=0)
+    rows = mm(take, coarse_ref[0]) + mm(take, coarse_ref[1]) + mm(take, coarse_ref[2])
+    return [rows[k * SCAP * CW : (k + 1) * SCAP * CW] for k in range(len(targets))]
 
 
 def put_rows(ref, first, rows):
@@ -208,24 +219,26 @@
 
 def first_faces_body(
     own0, own1, own2, own3, in0, in1, in2, in3, target_ref, weight_ref,
-    basis_high, basis_low, part_ref, coarse_ref, *rest, line,
+    basis_high, basis_low, part_ref, coarse_ref, turned_ref, *rest, line,
 ):
     targets = [target_ref[...], in0[NRHS + 8 :, :], in1[NRHS + 8 :, :]] + [
-        ref[...] for ref in rest[: line - 3]
+        ref[:8, :] for ref in rest[: line - 3]
     ]
     face_ref, contrib_ref, all_ref, *sides = rest[line - 3 :]
     faces = []
     for r, (own, inc) in enumerate(zip((own0, own1, own2, own3), (in0, in1, in2, in3))):
-        mine, theirs = maps_of(own, inc)
+        theirs = maps_of(own, inc)[1]
         link = weight_ref[NF + r : NF + r + 1, :]
-        came = select_lanes(inc[:NRHS, :], (mm(theirs, mine, NT) * link).astype(BF16))
+        came = select_lanes(inc[:NRHS, :], (mm(theirs, turned_ref[r]) * link).astype(BF16))
         faces.append(own[:NRHS, :] + came)
         face_ref[r] = faces[-1]
     add_faces(faces, weight_ref, basis_high, basis_low, part_ref, contrib_ref)
     all_ref[...] = jnp.concatenate([t[0:1, :] for t in targets], axis=1)
-    for side, target in zip(sides, targets[1:]):
+    for side, rows in zip(sides, rows_for(targets[1:], coarse_ref)):
         side[:NRHS, :] = contrib_ref[...]
-        put_rows(side, NRHS, rows_for(target, coarse_ref))
+        if side.shape[0] > NRHS + 2 * SCAP * CW:
+            side[NRHS + 2 * SCAP * CW :, :] = jnp.zeros_like(side[NRHS + 2 * SCAP * CW :, :])
+        put_rows(side, NRHS, rows)
 
 
 def under_line_body(
@@ -242,7 +255,7 @@
     for r, (own, inc) in enumerate(zip((own0, own1, own2, own3), (in0, in1, in2, in3))):
         mine, theirs = maps_of(own, inc)
         swap_ref[r] = (mm(mine, theirs, NT) * weight_ref[NF + r : NF + r + 1, :]).astype(BF16)
-    put_rows(rows_ref, 0, rows_for(target_ref[...], coarse_ref))
+    put_rows(rows_ref, 0, rows_for([target_ref[...]], coarse_ref)[0])
     here = lax.axis_index("gz")
     own = OCAP * CW
     goal = target_ref[...].astype(jnp.int32)
@@ -296,7 +309,8 @@
 def owner_rows(side, m):
     first = NRHS if m else 0
     return jnp.concatenate(
-        [side[first : first + SCAP * CW, :], side[first + SCAP * CW :, :]], axis=1
+        [side[first : first + SCAP * CW, :], side[first + SCAP * CW : first + 2 * SCAP * CW, :]],
+        axis=1,
     )
 
 
@@ -568,15 +582,15 @@
     block, face, small, side = f32(*inside), f32(*around), f32(NRHS, BS), f32(NRHS + 16, BS)
     nf = NF * BS
     width = line * CB * CW
-    target, column, weight, *sides = call(
-        prepare_body, "prepare", [f32(8, BS), jax.ShapeDtypeStruct((2, BS, BS), jnp.int32), f32(2 * NF, BS)] + [side] * NF, [HBM] * 4,
+    target, for_far, column, weight, *sides = call(
+        prepare_body, "prepare", [f32(8, BS), f32(NRHS + 64, BS), jax.ShapeDtypeStruct((2, BS, BS), jnp.int32), f32(2 * NF, BS)] + [side] * NF, [HBM] * 4,
         load_vector, row_map, coarse_id, face_link,
         scratch=[pltpu.SMEM((1, CB), jnp.int32), pltpu.SMEM((1, NF), jnp.int32),
                  pltpu.VMEM((1, NF, BS), jnp.int32), (NRHS, nf)],
         copies=4,
     )
     came = trade_faces(sides)
-    far = [trade(target, mask) for mask in range(3, line)]
+    far = [trade(for_far, mask) for mask in range(3, line)]
 
     own = OCAP * CW
     mat_outs = [block, small, bf16(nf, nf), bf16(nf, nf), bf16(BS, nf), bf16(BS, nf)]
@@ -584,9 +598,9 @@
     cols_scratch = pltpu.SMEM((TPR, NB), jnp.int32)
     face_tiles = (NF, TPR, BS, BS)
 
-    inner, part, *mats, coarse_parts = call(
-        load_inside_body, "inside_load", mat_outs + [bf16(3, own, own)], [HBM] * 5,
-        load_vector, interior_inv, coarse_basis, schur_inv, coarse_inv,
+    inner, part, *mats, coarse_parts, turned = call(
+        load_inside_body, "inside_load", mat_outs + [bf16(3, own, own), bf16(NF, BS, BS)],
+        [HBM] * 5 + [VMEM] * NF, load_vector, interior_inv, coarse_basis, schur_inv, coarse_inv, *sides,
         scratch=mat_scratch + [(NRHS, NIN * BS), (own, own)], copies=5,
     )
     width = line * CB * CW
@@ -595,8 +609,8 @@
     pre_outs = [f32(EARLY, TPR, BS, BS), f32(BS, NIN * BS)]
     r_face, contrib, targets, *sides = call(
         lambda *refs: first_faces_body(*refs, line=line), "faces_load",
-        [face, small, f32(1, width)] + [f32(NRHS + half, BS)] * (line - 1), [VMEM] * (11 + line),
-        *own_sides, *came, target, weight, *mats[2:], part, coarse_parts, *far,
+        [face, small, f32(1, width)] + [f32(NRHS + half + LINE_PADS[min(m, 3) - 1], BS) for m in range(1, line)], [VMEM] * (12 + line),
+        *own_sides, *came, target, weight, *mats[2:], part, coarse_parts, turned, *far,
     )
     others = [trade(value, mask) for value, mask in zip(sides, range(1, line))]
     block_high, block_low, outer, swap, rows, picks, mine, *early = call(

time: 66 us -> 65 us (0.985)
  waiting for transfers between devices: 5.7 us -> 3.99 us
  starting transfers between devices: 35.7 us -> 37 us
    ppermute x27, waiting for transfers between devices: 5.7 us -> 3.99 us  [trade(): return lax.ppermute(value, AXES, [(i, i ^ mask) for i in range(devices)])]
    ppermute x27, starting transfers between devices: 32 us -> 33.3 us  [trade(): return lax.ppermute(value, AXES, [(i, i ^ mask) for i in range(devices)])]
where the time goes in v6:
time: 65 us; the launch traced here: 64.7 us
  starting transfers between devices  37 us (57%)
  Pallas kernels  22.9 us (35%)
  waiting for transfers between devices  3.99 us (6%)
  between operations  0.83 us (1%)
    ppermute x27, starting transfers between devices, trade(): return lax.ppermute(value, AXES, [(i, i ^ mask) for i in range(devices)])  33.3 us
    pallas_call x15, Pallas kernels, call(): pl.pallas_call(body, name=name, out_shape=outs, in_specs=specs, out_specs...  22.9 us
    ppermute x27, waiting for transfers between devices, trade(): return lax.ppermute(value, AXES, [(i, i ^ mask) for i in range(devices)])  3.99 us
    all_to_all x1, starting transfers between devices, on_device(): spread = lax.all_to_all(dots, AXES, 0, 0)  3.66 us
  transfers between devices with their start and end apart: 28, of which 6 were waited for; matrix products, arithmetic and copies ran while one was open for 0% of the time, Pallas kernels for 26%

profile of v6, /device:TPU:0, one launch (start us, length us, event | category | flops | bytes accessed | tf_op | source)
XLA Modules:
  0.0 64.7 jit_solution(3639587471456064960)
XLA Ops:
  0.6 0.9 %prepare.1 = (f32[8,128]{1,0:T(8,128)S(1)}, f32[96,128]{1,0:T(8,128)S(1)}, s32[2,128,128]{2,1,0:T(8,128)S(1)}, f32[8,128]{1,0:T(8,128)S(1)}, f32[48,128]{1,0:T(8...) custom-call(f32[1,32,2048]{2,1,0:T(8,128)} %load_hbm.1, s32[1,4,128]{2,1,0:T(4,128)} %map_ref.1, ...), custom_call_target="tpu_custom_call" | custom-call | tf_op jit(solution)/shard_map/prepare/pallas_call | solution.py:548
  1.5 5.1 %collective-permute-start.4 = (f32[96,128]{1,0:T(8,128)S(1)}, f32[96,128]{1,0:T(8,128)S(1)}, u32[]{:S(2)}, u32[]{:S(2)}) collective-permute-start(f32[96,128]{1,0:T(8,128)S(1)} %get-tuple-element.86), channel_id=1, source_target_pairs={{0,3},{1,2},{2,1},{3,0},{4,7},{5,6},{6,5},{7,4},{8,11},{9,10},{10,... | collective-permute-start | bytes 147464 | tf_op jit(solution)/shard_map/ppermute | solution.py:571
  6.7 0.6 collective-permute-start.1
  7.3 1.6 %collective-permute-start.3 = (f32[48,128]{1,0:T(8,128)S(1)}, f32[48,128]{1,0:T(8,128)S(1)}, u32[]{:S(2)}, u32[]{:S(2)}) collective-permute-start(f32[48,128]{1,0:T(8,128)S(1)} %get-tuple-element.77.own3.refs_3_), channel_id=1, source_target_pairs={{0,8},{1,9},{2,10},{3,11},{4,12},{5,13},{6,14},{7,15},{8,0},{9,1},... | collective-permute-start | bytes 73736 | tf_op jit(solution)/shard_map/ppermute | solution.py:571
  8.9 2.3 %inside_load.1 = (f32[12,32,128]{2,1,0:T(8,128)S(1)}, f32[32,128]{1,0:T(8,128)S(1)}, bf16[512,512]{1,0:T(8,128)(2,1)S(1)}, bf16[512,512]{1,0:T(8,128)(2,1)S(1)},...) custom-call(f32[1,32,2048]{2,1,0:T(8,128)} %load_hbm.1, ...), custom_call_target="tpu_custom_call" | custom-call | tf_op jit(solution)/shard_map/inside_load/pallas_call | solution.py:548
  11.2 0.0 collective-permute-done.refs_4_
  11.2 0.2 collective-permute-done.1.refs_5_
  11.4 0.8 %faces_load.1 = (f32[4,32,128]{2,1,0:T(8,128)S(1)}, f32[32,128]{1,0:T(8,128)S(1)}, f32[1,512]{1,0:T(1,128)S(1)}, f32[168,128]{1,0:T(8,128)S(1)}, f32[176,128]{1,0:T(8,128)S(1)}, /*index=5*/f32[160,128]{1,0:T(8,128)S(1)}) custom-call(f32[48,128]{1,0:T(8,128)S(1)} %get-tuple-element.74.own0.refs_0_, f32[48,128]{1,0:T(8,128)S(1)} %get-tuple-element.75.own1.refs_1_, ...), custom_call_target="tpu_custom_call" | custom-call | tf_op jit(solution)/shard_map/faces_load/pallas_call | solution.py:548
  12.2 2.1 %collective-permute-start.6 = (f32[176,128]{1,0:T(8,128)S(1)}, f32[176,128]{1,0:T(8,128)S(1)}, u32[]{:S(2)}, u32[]{:S(2)}) collective-permute-start(f32[176,128]{1,0:T(8,128)S(1)} %get-tuple-element.96), channel_id=1, source_target_pairs={{0,2},{1,3},{2,0},{3,1},{4,6},{5,7},{6,4},{7,5},{8,10},{9,11},{10,... | collective-permute-start | bytes 270344 | tf_op jit(solution)/shard_map/ppermute | solution.py:571
  14.3 2.0 %collective-permute-start.5 = (f32[168,128]{1,0:T(8,128)S(1)}, f32[168,128]{1,0:T(8,128)S(1)}, u32[]{:S(2)}, u32[]{:S(2)}) collective-permute-start(f32[168,128]{1,0:T(8,128)S(1)} %get-tuple-element.95), channel_id=1, source_target_pairs={{0,1},{1,0},{2,3},{3,2},{4,5},{5,4},{6,7},{7,6},{8,9},{9,8},{10,11... | collective-permute-start | bytes 258056 | tf_op jit(solution)/shard_map/ppermute | solution.py:571
  16.3 0.4 collective-permute-start.7
  16.7 3.0 %under_line.1 = (bf16[4,4,128,128]{3,2,1,0:T(8,128)(2,1)S(1)}, bf16[4,4,128,128]{3,2,1,0:T(8,128)(2,1)S(1)}, f32[4,32,128]{2,1,0:T(8,128)S(1)}, bf16[4,128,128]{...) custom-call(f32[48,128]{1,0:T(8,128)S(1)} %get-tuple-element.74.own0, ...), custom_call_target="tpu_custom_call" | custom-call | tf_op jit(solution)/shard_map/under_line/pallas_call | solution.py:548
  19.7 2.9 %collective-permute-done.7.refs_6_.refs_11_ = f32[160,128]{1,0:T(8,128)S(1)} collective-permute-done((f32[160,128]{1,0:T(8,128)S(1)}, f32[160,128]{1,0:T(8,128)S(1)}, u32[]{:S(2)}, u32[]{:S(2)}) %collective-permute-start.7) | collective-permute-done | bytes 81952 | tf_op jit(solution)/shard_map/ppermute | solution.py:571
  22.6 0.0 collective-permute-done.5.refs_4_.refs_9_
  22.6 1.0 %coarse_load.1 = (f32[32,128]{1,0:T(8,128)S(1)}, f32[4,32,128]{2,1,0:T(8,128)S(1)}, f32[32,128]{1,0:T(8,128)S(1)}, f32[32,128]{1,0:T(8,128)S(1)}, f32[32,128]{1,0:T(8,128)S(1)}, /*index=5*/f32[32,128]{1,0:T(8,128)S(1)}) custom-call(f32[32,128]{1,0:T(8,128)S(1)} %get-tuple-element.87.refs_0_, f32[128,128]{1,0:T(8,128)S(1)} %get-tuple-element.92.refs_1_.refs_2_, ...), custom_call_target="tpu_custom_call" | custom-call | tf_op jit(solution)/shard_map/coarse_load/pallas_call | solution.py:548
  23.5 1.2 %collective-permute-start.8 = (f32[32,128]{1,0:T(8,128)S(1)}, f32[32,128]{1,0:T(8,128)S(1)}, u32[]{:S(2)}, u32[]{:S(2)}) collective-permute-start(f32[32,128]{1,0:T(8,128)S(1)} %get-tuple-element.104), channel_id=1, source_target_pairs={{0,1},{1,0},{2,3},{3,2},{4,5},{5,4},{6,7},{7,6},{8,9},{9,8},{10,11... | collective-permute-start | bytes 49160 | tf_op jit(solution)/shard_map/ppermute | solution.py:571
  24.7 1.7 %collective-permute-start.9 = (f32[32,128]{1,0:T(8,128)S(1)}, f32[32,128]{1,0:T(8,128)S(1)}, u32[]{:S(2)}, u32[]{:S(2)}) collective-permute-start(f32[32,128]{1,0:T(8,128)S(1)} %get-tuple-element.105), channel_id=1, source_target_pairs={{0,2},{1,3},{2,0},{3,1},{4,6},{5,7},{6,4},{7,5},{8,10},{9,11},{10,... | collective-permute-start | bytes 49160 | tf_op jit(solution)/shard_map/ppermute | solution.py:571
  26.4 0.0 collective-permute-start.10
  26.4 1.1 %collective-permute-start.11 = (f32[32,128]{1,0:T(8,128)S(1)}, f32[32,128]{1,0:T(8,128)S(1)}, u32[]{:S(2)}, u32[]{:S(2)}) collective-permute-start(f32[32,128]{1,0:T(8,128)S(1)} %get-tuple-element.107), channel_id=1, source_target_pairs={{0,8},{1,9},{2,10},{3,11},{4,12},{5,13},{6,14},{7,15},{8,0},{9,1},... | collective-permute-start | bytes 49160 | tf_op jit(solution)/shard_map/ppermute | solution.py:571
  27.5 2.3 %own_first.1 = (f32[12,32,128]{2,1,0:T(8,128)S(1)}, f32[16,32,128]{2,1,0:T(8,128)S(1)}) custom-call(f32[12,32,128]{2,1,0:T(8,128)S(1)} %get-tuple-element.78.refs_0_, f32[32,128]{1,0:T(8,128)S(1)} %get-tuple-element.100.refs_1_, f32[6,7,128,128]{3,2,1,0:T(8,128)S(1)} %get-tuple-element.101.refs_2_, f32[128,1536]{1,0:T(8,128)S(1)} %get-tuple-element.102.refs_3_, ...), custom_call_target="tpu_custom_call" | custom-call | tf_op jit(solution)/shard_map/own_first/pallas_call | solution.py:548
  29.9 0.2 collective-permute-done.11.in3
  30.2 0.4 face_first.1
  30.6 2.0 %collective-permute-start.12 = (f32[32,128]{1,0:T(8,128)S(1)}, f32[32,128]{1,0:T(8,128)S(1)}, u32[]{:S(2)}, u32[]{:S(2)}) collective-permute-start(f32[32,128]{1,0:T(8,128)S(1)} %get-tuple-element.114), channel_id=1, source_target_pairs={{0,1},{1,0},{2,3},{3,2},{4,5},{5,4},{6,7},{7,6},{8,9},{9,8},{10,11... | collective-permute-start | bytes 49160 | tf_op jit(solution)/shard_map/ppermute | solution.py:571
  32.6 0.9 %collective-permute-start.13 = (f32[32,128]{1,0:T(8,128)S(1)}, f32[32,128]{1,0:T(8,128)S(1)}, u32[]{:S(2)}, u32[]{:S(2)}) collective-permute-start(f32[32,128]{1,0:T(8,128)S(1)} %get-tuple-element.115), channel_id=1, source_target_pairs={{0,2},{1,3},{2,0},{3,1},{4,6},{5,7},{6,4},{7,5},{8,10},{9,11},{10,... | collective-permute-start | bytes 49160 | tf_op jit(solution)/shard_map/ppermute | solution.py:571
  33.5 0.8 %collective-permute-start.15 = (f32[32,128]{1,0:T(8,128)S(1)}, f32[32,128]{1,0:T(8,128)S(1)}, u32[]{:S(2)}, u32[]{:S(2)}) collective-permute-start(f32[32,128]{1,0:T(8,128)S(1)} %get-tuple-element.117), channel_id=1, source_target_pairs={{0,8},{1,9},{2,10},{3,11},{4,12},{5,13},{6,14},{7,15},{8,0},{9,1},... | collective-permute-start | bytes 49160 | tf_op jit(solution)/shard_map/ppermute | solution.py:571
  34.2 2.7 %inside_image.1 = (f32[12,32,128]{2,1,0:T(8,128)S(1)}, f32[12,32,128]{2,1,0:T(8,128)S(1)}, f32[32,128]{1,0:T(8,128)S(1)}) custom-call(f32[16,32,128]{2,1,0:T(8,128)S(1)} %get-tuple-element.103.acc_ref, f32[4,32,128]{2,1,0:T(8,128)S(1)} %get-tuple-element.111.face_ref.zf, s32[7,16]{1,0:T(8,128)} %bitcast.3, f32[16,7,128,128]{3,2,1,0:T(8,128)} %tiles_ref.5, ...), custom_call_target="tpu_custom_call" | custom-call | tf_op jit(solution)/shard_map/inside_image/pallas_call | solution.py:548
  37.0 0.2 collective-permute-done.13.in1
  37.2 0.0 collective-permute-done.15.in3
  37.2 0.2 faces_image.1
  37.4 1.7 %collective-permute-start.18 = (f32[32,128]{1,0:T(8,128)S(1)}, f32[32,128]{1,0:T(8,128)S(1)}, u32[]{:S(2)}, u32[]{:S(2)}) collective-permute-start(f32[32,128]{1,0:T(8,128)S(1)} %get-tuple-element.119.refs_0_), channel_id=1, source_target_pairs={{0,3},{1,2},{2,1},{3,0},{4,7},{5,6},{6,5},{7,4},{8,11},{9,10},{10,... | collective-permute-start | bytes 49160 | tf_op jit(solution)/shard_map/ppermute | solution.py:571
  39.1 0.4 collective-permute-start.17
  39.5 2.3 %collective-permute-start.16 = (f32[32,128]{1,0:T(8,128)S(1)}, f32[32,128]{1,0:T(8,128)S(1)}, u32[]{:S(2)}, u32[]{:S(2)}) collective-permute-start(f32[32,128]{1,0:T(8,128)S(1)} %get-tuple-element.119.refs_0_), channel_id=1, source_target_pairs={{0,1},{1,0},{2,3},{3,2},{4,5},{5,4},{6,7},{7,6},{8,9},{9,8},{10,11... | collective-permute-start | bytes 49160 | tf_op jit(solution)/shard_map/ppermute | solution.py:571
  41.8 2.3 %table.1 = (bf16[128,512]{1,0:T(8,128)(2,1)S(1)}, bf16[128,512]{1,0:T(8,128)(2,1)S(1)}, f32[4,32,128]{2,1,0:T(8,128)S(1)}, f32[6,7,128,128]{3,2,1,0:T(8,128)S(1)}, f32[128,1536]{1,0:T(8,128)S(1)}) custom-call(f32[16,7,128,128]{3,2,1,0:T(8,128)} %tiles_ref.5, f32[1,128,2048]{2,1,0:T(8,128)} %refs_1_.1, f32[128,128]{1,0:T(8,128)S(1)} %get-tuple-element.92.refs_1_.refs_2_, ...), custom_call_target="tpu_custom_call" | custom-call | tf_op jit(solution)/shard_map/table/pallas_call | solution.py:548
  44.1 0.6 coarse_image.1
  44.7 1.5 %collective-permute-start.19 = (f32[32,128]{1,0:T(8,128)S(1)}, f32[32,128]{1,0:T(8,128)S(1)}, u32[]{:S(2)}, u32[]{:S(2)}) collective-permute-start(f32[32,128]{1,0:T(8,128)S(1)} %get-tuple-element.131), channel_id=1, source_target_pairs={{0,1},{1,0},{2,3},{3,2},{4,5},{5,4},{6,7},{7,6},{8,9},{9,8},{10,11... | collective-permute-start | bytes 49160 | tf_op jit(solution)/shard_map/ppermute | solution.py:571
  46.2 1.1 %collective-permute-start.20 = (f32[32,128]{1,0:T(8,128)S(1)}, f32[32,128]{1,0:T(8,128)S(1)}, u32[]{:S(2)}, u32[]{:S(2)}) collective-permute-start(f32[32,128]{1,0:T(8,128)S(1)} %get-tuple-element.132), channel_id=1, source_target_pairs={{0,2},{1,3},{2,0},{3,1},{4,6},{5,7},{6,4},{7,5},{8,10},{9,11},{10,... | collective-permute-start | bytes 49160 | tf_op jit(solution)/shard_map/ppermute | solution.py:571
  47.3 1.1 %collective-permute-start.22 = (f32[32,128]{1,0:T(8,128)S(1)}, f32[32,128]{1,0:T(8,128)S(1)}, u32[]{:S(2)}, u32[]{:S(2)}) collective-permute-start(f32[32,128]{1,0:T(8,128)S(1)} %get-tuple-element.134), channel_id=1, source_target_pairs={{0,8},{1,9},{2,10},{3,11},{4,12},{5,13},{6,14},{7,15},{8,0},{9,1},... | collective-permute-start | bytes 49160 | tf_op jit(solution)/shard_map/ppermute | solution.py:571
  48.4 2.5 %own_second.1 = (f32[12,32,128]{2,1,0:T(8,128)S(1)}, f32[16,32,128]{2,1,0:T(8,128)S(1)}, f32[5,32,128]{2,1,0:T(8,128)S(1)}, f32[16,32,128]{2,1,0:T(8,128)S(1)}) custom-call(f32[12,32,128]{2,1,0:T(8,128)S(1)} %get-tuple-element.112.inner_ref, f32[32,128]{1,0:T(8,128)S(1)} %get-tuple-element.125.back_ref, f32[6,7,128,128]{3,2,1,0:T(8,128)S(1)} %get-tuple-element.126.early_ref, ...), custom_call_target="tpu_custom_call" | custom-call | tf_op jit(solution)/shard_map/own_second/pallas_call | solution.py:548
  50.9 0.1 collective-permute-done.20.in1
  51.0 0.0 collective-permute-done.22.in3
  51.1 1.0 %face_second.1 = (f32[4,32,128]{2,1,0:T(8,128)S(1)}, f32[4,32,128]{2,1,0:T(8,128)S(1)}, f32[32,2,128]{2,1,0:T(2,128)}, f32[32,128]{1,0:T(8,128)S(1)}, f32[32,128...) custom-call(f32[16,32,128]{2,1,0:T(8,128)S(1)} %get-tuple-element.130.acc_ref, ...), custom_call_target="tpu_custom_call" | custom-call | tf_op jit(solution)/shard_map/face_second/pallas_call | solution.py:548
  52.1 3.7 %all-to-all-start = ((f32[32,2,128]{2,1,0:T(2,128)}), f32[32,2,128]{2,1,0:T(2,128)S(1)}, u32[]{:S(2)}, u32[]{:S(2)}) async-start(f32[32,2,128]{2,1,0:T(2,128)} %get-tuple-element.138), calls=%async_computation | async-start | bytes 65536 | tf_op jit(solution)/shard_map/all_to_all | solution.py:673
  55.7 1.8 %collective-permute-start.23 = (f32[32,128]{1,0:T(8,128)S(1)}, f32[32,128]{1,0:T(8,128)S(1)}, u32[]{:S(2)}, u32[]{:S(2)}) collective-permute-start(f32[32,128]{1,0:T(8,128)S(1)} %get-tuple-element.139), channel_id=1, source_target_pairs={{0,1},{1,0},{2,3},{3,2},{4,5},{5,4},{6,7},{7,6},{8,9},{9,8},{10,11... | collective-permute-start | bytes 49160 | tf_op jit(solution)/shard_map/ppermute | solution.py:571
  57.6 2.4 %collective-permute-start.24 = (f32[32,128]{1,0:T(8,128)S(1)}, f32[32,128]{1,0:T(8,128)S(1)}, u32[]{:S(2)}, u32[]{:S(2)}) collective-permute-start(f32[32,128]{1,0:T(8,128)S(1)} %get-tuple-element.140), channel_id=1, source_target_pairs={{0,2},{1,3},{2,0},{3,1},{4,6},{5,7},{6,4},{7,5},{8,10},{9,11},{10,... | collective-permute-start | bytes 49160 | tf_op jit(solution)/shard_map/ppermute | solution.py:571
  60.0 1.5 %collective-permute-start.26 = (f32[32,128]{1,0:T(8,128)S(1)}, f32[32,128]{1,0:T(8,128)S(1)}, u32[]{:S(2)}, u32[]{:S(2)}) collective-permute-start(f32[32,128]{1,0:T(8,128)S(1)} %get-tuple-element.142), channel_id=1, source_target_pairs={{0,8},{1,9},{2,10},{3,11},{4,12},{5,13},{6,14},{7,15},{8,0},{9,1},... | collective-permute-start | bytes 49160 | tf_op jit(solution)/shard_map/ppermute | solution.py:571
  61.5 2.0 %inside_last.1.vi = f32[12,32,128]{2,1,0:T(8,128)S(1)} custom-call(f32[16,32,128]{2,1,0:T(8,128)S(1)} %get-tuple-element.130.acc_ref, f32[4,32,128]{2,1,0:T(8,128)S(1)} %get-tuple-element.144.face_ref.wf, s32[7,16]{1,0:T(8,128)} %bitcast.5, f32[16,7,128,128]{3,2,1,0:T(8,128)} %tiles_ref.5), custom_call_target="tpu_custom_call" | custom-call | tf_op jit(solution)/shard_map/inside_last/pallas_call | solution.py:548
  63.5 0.2 collective-permute-done.26.in3
  63.7 1.0 %combine.1 = (f32[1,32,2048]{2,1,0:T(8,128)}, f32[1,32,2048]{2,1,0:T(8,128)}) custom-call(f32[32,2,128]{2,1,0:T(2,128)S(1)} %all-to-all-done.dots_ref, f32[32,128]{1,0:T(8,128)S(1)} %collective-permute-done.23.in0, f32[32,128]{1,0:T(8,128)S(1)} %collective-permute-done.24.in1, f32[32,128]{1,0:T(8,128)S(1)} %collective-permute-done.25.in2, ...), custom_call_target="tpu_custom_call" | custom-call | tf_op jit(solution)/shard_map/combine/pallas_call | solution.py:548
  (23 shorter events, 0.1 us)
Async XLA Ops:
  1.5 9.9 %collective-permute-start.4 = (f32[96,128]{1,0:T(8,128)S(1)}, f32[96,128]{1,0:T(8,128)S(1)}, u32[]{:S(2)}, u32[]{:S(2)}) collective-permute-start(f32[96,128]{1,0:T(8,128)S(1)} %get-tuple-element.86), channel_id=1, source_target_pairs={{0,3},{1,2},{2,1},{3,0},{4,7},{5,6},{6,5},{7,4},{8,11},{9,10},{10,... | collective-permute-start | bytes 147464 | tf_op jit(solution)/shard_map/ppermute | solution.py:571
  6.7 4.5 %collective-permute-start = (f32[48,128]{1,0:T(8,128)S(1)}, f32[48,128]{1,0:T(8,128)S(1)}, u32[]{:S(2)}, u32[]{:S(2)}) collective-permute-start(f32[48,128]{1,0:T(8,128)S(1)} %get-tuple-element.74.own0.refs_0_), channel_id=1, source_target_pairs={{0,1},{1,0},{2,3},{3,2},{4,5},{5,4},{6,7},{7,6},{8,9},{9,8},{10,11... | collective-permute-start | bytes 73736 | tf_op jit(solution)/shard_map/ppermute | solution.py:571
  6.7 4.8 %collective-permute-start.1 = (f32[48,128]{1,0:T(8,128)S(1)}, f32[48,128]{1,0:T(8,128)S(1)}, u32[]{:S(2)}, u32[]{:S(2)}) collective-permute-start(f32[48,128]{1,0:T(8,128)S(1)} %get-tuple-element.75.own1.refs_1_), channel_id=1, source_target_pairs={{0,2},{1,3},{2,0},{3,1},{4,6},{5,7},{6,4},{7,5},{8,10},{9,11},{10,... | collective-permute-start | bytes 73736 | tf_op jit(solution)/shard_map/ppermute | solution.py:571
  7.3 4.1 %collective-permute-start.2 = (f32[48,128]{1,0:T(8,128)S(1)}, f32[48,128]{1,0:T(8,128)S(1)}, u32[]{:S(2)}, u32[]{:S(2)}) collective-permute-start(f32[48,128]{1,0:T(8,128)S(1)} %get-tuple-element.76.own2.refs_2_), channel_id=1, source_target_pairs={{0,4},{1,5},{2,6},{3,7},{4,0},{5,1},{6,2},{7,3},{8,12},{9,13},{10,... | collective-permute-start | bytes 73736 | tf_op jit(solution)/shard_map/ppermute | solution.py:571
  7.3 4.1 %collective-permute-start.3 = (f32[48,128]{1,0:T(8,128)S(1)}, f32[48,128]{1,0:T(8,128)S(1)}, u32[]{:S(2)}, u32[]{:S(2)}) collective-permute-start(f32[48,128]{1,0:T(8,128)S(1)} %get-tuple-element.77.own3.refs_3_), channel_id=1, source_target_pairs={{0,8},{1,9},{2,10},{3,11},{4,12},{5,13},{6,14},{7,15},{8,0},{9,1},... | collective-permute-start | bytes 73736 | tf_op jit(solution)/shard_map/ppermute | solution.py:571
  12.2 10.4 %collective-permute-start.6 = (f32[176,128]{1,0:T(8,128)S(1)}, f32[176,128]{1,0:T(8,128)S(1)}, u32[]{:S(2)}, u32[]{:S(2)}) collective-permute-start(f32[176,128]{1,0:T(8,128)S(1)} %get-tuple-element.96), channel_id=1, source_target_pairs={{0,2},{1,3},{2,0},{3,1},{4,6},{5,7},{6,4},{7,5},{8,10},{9,11},{10,... | collective-permute-start | bytes 270344 | tf_op jit(solution)/shard_map/ppermute | solution.py:571
  14.3 8.3 %collective-permute-start.5 = (f32[168,128]{1,0:T(8,128)S(1)}, f32[168,128]{1,0:T(8,128)S(1)}, u32[]{:S(2)}, u32[]{:S(2)}) collective-permute-start(f32[168,128]{1,0:T(8,128)S(1)} %get-tuple-element.95), channel_id=1, source_target_pairs={{0,1},{1,0},{2,3},{3,2},{4,5},{5,4},{6,7},{7,6},{8,9},{9,8},{10,11... | collective-permute-start | bytes 258056 | tf_op jit(solution)/shard_map/ppermute | solution.py:571
  16.3 6.3 %collective-permute-start.7 = (f32[160,128]{1,0:T(8,128)S(1)}, f32[160,128]{1,0:T(8,128)S(1)}, u32[]{:S(2)}, u32[]{:S(2)}) collective-permute-start(f32[160,128]{1,0:T(8,128)S(1)} %get-tuple-element.97), channel_id=1, source_target_pairs={{0,3},{1,2},{2,1},{3,0},{4,7},{5,6},{6,5},{7,4},{8,11},{9,10},{10,... | collective-permute-start | bytes 245768 | tf_op jit(solution)/shard_map/ppermute | solution.py:571
  23.5 6.4 %collective-permute-start.8 = (f32[32,128]{1,0:T(8,128)S(1)}, f32[32,128]{1,0:T(8,128)S(1)}, u32[]{:S(2)}, u32[]{:S(2)}) collective-permute-start(f32[32,128]{1,0:T(8,128)S(1)} %get-tuple-element.104), channel_id=1, source_target_pairs={{0,1},{1,0},{2,3},{3,2},{4,5},{5,4},{6,7},{7,6},{8,9},{9,8},{10,11... | collective-permute-start | bytes 49160 | tf_op jit(solution)/shard_map/ppermute | solution.py:571
  24.7 5.2 %collective-permute-start.9 = (f32[32,128]{1,0:T(8,128)S(1)}, f32[32,128]{1,0:T(8,128)S(1)}, u32[]{:S(2)}, u32[]{:S(2)}) collective-permute-start(f32[32,128]{1,0:T(8,128)S(1)} %get-tuple-element.105), channel_id=1, source_target_pairs={{0,2},{1,3},{2,0},{3,1},{4,6},{5,7},{6,4},{7,5},{8,10},{9,11},{10,... | collective-permute-start | bytes 49160 | tf_op jit(solution)/shard_map/ppermute | solution.py:571
  26.4 3.5 %collective-permute-start.10 = (f32[32,128]{1,0:T(8,128)S(1)}, f32[32,128]{1,0:T(8,128)S(1)}, u32[]{:S(2)}, u32[]{:S(2)}) collective-permute-start(f32[32,128]{1,0:T(8,128)S(1)} %get-tuple-element.106), channel_id=1, source_target_pairs={{0,4},{1,5},{2,6},{3,7},{4,0},{5,1},{6,2},{7,3},{8,12},{9,13},{10,... | collective-permute-start | bytes 49160 | tf_op jit(solution)/shard_map/ppermute | solution.py:571
  26.4 3.7 %collective-permute-start.11 = (f32[32,128]{1,0:T(8,128)S(1)}, f32[32,128]{1,0:T(8,128)S(1)}, u32[]{:S(2)}, u32[]{:S(2)}) collective-permute-start(f32[32,128]{1,0:T(8,128)S(1)} %get-tuple-element.107), channel_id=1, source_target_pairs={{0,8},{1,9},{2,10},{3,11},{4,12},{5,13},{6,14},{7,15},{8,0},{9,1},... | collective-permute-start | bytes 49160 | tf_op jit(solution)/shard_map/ppermute | solution.py:571
  30.6 6.4 %collective-permute-start.12 = (f32[32,128]{1,0:T(8,128)S(1)}, f32[32,128]{1,0:T(8,128)S(1)}, u32[]{:S(2)}, u32[]{:S(2)}) collective-permute-start(f32[32,128]{1,0:T(8,128)S(1)} %get-tuple-element.114), channel_id=1, source_target_pairs={{0,1},{1,0},{2,3},{3,2},{4,5},{5,4},{6,7},{7,6},{8,9},{9,8},{10,11... | collective-permute-start | bytes 49160 | tf_op jit(solution)/shard_map/ppermute | solution.py:571
  32.6 4.6 %collective-permute-start.13 = (f32[32,128]{1,0:T(8,128)S(1)}, f32[32,128]{1,0:T(8,128)S(1)}, u32[]{:S(2)}, u32[]{:S(2)}) collective-permute-start(f32[32,128]{1,0:T(8,128)S(1)} %get-tuple-element.115), channel_id=1, source_target_pairs={{0,2},{1,3},{2,0},{3,1},{4,6},{5,7},{6,4},{7,5},{8,10},{9,11},{10,... | collective-permute-start | bytes 49160 | tf_op jit(solution)/shard_map/ppermute | solution.py:571
  33.5 3.7 %collective-permute-start.14 = (f32[32,128]{1,0:T(8,128)S(1)}, f32[32,128]{1,0:T(8,128)S(1)}, u32[]{:S(2)}, u32[]{:S(2)}) collective-permute-start(f32[32,128]{1,0:T(8,128)S(1)} %get-tuple-element.116), channel_id=1, source_target_pairs={{0,4},{1,5},{2,6},{3,7},{4,0},{5,1},{6,2},{7,3},{8,12},{9,13},{10,... | collective-permute-start | bytes 49160 | tf_op jit(solution)/shard_map/ppermute | solution.py:571
  33.5 3.7 %collective-permute-start.15 = (f32[32,128]{1,0:T(8,128)S(1)}, f32[32,128]{1,0:T(8,128)S(1)}, u32[]{:S(2)}, u32[]{:S(2)}) collective-permute-start(f32[32,128]{1,0:T(8,128)S(1)} %get-tuple-element.117), channel_id=1, source_target_pairs={{0,8},{1,9},{2,10},{3,11},{4,12},{5,13},{6,14},{7,15},{8,0},{9,1},... | collective-permute-start | bytes 49160 | tf_op jit(solution)/shard_map/ppermute | solution.py:571
  37.4 6.7 %collective-permute-start.18 = (f32[32,128]{1,0:T(8,128)S(1)}, f32[32,128]{1,0:T(8,128)S(1)}, u32[]{:S(2)}, u32[]{:S(2)}) collective-permute-start(f32[32,128]{1,0:T(8,128)S(1)} %get-tuple-element.119.refs_0_), channel_id=1, source_target_pairs={{0,3},{1,2},{2,1},{3,0},{4,7},{5,6},{6,5},{7,4},{8,11},{9,10},{10,... | collective-permute-start | bytes 49160 | tf_op jit(solution)/shard_map/ppermute | solution.py:571
  39.1 5.0 %collective-permute-start.17 = (f32[32,128]{1,0:T(8,128)S(1)}, f32[32,128]{1,0:T(8,128)S(1)}, u32[]{:S(2)}, u32[]{:S(2)}) collective-permute-start(f32[32,128]{1,0:T(8,128)S(1)} %get-tuple-element.119.refs_0_), channel_id=1, source_target_pairs={{0,2},{1,3},{2,0},{3,1},{4,6},{5,7},{6,4},{7,5},{8,10},{9,11},{10,... | collective-permute-start | bytes 49160 | tf_op jit(solution)/shard_map/ppermute | solution.py:571
  39.5 4.6 %collective-permute-start.16 = (f32[32,128]{1,0:T(8,128)S(1)}, f32[32,128]{1,0:T(8,128)S(1)}, u32[]{:S(2)}, u32[]{:S(2)}) collective-permute-start(f32[32,128]{1,0:T(8,128)S(1)} %get-tuple-element.119.refs_0_), channel_id=1, source_target_pairs={{0,1},{1,0},{2,3},{3,2},{4,5},{5,4},{6,7},{7,6},{8,9},{9,8},{10,11... | collective-permute-start | bytes 49160 | tf_op jit(solution)/shard_map/ppermute | solution.py:571
  44.7 6.1 %collective-permute-start.19 = (f32[32,128]{1,0:T(8,128)S(1)}, f32[32,128]{1,0:T(8,128)S(1)}, u32[]{:S(2)}, u32[]{:S(2)}) collective-permute-start(f32[32,128]{1,0:T(8,128)S(1)} %get-tuple-element.131), channel_id=1, source_target_pairs={{0,1},{1,0},{2,3},{3,2},{4,5},{5,4},{6,7},{7,6},{8,9},{9,8},{10,11... | collective-permute-start | bytes 49160 | tf_op jit(solution)/shard_map/ppermute | solution.py:571
  46.2 4.8 %collective-permute-start.20 = (f32[32,128]{1,0:T(8,128)S(1)}, f32[32,128]{1,0:T(8,128)S(1)}, u32[]{:S(2)}, u32[]{:S(2)}) collective-permute-start(f32[32,128]{1,0:T(8,128)S(1)} %get-tuple-element.132), channel_id=1, source_target_pairs={{0,2},{1,3},{2,0},{3,1},{4,6},{5,7},{6,4},{7,5},{8,10},{9,11},{10,... | collective-permute-start | bytes 49160 | tf_op jit(solution)/shard_map/ppermute | solution.py:571
  47.3 3.7 %collective-permute-start.21 = (f32[32,128]{1,0:T(8,128)S(1)}, f32[32,128]{1,0:T(8,128)S(1)}, u32[]{:S(2)}, u32[]{:S(2)}) collective-permute-start(f32[32,128]{1,0:T(8,128)S(1)} %get-tuple-element.133), channel_id=1, source_target_pairs={{0,4},{1,5},{2,6},{3,7},{4,0},{5,1},{6,2},{7,3},{8,12},{9,13},{10,... | collective-permute-start | bytes 49160 | tf_op jit(solution)/shard_map/ppermute | solution.py:571
  47.3 3.7 %collective-permute-start.22 = (f32[32,128]{1,0:T(8,128)S(1)}, f32[32,128]{1,0:T(8,128)S(1)}, u32[]{:S(2)}, u32[]{:S(2)}) collective-permute-start(f32[32,128]{1,0:T(8,128)S(1)} %get-tuple-element.134), channel_id=1, source_target_pairs={{0,8},{1,9},{2,10},{3,11},{4,12},{5,13},{6,14},{7,15},{8,0},{9,1},... | collective-permute-start | bytes 49160 | tf_op jit(solution)/shard_map/ppermute | solution.py:571
  52.1 11.7 %all-to-all-start = ((f32[32,2,128]{2,1,0:T(2,128)}), f32[32,2,128]{2,1,0:T(2,128)S(1)}, u32[]{:S(2)}, u32[]{:S(2)}) async-start(f32[32,2,128]{2,1,0:T(2,128)} %get-tuple-element.138), calls=%async_computation | async-start | bytes 65536 | tf_op jit(solution)/shard_map/all_to_all | solution.py:673
  55.7 7.7 %collective-permute-start.23 = (f32[32,128]{1,0:T(8,128)S(1)}, f32[32,128]{1,0:T(8,128)S(1)}, u32[]{:S(2)}, u32[]{:S(2)}) collective-permute-start(f32[32,128]{1,0:T(8,128)S(1)} %get-tuple-element.139), channel_id=1, source_target_pairs={{0,1},{1,0},{2,3},{3,2},{4,5},{5,4},{6,7},{7,6},{8,9},{9,8},{10,11... | collective-permute-start | bytes 49160 | tf_op jit(solution)/shard_map/ppermute | solution.py:571
  57.6 5.9 %collective-permute-start.24 = (f32[32,128]{1,0:T(8,128)S(1)}, f32[32,128]{1,0:T(8,128)S(1)}, u32[]{:S(2)}, u32[]{:S(2)}) collective-permute-start(f32[32,128]{1,0:T(8,128)S(1)} %get-tuple-element.140), channel_id=1, source_target_pairs={{0,2},{1,3},{2,0},{3,1},{4,6},{5,7},{6,4},{7,5},{8,10},{9,11},{10,... | collective-permute-start | bytes 49160 | tf_op jit(solution)/shard_map/ppermute | solution.py:571
  60.0 3.5 %collective-permute-start.25 = (f32[32,128]{1,0:T(8,128)S(1)}, f32[32,128]{1,0:T(8,128)S(1)}, u32[]{:S(2)}, u32[]{:S(2)}) collective-permute-start(f32[32,128]{1,0:T(8,128)S(1)} %get-tuple-element.141), channel_id=1, source_target_pairs={{0,4},{1,5},{2,6},{3,7},{4,0},{5,1},{6,2},{7,3},{8,12},{9,13},{10,... | collective-permute-start | bytes 49160 | tf_op jit(solution)/shard_map/ppermute | solution.py:571
  60.0 3.7 %collective-permute-start.26 = (f32[32,128]{1,0:T(8,128)S(1)}, f32[32,128]{1,0:T(8,128)S(1)}, u32[]{:S(2)}, u32[]{:S(2)}) collective-permute-start(f32[32,128]{1,0:T(8,128)S(1)} %get-tuple-element.142), channel_id=1, source_target_pairs={{0,8},{1,9},{2,10},{3,11},{4,12},{5,13},{6,14},{7,15},{8,0},{9,1},... | collective-permute-start | bytes 49160 | tf_op jit(solution)/shard_map/ppermute | solution.py:571

commit v7 on v6

--- a/solution.py
+++ b/solution.py
@@ -14,7 +14,7 @@
 OCAP = 8
 SCAP = 2
 EARLY = 6
-LINE_PADS = (8, 16, 0)
+LINE_PADS = (0, 8, 0)
 CHUNKS = (4, 2)
 NB = 16
 TPR = 7
@@ -583,7 +583,7 @@
     nf = NF * BS
     width = line * CB * CW
     target, for_far, column, weight, *sides = call(
-        prepare_body, "prepare", [f32(8, BS), f32(NRHS + 64, BS), jax.ShapeDtypeStruct((2, BS, BS), jnp.int32), f32(2 * NF, BS)] + [side] * NF, [HBM] * 4,
+        prepare_body, "prepare", [f32(8, BS), f32(NRHS + 24, BS), jax.ShapeDtypeStruct((2, BS, BS), jnp.int32), f32(2 * NF, BS)] + [side] * NF, [HBM] * 4,
         load_vector, row_map, coarse_id, face_link,
         scratch=[pltpu.SMEM((1, CB), jnp.int32), pltpu.SMEM((1, NF), jnp.int32),
                  pltpu.VMEM((1, NF, BS), jnp.int32), (NRHS, nf)],

time: 65 us -> 64.8 us (level)
  transfers between devices with their start and end apart: 28 -> 28, of which waited for: 6 -> 6; matrix products, arithmetic and copies ran while one was open for 0% -> 0% of each run, Pallas kernels for 26% -> 27%
where the time goes in v7:
time: 64.8 us; the launch traced here: 64.5 us
  starting transfers between devices  36.9 us (57%)
  Pallas kernels  22.9 us (35%)
  waiting for transfers between devices  3.91 us (6%)
  between operations  0.84 us (1%)
    ppermute x27, starting transfers between devices, trade(): return lax.ppermute(value, AXES, [(i, i ^ mask) for i in range(devices)])  33.2 us
    pallas_call x15, Pallas kernels, call(): pl.pallas_call(body, name=name, out_shape=outs, in_specs=specs, out_specs...  22.9 us
    ppermute x27, waiting for transfers between devices, trade(): return lax.ppermute(value, AXES, [(i, i ^ mask) for i in range(devices)])  3.9 us
    all_to_all x1, starting transfers between devices, on_device(): spread = lax.all_to_all(dots, AXES, 0, 0)  3.66 us
  transfers between devices with their start and end apart: 28, of which 6 were waited for; matrix products, arithmetic and copies ran while one was open for 0% of the time, Pallas kernels for 27%

profile of v7, /device:TPU:0, one launch (start us, length us, event | category | flops | bytes accessed | tf_op | source)
XLA Modules:
  0.0 64.5 jit_solution(11620599780300101854)
XLA Ops:
  0.6 0.9 %prepare.1 = (f32[8,128]{1,0:T(8,128)S(1)}, f32[56,128]{1,0:T(8,128)S(1)}, s32[2,128,128]{2,1,0:T(8,128)S(1)}, f32[8,128]{1,0:T(8,128)S(1)}, f32[48,128]{1,0:T(8...) custom-call(f32[1,32,2048]{2,1,0:T(8,128)} %load_hbm.1, s32[1,4,128]{2,1,0:T(4,128)} %map_ref.1, ...), custom_call_target="tpu_custom_call" | custom-call | tf_op jit(solution)/shard_map/prepare/pallas_call | solution.py:548
  1.5 5.1 %collective-permute-start.4 = (f32[56,128]{1,0:T(8,128)S(1)}, f32[56,128]{1,0:T(8,128)S(1)}, u32[]{:S(2)}, u32[]{:S(2)}) collective-permute-start(f32[56,128]{1,0:T(8,128)S(1)} %get-tuple-element.86), channel_id=1, source_target_pairs={{0,3},{1,2},{2,1},{3,0},{4,7},{5,6},{6,5},{7,4},{8,11},{9,10},{10,... | collective-permute-start | bytes 86024 | tf_op jit(solution)/shard_map/ppermute | solution.py:571
  6.7 0.6 collective-permute-start.1
  7.3 1.6 %collective-permute-start.3 = (f32[48,128]{1,0:T(8,128)S(1)}, f32[48,128]{1,0:T(8,128)S(1)}, u32[]{:S(2)}, u32[]{:S(2)}) collective-permute-start(f32[48,128]{1,0:T(8,128)S(1)} %get-tuple-element.77.own3.refs_3_), channel_id=1, source_target_pairs={{0,8},{1,9},{2,10},{3,11},{4,12},{5,13},{6,14},{7,15},{8,0},{9,1},... | collective-permute-start | bytes 73736 | tf_op jit(solution)/shard_map/ppermute | solution.py:571
  8.9 2.3 %inside_load.1 = (f32[12,32,128]{2,1,0:T(8,128)S(1)}, f32[32,128]{1,0:T(8,128)S(1)}, bf16[512,512]{1,0:T(8,128)(2,1)S(1)}, bf16[512,512]{1,0:T(8,128)(2,1)S(1)},...) custom-call(f32[1,32,2048]{2,1,0:T(8,128)} %load_hbm.1, ...), custom_call_target="tpu_custom_call" | custom-call | tf_op jit(solution)/shard_map/inside_load/pallas_call | solution.py:548
  11.2 0.0 collective-permute-done.refs_4_
  11.2 0.2 collective-permute-done.1.refs_5_
  11.4 0.8 %faces_load.1 = (f32[4,32,128]{2,1,0:T(8,128)S(1)}, f32[32,128]{1,0:T(8,128)S(1)}, f32[1,512]{1,0:T(1,128)S(1)}, f32[160,128]{1,0:T(8,128)S(1)}, f32[168,128]{1,0:T(8,128)S(1)}, /*index=5*/f32[160,128]{1,0:T(8,128)S(1)}) custom-call(f32[48,128]{1,0:T(8,128)S(1)} %get-tuple-element.74.own0.refs_0_, f32[48,128]{1,0:T(8,128)S(1)} %get-tuple-element.75.own1.refs_1_, ...), custom_call_target="tpu_custom_call" | custom-call | tf_op jit(solution)/shard_map/faces_load/pallas_call | solution.py:548
  12.2 2.1 %collective-permute-start.6 = (f32[168,128]{1,0:T(8,128)S(1)}, f32[168,128]{1,0:T(8,128)S(1)}, u32[]{:S(2)}, u32[]{:S(2)}) collective-permute-start(f32[168,128]{1,0:T(8,128)S(1)} %get-tuple-element.96), channel_id=1, source_target_pairs={{0,2},{1,3},{2,0},{3,1},{4,6},{5,7},{6,4},{7,5},{8,10},{9,11},{10,... | collective-permute-start | bytes 258056 | tf_op jit(solution)/shard_map/ppermute | solution.py:571
  14.3 2.0 %collective-permute-start.5 = (f32[160,128]{1,0:T(8,128)S(1)}, f32[160,128]{1,0:T(8,128)S(1)}, u32[]{:S(2)}, u32[]{:S(2)}) collective-permute-start(f32[160,128]{1,0:T(8,128)S(1)} %get-tuple-element.95), channel_id=1, source_target_pairs={{0,1},{1,0},{2,3},{3,2},{4,5},{5,4},{6,7},{7,6},{8,9},{9,8},{10,11... | collective-permute-start | bytes 245768 | tf_op jit(solution)/shard_map/ppermute | solution.py:571
  16.3 0.4 collective-permute-start.7
  16.7 3.0 %under_line.1 = (bf16[4,4,128,128]{3,2,1,0:T(8,128)(2,1)S(1)}, bf16[4,4,128,128]{3,2,1,0:T(8,128)(2,1)S(1)}, f32[4,32,128]{2,1,0:T(8,128)S(1)}, bf16[4,128,128]{...) custom-call(f32[48,128]{1,0:T(8,128)S(1)} %get-tuple-element.74.own0, ...), custom_call_target="tpu_custom_call" | custom-call | tf_op jit(solution)/shard_map/under_line/pallas_call | solution.py:548
  19.7 2.9 %collective-permute-done.7.refs_6_.refs_11_ = f32[160,128]{1,0:T(8,128)S(1)} collective-permute-done((f32[160,128]{1,0:T(8,128)S(1)}, f32[160,128]{1,0:T(8,128)S(1)}, u32[]{:S(2)}, u32[]{:S(2)}) %collective-permute-start.7) | collective-permute-done | bytes 81952 | tf_op jit(solution)/shard_map/ppermute | solution.py:571
  22.6 0.0 collective-permute-done.6.refs_5_.refs_10_
  22.6 1.0 %coarse_load.1 = (f32[32,128]{1,0:T(8,128)S(1)}, f32[4,32,128]{2,1,0:T(8,128)S(1)}, f32[32,128]{1,0:T(8,128)S(1)}, f32[32,128]{1,0:T(8,128)S(1)}, f32[32,128]{1,0:T(8,128)S(1)}, /*index=5*/f32[32,128]{1,0:T(8,128)S(1)}) custom-call(f32[32,128]{1,0:T(8,128)S(1)} %get-tuple-element.87.refs_0_, f32[128,128]{1,0:T(8,128)S(1)} %get-tuple-element.92.refs_1_.refs_2_, ...), custom_call_target="tpu_custom_call" | custom-call | tf_op jit(solution)/shard_map/coarse_load/pallas_call | solution.py:548
  23.5 1.0 %collective-permute-start.8 = (f32[32,128]{1,0:T(8,128)S(1)}, f32[32,128]{1,0:T(8,128)S(1)}, u32[]{:S(2)}, u32[]{:S(2)}) collective-permute-start(f32[32,128]{1,0:T(8,128)S(1)} %get-tuple-element.104), channel_id=1, source_target_pairs={{0,1},{1,0},{2,3},{3,2},{4,5},{5,4},{6,7},{7,6},{8,9},{9,8},{10,11... | collective-permute-start | bytes 49160 | tf_op jit(solution)/shard_map/ppermute | solution.py:571
  24.6 1.7 %collective-permute-start.9 = (f32[32,128]{1,0:T(8,128)S(1)}, f32[32,128]{1,0:T(8,128)S(1)}, u32[]{:S(2)}, u32[]{:S(2)}) collective-permute-start(f32[32,128]{1,0:T(8,128)S(1)} %get-tuple-element.105), channel_id=1, source_target_pairs={{0,2},{1,3},{2,0},{3,1},{4,6},{5,7},{6,4},{7,5},{8,10},{9,11},{10,... | collective-permute-start | bytes 49160 | tf_op jit(solution)/shard_map/ppermute | solution.py:571
  26.2 0.0 collective-permute-start.10
  26.3 1.1 %collective-permute-start.11 = (f32[32,128]{1,0:T(8,128)S(1)}, f32[32,128]{1,0:T(8,128)S(1)}, u32[]{:S(2)}, u32[]{:S(2)}) collective-permute-start(f32[32,128]{1,0:T(8,128)S(1)} %get-tuple-element.107), channel_id=1, source_target_pairs={{0,8},{1,9},{2,10},{3,11},{4,12},{5,13},{6,14},{7,15},{8,0},{9,1},... | collective-permute-start | bytes 49160 | tf_op jit(solution)/shard_map/ppermute | solution.py:571
  27.4 2.3 %own_first.1 = (f32[12,32,128]{2,1,0:T(8,128)S(1)}, f32[16,32,128]{2,1,0:T(8,128)S(1)}) custom-call(f32[12,32,128]{2,1,0:T(8,128)S(1)} %get-tuple-element.78.refs_0_, f32[32,128]{1,0:T(8,128)S(1)} %get-tuple-element.100.refs_1_, f32[6,7,128,128]{3,2,1,0:T(8,128)S(1)} %get-tuple-element.101.refs_2_, f32[128,1536]{1,0:T(8,128)S(1)} %get-tuple-element.102.refs_3_, ...), custom_call_target="tpu_custom_call" | custom-call | tf_op jit(solution)/shard_map/own_first/pallas_call | solution.py:548
  29.8 0.2 collective-permute-done.11.in3
  30.0 0.4 face_first.1
  30.4 2.0 %collective-permute-start.12 = (f32[32,128]{1,0:T(8,128)S(1)}, f32[32,128]{1,0:T(8,128)S(1)}, u32[]{:S(2)}, u32[]{:S(2)}) collective-permute-start(f32[32,128]{1,0:T(8,128)S(1)} %get-tuple-element.114), channel_id=1, source_target_pairs={{0,1},{1,0},{2,3},{3,2},{4,5},{5,4},{6,7},{7,6},{8,9},{9,8},{10,11... | collective-permute-start | bytes 49160 | tf_op jit(solution)/shard_map/ppermute | solution.py:571
  32.4 0.9 %collective-permute-start.13 = (f32[32,128]{1,0:T(8,128)S(1)}, f32[32,128]{1,0:T(8,128)S(1)}, u32[]{:S(2)}, u32[]{:S(2)}) collective-permute-start(f32[32,128]{1,0:T(8,128)S(1)} %get-tuple-element.115), channel_id=1, source_target_pairs={{0,2},{1,3},{2,0},{3,1},{4,6},{5,7},{6,4},{7,5},{8,10},{9,11},{10,... | collective-permute-start | bytes 49160 | tf_op jit(solution)/shard_map/ppermute | solution.py:571
  33.3 0.8 %collective-permute-start.15 = (f32[32,128]{1,0:T(8,128)S(1)}, f32[32,128]{1,0:T(8,128)S(1)}, u32[]{:S(2)}, u32[]{:S(2)}) collective-permute-start(f32[32,128]{1,0:T(8,128)S(1)} %get-tuple-element.117), channel_id=1, source_target_pairs={{0,8},{1,9},{2,10},{3,11},{4,12},{5,13},{6,14},{7,15},{8,0},{9,1},... | collective-permute-start | bytes 49160 | tf_op jit(solution)/shard_map/ppermute | solution.py:571
  34.1 2.7 %inside_image.1 = (f32[12,32,128]{2,1,0:T(8,128)S(1)}, f32[12,32,128]{2,1,0:T(8,128)S(1)}, f32[32,128]{1,0:T(8,128)S(1)}) custom-call(f32[16,32,128]{2,1,0:T(8,128)S(1)} %get-tuple-element.103.acc_ref, f32[4,32,128]{2,1,0:T(8,128)S(1)} %get-tuple-element.111.face_ref.zf, s32[7,16]{1,0:T(8,128)} %bitcast.3, f32[16,7,128,128]{3,2,1,0:T(8,128)} %tiles_ref.5, ...), custom_call_target="tpu_custom_call" | custom-call | tf_op jit(solution)/shard_map/inside_image/pallas_call | solution.py:548
  36.9 0.2 collective-permute-done.13.in1
  37.0 0.0 collective-permute-done.15.in3
  37.0 0.2 faces_image.1
  37.2 1.7 %collective-permute-start.18 = (f32[32,128]{1,0:T(8,128)S(1)}, f32[32,128]{1,0:T(8,128)S(1)}, u32[]{:S(2)}, u32[]{:S(2)}) collective-permute-start(f32[32,128]{1,0:T(8,128)S(1)} %get-tuple-element.119.refs_0_), channel_id=1, source_target_pairs={{0,3},{1,2},{2,1},{3,0},{4,7},{5,6},{6,5},{7,4},{8,11},{9,10},{10,... | collective-permute-start | bytes 49160 | tf_op jit(solution)/shard_map/ppermute | solution.py:571
  38.9 0.4 collective-permute-start.17
  39.4 2.3 %collective-permute-start.16 = (f32[32,128]{1,0:T(8,128)S(1)}, f32[32,128]{1,0:T(8,128)S(1)}, u32[]{:S(2)}, u32[]{:S(2)}) collective-permute-start(f32[32,128]{1,0:T(8,128)S(1)} %get-tuple-element.119.refs_0_), channel_id=1, source_target_pairs={{0,1},{1,0},{2,3},{3,2},{4,5},{5,4},{6,7},{7,6},{8,9},{9,8},{10,11... | collective-permute-start | bytes 49160 | tf_op jit(solution)/shard_map/ppermute | solution.py:571
  41.7 2.3 %table.1 = (bf16[128,512]{1,0:T(8,128)(2,1)S(1)}, bf16[128,512]{1,0:T(8,128)(2,1)S(1)}, f32[4,32,128]{2,1,0:T(8,128)S(1)}, f32[6,7,128,128]{3,2,1,0:T(8,128)S(1)}, f32[128,1536]{1,0:T(8,128)S(1)}) custom-call(f32[16,7,128,128]{3,2,1,0:T(8,128)} %tiles_ref.5, f32[1,128,2048]{2,1,0:T(8,128)} %refs_1_.1, f32[128,128]{1,0:T(8,128)S(1)} %get-tuple-element.92.refs_1_.refs_2_, ...), custom_call_target="tpu_custom_call" | custom-call | tf_op jit(solution)/shard_map/table/pallas_call | solution.py:548
  44.0 0.6 coarse_image.1
  44.6 1.5 %collective-permute-start.19 = (f32[32,128]{1,0:T(8,128)S(1)}, f32[32,128]{1,0:T(8,128)S(1)}, u32[]{:S(2)}, u32[]{:S(2)}) collective-permute-start(f32[32,128]{1,0:T(8,128)S(1)} %get-tuple-element.131), channel_id=1, source_target_pairs={{0,1},{1,0},{2,3},{3,2},{4,5},{5,4},{6,7},{7,6},{8,9},{9,8},{10,11... | collective-permute-start | bytes 49160 | tf_op jit(solution)/shard_map/ppermute | solution.py:571
  46.0 1.1 %collective-permute-start.20 = (f32[32,128]{1,0:T(8,128)S(1)}, f32[32,128]{1,0:T(8,128)S(1)}, u32[]{:S(2)}, u32[]{:S(2)}) collective-permute-start(f32[32,128]{1,0:T(8,128)S(1)} %get-tuple-element.132), channel_id=1, source_target_pairs={{0,2},{1,3},{2,0},{3,1},{4,6},{5,7},{6,4},{7,5},{8,10},{9,11},{10,... | collective-permute-start | bytes 49160 | tf_op jit(solution)/shard_map/ppermute | solution.py:571
  47.2 1.1 %collective-permute-start.22 = (f32[32,128]{1,0:T(8,128)S(1)}, f32[32,128]{1,0:T(8,128)S(1)}, u32[]{:S(2)}, u32[]{:S(2)}) collective-permute-start(f32[32,128]{1,0:T(8,128)S(1)} %get-tuple-element.134), channel_id=1, source_target_pairs={{0,8},{1,9},{2,10},{3,11},{4,12},{5,13},{6,14},{7,15},{8,0},{9,1},... | collective-permute-start | bytes 49160 | tf_op jit(solution)/shard_map/ppermute | solution.py:571
  48.2 2.5 %own_second.1 = (f32[12,32,128]{2,1,0:T(8,128)S(1)}, f32[16,32,128]{2,1,0:T(8,128)S(1)}, f32[5,32,128]{2,1,0:T(8,128)S(1)}, f32[16,32,128]{2,1,0:T(8,128)S(1)}) custom-call(f32[12,32,128]{2,1,0:T(8,128)S(1)} %get-tuple-element.112.inner_ref, f32[32,128]{1,0:T(8,128)S(1)} %get-tuple-element.125.back_ref, f32[6,7,128,128]{3,2,1,0:T(8,128)S(1)} %get-tuple-element.126.early_ref, ...), custom_call_target="tpu_custom_call" | custom-call | tf_op jit(solution)/shard_map/own_second/pallas_call | solution.py:548
  50.7 0.1 collective-permute-done.20.in1
  50.8 0.0 collective-permute-done.22.in3
  50.9 1.0 %face_second.1 = (f32[4,32,128]{2,1,0:T(8,128)S(1)}, f32[4,32,128]{2,1,0:T(8,128)S(1)}, f32[32,2,128]{2,1,0:T(2,128)}, f32[32,128]{1,0:T(8,128)S(1)}, f32[32,128...) custom-call(f32[16,32,128]{2,1,0:T(8,128)S(1)} %get-tuple-element.130.acc_ref, ...), custom_call_target="tpu_custom_call" | custom-call | tf_op jit(solution)/shard_map/face_second/pallas_call | solution.py:548
  51.9 3.7 %all-to-all-start = ((f32[32,2,128]{2,1,0:T(2,128)}), f32[32,2,128]{2,1,0:T(2,128)S(1)}, u32[]{:S(2)}, u32[]{:S(2)}) async-start(f32[32,2,128]{2,1,0:T(2,128)} %get-tuple-element.138), calls=%async_computation | async-start | bytes 65536 | tf_op jit(solution)/shard_map/all_to_all | solution.py:673
  55.6 1.8 %collective-permute-start.23 = (f32[32,128]{1,0:T(8,128)S(1)}, f32[32,128]{1,0:T(8,128)S(1)}, u32[]{:S(2)}, u32[]{:S(2)}) collective-permute-start(f32[32,128]{1,0:T(8,128)S(1)} %get-tuple-element.139), channel_id=1, source_target_pairs={{0,1},{1,0},{2,3},{3,2},{4,5},{5,4},{6,7},{7,6},{8,9},{9,8},{10,11... | collective-permute-start | bytes 49160 | tf_op jit(solution)/shard_map/ppermute | solution.py:571
  57.4 2.4 %collective-permute-start.24 = (f32[32,128]{1,0:T(8,128)S(1)}, f32[32,128]{1,0:T(8,128)S(1)}, u32[]{:S(2)}, u32[]{:S(2)}) collective-permute-start(f32[32,128]{1,0:T(8,128)S(1)} %get-tuple-element.140), channel_id=1, source_target_pairs={{0,2},{1,3},{2,0},{3,1},{4,6},{5,7},{6,4},{7,5},{8,10},{9,11},{10,... | collective-permute-start | bytes 49160 | tf_op jit(solution)/shard_map/ppermute | solution.py:571
  59.8 1.5 %collective-permute-start.26 = (f32[32,128]{1,0:T(8,128)S(1)}, f32[32,128]{1,0:T(8,128)S(1)}, u32[]{:S(2)}, u32[]{:S(2)}) collective-permute-start(f32[32,128]{1,0:T(8,128)S(1)} %get-tuple-element.142), channel_id=1, source_target_pairs={{0,8},{1,9},{2,10},{3,11},{4,12},{5,13},{6,14},{7,15},{8,0},{9,1},... | collective-permute-start | bytes 49160 | tf_op jit(solution)/shard_map/ppermute | solution.py:571
  61.3 2.0 %inside_last.1.vi = f32[12,32,128]{2,1,0:T(8,128)S(1)} custom-call(f32[16,32,128]{2,1,0:T(8,128)S(1)} %get-tuple-element.130.acc_ref, f32[4,32,128]{2,1,0:T(8,128)S(1)} %get-tuple-element.144.face_ref.wf, s32[7,16]{1,0:T(8,128)} %bitcast.5, f32[16,7,128,128]{3,2,1,0:T(8,128)} %tiles_ref.5), custom_call_target="tpu_custom_call" | custom-call | tf_op jit(solution)/shard_map/inside_last/pallas_call | solution.py:548
  63.3 0.2 collective-permute-done.26.in3
  63.6 1.0 %combine.1 = (f32[1,32,2048]{2,1,0:T(8,128)}, f32[1,32,2048]{2,1,0:T(8,128)}) custom-call(f32[32,2,128]{2,1,0:T(2,128)S(1)} %all-to-all-done.dots_ref, f32[32,128]{1,0:T(8,128)S(1)} %collective-permute-done.23.in0, f32[32,128]{1,0:T(8,128)S(1)} %collective-permute-done.24.in1, f32[32,128]{1,0:T(8,128)S(1)} %collective-permute-done.25.in2, ...), custom_call_target="tpu_custom_call" | custom-call | tf_op jit(solution)/shard_map/combine/pallas_call | solution.py:548
  (23 shorter events, 0.1 us)
Async XLA Ops:
  1.5 9.9 %collective-permute-start.4 = (f32[56,128]{1,0:T(8,128)S(1)}, f32[56,128]{1,0:T(8,128)S(1)}, u32[]{:S(2)}, u32[]{:S(2)}) collective-permute-start(f32[56,128]{1,0:T(8,128)S(1)} %get-tuple-element.86), channel_id=1, source_target_pairs={{0,3},{1,2},{2,1},{3,0},{4,7},{5,6},{6,5},{7,4},{8,11},{9,10},{10,... | collective-permute-start | bytes 86024 | tf_op jit(solution)/shard_map/ppermute | solution.py:571
  6.7 4.5 %collective-permute-start = (f32[48,128]{1,0:T(8,128)S(1)}, f32[48,128]{1,0:T(8,128)S(1)}, u32[]{:S(2)}, u32[]{:S(2)}) collective-permute-start(f32[48,128]{1,0:T(8,128)S(1)} %get-tuple-element.74.own0.refs_0_), channel_id=1, source_target_pairs={{0,1},{1,0},{2,3},{3,2},{4,5},{5,4},{6,7},{7,6},{8,9},{9,8},{10,11... | collective-permute-start | bytes 73736 | tf_op jit(solution)/shard_map/ppermute | solution.py:571
  6.7 4.8 %collective-permute-start.1 = (f32[48,128]{1,0:T(8,128)S(1)}, f32[48,128]{1,0:T(8,128)S(1)}, u32[]{:S(2)}, u32[]{:S(2)}) collective-permute-start(f32[48,128]{1,0:T(8,128)S(1)} %get-tuple-element.75.own1.refs_1_), channel_id=1, source_target_pairs={{0,2},{1,3},{2,0},{3,1},{4,6},{5,7},{6,4},{7,5},{8,10},{9,11},{10,... | collective-permute-start | bytes 73736 | tf_op jit(solution)/shard_map/ppermute | solution.py:571
  7.3 4.1 %collective-permute-start.2 = (f32[48,128]{1,0:T(8,128)S(1)}, f32[48,128]{1,0:T(8,128)S(1)}, u32[]{:S(2)}, u32[]{:S(2)}) collective-permute-start(f32[48,128]{1,0:T(8,128)S(1)} %get-tuple-element.76.own2.refs_2_), channel_id=1, source_target_pairs={{0,4},{1,5},{2,6},{3,7},{4,0},{5,1},{6,2},{7,3},{8,12},{9,13},{10,... | collective-permute-start | bytes 73736 | tf_op jit(solution)/shard_map/ppermute | solution.py:571
  7.3 4.1 %collective-permute-start.3 = (f32[48,128]{1,0:T(8,128)S(1)}, f32[48,128]{1,0:T(8,128)S(1)}, u32[]{:S(2)}, u32[]{:S(2)}) collective-permute-start(f32[48,128]{1,0:T(8,128)S(1)} %get-tuple-element.77.own3.refs_3_), channel_id=1, source_target_pairs={{0,8},{1,9},{2,10},{3,11},{4,12},{5,13},{6,14},{7,15},{8,0},{9,1},... | collective-permute-start | bytes 73736 | tf_op jit(solution)/shard_map/ppermute | solution.py:571
  12.2 10.4 %collective-permute-start.6 = (f32[168,128]{1,0:T(8,128)S(1)}, f32[168,128]{1,0:T(8,128)S(1)}, u32[]{:S(2)}, u32[]{:S(2)}) collective-permute-start(f32[168,128]{1,0:T(8,128)S(1)} %get-tuple-element.96), channel_id=1, source_target_pairs={{0,2},{1,3},{2,0},{3,1},{4,6},{5,7},{6,4},{7,5},{8,10},{9,11},{10,... | collective-permute-start | bytes 258056 | tf_op jit(solution)/shard_map/ppermute | solution.py:571
  14.3 5.5 %collective-permute-start.5 = (f32[160,128]{1,0:T(8,128)S(1)}, f32[160,128]{1,0:T(8,128)S(1)}, u32[]{:S(2)}, u32[]{:S(2)}) collective-permute-start(f32[160,128]{1,0:T(8,128)S(1)} %get-tuple-element.95), channel_id=1, source_target_pairs={{0,1},{1,0},{2,3},{3,2},{4,5},{5,4},{6,7},{7,6},{8,9},{9,8},{10,11... | collective-permute-start | bytes 245768 | tf_op jit(solution)/shard_map/ppermute | solution.py:571
  16.3 6.3 %collective-permute-start.7 = (f32[160,128]{1,0:T(8,128)S(1)}, f32[160,128]{1,0:T(8,128)S(1)}, u32[]{:S(2)}, u32[]{:S(2)}) collective-permute-start(f32[160,128]{1,0:T(8,128)S(1)} %get-tuple-element.97), channel_id=1, source_target_pairs={{0,3},{1,2},{2,1},{3,0},{4,7},{5,6},{6,5},{7,4},{8,11},{9,10},{10,... | collective-permute-start | bytes 245768 | tf_op jit(solution)/shard_map/ppermute | solution.py:571
  23.5 6.2 %collective-permute-start.8 = (f32[32,128]{1,0:T(8,128)S(1)}, f32[32,128]{1,0:T(8,128)S(1)}, u32[]{:S(2)}, u32[]{:S(2)}) collective-permute-start(f32[32,128]{1,0:T(8,128)S(1)} %get-tuple-element.104), channel_id=1, source_target_pairs={{0,1},{1,0},{2,3},{3,2},{4,5},{5,4},{6,7},{7,6},{8,9},{9,8},{10,11... | collective-permute-start | bytes 49160 | tf_op jit(solution)/shard_map/ppermute | solution.py:571
  24.6 5.2 %collective-permute-start.9 = (f32[32,128]{1,0:T(8,128)S(1)}, f32[32,128]{1,0:T(8,128)S(1)}, u32[]{:S(2)}, u32[]{:S(2)}) collective-permute-start(f32[32,128]{1,0:T(8,128)S(1)} %get-tuple-element.105), channel_id=1, source_target_pairs={{0,2},{1,3},{2,0},{3,1},{4,6},{5,7},{6,4},{7,5},{8,10},{9,11},{10,... | collective-permute-start | bytes 49160 | tf_op jit(solution)/shard_map/ppermute | solution.py:571
  26.2 3.5 %collective-permute-start.10 = (f32[32,128]{1,0:T(8,128)S(1)}, f32[32,128]{1,0:T(8,128)S(1)}, u32[]{:S(2)}, u32[]{:S(2)}) collective-permute-start(f32[32,128]{1,0:T(8,128)S(1)} %get-tuple-element.106), channel_id=1, source_target_pairs={{0,4},{1,5},{2,6},{3,7},{4,0},{5,1},{6,2},{7,3},{8,12},{9,13},{10,... | collective-permute-start | bytes 49160 | tf_op jit(solution)/shard_map/ppermute | solution.py:571
  26.3 3.7 %collective-permute-start.11 = (f32[32,128]{1,0:T(8,128)S(1)}, f32[32,128]{1,0:T(8,128)S(1)}, u32[]{:S(2)}, u32[]{:S(2)}) collective-permute-start(f32[32,128]{1,0:T(8,128)S(1)} %get-tuple-element.107), channel_id=1, source_target_pairs={{0,8},{1,9},{2,10},{3,11},{4,12},{5,13},{6,14},{7,15},{8,0},{9,1},... | collective-permute-start | bytes 49160 | tf_op jit(solution)/shard_map/ppermute | solution.py:571
  30.4 6.5 %collective-permute-start.12 = (f32[32,128]{1,0:T(8,128)S(1)}, f32[32,128]{1,0:T(8,128)S(1)}, u32[]{:S(2)}, u32[]{:S(2)}) collective-permute-start(f32[32,128]{1,0:T(8,128)S(1)} %get-tuple-element.114), channel_id=1, source_target_pairs={{0,1},{1,0},{2,3},{3,2},{4,5},{5,4},{6,7},{7,6},{8,9},{9,8},{10,11... | collective-permute-start | bytes 49160 | tf_op jit(solution)/shard_map/ppermute | solution.py:571
  32.4 4.6 %collective-permute-start.13 = (f32[32,128]{1,0:T(8,128)S(1)}, f32[32,128]{1,0:T(8,128)S(1)}, u32[]{:S(2)}, u32[]{:S(2)}) collective-permute-start(f32[32,128]{1,0:T(8,128)S(1)} %get-tuple-element.115), channel_id=1, source_target_pairs={{0,2},{1,3},{2,0},{3,1},{4,6},{5,7},{6,4},{7,5},{8,10},{9,11},{10,... | collective-permute-start | bytes 49160 | tf_op jit(solution)/shard_map/ppermute | solution.py:571
  33.3 3.7 %collective-permute-start.14 = (f32[32,128]{1,0:T(8,128)S(1)}, f32[32,128]{1,0:T(8,128)S(1)}, u32[]{:S(2)}, u32[]{:S(2)}) collective-permute-start(f32[32,128]{1,0:T(8,128)S(1)} %get-tuple-element.116), channel_id=1, source_target_pairs={{0,4},{1,5},{2,6},{3,7},{4,0},{5,1},{6,2},{7,3},{8,12},{9,13},{10,... | collective-permute-start | bytes 49160 | tf_op jit(solution)/shard_map/ppermute | solution.py:571
  33.3 3.7 %collective-permute-start.15 = (f32[32,128]{1,0:T(8,128)S(1)}, f32[32,128]{1,0:T(8,128)S(1)}, u32[]{:S(2)}, u32[]{:S(2)}) collective-permute-start(f32[32,128]{1,0:T(8,128)S(1)} %get-tuple-element.117), channel_id=1, source_target_pairs={{0,8},{1,9},{2,10},{3,11},{4,12},{5,13},{6,14},{7,15},{8,0},{9,1},... | collective-permute-start | bytes 49160 | tf_op jit(solution)/shard_map/ppermute | solution.py:571
  37.2 6.7 %collective-permute-start.18 = (f32[32,128]{1,0:T(8,128)S(1)}, f32[32,128]{1,0:T(8,128)S(1)}, u32[]{:S(2)}, u32[]{:S(2)}) collective-permute-start(f32[32,128]{1,0:T(8,128)S(1)} %get-tuple-element.119.refs_0_), channel_id=1, source_target_pairs={{0,3},{1,2},{2,1},{3,0},{4,7},{5,6},{6,5},{7,4},{8,11},{9,10},{10,... | collective-permute-start | bytes 49160 | tf_op jit(solution)/shard_map/ppermute | solution.py:571
  38.9 5.0 %collective-permute-start.17 = (f32[32,128]{1,0:T(8,128)S(1)}, f32[32,128]{1,0:T(8,128)S(1)}, u32[]{:S(2)}, u32[]{:S(2)}) collective-permute-start(f32[32,128]{1,0:T(8,128)S(1)} %get-tuple-element.119.refs_0_), channel_id=1, source_target_pairs={{0,2},{1,3},{2,0},{3,1},{4,6},{5,7},{6,4},{7,5},{8,10},{9,11},{10,... | collective-permute-start | bytes 49160 | tf_op jit(solution)/shard_map/ppermute | solution.py:571
  39.4 4.6 %collective-permute-start.16 = (f32[32,128]{1,0:T(8,128)S(1)}, f32[32,128]{1,0:T(8,128)S(1)}, u32[]{:S(2)}, u32[]{:S(2)}) collective-permute-start(f32[32,128]{1,0:T(8,128)S(1)} %get-tuple-element.119.refs_0_), channel_id=1, source_target_pairs={{0,1},{1,0},{2,3},{3,2},{4,5},{5,4},{6,7},{7,6},{8,9},{9,8},{10,11... | collective-permute-start | bytes 49160 | tf_op jit(solution)/shard_map/ppermute | solution.py:571
  44.6 6.1 %collective-permute-start.19 = (f32[32,128]{1,0:T(8,128)S(1)}, f32[32,128]{1,0:T(8,128)S(1)}, u32[]{:S(2)}, u32[]{:S(2)}) collective-permute-start(f32[32,128]{1,0:T(8,128)S(1)} %get-tuple-element.131), channel_id=1, source_target_pairs={{0,1},{1,0},{2,3},{3,2},{4,5},{5,4},{6,7},{7,6},{8,9},{9,8},{10,11... | collective-permute-start | bytes 49160 | tf_op jit(solution)/shard_map/ppermute | solution.py:571
  46.0 4.8 %collective-permute-start.20 = (f32[32,128]{1,0:T(8,128)S(1)}, f32[32,128]{1,0:T(8,128)S(1)}, u32[]{:S(2)}, u32[]{:S(2)}) collective-permute-start(f32[32,128]{1,0:T(8,128)S(1)} %get-tuple-element.132), channel_id=1, source_target_pairs={{0,2},{1,3},{2,0},{3,1},{4,6},{5,7},{6,4},{7,5},{8,10},{9,11},{10,... | collective-permute-start | bytes 49160 | tf_op jit(solution)/shard_map/ppermute | solution.py:571
  47.2 3.7 %collective-permute-start.21 = (f32[32,128]{1,0:T(8,128)S(1)}, f32[32,128]{1,0:T(8,128)S(1)}, u32[]{:S(2)}, u32[]{:S(2)}) collective-permute-start(f32[32,128]{1,0:T(8,128)S(1)} %get-tuple-element.133), channel_id=1, source_target_pairs={{0,4},{1,5},{2,6},{3,7},{4,0},{5,1},{6,2},{7,3},{8,12},{9,13},{10,... | collective-permute-start | bytes 49160 | tf_op jit(solution)/shard_map/ppermute | solution.py:571
  47.2 3.7 %collective-permute-start.22 = (f32[32,128]{1,0:T(8,128)S(1)}, f32[32,128]{1,0:T(8,128)S(1)}, u32[]{:S(2)}, u32[]{:S(2)}) collective-permute-start(f32[32,128]{1,0:T(8,128)S(1)} %get-tuple-element.134), channel_id=1, source_target_pairs={{0,8},{1,9},{2,10},{3,11},{4,12},{5,13},{6,14},{7,15},{8,0},{9,1},... | collective-permute-start | bytes 49160 | tf_op jit(solution)/shard_map/ppermute | solution.py:571
  51.9 11.7 %all-to-all-start = ((f32[32,2,128]{2,1,0:T(2,128)}), f32[32,2,128]{2,1,0:T(2,128)S(1)}, u32[]{:S(2)}, u32[]{:S(2)}) async-start(f32[32,2,128]{2,1,0:T(2,128)} %get-tuple-element.138), calls=%async_computation | async-start | bytes 65536 | tf_op jit(solution)/shard_map/all_to_all | solution.py:673
  55.6 7.7 %collective-permute-start.23 = (f32[32,128]{1,0:T(8,128)S(1)}, f32[32,128]{1,0:T(8,128)S(1)}, u32[]{:S(2)}, u32[]{:S(2)}) collective-permute-start(f32[32,128]{1,0:T(8,128)S(1)} %get-tuple-element.139), channel_id=1, source_target_pairs={{0,1},{1,0},{2,3},{3,2},{4,5},{5,4},{6,7},{7,6},{8,9},{9,8},{10,11... | collective-permute-start | bytes 49160 | tf_op jit(solution)/shard_map/ppermute | solution.py:571
  57.4 5.9 %collective-permute-start.24 = (f32[32,128]{1,0:T(8,128)S(1)}, f32[32,128]{1,0:T(8,128)S(1)}, u32[]{:S(2)}, u32[]{:S(2)}) collective-permute-start(f32[32,128]{1,0:T(8,128)S(1)} %get-tuple-element.140), channel_id=1, source_target_pairs={{0,2},{1,3},{2,0},{3,1},{4,6},{5,7},{6,4},{7,5},{8,10},{9,11},{10,... | collective-permute-start | bytes 49160 | tf_op jit(solution)/shard_map/ppermute | solution.py:571
  59.8 3.5 %collective-permute-start.25 = (f32[32,128]{1,0:T(8,128)S(1)}, f32[32,128]{1,0:T(8,128)S(1)}, u32[]{:S(2)}, u32[]{:S(2)}) collective-permute-start(f32[32,128]{1,0:T(8,128)S(1)} %get-tuple-element.141), channel_id=1, source_target_pairs={{0,4},{1,5},{2,6},{3,7},{4,0},{5,1},{6,2},{7,3},{8,12},{9,13},{10,... | collective-permute-start | bytes 49160 | tf_op jit(solution)/shard_map/ppermute | solution.py:571
  59.8 3.7 %collective-permute-start.26 = (f32[32,128]{1,0:T(8,128)S(1)}, f32[32,128]{1,0:T(8,128)S(1)}, u32[]{:S(2)}, u32[]{:S(2)}) collective-permute-start(f32[32,128]{1,0:T(8,128)S(1)} %get-tuple-element.142), channel_id=1, source_target_pairs={{0,8},{1,9},{2,10},{3,11},{4,12},{5,13},{6,14},{7,15},{8,0},{9,1},... | collective-permute-start | bytes 49160 | tf_op jit(solution)/shard_map/ppermute | solution.py:571

commit v8 on v7

--- a/solution.py
+++ b/solution.py
@@ -102,8 +102,7 @@
     copies[3].wait()
     for r, out in enumerate((side0, side1, side2, side3)):
         out[:NRHS, :] = faces[:, lanes(r)]
-        out[NRHS : NRHS + 8, :] = jnp.broadcast_to(maps[0, r : r + 1, :], (8, BS)).astype(F32)
-        out[NRHS + 8 :, :] = target
+        out[NRHS:, :] = jnp.where(line == 2, maps[0, r : r + 1, :].astype(F32), target)
 
 
 def face_rows(acc_ref, face_ref, tiles, cols, out_ref, spare_ref):
@@ -137,7 +136,7 @@
     )
     rows = lax.broadcasted_iota(jnp.int32, (BS, BS), 0).astype(F32)
     for r, side in enumerate((own0, own1, own2, own3)):
-        mine_ref[r] = (rows == side[NRHS : NRHS + 1, :]).astype(F32).T.astype(BF16)
+        mine_ref[r] = (rows == side[NRHS + 2 : NRHS + 3, :]).astype(F32).T.astype(BF16)
     first.wait()
     solve_inside(lambda b: x[:, lanes(b)], inv, basis, copies, inner_ref, part_ref)
     basis_high[...], basis_low[...] = halves(basis[:, NIN * BS :])
@@ -194,7 +193,7 @@
 
 def maps_of(own, inc):
     rows = lax.broadcasted_iota(jnp.int32, (BS, BS), 0).astype(F32)
-    return onehot(rows == own[NRHS : NRHS + 1, :]), onehot(rows == inc[NRHS : NRHS + 1, :])
+    return onehot(rows == own[NRHS + 2 : NRHS + 3, :]), onehot(rows == inc[NRHS + 2 : NRHS + 3, :])
 
 
 def rows_for(targets, coarse_ref):
@@ -221,7 +220,7 @@
     own0, own1, own2, own3, in0, in1, in2, in3, target_ref, weight_ref,
     basis_high, basis_low, part_ref, coarse_ref, turned_ref, *rest, line,
 ):
-    targets = [target_ref[...], in0[NRHS + 8 :, :], in1[NRHS + 8 :, :]] + [
+    targets = [target_ref[...], in0[NRHS:, :], in1[NRHS:, :]] + [
         ref[:8, :] for ref in rest[: line - 3]
     ]
     face_ref, contrib_ref, all_ref, *sides = rest[line - 3 :]
@@ -579,11 +578,11 @@
     inside = (NIN, NRHS, BS)
     around = (NF, NRHS, BS)
     every = (NB, NRHS, BS)
-    block, face, small, side = f32(*inside), f32(*around), f32(NRHS, BS), f32(NRHS + 16, BS)
+    block, face, small, side = f32(*inside), f32(*around), f32(NRHS, BS), f32(NRHS + 8, BS)
     nf = NF * BS
     width = line * CB * CW
     target, for_far, column, weight, *sides = call(
-        prepare_body, "prepare", [f32(8, BS), f32(NRHS + 24, BS), jax.ShapeDtypeStruct((2, BS, BS), jnp.int32), f32(2 * NF, BS)] + [side] * NF, [HBM] * 4,
+        prepare_body, "prepare", [f32(8, BS), f32(NRHS + 16, BS), jax.ShapeDtypeStruct((2, BS, BS), jnp.int32), f32(2 * NF, BS)] + [side] * NF, [HBM] * 4,
         load_vector, row_map, coarse_id, face_link,
         scratch=[pltpu.SMEM((1, CB), jnp.int32), pltpu.SMEM((1, NF), jnp.int32),
                  pltpu.VMEM((1, NF, BS), jnp.int32), (NRHS, nf)],

time: 64.8 us -> 64.8 us (level)
  no operation moved by 1% of the time
where the time goes in v8:
time: 64.8 us; the launch traced here: 64.5 us
  starting transfers between devices  36.8 us (57%)
  Pallas kernels  22.9 us (35%)
  waiting for transfers between devices  4 us (6%)
  between operations  0.84 us (1%)
    ppermute x27, starting transfers between devices, trade(): return lax.ppermute(value, AXES, [(i, i ^ mask) for i in range(devices)])  33.1 us
    pallas_call x15, Pallas kernels, call(): pl.pallas_call(body, name=name, out_shape=outs, in_specs=specs, out_specs...  22.9 us
    ppermute x27, waiting for transfers between devices, trade(): return lax.ppermute(value, AXES, [(i, i ^ mask) for i in range(devices)])  3.99 us
    all_to_all x1, starting transfers between devices, on_device(): spread = lax.all_to_all(dots, AXES, 0, 0)  3.66 us
  transfers between devices with their start and end apart: 28, of which 6 were waited for; matrix products, arithmetic and copies ran while one was open for 0% of the time, Pallas kernels for 27%

profile of v8, /device:TPU:0, one launch (start us, length us, event | category | flops | bytes accessed | tf_op | source)
XLA Modules:
  0.0 64.5 jit_solution(14858879235973308944)
XLA Ops:
  0.6 0.9 %prepare.1 = (f32[8,128]{1,0:T(8,128)S(1)}, f32[48,128]{1,0:T(8,128)S(1)}, s32[2,128,128]{2,1,0:T(8,128)S(1)}, f32[8,128]{1,0:T(8,128)S(1)}, f32[40,128]{1,0:T(8...) custom-call(f32[1,32,2048]{2,1,0:T(8,128)} %load_hbm.1, s32[1,4,128]{2,1,0:T(4,128)} %map_ref.1, ...), custom_call_target="tpu_custom_call" | custom-call | tf_op jit(solution)/shard_map/prepare/pallas_call | solution.py:547
  1.5 5.1 %collective-permute-start.4 = (f32[48,128]{1,0:T(8,128)S(1)}, f32[48,128]{1,0:T(8,128)S(1)}, u32[]{:S(2)}, u32[]{:S(2)}) collective-permute-start(f32[48,128]{1,0:T(8,128)S(1)} %get-tuple-element.86), channel_id=1, source_target_pairs={{0,3},{1,2},{2,1},{3,0},{4,7},{5,6},{6,5},{7,4},{8,11},{9,10},{10,... | collective-permute-start | bytes 73736 | tf_op jit(solution)/shard_map/ppermute | solution.py:570
  6.7 0.6 collective-permute-start.1
  7.3 1.6 %collective-permute-start.3 = (f32[40,128]{1,0:T(8,128)S(1)}, f32[40,128]{1,0:T(8,128)S(1)}, u32[]{:S(2)}, u32[]{:S(2)}) collective-permute-start(f32[40,128]{1,0:T(8,128)S(1)} %get-tuple-element.77.own3.refs_3_), channel_id=1, source_target_pairs={{0,8},{1,9},{2,10},{3,11},{4,12},{5,13},{6,14},{7,15},{8,0},{9,1},... | collective-permute-start | bytes 61448 | tf_op jit(solution)/shard_map/ppermute | solution.py:570
  8.9 2.3 %inside_load.1 = (f32[12,32,128]{2,1,0:T(8,128)S(1)}, f32[32,128]{1,0:T(8,128)S(1)}, bf16[512,512]{1,0:T(8,128)(2,1)S(1)}, bf16[512,512]{1,0:T(8,128)(2,1)S(1)},...) custom-call(f32[1,32,2048]{2,1,0:T(8,128)} %load_hbm.1, ...), custom_call_target="tpu_custom_call" | custom-call | tf_op jit(solution)/shard_map/inside_load/pallas_call | solution.py:547
  11.2 0.0 collective-permute-done.refs_4_
  11.2 0.1 collective-permute-done.1.refs_5_
  11.4 0.8 %faces_load.1 = (f32[4,32,128]{2,1,0:T(8,128)S(1)}, f32[32,128]{1,0:T(8,128)S(1)}, f32[1,512]{1,0:T(1,128)S(1)}, f32[160,128]{1,0:T(8,128)S(1)}, f32[168,128]{1,0:T(8,128)S(1)}, /*index=5*/f32[160,128]{1,0:T(8,128)S(1)}) custom-call(f32[40,128]{1,0:T(8,128)S(1)} %get-tuple-element.74.own0.refs_0_, f32[40,128]{1,0:T(8,128)S(1)} %get-tuple-element.75.own1.refs_1_, ...), custom_call_target="tpu_custom_call" | custom-call | tf_op jit(solution)/shard_map/faces_load/pallas_call | solution.py:547
  12.1 2.1 %collective-permute-start.6 = (f32[168,128]{1,0:T(8,128)S(1)}, f32[168,128]{1,0:T(8,128)S(1)}, u32[]{:S(2)}, u32[]{:S(2)}) collective-permute-start(f32[168,128]{1,0:T(8,128)S(1)} %get-tuple-element.96), channel_id=1, source_target_pairs={{0,2},{1,3},{2,0},{3,1},{4,6},{5,7},{6,4},{7,5},{8,10},{9,11},{10,... | collective-permute-start | bytes 258056 | tf_op jit(solution)/shard_map/ppermute | solution.py:570
  14.2 2.0 %collective-permute-start.5 = (f32[160,128]{1,0:T(8,128)S(1)}, f32[160,128]{1,0:T(8,128)S(1)}, u32[]{:S(2)}, u32[]{:S(2)}) collective-permute-start(f32[160,128]{1,0:T(8,128)S(1)} %get-tuple-element.95), channel_id=1, source_target_pairs={{0,1},{1,0},{2,3},{3,2},{4,5},{5,4},{6,7},{7,6},{8,9},{9,8},{10,11... | collective-permute-start | bytes 245768 | tf_op jit(solution)/shard_map/ppermute | solution.py:570
  16.3 0.3 collective-permute-start.7
  16.6 3.0 %under_line.1 = (bf16[4,4,128,128]{3,2,1,0:T(8,128)(2,1)S(1)}, bf16[4,4,128,128]{3,2,1,0:T(8,128)(2,1)S(1)}, f32[4,32,128]{2,1,0:T(8,128)S(1)}, bf16[4,128,128]{...) custom-call(f32[40,128]{1,0:T(8,128)S(1)} %get-tuple-element.74.own0, ...), custom_call_target="tpu_custom_call" | custom-call | tf_op jit(solution)/shard_map/under_line/pallas_call | solution.py:547
  19.6 0.0 collective-permute-done.5.refs_4_.refs_9_
  19.7 2.9 %collective-permute-done.7.refs_6_.refs_11_ = f32[160,128]{1,0:T(8,128)S(1)} collective-permute-done((f32[160,128]{1,0:T(8,128)S(1)}, f32[160,128]{1,0:T(8,128)S(1)}, u32[]{:S(2)}, u32[]{:S(2)}) %collective-permute-start.7) | collective-permute-done | bytes 81952 | tf_op jit(solution)/shard_map/ppermute | solution.py:570
  22.6 1.0 %coarse_load.1 = (f32[32,128]{1,0:T(8,128)S(1)}, f32[4,32,128]{2,1,0:T(8,128)S(1)}, f32[32,128]{1,0:T(8,128)S(1)}, f32[32,128]{1,0:T(8,128)S(1)}, f32[32,128]{1,0:T(8,128)S(1)}, /*index=5*/f32[32,128]{1,0:T(8,128)S(1)}) custom-call(f32[32,128]{1,0:T(8,128)S(1)} %get-tuple-element.87.refs_0_, f32[128,128]{1,0:T(8,128)S(1)} %get-tuple-element.92.refs_1_.refs_2_, ...), custom_call_target="tpu_custom_call" | custom-call | tf_op jit(solution)/shard_map/coarse_load/pallas_call | solution.py:547
  23.5 1.0 %collective-permute-start.8 = (f32[32,128]{1,0:T(8,128)S(1)}, f32[32,128]{1,0:T(8,128)S(1)}, u32[]{:S(2)}, u32[]{:S(2)}) collective-permute-start(f32[32,128]{1,0:T(8,128)S(1)} %get-tuple-element.104), channel_id=1, source_target_pairs={{0,1},{1,0},{2,3},{3,2},{4,5},{5,4},{6,7},{7,6},{8,9},{9,8},{10,11... | collective-permute-start | bytes 49160 | tf_op jit(solution)/shard_map/ppermute | solution.py:570
  24.6 1.7 %collective-permute-start.9 = (f32[32,128]{1,0:T(8,128)S(1)}, f32[32,128]{1,0:T(8,128)S(1)}, u32[]{:S(2)}, u32[]{:S(2)}) collective-permute-start(f32[32,128]{1,0:T(8,128)S(1)} %get-tuple-element.105), channel_id=1, source_target_pairs={{0,2},{1,3},{2,0},{3,1},{4,6},{5,7},{6,4},{7,5},{8,10},{9,11},{10,... | collective-permute-start | bytes 49160 | tf_op jit(solution)/shard_map/ppermute | solution.py:570
  26.3 0.0 collective-permute-start.10
  26.3 1.1 %collective-permute-start.11 = (f32[32,128]{1,0:T(8,128)S(1)}, f32[32,128]{1,0:T(8,128)S(1)}, u32[]{:S(2)}, u32[]{:S(2)}) collective-permute-start(f32[32,128]{1,0:T(8,128)S(1)} %get-tuple-element.107), channel_id=1, source_target_pairs={{0,8},{1,9},{2,10},{3,11},{4,12},{5,13},{6,14},{7,15},{8,0},{9,1},... | collective-permute-start | bytes 49160 | tf_op jit(solution)/shard_map/ppermute | solution.py:570
  27.3 2.3 %own_first.1 = (f32[12,32,128]{2,1,0:T(8,128)S(1)}, f32[16,32,128]{2,1,0:T(8,128)S(1)}) custom-call(f32[12,32,128]{2,1,0:T(8,128)S(1)} %get-tuple-element.78.refs_0_, f32[32,128]{1,0:T(8,128)S(1)} %get-tuple-element.100.refs_1_, f32[6,7,128,128]{3,2,1,0:T(8,128)S(1)} %get-tuple-element.101.refs_2_, f32[128,1536]{1,0:T(8,128)S(1)} %get-tuple-element.102.refs_3_, ...), custom_call_target="tpu_custom_call" | custom-call | tf_op jit(solution)/shard_map/own_first/pallas_call | solution.py:547
  29.7 0.3 collective-permute-done.11.in3
  30.0 0.4 face_first.1
  30.4 2.0 %collective-permute-start.12 = (f32[32,128]{1,0:T(8,128)S(1)}, f32[32,128]{1,0:T(8,128)S(1)}, u32[]{:S(2)}, u32[]{:S(2)}) collective-permute-start(f32[32,128]{1,0:T(8,128)S(1)} %get-tuple-element.114), channel_id=1, source_target_pairs={{0,1},{1,0},{2,3},{3,2},{4,5},{5,4},{6,7},{7,6},{8,9},{9,8},{10,11... | collective-permute-start | bytes 49160 | tf_op jit(solution)/shard_map/ppermute | solution.py:570
  32.4 0.9 %collective-permute-start.13 = (f32[32,128]{1,0:T(8,128)S(1)}, f32[32,128]{1,0:T(8,128)S(1)}, u32[]{:S(2)}, u32[]{:S(2)}) collective-permute-start(f32[32,128]{1,0:T(8,128)S(1)} %get-tuple-element.115), channel_id=1, source_target_pairs={{0,2},{1,3},{2,0},{3,1},{4,6},{5,7},{6,4},{7,5},{8,10},{9,11},{10,... | collective-permute-start | bytes 49160 | tf_op jit(solution)/shard_map/ppermute | solution.py:570
  33.3 0.8 %collective-permute-start.15 = (f32[32,128]{1,0:T(8,128)S(1)}, f32[32,128]{1,0:T(8,128)S(1)}, u32[]{:S(2)}, u32[]{:S(2)}) collective-permute-start(f32[32,128]{1,0:T(8,128)S(1)} %get-tuple-element.117), channel_id=1, source_target_pairs={{0,8},{1,9},{2,10},{3,11},{4,12},{5,13},{6,14},{7,15},{8,0},{9,1},... | collective-permute-start | bytes 49160 | tf_op jit(solution)/shard_map/ppermute | solution.py:570
  34.1 2.7 %inside_image.1 = (f32[12,32,128]{2,1,0:T(8,128)S(1)}, f32[12,32,128]{2,1,0:T(8,128)S(1)}, f32[32,128]{1,0:T(8,128)S(1)}) custom-call(f32[16,32,128]{2,1,0:T(8,128)S(1)} %get-tuple-element.103.acc_ref, f32[4,32,128]{2,1,0:T(8,128)S(1)} %get-tuple-element.111.face_ref.zf, s32[7,16]{1,0:T(8,128)} %bitcast.3, f32[16,7,128,128]{3,2,1,0:T(8,128)} %tiles_ref.5, ...), custom_call_target="tpu_custom_call" | custom-call | tf_op jit(solution)/shard_map/inside_image/pallas_call | solution.py:547
  36.8 0.2 collective-permute-done.13.in1
  37.0 0.0 collective-permute-done.15.in3
  37.0 0.2 faces_image.1
  37.2 1.7 %collective-permute-start.18 = (f32[32,128]{1,0:T(8,128)S(1)}, f32[32,128]{1,0:T(8,128)S(1)}, u32[]{:S(2)}, u32[]{:S(2)}) collective-permute-start(f32[32,128]{1,0:T(8,128)S(1)} %get-tuple-element.119.refs_0_), channel_id=1, source_target_pairs={{0,3},{1,2},{2,1},{3,0},{4,7},{5,6},{6,5},{7,4},{8,11},{9,10},{10,... | collective-permute-start | bytes 49160 | tf_op jit(solution)/shard_map/ppermute | solution.py:570
  38.9 0.5 collective-permute-start.17
  39.4 2.3 %collective-permute-start.16 = (f32[32,128]{1,0:T(8,128)S(1)}, f32[32,128]{1,0:T(8,128)S(1)}, u32[]{:S(2)}, u32[]{:S(2)}) collective-permute-start(f32[32,128]{1,0:T(8,128)S(1)} %get-tuple-element.119.refs_0_), channel_id=1, source_target_pairs={{0,1},{1,0},{2,3},{3,2},{4,5},{5,4},{6,7},{7,6},{8,9},{9,8},{10,11... | collective-permute-start | bytes 49160 | tf_op jit(solution)/shard_map/ppermute | solution.py:570
  41.7 2.3 %table.1 = (bf16[128,512]{1,0:T(8,128)(2,1)S(1)}, bf16[128,512]{1,0:T(8,128)(2,1)S(1)}, f32[4,32,128]{2,1,0:T(8,128)S(1)}, f32[6,7,128,128]{3,2,1,0:T(8,128)S(1)}, f32[128,1536]{1,0:T(8,128)S(1)}) custom-call(f32[16,7,128,128]{3,2,1,0:T(8,128)} %tiles_ref.5, f32[1,128,2048]{2,1,0:T(8,128)} %refs_1_.1, f32[128,128]{1,0:T(8,128)S(1)} %get-tuple-element.92.refs_1_.refs_2_, ...), custom_call_target="tpu_custom_call" | custom-call | tf_op jit(solution)/shard_map/table/pallas_call | solution.py:547
  44.0 0.6 coarse_image.1
  44.6 1.5 %collective-permute-start.19 = (f32[32,128]{1,0:T(8,128)S(1)}, f32[32,128]{1,0:T(8,128)S(1)}, u32[]{:S(2)}, u32[]{:S(2)}) collective-permute-start(f32[32,128]{1,0:T(8,128)S(1)} %get-tuple-element.131), channel_id=1, source_target_pairs={{0,1},{1,0},{2,3},{3,2},{4,5},{5,4},{6,7},{7,6},{8,9},{9,8},{10,11... | collective-permute-start | bytes 49160 | tf_op jit(solution)/shard_map/ppermute | solution.py:570
  46.0 1.1 %collective-permute-start.20 = (f32[32,128]{1,0:T(8,128)S(1)}, f32[32,128]{1,0:T(8,128)S(1)}, u32[]{:S(2)}, u32[]{:S(2)}) collective-permute-start(f32[32,128]{1,0:T(8,128)S(1)} %get-tuple-element.132), channel_id=1, source_target_pairs={{0,2},{1,3},{2,0},{3,1},{4,6},{5,7},{6,4},{7,5},{8,10},{9,11},{10,... | collective-permute-start | bytes 49160 | tf_op jit(solution)/shard_map/ppermute | solution.py:570
  47.2 1.1 %collective-permute-start.22 = (f32[32,128]{1,0:T(8,128)S(1)}, f32[32,128]{1,0:T(8,128)S(1)}, u32[]{:S(2)}, u32[]{:S(2)}) collective-permute-start(f32[32,128]{1,0:T(8,128)S(1)} %get-tuple-element.134), channel_id=1, source_target_pairs={{0,8},{1,9},{2,10},{3,11},{4,12},{5,13},{6,14},{7,15},{8,0},{9,1},... | collective-permute-start | bytes 49160 | tf_op jit(solution)/shard_map/ppermute | solution.py:570
  48.2 2.5 %own_second.1 = (f32[12,32,128]{2,1,0:T(8,128)S(1)}, f32[16,32,128]{2,1,0:T(8,128)S(1)}, f32[5,32,128]{2,1,0:T(8,128)S(1)}, f32[16,32,128]{2,1,0:T(8,128)S(1)}) custom-call(f32[12,32,128]{2,1,0:T(8,128)S(1)} %get-tuple-element.112.inner_ref, f32[32,128]{1,0:T(8,128)S(1)} %get-tuple-element.125.back_ref, f32[6,7,128,128]{3,2,1,0:T(8,128)S(1)} %get-tuple-element.126.early_ref, ...), custom_call_target="tpu_custom_call" | custom-call | tf_op jit(solution)/shard_map/own_second/pallas_call | solution.py:547
  50.7 0.1 collective-permute-done.20.in1
  50.8 0.0 collective-permute-done.22.in3
  50.9 1.0 %face_second.1 = (f32[4,32,128]{2,1,0:T(8,128)S(1)}, f32[4,32,128]{2,1,0:T(8,128)S(1)}, f32[32,2,128]{2,1,0:T(2,128)}, f32[32,128]{1,0:T(8,128)S(1)}, f32[32,128...) custom-call(f32[16,32,128]{2,1,0:T(8,128)S(1)} %get-tuple-element.130.acc_ref, ...), custom_call_target="tpu_custom_call" | custom-call | tf_op jit(solution)/shard_map/face_second/pallas_call | solution.py:547
  51.9 3.7 %all-to-all-start = ((f32[32,2,128]{2,1,0:T(2,128)}), f32[32,2,128]{2,1,0:T(2,128)S(1)}, u32[]{:S(2)}, u32[]{:S(2)}) async-start(f32[32,2,128]{2,1,0:T(2,128)} %get-tuple-element.138), calls=%async_computation | async-start | bytes 65536 | tf_op jit(solution)/shard_map/all_to_all | solution.py:672
  55.6 1.8 %collective-permute-start.23 = (f32[32,128]{1,0:T(8,128)S(1)}, f32[32,128]{1,0:T(8,128)S(1)}, u32[]{:S(2)}, u32[]{:S(2)}) collective-permute-start(f32[32,128]{1,0:T(8,128)S(1)} %get-tuple-element.139), channel_id=1, source_target_pairs={{0,1},{1,0},{2,3},{3,2},{4,5},{5,4},{6,7},{7,6},{8,9},{9,8},{10,11... | collective-permute-start | bytes 49160 | tf_op jit(solution)/shard_map/ppermute | solution.py:570
  57.4 2.4 %collective-permute-start.24 = (f32[32,128]{1,0:T(8,128)S(1)}, f32[32,128]{1,0:T(8,128)S(1)}, u32[]{:S(2)}, u32[]{:S(2)}) collective-permute-start(f32[32,128]{1,0:T(8,128)S(1)} %get-tuple-element.140), channel_id=1, source_target_pairs={{0,2},{1,3},{2,0},{3,1},{4,6},{5,7},{6,4},{7,5},{8,10},{9,11},{10,... | collective-permute-start | bytes 49160 | tf_op jit(solution)/shard_map/ppermute | solution.py:570
  59.8 1.5 %collective-permute-start.26 = (f32[32,128]{1,0:T(8,128)S(1)}, f32[32,128]{1,0:T(8,128)S(1)}, u32[]{:S(2)}, u32[]{:S(2)}) collective-permute-start(f32[32,128]{1,0:T(8,128)S(1)} %get-tuple-element.142), channel_id=1, source_target_pairs={{0,8},{1,9},{2,10},{3,11},{4,12},{5,13},{6,14},{7,15},{8,0},{9,1},... | collective-permute-start | bytes 49160 | tf_op jit(solution)/shard_map/ppermute | solution.py:570
  61.3 2.0 %inside_last.1.vi = f32[12,32,128]{2,1,0:T(8,128)S(1)} custom-call(f32[16,32,128]{2,1,0:T(8,128)S(1)} %get-tuple-element.130.acc_ref, f32[4,32,128]{2,1,0:T(8,128)S(1)} %get-tuple-element.144.face_ref.wf, s32[7,16]{1,0:T(8,128)} %bitcast.5, f32[16,7,128,128]{3,2,1,0:T(8,128)} %tiles_ref.5), custom_call_target="tpu_custom_call" | custom-call | tf_op jit(solution)/shard_map/inside_last/pallas_call | solution.py:547
  63.3 0.2 collective-permute-done.26.in3
  63.6 1.0 %combine.1 = (f32[1,32,2048]{2,1,0:T(8,128)}, f32[1,32,2048]{2,1,0:T(8,128)}) custom-call(f32[32,2,128]{2,1,0:T(2,128)S(1)} %all-to-all-done.dots_ref, f32[32,128]{1,0:T(8,128)S(1)} %collective-permute-done.23.in0, f32[32,128]{1,0:T(8,128)S(1)} %collective-permute-done.24.in1, f32[32,128]{1,0:T(8,128)S(1)} %collective-permute-done.25.in2, ...), custom_call_target="tpu_custom_call" | custom-call | tf_op jit(solution)/shard_map/combine/pallas_call | solution.py:547
  (23 shorter events, 0.1 us)
Async XLA Ops:
  1.5 9.8 %collective-permute-start.4 = (f32[48,128]{1,0:T(8,128)S(1)}, f32[48,128]{1,0:T(8,128)S(1)}, u32[]{:S(2)}, u32[]{:S(2)}) collective-permute-start(f32[48,128]{1,0:T(8,128)S(1)} %get-tuple-element.86), channel_id=1, source_target_pairs={{0,3},{1,2},{2,1},{3,0},{4,7},{5,6},{6,5},{7,4},{8,11},{9,10},{10,... | collective-permute-start | bytes 73736 | tf_op jit(solution)/shard_map/ppermute | solution.py:570
  6.7 4.5 %collective-permute-start = (f32[40,128]{1,0:T(8,128)S(1)}, f32[40,128]{1,0:T(8,128)S(1)}, u32[]{:S(2)}, u32[]{:S(2)}) collective-permute-start(f32[40,128]{1,0:T(8,128)S(1)} %get-tuple-element.74.own0.refs_0_), channel_id=1, source_target_pairs={{0,1},{1,0},{2,3},{3,2},{4,5},{5,4},{6,7},{7,6},{8,9},{9,8},{10,11... | collective-permute-start | bytes 61448 | tf_op jit(solution)/shard_map/ppermute | solution.py:570
  6.7 4.7 %collective-permute-start.1 = (f32[40,128]{1,0:T(8,128)S(1)}, f32[40,128]{1,0:T(8,128)S(1)}, u32[]{:S(2)}, u32[]{:S(2)}) collective-permute-start(f32[40,128]{1,0:T(8,128)S(1)} %get-tuple-element.75.own1.refs_1_), channel_id=1, source_target_pairs={{0,2},{1,3},{2,0},{3,1},{4,6},{5,7},{6,4},{7,5},{8,10},{9,11},{10,... | collective-permute-start | bytes 61448 | tf_op jit(solution)/shard_map/ppermute | solution.py:570
  7.3 4.0 %collective-permute-start.2 = (f32[40,128]{1,0:T(8,128)S(1)}, f32[40,128]{1,0:T(8,128)S(1)}, u32[]{:S(2)}, u32[]{:S(2)}) collective-permute-start(f32[40,128]{1,0:T(8,128)S(1)} %get-tuple-element.76.own2.refs_2_), channel_id=1, source_target_pairs={{0,4},{1,5},{2,6},{3,7},{4,0},{5,1},{6,2},{7,3},{8,12},{9,13},{10,... | collective-permute-start | bytes 61448 | tf_op jit(solution)/shard_map/ppermute | solution.py:570
  7.3 4.0 %collective-permute-start.3 = (f32[40,128]{1,0:T(8,128)S(1)}, f32[40,128]{1,0:T(8,128)S(1)}, u32[]{:S(2)}, u32[]{:S(2)}) collective-permute-start(f32[40,128]{1,0:T(8,128)S(1)} %get-tuple-element.77.own3.refs_3_), channel_id=1, source_target_pairs={{0,8},{1,9},{2,10},{3,11},{4,12},{5,13},{6,14},{7,15},{8,0},{9,1},... | collective-permute-start | bytes 61448 | tf_op jit(solution)/shard_map/ppermute | solution.py:570
  12.1 10.4 %collective-permute-start.6 = (f32[168,128]{1,0:T(8,128)S(1)}, f32[168,128]{1,0:T(8,128)S(1)}, u32[]{:S(2)}, u32[]{:S(2)}) collective-permute-start(f32[168,128]{1,0:T(8,128)S(1)} %get-tuple-element.96), channel_id=1, source_target_pairs={{0,2},{1,3},{2,0},{3,1},{4,6},{5,7},{6,4},{7,5},{8,10},{9,11},{10,... | collective-permute-start | bytes 258056 | tf_op jit(solution)/shard_map/ppermute | solution.py:570
  14.2 5.4 %collective-permute-start.5 = (f32[160,128]{1,0:T(8,128)S(1)}, f32[160,128]{1,0:T(8,128)S(1)}, u32[]{:S(2)}, u32[]{:S(2)}) collective-permute-start(f32[160,128]{1,0:T(8,128)S(1)} %get-tuple-element.95), channel_id=1, source_target_pairs={{0,1},{1,0},{2,3},{3,2},{4,5},{5,4},{6,7},{7,6},{8,9},{9,8},{10,11... | collective-permute-start | bytes 245768 | tf_op jit(solution)/shard_map/ppermute | solution.py:570
  16.3 6.3 %collective-permute-start.7 = (f32[160,128]{1,0:T(8,128)S(1)}, f32[160,128]{1,0:T(8,128)S(1)}, u32[]{:S(2)}, u32[]{:S(2)}) collective-permute-start(f32[160,128]{1,0:T(8,128)S(1)} %get-tuple-element.97), channel_id=1, source_target_pairs={{0,3},{1,2},{2,1},{3,0},{4,7},{5,6},{6,5},{7,4},{8,11},{9,10},{10,... | collective-permute-start | bytes 245768 | tf_op jit(solution)/shard_map/ppermute | solution.py:570
  23.5 6.2 %collective-permute-start.8 = (f32[32,128]{1,0:T(8,128)S(1)}, f32[32,128]{1,0:T(8,128)S(1)}, u32[]{:S(2)}, u32[]{:S(2)}) collective-permute-start(f32[32,128]{1,0:T(8,128)S(1)} %get-tuple-element.104), channel_id=1, source_target_pairs={{0,1},{1,0},{2,3},{3,2},{4,5},{5,4},{6,7},{7,6},{8,9},{9,8},{10,11... | collective-permute-start | bytes 49160 | tf_op jit(solution)/shard_map/ppermute | solution.py:570
  24.6 5.1 %collective-permute-start.9 = (f32[32,128]{1,0:T(8,128)S(1)}, f32[32,128]{1,0:T(8,128)S(1)}, u32[]{:S(2)}, u32[]{:S(2)}) collective-permute-start(f32[32,128]{1,0:T(8,128)S(1)} %get-tuple-element.105), channel_id=1, source_target_pairs={{0,2},{1,3},{2,0},{3,1},{4,6},{5,7},{6,4},{7,5},{8,10},{9,11},{10,... | collective-permute-start | bytes 49160 | tf_op jit(solution)/shard_map/ppermute | solution.py:570
  26.3 3.4 %collective-permute-start.10 = (f32[32,128]{1,0:T(8,128)S(1)}, f32[32,128]{1,0:T(8,128)S(1)}, u32[]{:S(2)}, u32[]{:S(2)}) collective-permute-start(f32[32,128]{1,0:T(8,128)S(1)} %get-tuple-element.106), channel_id=1, source_target_pairs={{0,4},{1,5},{2,6},{3,7},{4,0},{5,1},{6,2},{7,3},{8,12},{9,13},{10,... | collective-permute-start | bytes 49160 | tf_op jit(solution)/shard_map/ppermute | solution.py:570
  26.3 3.7 %collective-permute-start.11 = (f32[32,128]{1,0:T(8,128)S(1)}, f32[32,128]{1,0:T(8,128)S(1)}, u32[]{:S(2)}, u32[]{:S(2)}) collective-permute-start(f32[32,128]{1,0:T(8,128)S(1)} %get-tuple-element.107), channel_id=1, source_target_pairs={{0,8},{1,9},{2,10},{3,11},{4,12},{5,13},{6,14},{7,15},{8,0},{9,1},... | collective-permute-start | bytes 49160 | tf_op jit(solution)/shard_map/ppermute | solution.py:570
  30.4 6.4 %collective-permute-start.12 = (f32[32,128]{1,0:T(8,128)S(1)}, f32[32,128]{1,0:T(8,128)S(1)}, u32[]{:S(2)}, u32[]{:S(2)}) collective-permute-start(f32[32,128]{1,0:T(8,128)S(1)} %get-tuple-element.114), channel_id=1, source_target_pairs={{0,1},{1,0},{2,3},{3,2},{4,5},{5,4},{6,7},{7,6},{8,9},{9,8},{10,11... | collective-permute-start | bytes 49160 | tf_op jit(solution)/shard_map/ppermute | solution.py:570
  32.4 4.6 %collective-permute-start.13 = (f32[32,128]{1,0:T(8,128)S(1)}, f32[32,128]{1,0:T(8,128)S(1)}, u32[]{:S(2)}, u32[]{:S(2)}) collective-permute-start(f32[32,128]{1,0:T(8,128)S(1)} %get-tuple-element.115), channel_id=1, source_target_pairs={{0,2},{1,3},{2,0},{3,1},{4,6},{5,7},{6,4},{7,5},{8,10},{9,11},{10,... | collective-permute-start | bytes 49160 | tf_op jit(solution)/shard_map/ppermute | solution.py:570
  33.3 3.7 %collective-permute-start.14 = (f32[32,128]{1,0:T(8,128)S(1)}, f32[32,128]{1,0:T(8,128)S(1)}, u32[]{:S(2)}, u32[]{:S(2)}) collective-permute-start(f32[32,128]{1,0:T(8,128)S(1)} %get-tuple-element.116), channel_id=1, source_target_pairs={{0,4},{1,5},{2,6},{3,7},{4,0},{5,1},{6,2},{7,3},{8,12},{9,13},{10,... | collective-permute-start | bytes 49160 | tf_op jit(solution)/shard_map/ppermute | solution.py:570
  33.3 3.7 %collective-permute-start.15 = (f32[32,128]{1,0:T(8,128)S(1)}, f32[32,128]{1,0:T(8,128)S(1)}, u32[]{:S(2)}, u32[]{:S(2)}) collective-permute-start(f32[32,128]{1,0:T(8,128)S(1)} %get-tuple-element.117), channel_id=1, source_target_pairs={{0,8},{1,9},{2,10},{3,11},{4,12},{5,13},{6,14},{7,15},{8,0},{9,1},... | collective-permute-start | bytes 49160 | tf_op jit(solution)/shard_map/ppermute | solution.py:570
  37.2 6.7 %collective-permute-start.18 = (f32[32,128]{1,0:T(8,128)S(1)}, f32[32,128]{1,0:T(8,128)S(1)}, u32[]{:S(2)}, u32[]{:S(2)}) collective-permute-start(f32[32,128]{1,0:T(8,128)S(1)} %get-tuple-element.119.refs_0_), channel_id=1, source_target_pairs={{0,3},{1,2},{2,1},{3,0},{4,7},{5,6},{6,5},{7,4},{8,11},{9,10},{10,... | collective-permute-start | bytes 49160 | tf_op jit(solution)/shard_map/ppermute | solution.py:570
  38.9 5.1 %collective-permute-start.17 = (f32[32,128]{1,0:T(8,128)S(1)}, f32[32,128]{1,0:T(8,128)S(1)}, u32[]{:S(2)}, u32[]{:S(2)}) collective-permute-start(f32[32,128]{1,0:T(8,128)S(1)} %get-tuple-element.119.refs_0_), channel_id=1, source_target_pairs={{0,2},{1,3},{2,0},{3,1},{4,6},{5,7},{6,4},{7,5},{8,10},{9,11},{10,... | collective-permute-start | bytes 49160 | tf_op jit(solution)/shard_map/ppermute | solution.py:570
  39.4 4.6 %collective-permute-start.16 = (f32[32,128]{1,0:T(8,128)S(1)}, f32[32,128]{1,0:T(8,128)S(1)}, u32[]{:S(2)}, u32[]{:S(2)}) collective-permute-start(f32[32,128]{1,0:T(8,128)S(1)} %get-tuple-element.119.refs_0_), channel_id=1, source_target_pairs={{0,1},{1,0},{2,3},{3,2},{4,5},{5,4},{6,7},{7,6},{8,9},{9,8},{10,11... | collective-permute-start | bytes 49160 | tf_op jit(solution)/shard_map/ppermute | solution.py:570
  44.6 6.1 %collective-permute-start.19 = (f32[32,128]{1,0:T(8,128)S(1)}, f32[32,128]{1,0:T(8,128)S(1)}, u32[]{:S(2)}, u32[]{:S(2)}) collective-permute-start(f32[32,128]{1,0:T(8,128)S(1)} %get-tuple-element.131), channel_id=1, source_target_pairs={{0,1},{1,0},{2,3},{3,2},{4,5},{5,4},{6,7},{7,6},{8,9},{9,8},{10,11... | collective-permute-start | bytes 49160 | tf_op jit(solution)/shard_map/ppermute | solution.py:570
  46.0 4.8 %collective-permute-start.20 = (f32[32,128]{1,0:T(8,128)S(1)}, f32[32,128]{1,0:T(8,128)S(1)}, u32[]{:S(2)}, u32[]{:S(2)}) collective-permute-start(f32[32,128]{1,0:T(8,128)S(1)} %get-tuple-element.132), channel_id=1, source_target_pairs={{0,2},{1,3},{2,0},{3,1},{4,6},{5,7},{6,4},{7,5},{8,10},{9,11},{10,... | collective-permute-start | bytes 49160 | tf_op jit(solution)/shard_map/ppermute | solution.py:570
  47.2 3.7 %collective-permute-start.21 = (f32[32,128]{1,0:T(8,128)S(1)}, f32[32,128]{1,0:T(8,128)S(1)}, u32[]{:S(2)}, u32[]{:S(2)}) collective-permute-start(f32[32,128]{1,0:T(8,128)S(1)} %get-tuple-element.133), channel_id=1, source_target_pairs={{0,4},{1,5},{2,6},{3,7},{4,0},{5,1},{6,2},{7,3},{8,12},{9,13},{10,... | collective-permute-start | bytes 49160 | tf_op jit(solution)/shard_map/ppermute | solution.py:570
  47.2 3.7 %collective-permute-start.22 = (f32[32,128]{1,0:T(8,128)S(1)}, f32[32,128]{1,0:T(8,128)S(1)}, u32[]{:S(2)}, u32[]{:S(2)}) collective-permute-start(f32[32,128]{1,0:T(8,128)S(1)} %get-tuple-element.134), channel_id=1, source_target_pairs={{0,8},{1,9},{2,10},{3,11},{4,12},{5,13},{6,14},{7,15},{8,0},{9,1},... | collective-permute-start | bytes 49160 | tf_op jit(solution)/shard_map/ppermute | solution.py:570
  51.9 11.7 %all-to-all-start = ((f32[32,2,128]{2,1,0:T(2,128)}), f32[32,2,128]{2,1,0:T(2,128)S(1)}, u32[]{:S(2)}, u32[]{:S(2)}) async-start(f32[32,2,128]{2,1,0:T(2,128)} %get-tuple-element.138), calls=%async_computation | async-start | bytes 65536 | tf_op jit(solution)/shard_map/all_to_all | solution.py:672
  55.6 7.7 %collective-permute-start.23 = (f32[32,128]{1,0:T(8,128)S(1)}, f32[32,128]{1,0:T(8,128)S(1)}, u32[]{:S(2)}, u32[]{:S(2)}) collective-permute-start(f32[32,128]{1,0:T(8,128)S(1)} %get-tuple-element.139), channel_id=1, source_target_pairs={{0,1},{1,0},{2,3},{3,2},{4,5},{5,4},{6,7},{7,6},{8,9},{9,8},{10,11... | collective-permute-start | bytes 49160 | tf_op jit(solution)/shard_map/ppermute | solution.py:570
  57.4 5.9 %collective-permute-start.24 = (f32[32,128]{1,0:T(8,128)S(1)}, f32[32,128]{1,0:T(8,128)S(1)}, u32[]{:S(2)}, u32[]{:S(2)}) collective-permute-start(f32[32,128]{1,0:T(8,128)S(1)} %get-tuple-element.140), channel_id=1, source_target_pairs={{0,2},{1,3},{2,0},{3,1},{4,6},{5,7},{6,4},{7,5},{8,10},{9,11},{10,... | collective-permute-start | bytes 49160 | tf_op jit(solution)/shard_map/ppermute | solution.py:570
  59.8 3.5 %collective-permute-start.25 = (f32[32,128]{1,0:T(8,128)S(1)}, f32[32,128]{1,0:T(8,128)S(1)}, u32[]{:S(2)}, u32[]{:S(2)}) collective-permute-start(f32[32,128]{1,0:T(8,128)S(1)} %get-tuple-element.141), channel_id=1, source_target_pairs={{0,4},{1,5},{2,6},{3,7},{4,0},{5,1},{6,2},{7,3},{8,12},{9,13},{10,... | collective-permute-start | bytes 49160 | tf_op jit(solution)/shard_map/ppermute | solution.py:570
  59.8 3.7 %collective-permute-start.26 = (f32[32,128]{1,0:T(8,128)S(1)}, f32[32,128]{1,0:T(8,128)S(1)}, u32[]{:S(2)}, u32[]{:S(2)}) collective-permute-start(f32[32,128]{1,0:T(8,128)S(1)} %get-tuple-element.142), channel_id=1, source_target_pairs={{0,8},{1,9},{2,10},{3,11},{4,12},{5,13},{6,14},{7,15},{8,0},{9,1},... | collective-permute-start | bytes 49160 | tf_op jit(solution)/shard_map/ppermute | solution.py:570
